TPU v7x, 32 devices: a whole 2x2x4 slice. The times are simulated.
32 devices in a mesh: dp: 8 (over y, x, core), mp: 4 (over z).
Axes of the slice: x: 2, y: 2, z: 4, core: 2. Of those that a mesh axis runs over, the one named last changes fastest.
Arguments:
- tokens_in: bfloat16 [16384, 768], P(('dp', 'mp')), may hold values from -5 to 5
- timesteps: int32 [8], replicated, may hold values from 0 to 999
- lengths: int32 [8], replicated, may hold values from 512 to 2048, as said below
- time_table: bfloat16 [1000, 768], replicated, may hold values from -0.8984375 to 0.8984375
- norm_gains: float32 [2, 768], replicated, may hold values from 0.5 to 1.5
- norm_biases: float32 [2, 768], replicated, may hold values from -0.6 to 0.6
- w_qkv: bfloat16 [3, 768, 768], P(None, 'dp', 'mp'), may hold values from -0.3125 to 0.3125
- qv_bias: float32 [2, 768], replicated, may hold values from -0.42 to 0.42
- w_out: bfloat16 [768, 768], P('mp', 'dp'), may hold values from -0.21875 to 0.21875
- out_bias: float32 [768], replicated, may hold values from -0.6 to 0.6
- w_up: bfloat16 [768, 3072], P('dp', 'mp'), may hold values from -0.21875 to 0.21875
- up_bias: float32 [3072], replicated, may hold values from -0.8 to 0
- w_down: bfloat16 [3072, 768], P('mp', 'dp'), may hold values from -0.109375 to 0.109375
- down_bias: float32 [768], replicated, may hold values from -0.6 to 0.6
- cotangent: bfloat16 [16384, 768], P(('dp', 'mp')), may hold values from -50 to 50
- teacher: bfloat16 [16384, 768], P(('dp', 'mp')), may hold values from -5 to 5
Outputs:
- output: bfloat16 [16384, 768], P(('dp', 'mp'))
- input_grad: float32 [16384, 768], P(('dp', 'mp'))
- table_grad: float32 [1000, 768], replicated
- norm_gain_grad: float32 [2, 768], replicated
- norm_bias_grad: float32 [2, 768], replicated
- w_qkv_grad: float32 [3, 768, 768], P(None, 'dp', 'mp')
- qv_bias_grad: float32 [2, 768], replicated
- w_out_grad: float32 [768, 768], P('mp', 'dp')
- out_bias_grad: float32 [768], replicated
- w_up_grad: float32 [768, 3072], P('dp', 'mp')
- up_bias_grad: float32 [3072], replicated
- w_down_grad: float32 [3072, 768], P('mp', 'dp')
- down_bias_grad: float32 [768], replicated
Inputs may be any that keep to these rules, and one draw needn't show every extreme that they name: Sequence s holds its valid tokens in its first lengths[s] slots and padding after them; some sequence fills all 2048 slots.
All inputs are finite; a program needn't handle non-finite values.
Results may differ from a plain program's by a relative error of at most 0.0095.
The roundings to bfloat16 on the way count: a program that leaves them out, or rounds other values in their place, can miss the bound.
Values may be sent and summed in bfloat16 or wider, within the bound.
No kernel may reach another device: no remote copies, remote signals or barrier semaphores. Data moves between devices by JAX's collectives and lax.ppermute only.
A program may use at most 128 MiB of HBM per device.

v0:
```python
import functools

import jax
import jax.numpy as jnp
from jax import lax
from jax.experimental import pallas as pl
from jax.experimental.pallas import tpu as pltpu
from jax.sharding import PartitionSpec as P

D = 768
HEADS = 12
HEAD_DIM = 64
FF = 3072
MAXLEN = 2048
PAIR = 2 * HEAD_DIM
PAIRS = HEADS // 2
VMEM_LIMIT = 58 << 20
SMALL_COST = pl.CostEstimate(flops=1 << 20, bytes_accessed=1 << 16, transcendentals=0)

far_below = -1e30
epsilon = 1e-05
score_scale = HEAD_DIM ** (-0.5)
low = jnp.bfloat16
full = jnp.float32
both = ("dp", "mp")


def norm_stats(values):
    center = values - jnp.mean(values, axis=-1, keepdims=True)
    spread = jnp.mean(center * center, axis=-1, keepdims=True)
    inverse = lax.rsqrt(spread + epsilon)
    return center * inverse, inverse


def norm_back(unit, inverse, gain_row, grad):
    scaled = grad * gain_row
    mean_scaled = jnp.mean(scaled, axis=-1, keepdims=True)
    mean_unit = jnp.mean(scaled * unit, axis=-1, keepdims=True)
    return (
        inverse * (scaled - mean_scaled - unit * mean_unit),
        jnp.sum(grad * unit, axis=0),
        jnp.sum(grad, axis=0),
    )


def dot_of(left_side, right_side, left_dim, right_dim):
    return lax.dot_general(
        left_side,
        right_side,
        (((left_dim,), (right_dim,)), ((), ())),
        preferred_element_type=full,
    )


def first_half(shape):
    return lax.broadcasted_iota(jnp.int32, shape, len(shape) - 1) < HEAD_DIM


def forward_kernel(numbers, first, scalars, *refs):
    count = len(numbers)
    chunk_refs = refs[:count]
    wk_ref, wv_ref, value_bias_ref = refs[count : count + 3]
    refs = refs[count + 3 :]
    if first:
        wq_ref, query_bias_ref = refs[:2]
        key_outs, value_outs = refs[2 : 2 + count], refs[2 + count : 2 + 2 * count]
        query_out, top_ref, sum_ref, acc_ref = refs[2 + 2 * count :]
        q_pair = (dot_of(chunk_refs[0][...], wq_ref[...], 1, 0) + query_bias_ref[...]).astype(low)
        q_pair = q_pair * jnp.asarray(score_scale, low)
        query_out[...] = q_pair
    else:
        q_ref, top_in, sum_in, acc_in = refs[:4]
        key_outs, value_outs = refs[4 : 4 + count], refs[4 + count : 4 + 2 * count]
        out_ref, log_ref = refs[4 + 2 * count :]
        q_pair = q_ref[...]
    weight = jnp.concatenate([wk_ref[...], wv_ref[...]], axis=1)
    keys = []
    values = []
    for n in range(count):
        both_parts = dot_of(chunk_refs[n][...], weight, 1, 0)
        keys.append(both_parts[:, :PAIR].astype(low))
        values.append((both_parts[:, PAIR:] + value_bias_ref[...]).astype(low))
        key_outs[n][...] = keys[n]
        value_outs[n][...] = values[n]
    rows = q_pair.shape[0]
    size = keys[0].shape[0]
    place = lax.broadcasted_iota(jnp.int32, (1, size), 1)
    lower = first_half((rows, PAIR))
    parts = []
    for half in range(2):
        kept = lower if half == 0 else jnp.logical_not(lower)
        q_half = jnp.where(kept, q_pair, jnp.zeros_like(q_pair))
        scores = []
        for n in range(count):
            bias = jnp.where(place + scalars[numbers[n]] * size < scalars[4], 0.0, far_below)
            scores.append(dot_of(q_half, keys[n], 1, 1) + bias)
        highest = functools.reduce(
            jnp.maximum, [jnp.max(score, axis=-1, keepdims=True) for score in scores]
        )
        totals = jnp.zeros_like(highest)
        mixed = jnp.zeros((rows, PAIR), full)
        for n in range(count):
            exp_scores = jnp.exp(scores[n] - highest)
            totals = totals + jnp.sum(exp_scores, axis=-1, keepdims=True)
            mixed = mixed + dot_of(exp_scores.astype(low), values[n], 1, 0)
        parts.append((highest, totals, mixed))
    top = jnp.where(lower, parts[0][0], parts[1][0])
    total = jnp.where(lower, parts[0][1], parts[1][1])
    mixed = jnp.where(lower, parts[0][2], parts[1][2])
    if first:
        top_ref[...] = top
        sum_ref[...] = total
        acc_ref[...] = mixed
    else:
        highest = jnp.maximum(top, top_in[...])
        here = jnp.exp(top - highest)
        before = jnp.exp(top_in[...] - highest)
        total = total * here + sum_in[...] * before
        out_ref[...] = (mixed * here + acc_in[...] * before) / total
        log_ref[...] = highest + jnp.log(total)


def attend_forward(chunks, numbers, scalars, query_weight, pair_weight, query_bias, value_bias, carried):
    rows = chunks[0].shape[0]
    count = len(chunks)
    first = carried is None
    column = lambda height, c: pl.BlockSpec((height, PAIR), lambda i, n: (0, c * PAIRS + i))
    whole = pl.BlockSpec((rows, D), lambda i, n: (0, 0))
    wide = jax.ShapeDtypeStruct((rows, D), full)
    narrow = jax.ShapeDtypeStruct((rows, D), low)
    extra = (query_weight, query_bias) if first else carried
    results = (narrow, wide, wide, wide) if first else (wide, wide)
    return pl.pallas_call(
        functools.partial(forward_kernel, numbers, first),
        out_shape=(narrow,) * (2 * count) + results,
        grid_spec=pltpu.PrefetchScalarGridSpec(
            num_scalar_prefetch=1,
            grid=(PAIRS,),
            in_specs=[whole] * count
            + [column(D, 0), column(D, 1), column(1, 0)]
            + ([column(D, 0), column(1, 0)] if first else [column(rows, 0)] * 4),
            out_specs=[column(rows, 0)] * (2 * count + len(results)),
        ),
        compiler_params=pltpu.CompilerParams(vmem_limit_bytes=VMEM_LIMIT),
        cost_estimate=SMALL_COST,
        name="attend_forward",
    )(scalars, *chunks, pair_weight, pair_weight, value_bias, *extra)


def backward_kernel(
    number,
    first,
    last,
    scalars,
    q_ref,
    k_ref,
    v_ref,
    g_ref,
    log_ref,
    delta_ref,
    wk_ref,
    wv_ref,
    *refs
):
    if last:
        wq_ref = refs[0]
        refs = refs[1:]
    if not first:
        dq_in = refs[0]
        refs = refs[1:]
    dq_ref, dk_ref, dv_ref, back_ref, accum = refs
    step = pl.program_id(0)
    rows = q_ref.shape[0]
    keys = k_ref.shape[0]
    limit = scalars[4] - scalars[number] * keys
    q_pair = q_ref[...]
    g_pair = g_ref[...]
    k_pair = k_ref[...]
    v_pair = v_ref[...]
    lower = first_half((rows, PAIR))
    lower_keys = first_half((keys, PAIR))
    place = lax.broadcasted_iota(jnp.int32, (keys, 1), 0)
    bias = jnp.where(place < limit, 0.0, far_below)
    dq = []
    dk = []
    dv = []
    for half in range(2):
        kept = lower if half == 0 else jnp.logical_not(lower)
        q_half = jnp.where(kept, q_pair, jnp.zeros_like(q_pair))
        g_half = jnp.where(kept, g_pair, jnp.zeros_like(g_pair))
        log_row = log_ref[0, half : half + 1, :]
        delta_row = delta_ref[0, half : half + 1, :]
        scores = dot_of(k_pair, q_half, 1, 1) + bias
        probs = jnp.exp(scores - log_row)
        dv.append(dot_of(probs.astype(low), g_pair, 1, 0))
        prob_grad = dot_of(v_pair, g_half, 1, 1)
        score_grad = (probs * (prob_grad - delta_row)).astype(low)
        dk.append(dot_of(score_grad, q_pair, 1, 0))
        dq.append(dot_of(score_grad, k_pair, 0, 0))
    dk_low = jnp.where(lower_keys, dk[0], dk[1]).astype(low)
    dv_low = jnp.where(lower_keys, dv[0], dv[1]).astype(low)
    dk_ref[...] = dk_low
    dv_ref[...] = dv_low
    grads = [dk_low, dv_low]
    weights = [wk_ref[...], wv_ref[...]]
    dq_all = jnp.where(lower, dq[0], dq[1])
    if not first:
        dq_all = dq_all + dq_in[...]
    back = dot_of(jnp.concatenate(grads, axis=1), jnp.concatenate(weights, axis=1), 1, 1)
    if last:
        dq_low = (dq_all * score_scale).astype(low)
        dq_ref[...] = dq_low
        back = back + dot_of(dq_low, wq_ref[...], 1, 1)
    else:
        dq_ref[...] = dq_all

    @pl.when(step == 0)
    def _():
        accum[...] = back

    @pl.when(step > 0)
    def _():
        accum[...] += back

    @pl.when(step == PAIRS - 1)
    def _():
        back_ref[...] = accum[...].astype(back_ref.dtype)


def attend_backward(
    number,
    queries,
    keys,
    values,
    grads,
    logs,
    deltas,
    query_weight,
    pair_weight,
    scalars,
    carried,
    last,
):
    rows, total = queries.shape[0], keys.shape[0]
    first = carried is None
    column = lambda count, c: pl.BlockSpec((count, PAIR), lambda i, n: (0, c * PAIRS + i))
    stats = pl.BlockSpec((1, 2, rows), lambda i, n: (i, 0, 0))
    extra = (query_weight,) * last + (() if first else (carried,))
    extra_specs = [column(D, 0)] * last + ([] if first else [column(rows, 0)])
    return pl.pallas_call(
        functools.partial(backward_kernel, number, first, last),
        out_shape=(
            jax.ShapeDtypeStruct((rows, D), low if last else full),
            jax.ShapeDtypeStruct((total, D), low),
            jax.ShapeDtypeStruct((total, D), low),
            jax.ShapeDtypeStruct((total, D), low if first else full),
        ),
        grid_spec=pltpu.PrefetchScalarGridSpec(
            num_scalar_prefetch=1,
            grid=(PAIRS,),
            in_specs=[
                column(rows, 0),
                column(total, 0),
                column(total, 0),
                column(rows, 0),
                stats,
                stats,
                column(D, 0),
                column(D, 1),
            ]
            + extra_specs,
            out_specs=[
                column(rows, 0),
                column(total, 0),
                column(total, 0),
                pl.BlockSpec((total, D), lambda i, n: (0, 0)),
            ],
            scratch_shapes=[pltpu.VMEM((total, D), full)],
        ),
        compiler_params=pltpu.CompilerParams(vmem_limit_bytes=VMEM_LIMIT),
        cost_estimate=SMALL_COST,
        name="attend_backward",
    )(
        scalars,
        queries,
        keys,
        values,
        grads,
        logs,
        deltas,
        pair_weight,
        pair_weight,
        *extra,
    )


def swap(value, axis, bit):
    count = lax.axis_size(axis)
    return lax.ppermute(value, axis, [(i, i ^ bit) for i in range(count)])


class Order:
    def __init__(self):
        self.marks = ()

    def __call__(self, *values):
        values = lax.optimization_barrier(values + self.marks)[: len(values)]
        self.marks = values
        return values[0] if len(values) == 1 else values


def outer_bits():
    bits = []
    bit = 2
    while bit < lax.axis_size("dp"):
        bits.append(bit)
        bit *= 2
    return bits


class Gather:
    def __init__(self, parts):
        self.bits = outer_bits()
        half = len(self.bits) // 2
        self.orders = [
            self.bits[half * (n % 2) :] + self.bits[: half * (n % 2)] for n in range(len(parts))
        ]
        self.result = [[([0], part)] for part in parts]
        self.step = 0

    def advance(self, order):
        held = self.result
        if self.step < len(self.bits):
            masks = [[m for mask, _ in pieces for m in mask] for pieces in held]
            blocks = [
                jnp.concatenate([array for _, array in pieces]) if self.step else pieces[0][1]
                for pieces in held
            ]
            blocks = order(*blocks)
            bits = [turn[self.step] for turn in self.orders]
            self.result = [
                [(mask, block), ([m ^ bit for m in mask], swap(block, "dp", bit))]
                for mask, block, bit in zip(masks, blocks, bits)
            ]
        else:
            arrays = order(*[array for pieces in held for _, array in pieces])
            arrays = iter(arrays)
            self.result = []
            for pieces in held:
                kept = [(masks, next(arrays)) for masks, _ in pieces]
                self.result.append(
                    kept + [([m ^ 1 for m in masks], swap(array, "dp", 1)) for masks, array in kept]
                )
        self.step += 1


def canonical_row(me, rank, block, mask, rank_mask, stride, offset):
    if mask is None:
        return offset
    row = (me ^ mask) * block + offset
    if stride:
        row = row + (rank ^ rank_mask) * stride
    return pl.multiple_of(row, 16)


def place_kernel(plan, block, *refs):
    count = len(plan)
    ins = refs[:count]
    outs = refs[count:-1]
    sems = refs[-1]
    me = lax.axis_index("dp")
    rank = lax.axis_index("mp")
    copies = []
    for ref, moves in zip(ins, plan):
        for start, size, which, mask, column, _, offset in moves:
            row = canonical_row(me, rank, block, mask, 0, 0, offset)
            copy = pltpu.make_async_copy(
                ref.at[pl.ds(start, size), :],
                outs[which].at[pl.ds(row, size), pl.ds(column * D, D)],
                sems.at[len(copies)],
            )
            copy.start()
            copies.append(copy)
    for copy in copies:
        copy.wait()


def plan_of(gathered, layouts):
    arrays = []
    plan = []
    for pieces, layout in zip(gathered, layouts):
        rows = sum(size for _, size, *_ in layout)
        for masks, array in pieces:
            moves = []
            for j, mask in enumerate(masks):
                for start, size, which, rank_mask, stride, offset in layout:
                    moves.append((j * rows + start, size, which, mask, rank_mask, stride, offset))
            arrays.append(array)
            plan.append(moves)
    return arrays, plan


def place(arrays, plan, block, shapes):
    return pl.pallas_call(
        functools.partial(place_kernel, plan, block),
        out_shape=[jax.ShapeDtypeStruct(shape, low) for shape in shapes],
        in_specs=[pl.BlockSpec(memory_space=pl.ANY)] * len(arrays),
        out_specs=[pl.BlockSpec(memory_space=pltpu.VMEM)] * len(shapes),
        scratch_shapes=[pltpu.SemaphoreType.DMA((sum(len(moves) for moves in plan),))],
        compiler_params=pltpu.CompilerParams(vmem_limit_bytes=VMEM_LIMIT),
        cost_estimate=SMALL_COST,
        name="place",
    )(*arrays)


def middle_kernel(plan, block, total, *refs):
    limit_ref, vector_ref = refs[:2]
    token_hbm, mixed_hbm, log_hbm, cot_hbm, teach_hbm = refs[2:7]
    pieces = refs[7 : 7 + total]
    (
        out_hbm,
        final_hbm,
        act_hbm,
        pre_hbm,
        second_hbm,
        middle_low_hbm,
        attended_hbm,
        middle_hbm,
        grad_hbm,
        delta_ref,
        log_ref,
        sum_ref,
    ) = refs[7 + total : 19 + total]
    (
        token,
        mixed,
        logs,
        cot,
        teach,
        up,
        down,
        proj,
        act,
        pre,
        slope,
        second,
        attended,
        middle,
        final,
        out,
        final_low,
        middle_low,
        grad,
        accum,
        in_sems,
        weight_sems,
        out_sems,
    ) = refs[19 + total :]
    targets = (up, down, proj)
    rows = token.shape[0]
    me = lax.axis_index("dp")
    rank = lax.axis_index("mp")

    def fetch(ref, scratch, n):
        copy = pltpu.make_async_copy(ref, scratch, in_sems.at[n])
        copy.start()
        return copy

    def send(scratch, ref, n):
        copy = pltpu.make_async_copy(scratch, ref, out_sems.at[n])
        copy.start()
        return copy

    gets = [
        fetch(token_hbm, token, 0),
        fetch(mixed_hbm, mixed, 1),
        fetch(log_hbm, logs, 2),
        fetch(cot_hbm, cot, 3),
        fetch(teach_hbm, teach, 4),
    ]
    loads = {0: [], 1: [], 2: []}
    number = 0
    for want in (2, 0, 1):
        for ref, moves in zip(pieces, plan):
            for start, size, which, mask, rank_mask, stride, offset in moves:
                if which != want:
                    continue
                row = canonical_row(me, rank, block, mask, rank_mask, stride, offset)
                copy = pltpu.make_async_copy(
                    ref.at[pl.ds(start, size), :],
                    targets[which].at[pl.ds(row, size), :],
                    weight_sems.at[number],
                )
                copy.start()
                loads[which].append(copy)
                number += 1

    table_row = vector_ref[0:1, :]
    out_bias = vector_ref[1:2, :]
    gain = vector_ref[2:3, :]
    shift = vector_ref[3:4, :]
    down_bias = vector_ref[4:5, :]
    weight = vector_ref[5:6, :]
    gets[0].wait()
    gets[1].wait()
    attended[...] = mixed[...].astype(low)
    puts = [send(attended, attended_hbm, 0)]
    for copy in loads[2]:
        copy.wait()
    state = token[...].astype(full) + table_row + out_bias
    state = state + dot_of(attended[...], proj[...], 1, 1)
    middle[...] = state
    unit, _ = norm_stats(state)
    second[...] = (unit * gain + shift).astype(low)
    puts.append(send(second, second_hbm, 1))
    accum[...] = jnp.zeros((rows, D), full)
    for copy in loads[0]:
        copy.wait()
    for copy in loads[1]:
        copy.wait()

    def forward(m, _):
        place = pl.ds(pl.multiple_of(m * D, D), D)
        value = dot_of(second[...], up[place, :], 1, 0) + vector_ref[pl.ds(8 + m, 1), :]
        cumulative = 0.5 + 0.5 * lax.erf(value * (0.5**0.5))
        act[m] = (value * cumulative).astype(low)
        slope[m] = cumulative + value * jnp.exp(-0.5 * value * value) * 0.3989422804014327
        accum[...] += dot_of(act[m], down[place, :], 1, 1)
        return 0

    lax.fori_loop(0, FF // D, forward, 0)
    puts.append(send(act, act_hbm, 2))
    final_state = middle[...] + accum[...] + down_bias
    out[...] = final_state.astype(low)
    puts.append(send(out, out_hbm, 3))
    gets[3].wait()
    gets[4].wait()
    place = lax.broadcasted_iota(jnp.int32, (rows, 1), 0)
    grads = cot[...].astype(full) + weight * (final_state - teach[...].astype(full))
    grads = jnp.where(place < limit_ref[5], grads, 0.0)
    final[...] = grads
    final_low[...] = grads.astype(low)
    puts.append(send(final_low, final_hbm, 4))
    sum_ref[3:4, :] = jnp.sum(grads, axis=0, keepdims=True)
    accum[...] = jnp.zeros((rows, D), full)

    def backward(m, _):
        place = pl.ds(pl.multiple_of(m * D, D), D)
        value = slope[m] * dot_of(final_low[...], down[place, :], 1, 0)
        value = value.astype(low)
        pre[m] = value
        sum_ref[pl.ds(8 + m, 1), :] = jnp.sum(value.astype(full), axis=0, keepdims=True)
        accum[...] += dot_of(value, up[place, :], 1, 1)
        return 0

    lax.fori_loop(0, FF // D, backward, 0)
    puts.append(send(pre, pre_hbm, 5))
    unit, inverse = norm_stats(middle[...])
    second_grad = accum[...]
    sum_ref[0:1, :] = jnp.sum(second_grad * unit, axis=0, keepdims=True)
    sum_ref[1:2, :] = jnp.sum(second_grad, axis=0, keepdims=True)
    scaled = second_grad * gain
    mean_scaled = jnp.mean(scaled, axis=-1, keepdims=True)
    mean_unit = jnp.mean(scaled * unit, axis=-1, keepdims=True)
    total_grad = final[...] + inverse * (scaled - mean_scaled - unit * mean_unit)
    middle[...] = total_grad
    puts.append(send(middle, middle_hbm, 6))
    middle_low[...] = total_grad.astype(low)
    puts.append(send(middle_low, middle_low_hbm, 7))
    sum_ref[2:3, :] = jnp.sum(total_grad, axis=0, keepdims=True)
    attended_grad = dot_of(middle_low[...], proj[...], 1, 0).astype(low)
    grad[...] = attended_grad
    puts.append(send(grad, grad_hbm, 8))
    gets[2].wait()
    head = lax.broadcasted_iota(jnp.int32, (16, D), 0)
    lane = lax.broadcasted_iota(jnp.int32, (16, D), 1)
    member = jnp.where(lane // HEAD_DIM == head, 1.0, 0.0)
    leader = jnp.where(lane == head * HEAD_DIM, 1.0, 0.0)
    exact = functools.partial(
        lax.dot_general,
        dimension_numbers=(((1,), (1,)), ((), ())),
        precision=lax.Precision.HIGHEST,
        preferred_element_type=full,
    )
    deltas = exact(member, attended_grad.astype(full) * mixed[...])
    tops = exact(leader, logs[...])
    for pair in range(PAIRS):
        delta_ref[pair] = deltas[2 * pair : 2 * pair + 2]
        log_ref[pair] = tops[2 * pair : 2 * pair + 2]
    for copy in puts:
        copy.wait()


def middle_call(limit, vectors, tokens, mixed, logs, cot, teach, arrays, plan, block):
    rows = tokens.shape[0]
    hidden = FF // D
    narrow = jax.ShapeDtypeStruct((rows, D), low)
    wide = jax.ShapeDtypeStruct((rows, D), full)
    many = jax.ShapeDtypeStruct((hidden, rows, D), low)
    stats = jax.ShapeDtypeStruct((PAIRS, 2, rows), full)
    anywhere = pl.BlockSpec(memory_space=pl.ANY)
    inside = pl.BlockSpec(memory_space=pltpu.VMEM)
    moves = sum(len(part) for part in plan)
    return pl.pallas_call(
        functools.partial(middle_kernel, plan, block, len(arrays)),
        out_shape=(
            narrow,
            narrow,
            many,
            many,
            narrow,
            narrow,
            narrow,
            wide,
            narrow,
            stats,
            stats,
            jax.ShapeDtypeStruct((8 + 8, D), full),
        ),
        in_specs=[pl.BlockSpec(memory_space=pltpu.SMEM), inside]
        + [anywhere] * (5 + len(arrays)),
        out_specs=[anywhere] * 9 + [inside] * 3,
        scratch_shapes=[
            pltpu.VMEM((rows, D), low),
            pltpu.VMEM((rows, D), full),
            pltpu.VMEM((rows, D), full),
            pltpu.VMEM((rows, D), low),
            pltpu.VMEM((rows, D), low),
            pltpu.VMEM((FF, D), low),
            pltpu.VMEM((FF, D), low),
            pltpu.VMEM((D, D), low),
            pltpu.VMEM((hidden, rows, D), low),
            pltpu.VMEM((hidden, rows, D), low),
            pltpu.VMEM((hidden, rows, D), full),
            pltpu.VMEM((rows, D), low),
            pltpu.VMEM((rows, D), low),
            pltpu.VMEM((rows, D), full),
            pltpu.VMEM((rows, D), full),
            pltpu.VMEM((rows, D), low),
            pltpu.VMEM((rows, D), low),
            pltpu.VMEM((rows, D), low),
            pltpu.VMEM((rows, D), low),
            pltpu.VMEM((rows, D), full),
            pltpu.SemaphoreType.DMA((5,)),
            pltpu.SemaphoreType.DMA((moves,)),
            pltpu.SemaphoreType.DMA((9,)),
        ],
        compiler_params=pltpu.CompilerParams(vmem_limit_bytes=VMEM_LIMIT),
        cost_estimate=SMALL_COST,
        name="middle",
    )(limit, vectors, tokens, mixed, logs, cot, teach, *arrays)


def feed_grad_kernel(
    final_ref, act_ref, second_ref, pre_ref, middle_ref, attended_ref, *refs
):
    down_keep, down_send, up_keep, up_send, left, right = refs
    block = down_keep.shape[2]
    m = pl.program_id(0)
    even = lax.axis_index("dp") % 2 == 0

    @pl.when(m == 0)
    def _():
        left[...] = final_ref[...].T
        right[...] = second_ref[...].T

    def store(value, keep, send, index):
        for outer in range(down_keep.shape[1]):
            first = value[2 * outer * block : (2 * outer + 1) * block]
            other = value[(2 * outer + 1) * block : (2 * outer + 2) * block]
            keep[index, outer] = jnp.where(even, first, other).astype(low)
            send[index, outer] = jnp.where(even, other, first).astype(low)

    @pl.when(m < FF // D)
    def _():
        store(dot_of(left[...], act_ref[0], 1, 0), down_keep, down_send, 0)
        store(dot_of(right[...], pre_ref[0], 1, 0), up_keep, up_send, 0)

    @pl.when(m == FF // D)
    def _():
        store(dot_of(middle_ref[...].T, attended_ref[...], 1, 0), up_keep, up_send, 0)


def feed_grads(final_low, act, second, pre, middle_low, attended, dp):
    rows = final_low.shape[0]
    hidden = FF // D
    whole = pl.BlockSpec((rows, D), lambda m: (0, 0))
    last = hidden - 1
    slice_of = pl.BlockSpec((1, rows, D), lambda m: (jnp.minimum(m, last), 0, 0))
    shape = (hidden, dp // 2, D // dp, D)
    longer = (hidden + 1,) + shape[1:]
    down_spec = pl.BlockSpec((1,) + shape[1:], lambda m: (jnp.minimum(m, last), 0, 0, 0))
    up_spec = pl.BlockSpec((1,) + shape[1:], lambda m: (m, 0, 0, 0))
    return pl.pallas_call(
        feed_grad_kernel,
        out_shape=[jax.ShapeDtypeStruct(shape, low)] * 2
        + [jax.ShapeDtypeStruct(longer, low)] * 2,
        grid=(hidden + 1,),
        in_specs=[whole, slice_of, whole, slice_of, whole, whole],
        out_specs=[down_spec, down_spec, up_spec, up_spec],
        scratch_shapes=[pltpu.VMEM((D, rows), low)] * 2,
        compiler_params=pltpu.CompilerParams(vmem_limit_bytes=VMEM_LIMIT),
        cost_estimate=SMALL_COST,
        name="feed_grads",
    )(final_low, act, second, pre, middle_low, attended)


def qkv_grad_kernel(count, *refs):
    chunk_refs = refs[:count]
    query_ref = refs[count]
    key_refs = refs[count + 1 : 2 * count + 1]
    value_refs = refs[2 * count + 1 : 3 * count + 1]
    keep_ref, send_ref, sum_ref, turned = refs[3 * count + 1 :]
    block = keep_ref.shape[2]
    rows = query_ref.shape[0]
    c = pl.program_id(0)
    even = lax.axis_index("dp") % 2 == 0
    ones = jnp.ones((16, rows), low)

    def store(value):
        for outer in range(keep_ref.shape[1]):
            first = value[2 * outer * block : (2 * outer + 1) * block]
            other = value[(2 * outer + 1) * block : (2 * outer + 2) * block]
            keep_ref[0, outer] = jnp.where(even, first, other).astype(low)
            send_ref[0, outer] = jnp.where(even, other, first).astype(low)

    @pl.when(c == 0)
    def _():
        for n in range(count):
            turned[n] = chunk_refs[n][...].T
        store(dot_of(turned[0], query_ref[...], 1, 0))
        sum_ref[0:8, :] = dot_of(ones, query_ref[...], 1, 0)[0:8]

    def many(sources):
        value = dot_of(turned[0], sources[0][...], 1, 0)
        for n in range(1, count):
            value = value + dot_of(turned[n], sources[n][...], 1, 0)
        store(value)

    @pl.when(c == 1)
    def _():
        many(key_refs)

    @pl.when(c == 2)
    def _():
        many(value_refs)
        value = dot_of(ones, value_refs[0][...], 1, 0)
        for n in range(1, count):
            value = value + dot_of(ones, value_refs[n][...], 1, 0)
        sum_ref[8:16, :] = value[0:8]


def qkv_grads(chunks, query_grad, key_grads, value_grads, dp):
    rows = query_grad.shape[0]
    count = len(chunks)
    whole = pl.BlockSpec((rows, D), lambda c: (0, 0))
    shape = (3, dp // 2, D // dp, D)
    part = pl.BlockSpec((1,) + shape[1:], lambda c: (c, 0, 0, 0))
    return pl.pallas_call(
        functools.partial(qkv_grad_kernel, count),
        out_shape=[jax.ShapeDtypeStruct(shape, low)] * 2
        + [jax.ShapeDtypeStruct((16, D), full)],
        grid=(3,),
        in_specs=[whole] * (3 * count + 1),
        out_specs=[part, part, pl.BlockSpec((16, D), lambda c: (0, 0))],
        scratch_shapes=[pltpu.VMEM((count, D, rows), low)],
        compiler_params=pltpu.CompilerParams(vmem_limit_bytes=VMEM_LIMIT),
        cost_estimate=SMALL_COST,
        name="qkv_grads",
    )(*chunks, query_grad, *key_grads, *value_grads)


def two_parts(value, axis, mine):
    keep = lax.dynamic_index_in_dim(value, mine, axis, keepdims=False)
    send = lax.dynamic_index_in_dim(value, 1 - mine, axis, keepdims=False)
    return keep, send.astype(low)


def scatter_dp(parts):
    bits = outer_bits()
    half = len(bits) // 2
    orders = [bits[half * (n % 2) :] + bits[: half * (n % 2)] for n in range(len(parts))]
    me = lax.axis_index("dp")
    sends = yield [send for _, send in parts]
    held = [
        (keep.astype(full) + swap(send, "dp", 1).astype(full)).astype(low)
        for (keep, _), send in zip(parts, sends)
    ]
    held = [
        value.reshape(value.shape[:1] + (2,) * len(bits) + value.shape[2:]) for value in held
    ]
    axes = [list(reversed(bits)) for _ in parts]
    for step in range(len(bits)):
        parts = []
        for n, value in enumerate(held):
            bit = orders[n][step]
            axis = 1 + axes[n].index(bit)
            axes[n].remove(bit)
            parts.append(two_parts(value, axis, (me // bit) % 2))
        sends = yield [send for _, send in parts]
        held = [
            keep.astype(full) + swap(sends[n], "dp", orders[n][step]).astype(full)
            for n, (keep, _) in enumerate(parts)
        ]
        if step < len(bits) - 1:
            held = [value.astype(low) for value in held]
    return held


def scatter_mp(values):
    rank = lax.axis_index("mp")
    for bit in (2, 1):
        parts = []
        for value in values:
            pair = value.reshape((2, value.shape[0] // 2) + value.shape[1:])
            parts.append(two_parts(pair, 0, (rank // bit) % 2))
        sends = yield [send for _, send in parts]
        values = [
            keep.astype(full) + swap(send, "mp", bit).astype(full)
            for (keep, _), send in zip(parts, sends)
        ]
    return [value[0] for value in values]


def scatter_feed(up_parts, down_parts):
    mp = lax.axis_size("mp")
    up_own, down_own = yield from scatter_dp([up_parts, down_parts])
    block = down_own.shape[1]
    out_own = up_own[mp].reshape(block, mp, -1).transpose(1, 0, 2)
    tall, out_grad = yield from scatter_mp(
        [jnp.concatenate([up_own[:mp], down_own], axis=1), out_own]
    )
    return tall[:block], tall[block:].T, out_grad.T


def scatter_qkv(keep, send):
    rank = lax.axis_index("mp")
    left_part, right_part = yield from scatter_dp(
        [(keep[..., : D // 2], send[..., : D // 2]), (keep[..., D // 2 :], send[..., D // 2 :])]
    )
    upper = rank >= 2
    odd = rank % 2 == 1
    (send,) = yield [jnp.where(upper, left_part, right_part).astype(low)]
    keep = jnp.where(upper, right_part, left_part) + swap(send, "mp", 2).astype(full)
    width = D // lax.axis_size("mp")
    (send,) = yield [jnp.where(odd, keep[..., :width], keep[..., width:]).astype(low)]
    return jnp.where(odd, keep[..., width:], keep[..., :width]) + swap(
        send, "mp", 1
    ).astype(full)


def butterfly(value):
    for bit in [1] + outer_bits():
        (value,) = yield [value]
        value = value + swap(value, "dp", bit)
    for bit in (1, 2):
        (value,) = yield [value]
        value = value + swap(value, "mp", bit)
    return value


class Steps:
    def __init__(self, steps):
        self.steps = steps
        self.pending = next(steps)
        self.result = None

    def advance(self, order):
        if self.pending is None:
            return
        sends = order(*self.pending)
        sends = [sends] if len(self.pending) == 1 else list(sends)
        try:
            self.pending = self.steps.send(sends)
        except StopIteration as stop:
            self.pending = None
            self.result = stop.value

    def finish(self, order):
        while self.pending is not None:
            self.advance(order)
        return self.result


def shards(
    tokens_in,
    timesteps,
    lengths,
    time_table,
    norm_gains,
    norm_biases,
    w_qkv,
    qv_bias,
    w_out,
    out_bias,
    w_up,
    up_bias,
    w_down,
    down_bias,
    cotangent,
    teacher,
):
    rank = lax.axis_index("mp")
    data_rank = lax.axis_index("dp")
    mp = lax.axis_size("mp")
    dp = lax.axis_size("dp")
    own_rows = tokens_in.shape[0]
    length = lax.dynamic_index_in_dim(lengths, data_rank, keepdims=False)
    own_time = lax.dynamic_index_in_dim(timesteps, data_rank, keepdims=False)
    odd = rank % 2 == 1
    upper = rank >= 2
    middle = jnp.logical_or(rank == 1, rank == 2)
    order = Order()
    along = lambda value, pairs: lax.ppermute(value, "mp", pairs)

    block = w_qkv.shape[1]
    aligned = block % 32 == 0
    narrow = order(jnp.concatenate([w_qkv.reshape(3 * block, -1), w_out.T]))
    first_swap = swap(narrow, "mp", 1)
    up_own = order(w_up)
    up_swap = swap(up_own, "mp", 1)
    pair = order(
        jnp.concatenate(
            [jnp.where(odd, first_swap, narrow), jnp.where(odd, narrow, first_swap)], axis=1
        )
    )
    second_swap = swap(pair, "mp", 2)
    tokens, lengths, own_time, norm_gains, norm_biases, out_bias, down_bias, up_bias, length = order(
        tokens_in, lengths, own_time, norm_gains, norm_biases, out_bias, down_bias, up_bias, length
    )
    table_row = lax.dynamic_slice_in_dim(time_table, own_time, 1).astype(full)
    unit_one, _ = norm_stats(tokens.astype(full) + table_row)
    first_norm = (unit_one * norm_gains[0] + norm_biases[0]).astype(low)
    loss_weight = lengths.shape[0] * MAXLEN / jnp.sum(lengths).astype(full)
    vectors = jnp.concatenate(
        [
            table_row,
            out_bias[None],
            norm_gains[1:2],
            norm_biases[1:2],
            down_bias[None],
            jnp.full((3, D), loss_weight),
            up_bias.reshape(-1, D),
            jnp.zeros((4, D), full),
        ]
    )
    scalars = jnp.stack(
        [
            rank,
            jnp.where(rank == 0, 1, rank - 1),
            jnp.where(upper, rank - 2, rank + 2),
            jnp.where(middle, rank + 1, 3 - rank),
            length,
            length - rank * own_rows,
        ]
    ).astype(jnp.int32)
    first_norm, vectors, scalars = order(first_norm, vectors, scalars)
    wide = jnp.concatenate(
        [jnp.where(upper, second_swap, pair), jnp.where(upper, pair, second_swap)], axis=1
    )
    qkv_rows, out_rows = wide[: 3 * block], wide[3 * block :]
    if aligned:
        split = 3 * block // 2
        qkv_gather = Gather([qkv_rows[:split], qkv_rows[split:]])
        qkv_gather.advance(order)
    sent, up_pair = order(first_norm, jnp.concatenate([up_own, up_swap]))
    from_left = along(sent, [(0, 1), (1, 2), (2, 3)])
    from_right = along(sent, [(1, 0), (2, 1), (3, 2)])
    down_own = order(w_down.T)
    down_swap = swap(down_own, "mp", 1)
    up_other = swap(up_pair, "mp", 2)

    if aligned:
        while qkv_gather.step < len(qkv_gather.bits):
            qkv_gather.advance(order)
    hop_right, hop_left = order(from_left, from_right)
    second_right = along(hop_right, [(1, 2), (2, 3)])
    second_left = along(hop_left, [(1, 0), (2, 1)])
    near = jnp.where(rank == 0, hop_left, hop_right)
    if aligned:
        qkv_gather.advance(order)
        arrays, plan = plan_of(
            qkv_gather.result,
            [
                [(0, block, 0, 0, 0, 0), (block, split - block, 1, 0, 0, 0)],
                [
                    (0, 2 * block - split, 1, 0, 0, split - block),
                    (2 * block - split, block, 1, 1, 0, 0),
                ],
            ],
        )
        query_weight, pair_weight = place(arrays, plan, block, [(D, D), (D, 2 * D)])
    else:
        weights = lax.all_gather(qkv_rows.reshape(3, block, D), "dp", axis=1, tiled=True)
        query_weight = weights[0]
        pair_weight = jnp.concatenate([weights[1], weights[2]], axis=1)
    down_pair, up_other, query_weight, pair_weight = order(
        jnp.concatenate([down_own, down_swap]), up_other, query_weight, pair_weight
    )
    down_other = swap(down_pair, "mp", 2)

    if aligned:
        ups = Gather([up_pair, up_other])
        ups.advance(order)
    attend = lambda chunks, numbers, carried: order(
        *attend_forward(
            chunks,
            numbers,
            scalars,
            query_weight,
            pair_weight,
            qv_bias[0:1],
            qv_bias[1:2],
            carried,
        )
    )
    key_own, key_near, value_own, value_near, queries, *state = attend(
        [first_norm, near], (0, 1), None
    )
    if aligned:
        while ups.step < len(ups.bits):
            ups.advance(order)
    second = order(jnp.where(upper, second_right, second_left))
    third = along(second, [(1, 0), (2, 3)])
    if aligned:
        downs = Gather(
            [
                jnp.concatenate([down_pair, out_rows[: block // 2]]),
                jnp.concatenate([down_other, out_rows[block // 2 :]]),
            ]
        )
        downs.advance(order)
        ups.advance(order)
        while downs.step < len(downs.bits):
            downs.advance(order)
    last = order(jnp.where(middle, hop_left, third))
    key_second, key_last, value_second, value_last, mixed, logs = attend(
        [second, last], (2, 3), (queries, *state)
    )
    if aligned:
        downs.advance(order)
        up_arrays, up_plan = plan_of(
            ups.result,
            [
                [(0, block, 0, 0, D, 0), (block, block, 0, 1, D, 0)],
                [(0, block, 0, 2, D, 0), (block, block, 0, 3, D, 0)],
            ],
        )
        down_arrays, down_plan = plan_of(
            downs.result,
            [
                [
                    (0, block, 1, 0, D, 0),
                    (block, block, 1, 1, D, 0),
                    (2 * block, block // 2, 2, 0, 0, 0),
                ],
                [
                    (0, block, 1, 2, D, 0),
                    (block, block, 1, 3, D, 0),
                    (2 * block, block // 2, 2, 0, 0, block // 2),
                ],
            ],
        )
        arrays, plan = up_arrays + down_arrays, up_plan + down_plan
    else:
        arrays = [
            lax.all_gather(w_up, ("mp", "dp"), axis=0, tiled=True),
            lax.all_gather(w_down.T, ("mp", "dp"), axis=0, tiled=True),
            lax.all_gather(out_rows, "dp", axis=0, tiled=True),
        ]
        plan = [[(0, array.shape[0], n, None, 0, 0, 0)] for n, array in enumerate(arrays)]
    chunks = [first_norm, near, second, last]
    keys = [key_own, key_near, key_second, key_last]
    values = [value_own, value_near, value_second, value_last]

    (
        output,
        final_low,
        hidden_act,
        pre_grad,
        second_norm,
        middle_low,
        attended,
        middle_grad,
        attended_grad,
        deltas,
        log_rows,
        sums,
    ) = middle_call(
        scalars, vectors, tokens, mixed, logs, cotangent, teacher, arrays, plan, block
    )
    gain_two, shift_two, middle_sum, final_sum = sums[0], sums[1], sums[2], sums[3]
    down_keep, down_send, up_keep, up_send = feed_grads(
        final_low, hidden_act, second_norm, pre_grad, middle_low, attended, dp
    )

    feed = Steps(scatter_feed((up_keep, up_send), (down_keep, down_send)))
    key_grads = [None] * 4
    value_grads = [None] * 4
    firsts = [None] * 4
    query_grad = None
    feed.advance(order)
    for n in (3, 2, 1, 0):
        query_grad, key_grads[n], value_grads[n], firsts[n] = attend_backward(
            n,
            queries,
            keys[n],
            values[n],
            order(attended_grad),
            log_rows,
            deltas,
            query_weight,
            pair_weight,
            scalars,
            query_grad,
            n == 0,
        )
        firsts[n] = order(firsts[n])
        if n == 3:
            back_last = along(firsts[3], [(0, 1), (3, 2)]).astype(full)
            feed.advance(order)
        elif n == 2:
            payload = order((firsts[2] + back_last).astype(low))
            back_right = along(payload, [(0, 1), (1, 2)]).astype(full)
            back_left = along(payload, [(3, 2), (2, 1)]).astype(full)
        elif n == 1:
            feed.advance(order)
            to_right = jnp.where(
                rank == 0, firsts[1], firsts[3].astype(full) + back_right
            ).astype(low)
            to_left = (firsts[1] + back_left).astype(low)
            to_right, to_left = order(to_right, to_left)
            final_right = along(to_right, [(0, 1), (1, 2), (2, 3)])
            final_left = along(to_left, [(3, 2), (2, 1), (1, 0)])
    query_grad, final_right, final_left = order(query_grad, final_right, final_left)
    qkv_keep, qkv_send, bias_sums = qkv_grads(chunks, query_grad, key_grads, value_grads, dp)
    qkv = Steps(scatter_qkv(qkv_keep, qkv_send))
    qkv.advance(order)
    feed.advance(order)
    qkv.advance(order)
    tokens, first_own = order(tokens, firsts[0])
    first_grad = first_own + final_right.astype(full) + final_left.astype(full)
    unit_one, inverse_one = norm_stats(tokens.astype(full) + table_row)
    start_part, gain_one, shift_one = norm_back(
        unit_one, inverse_one, norm_gains[0], first_grad
    )
    input_grad = middle_grad + start_part
    sequence_sum = jnp.sum(input_grad, axis=0)
    own_slot = (jnp.arange(dp) == data_rank).astype(full)
    packed = jnp.concatenate(
        [
            jnp.stack([gain_one, gain_two, shift_one, shift_two]),
            jnp.stack([bias_sums[0], bias_sums[8]]),
            jnp.stack([middle_sum, final_sum]),
            sums[8 : 8 + FF // D],
            own_slot[:, None] * sequence_sum[None, :],
        ]
    )
    small = Steps(butterfly(packed))
    small.advance(order)
    small.advance(order)
    qkv.advance(order)
    small.advance(order)
    feed.advance(order)
    small.advance(order)
    qkv.advance(order)
    small.advance(order)
    qkv_grad = qkv.finish(order)
    total = small.finish(order)
    up_grad, down_grad, out_grad = feed.finish(order)
    fixed = 8 + FF // D
    chosen = (timesteps[None, :] == jnp.arange(time_table.shape[0])[:, None]).astype(full)
    table_grad = lax.dot_general(
        chosen,
        total[fixed:],
        (((1,), (0,)), ((), ())),
        precision=lax.Precision.HIGHEST,
        preferred_element_type=full,
    )
    return (
        output,
        input_grad,
        table_grad,
        total[0:2],
        total[2:4],
        qkv_grad,
        total[4:6],
        out_grad,
        total[6],
        up_grad,
        total[8:fixed].reshape(FF),
        down_grad,
        total[7],
    )


def solution(mesh):
    rows = P(both, None)
    placed = (
        rows,
        P(),
        P(),
        P(),
        P(),
        P(),
        P(None, "dp", "mp"),
        P(),
        P("mp", "dp"),
        P(),
        P("dp", "mp"),
        P(),
        P("mp", "dp"),
        P(),
        rows,
        rows,
    )
    return jax.shard_map(
        shards,
        mesh=mesh,
        in_specs=placed,
        out_specs=(
            rows,
            rows,
            P(),
            P(),
            P(),
            P(None, "dp", "mp"),
            P(),
            P("mp", "dp"),
            P(),
            P("dp", "mp"),
            P(),
            P("mp", "dp"),
            P(),
        ),
        check_vma=False,
    )
```

profile of v0, /device:TPU:0, one launch (start us, length us, event | category | flops | bytes accessed | tf_op | source)
XLA Modules:
  0.0 408.3 jit_solution(13640055809543667082)
XLA Ops:
  37.4 12.2 %collective-permute-done.3 = bf16[512,768]{1,0:T(8,128)(2,1)S(1)} collective-permute-done((bf16[512,768]{1,0:T(8,128)(2,1)S(1)}, bf16[512,768]{1,0:T(8,128)(2,1)S(1)}, u32[]{:S(2)}, u32[]{:S(2)}) %collective-permute-start.3) | collective-permute-done | bytes 786464 | tf_op jit(solution)/shard_map/ppermute | solution.py:914
  49.6 4.2 %collective-permute-done.4 = bf16[512,768]{1,0:T(8,128)(2,1)S(1)} collective-permute-done((bf16[512,768]{1,0:T(8,128)(2,1)S(1)}, bf16[512,768]{1,0:T(8,128)(2,1)S(1)}, u32[]{:S(2)}, u32[]{:S(2)}) %collective-permute-start.4) | collective-permute-done | bytes 786464 | tf_op jit(solution)/shard_map/ppermute | solution.py:914
  54.4 3.3 collective-permute-start.10
  62.5 4.2 %place.1 = (bf16[768,768]{1,0:T(8,128)(2,1)}, bf16[768,1536]{1,0:T(8,128)(2,1)}) custom-call(bf16[288,768]{1,0:T(8,128)(2,1)} %copy-done.22, bf16[288,768]{1,0:T(8,128)(2,1)} %copy-done.42, bf16[288,768]{1,0:T(8,128)(2,1)} %copy-done.44, bf16[288,768]{1,0:T(8,128)(2,1)} %copy-done.45, bf16[288,768]{1,0:T(8,128)(2,1)} %copy-done.21, ...), custom_call_target="tpu_custom_call" | custom-call | flops 1048576 | bytes 65536 | tf_op jit(solution)/shard_map/place/pallas_call | solution.py:404
  66.7 4.3 %collective-permute-done.10 = bf16[192,768]{1,0:T(8,128)(2,1)} collective-permute-done((bf16[192,768]{1,0:T(8,128)(2,1)S(1)}, bf16[192,768]{1,0:T(8,128)(2,1)}, u32[]{:S(2)}, u32[]{:S(2)}) %collective-permute-start.10) | collective-permute-done | bytes 294944 | tf_op jit(solution)/shard_map/ppermute | solution.py:299
  74.1 20.2 %attend_forward.2 = (bf16[512,768]{1,0:T(8,128)(2,1)}, bf16[512,768]{1,0:T(8,128)(2,1)}, bf16[512,768]{1,0:T(8,128)(2,1)}, bf16[512,768]{1,0:T(8,128)(2,1)}, bf1...) custom-call(s32[6]{0:T(128)} %stack.33.scalars.refs_0_, ...), custom_call_target="tpu_custom_call" | custom-call | flops 1048576 | bytes 65536 | tf_op jit(solution)/shard_map/attend_forward/pallas_call | solution.py:133
  95.4 4.8 %collective-permute-done.20 = bf16[192,768]{1,0:T(8,128)(2,1)S(1)} collective-permute-done((bf16[192,768]{1,0:T(8,128)(2,1)S(1)}, bf16[192,768]{1,0:T(8,128)(2,1)S(1)}, u32[]{:S(2)}, u32[]{:S(2)}) %collective-permute-start.20) | collective-permute-done | bytes 294944 | tf_op jit(solution)/shard_map/ppermute | solution.py:299
  107.0 6.1 %collective-permute-done.22 = bf16[240,768]{1,0:T(8,128)(2,1)S(1)} collective-permute-done((bf16[240,768]{1,0:T(8,128)(2,1)S(1)}, bf16[240,768]{1,0:T(8,128)(2,1)S(1)}, u32[]{:S(2)}, u32[]{:S(2)}) %collective-permute-start.22) | collective-permute-done | bytes 368672 | tf_op jit(solution)/shard_map/ppermute | solution.py:299
  113.2 13.1 %collective-permute-done.21 = bf16[240,768]{1,0:T(8,128)(2,1)S(1)} collective-permute-done((bf16[240,768]{1,0:T(8,128)(2,1)S(1)}, bf16[240,768]{1,0:T(8,128)(2,1)S(1)}, u32[]{:S(2)}, u32[]{:S(2)}) %collective-permute-start.21) | collective-permute-done | bytes 368672 | tf_op jit(solution)/shard_map/ppermute | solution.py:299
  129.1 19.3 %attend_forward.3 = (bf16[512,768]{1,0:T(8,128)(2,1)}, bf16[512,768]{1,0:T(8,128)(2,1)}, bf16[512,768]{1,0:T(8,128)(2,1)}, bf16[512,768]{1,0:T(8,128)(2,1)}, f32[512,768]{1,0:T(8,128)}, /*index=5*/f32[512,768]{1,0:T(8,128)}) custom-call(s32[6]{0:T(128)} %stack.33.scalars.refs_0_, bf16[512,768]{1,0:T(8,128)(2,1)} %copy-done.3, ...), custom_call_target="tpu_custom_call" | custom-call | flops 1048576 | bytes 65536 | tf_op jit(solution)/shard_map/attend_forward/pallas_call | solution.py:133
  149.9 3.5 collective-permute-done.28.refs_14_
  155.7 27.4 %middle.1 = (bf16[512,768]{1,0:T(8,128)(2,1)}, bf16[512,768]{1,0:T(8,128)(2,1)}, bf16[4,512,768]{2,1,0:T(8,128)(2,1)}, bf16[4,512,768]{2,1,0:T(8,128)(2,1)}, bf1...) custom-call(s32[6]{0:T(128)} %stack.33.scalars.refs_0_, ...), custom_call_target="tpu_custom_call" | custom-call | flops 1048576 | bytes 65536 | tf_op jit(solution)/shard_map/middle/pallas_call | solution.py:604
  183.1 12.0 %feed_grads.1 = (bf16[4,4,96,768]{3,2,1,0:T(8,128)(2,1)}, bf16[4,4,96,768]{3,2,1,0:T(8,128)(2,1)}, bf16[5,4,96,768]{3,2,1,0:T(8,128)(2,1)}, bf16[5,4,96,768]{3,2,1,0:T(8,128)(2,1)}) custom-call(bf16[512,768]{1,0:T(8,128)(2,1)} %get-tuple-element.248.final_ref, bf16[4,512,768]{2,1,0:T(8,128)(2,1)} %get-tuple-element.249.act_ref, ...), custom_call_target="tpu_custom_call" | custom-call | flops 1048576 | bytes 65536 | tf_op jit(solution)/shard_map/feed_grads/pallas_call | solution.py:694
  195.6 15.3 %attend_backward.4 = (f32[512,768]{1,0:T(8,128)}, bf16[512,768]{1,0:T(8,128)(2,1)}, bf16[512,768]{1,0:T(8,128)(2,1)}, bf16[512,768]{1,0:T(8,128)(2,1)}) custom-call(s32[6]{0:T(128)} %stack.33.scalars.refs_0_, bf16[512,768]{1,0:T(8,128)(2,1)} %get-tuple-element.213.refs_5_.q_ref, bf16[512,768]{1,0:T(8,128)(2,1)} %get-tuple-element.238.k_ref, ...), custom_call_target="tpu_custom_call" | custom-call | flops 1048576 | bytes 65536 | tf_op jit(solution)/shard_map/attend_backward/pallas_call | solution.py:250
  224.9 15.5 %attend_backward.5 = (f32[512,768]{1,0:T(8,128)}, bf16[512,768]{1,0:T(8,128)(2,1)}, bf16[512,768]{1,0:T(8,128)(2,1)}, f32[512,768]{1,0:T(8,128)}) custom-call(s32[6]{0:T(128)} %stack.33.scalars.refs_0_, bf16[512,768]{1,0:T(8,128)(2,1)} %get-tuple-element.213.refs_5_.q_ref, bf16[512,768]{1,0:T(8,128)(2,1)} %get-tuple-element.237.k_ref, ...), custom_call_target="tpu_custom_call" | custom-call | flops 1048576 | bytes 65536 | tf_op jit(solution)/shard_map/attend_backward/pallas_call | solution.py:250
  247.4 15.9 %attend_backward.6 = (f32[512,768]{1,0:T(8,128)}, bf16[512,768]{1,0:T(8,128)(2,1)}, bf16[512,768]{1,0:T(8,128)(2,1)}, f32[512,768]{1,0:T(8,128)}) custom-call(s32[6]{0:T(128)} %stack.33.scalars.refs_0_, bf16[512,768]{1,0:T(8,128)(2,1)} %get-tuple-element.213.refs_5_.q_ref, bf16[512,768]{1,0:T(8,128)(2,1)} %get-tuple-element.210.k_ref, ...), custom_call_target="tpu_custom_call" | custom-call | flops 1048576 | bytes 65536 | tf_op jit(solution)/shard_map/attend_backward/pallas_call | solution.py:250
  268.7 11.0 %collective-permute-done.40 = bf16[5,2,96,768]{3,2,1,0:T(8,128)(2,1)} collective-permute-done((bf16[5,2,96,768]{3,2,1,0:T(8,128)(2,1)}, bf16[5,2,96,768]{3,2,1,0:T(8,128)(2,1)}, u32[]{:S(2)}, u32[]{:S(2)}) %collective-permute-start.40) | collective-permute-done | bytes 1474592 | tf_op jit(solution)/shard_map/ppermute | solution.py:299
  289.3 18.3 %attend_backward.7 = (bf16[512,768]{1,0:T(8,128)(2,1)}, bf16[512,768]{1,0:T(8,128)(2,1)}, bf16[512,768]{1,0:T(8,128)(2,1)}, f32[512,768]{1,0:T(8,128)}) custom-call(s32[6]{0:T(128)} %stack.33.scalars.refs_0_, bf16[512,768]{1,0:T(8,128)(2,1)} %get-tuple-element.213.refs_5_.q_ref, bf16[512,768]{1,0:T(8,128)(2,1)} %get-tuple-element.209.k_ref, ...), custom_call_target="tpu_custom_call" | custom-call | flops 1048576 | bytes 65536 | tf_op jit(solution)/shard_map/attend_backward/pallas_call | solution.py:250
  308.8 12.4 %qkv_grads.1 = (bf16[3,4,96,768]{3,2,1,0:T(8,128)(2,1)}, bf16[3,4,96,768]{3,2,1,0:T(8,128)(2,1)}, f32[16,768]{1,0:T(8,128)}) custom-call(bf16[512,768]{1,0:T(8,128)(2,1)} %copy-done.2, bf16[512,768]{1,0:T(8,128)(2,1)} %broadcast_select_fusion.1.refs_1_, bf16[512,768]{1,0:T(8,128)(2,1)} %copy-done.3, bf16[512,768]{1,0:T(8,128)(2,1)} %broadcast_select_fusion.refs_1_.refs_3_, ...), custom_call_target="tpu_custom_call" | custom-call | flops 1048576 | bytes 65536 | tf_op jit(solution)/shard_map/qkv_grads/pallas_call | solution.py:759
  356.5 6.1 %collective-permute-done.53 = bf16[2,192,768]{2,1,0:T(8,128)(2,1)} collective-permute-done((bf16[2,192,768]{2,1,0:T(8,128)(2,1)}, bf16[2,192,768]{2,1,0:T(8,128)(2,1)}, u32[]{:S(2)}, u32[]{:S(2)}) %collective-permute-start.53) | collective-permute-done | bytes 589856 | tf_op jit(solution)/shard_map/ppermute | solution.py:299
  368.3 10.6 %collective-permute-start.55 = (f32[20,768]{1,0:T(8,128)S(1)}, f32[20,768]{1,0:T(8,128)S(1)}, u32[]{:S(2)}, u32[]{:S(2)}) collective-permute-start(f32[20,768]{1,0:T(8,128)S(1)} %add.267), channel_id=1, source_target_pairs={{0,1},{1,0},{2,3},{3,2},{4,5},{5,4},{6,7},{7,6},{8,9},{9,8},{10,11... | collective-permute-start | bytes 184328 | tf_op jit(solution)/shard_map/ppermute | solution.py:299
  383.4 3.4 collective-permute-start.58
  389.0 3.8 collective-permute-start.59
  402.7 4.3 %collective-permute-done.60 = bf16[3,96,192]{2,1,0:T(8,128)(2,1)S(1)} collective-permute-done((bf16[3,96,192]{2,1,0:T(8,128)(2,1)S(1)}, bf16[3,96,192]{2,1,0:T(8,128)(2,1)S(1)}, u32[]{:S(2)}, u32[]{:S(2)}) %collective-permute-start.60) | collective-permute-done | bytes 110624 | tf_op jit(solution)/shard_map/ppermute | solution.py:299
  (336 shorter events, 151.4 us)
Async XLA Ops:
  5.7 23.7 %collective-permute-start.1 = (bf16[96,768]{1,0:T(8,128)(2,1)}, bf16[96,768]{1,0:T(8,128)(2,1)S(1)}, u32[]{:S(2)}, u32[]{:S(2)}) collective-permute-start(bf16[96,768]{1,0:T(8,128)(2,1)} %param.26), channel_id=1, source_target_pairs={{0,1},{1,0},{2,3},{3,2},{4,5},{5,4},{6,7},{7,6},{8,9},{9,8},{10,11... | collective-permute-start | bytes 442376 | tf_op jit(solution)/shard_map/ppermute | solution.py:299
  58.8 41.5 %collective-permute-start.7 = (bf16[512,768]{1,0:T(8,128)(2,1)S(1)}, bf16[512,768]{1,0:T(8,128)(2,1)}, u32[]{:S(2)}, u32[]{:S(2)}) collective-permute-start(bf16[512,768]{1,0:T(8,128)(2,1)S(1)} %collective-permute-done.3), channel_id=1, source_target_pairs={{1,2},{2,3},{5,6},{6,7},{9,10},{10,11},{13,14},{14,15},{17,18},{18... | collective-permute-start | bytes 2359304 | tf_op jit(solution)/shard_map/ppermute | solution.py:914
  60.4 39.9 %collective-permute-start.8 = (bf16[512,768]{1,0:T(8,128)(2,1)S(1)}, bf16[512,768]{1,0:T(8,128)(2,1)}, u32[]{:S(2)}, u32[]{:S(2)}) collective-permute-start(bf16[512,768]{1,0:T(8,128)(2,1)S(1)} %collective-permute-done.4), channel_id=1, source_target_pairs={{1,0},{2,1},{5,4},{6,5},{9,8},{10,9},{13,12},{14,13},{17,16},{18,1... | collective-permute-start | bytes 2359304 | tf_op jit(solution)/shard_map/ppermute | solution.py:914
  71.0 23.4 %collective-permute-start.18 = (bf16[192,768]{1,0:T(8,128)(2,1)}, bf16[192,768]{1,0:T(8,128)(2,1)S(1)}, u32[]{:S(2)}, u32[]{:S(2)}) collective-permute-start(bf16[192,768]{1,0:T(8,128)(2,1)} %collective-permute-done.10), channel_id=1, source_target_pairs={{0,16},{4,20},{8,24},{12,28},{16,0},{20,4},{24,8},{28,12},{1,17},{... | collective-permute-start | bytes 884744 | tf_op jit(solution)/shard_map/ppermute | solution.py:299
  71.5 23.9 %collective-permute-start.17 = (bf16[192,768]{1,0:T(8,128)(2,1)S(1)}, bf16[192,768]{1,0:T(8,128)(2,1)S(1)}, u32[]{:S(2)}, u32[]{:S(2)}) collective-permute-start(bf16[192,768]{1,0:T(8,128)(2,1)S(1)} %pad_maximum_fusion.9), channel_id=1, source_target_pairs={{0,8},{4,12},{8,0},{12,4},{16,24},{20,28},{24,16},{28,20},{1,9},{5... | collective-permute-start | bytes 884744 | tf_op jit(solution)/shard_map/ppermute | solution.py:299
  73.0 27.3 %collective-permute-start.20 = (bf16[192,768]{1,0:T(8,128)(2,1)S(1)}, bf16[192,768]{1,0:T(8,128)(2,1)S(1)}, u32[]{:S(2)}, u32[]{:S(2)}) collective-permute-start(bf16[192,768]{1,0:T(8,128)(2,1)S(1)} %pad_maximum_fusion.10), channel_id=1, source_target_pairs={{0,2},{1,3},{2,0},{3,1},{4,6},{5,7},{6,4},{7,5},{8,10},{9,11},{10,... | collective-permute-start | bytes 884744 | tf_op jit(solution)/shard_map/ppermute | solution.py:299
  102.2 24.2 %collective-permute-start.23 = (bf16[384,768]{1,0:T(8,128)(2,1)S(1)}, bf16[384,768]{1,0:T(8,128)(2,1)}, u32[]{:S(2)}, u32[]{:S(2)}) collective-permute-start(bf16[384,768]{1,0:T(8,128)(2,1)S(1)} %pad_maximum_fusion.3.refs_7_), channel_id=1, source_target_pairs={{0,16},{4,20},{8,24},{12,28},{16,0},{20,4},{24,8},{28,12},{1,17},{... | collective-permute-start | bytes 1769480 | tf_op jit(solution)/shard_map/ppermute | solution.py:299
  103.7 22.7 %collective-permute-start.24 = (bf16[384,768]{1,0:T(8,128)(2,1)S(1)}, bf16[384,768]{1,0:T(8,128)(2,1)S(1)}, u32[]{:S(2)}, u32[]{:S(2)}) collective-permute-start(bf16[384,768]{1,0:T(8,128)(2,1)S(1)} %pad_maximum_fusion.4.refs_11_), channel_id=1, source_target_pairs={{0,8},{4,12},{8,0},{12,4},{16,24},{20,28},{24,16},{28,20},{1,9},{5... | collective-permute-start | bytes 1769480 | tf_op jit(solution)/shard_map/ppermute | solution.py:299
  104.2 22.1 %collective-permute-start.21 = (bf16[240,768]{1,0:T(8,128)(2,1)S(1)}, bf16[240,768]{1,0:T(8,128)(2,1)S(1)}, u32[]{:S(2)}, u32[]{:S(2)}) collective-permute-start(bf16[240,768]{1,0:T(8,128)(2,1)S(1)} %pad_maximum_fusion.7), channel_id=1, source_target_pairs={{0,8},{4,12},{8,0},{12,4},{16,24},{20,28},{24,16},{28,20},{1,9},{5... | collective-permute-start | bytes 1105928 | tf_op jit(solution)/shard_map/ppermute | solution.py:299
  105.7 22.3 %collective-permute-start.19 = (bf16[512,768]{1,0:T(8,128)(2,1)S(1)}, bf16[512,768]{1,0:T(8,128)(2,1)S(1)}, u32[]{:S(2)}, u32[]{:S(2)}) collective-permute-start(bf16[512,768]{1,0:T(8,128)(2,1)S(1)} %broadcast_select_fusion.2.refs_0_.refs_2_), channel_id=1, source_target_pairs={{1,0},{2,3},{5,4},{6,7},{9,8},{10,11},{13,12},{14,15},{17,16},{18,... | collective-permute-start | bytes 2359304 | tf_op jit(solution)/shard_map/ppermute | solution.py:914
  126.4 21.9 %collective-permute-start.29 = (bf16[480,768]{1,0:T(8,128)(2,1)S(1)}, bf16[480,768]{1,0:T(8,128)(2,1)S(1)}, u32[]{:S(2)}, u32[]{:S(2)}) collective-permute-start(bf16[480,768]{1,0:T(8,128)(2,1)S(1)} %pad_maximum_fusion.1.refs_15_), channel_id=1, source_target_pairs={{0,16},{4,20},{8,24},{12,28},{16,0},{20,4},{24,8},{28,12},{1,17},{... | collective-permute-start | bytes 2211848 | tf_op jit(solution)/shard_map/ppermute | solution.py:299
  127.5 21.9 %collective-permute-start.26 = (bf16[384,768]{1,0:T(8,128)(2,1)}, bf16[384,768]{1,0:T(8,128)(2,1)}, u32[]{:S(2)}, u32[]{:S(2)}) collective-permute-start(bf16[384,768]{1,0:T(8,128)(2,1)} %collective-permute-done.23.refs_8_), channel_id=1, source_target_pairs={{0,4},{4,0},{8,12},{12,8},{16,20},{20,16},{24,28},{28,24},{1,5},{5... | collective-permute-start | bytes 1769480 | tf_op jit(solution)/shard_map/ppermute | solution.py:299
  195.0 22.7 %collective-permute-start.35 = (bf16[5,4,96,768]{3,2,1,0:T(8,128)(2,1)}, bf16[5,4,96,768]{3,2,1,0:T(8,128)(2,1)S(1)}, u32[]{:S(2)}, u32[]{:S(2)}) collective-permute-start(bf16[5,4,96,768]{3,2,1,0:T(8,128)(2,1)} %get-tuple-element.257), channel_id=1, source_target_pairs={{0,4},{4,0},{8,12},{12,8},{16,20},{20,16},{24,28},{28,24},{1,5},{5... | collective-permute-start | bytes 8847368 | tf_op jit(solution)/shard_map/ppermute | solution.py:299
  210.8 29.5 %collective-permute-start.37 = (bf16[512,768]{1,0:T(8,128)(2,1)}, bf16[512,768]{1,0:T(8,128)(2,1)}, u32[]{:S(2)}, u32[]{:S(2)}) collective-permute-start(bf16[512,768]{1,0:T(8,128)(2,1)} %get-tuple-element.264), channel_id=1, source_target_pairs={{0,1},{3,2},{4,5},{7,6},{8,9},{11,10},{12,13},{15,14},{16,17},{19,... | collective-permute-start | bytes 2359304 | tf_op jit(solution)/shard_map/ppermute | solution.py:914
  223.3 42.8 %collective-permute-start.41 = (bf16[4,2,96,768]{3,2,0,1:T(8,128)(2,1)}, bf16[4,2,96,768]{3,2,0,1:T(8,128)(2,1)}, u32[]{:S(2)}, u32[]{:S(2)}) collective-permute-start(bf16[4,2,96,768]{3,2,0,1:T(8,128)(2,1)} %bitcast.87), channel_id=1, source_target_pairs={{0,16},{4,20},{8,24},{12,28},{16,0},{20,4},{24,8},{28,12},{1,17},{... | collective-permute-start | bytes 3538952 | tf_op jit(solution)/shard_map/ppermute | solution.py:299
  245.1 34.6 %collective-permute-start.40 = (bf16[5,2,96,768]{3,2,1,0:T(8,128)(2,1)}, bf16[5,2,96,768]{3,2,1,0:T(8,128)(2,1)}, u32[]{:S(2)}, u32[]{:S(2)}) collective-permute-start(bf16[5,2,96,768]{3,2,1,0:T(8,128)(2,1)} %dynamic-slice_bitcast_fusion), channel_id=1, source_target_pairs={{0,8},{4,12},{8,0},{12,4},{16,24},{20,28},{24,16},{28,20},{1,9},{5... | collective-permute-start | bytes 4423688 | tf_op jit(solution)/shard_map/ppermute | solution.py:299
  246.6 37.5 %collective-permute-start.39 = (bf16[512,768]{1,0:T(8,128)(2,1)}, bf16[512,768]{1,0:T(8,128)(2,1)S(1)}, u32[]{:S(2)}, u32[]{:S(2)}) collective-permute-start(bf16[512,768]{1,0:T(8,128)(2,1)} %add_convert_fusion.5), channel_id=1, source_target_pairs={{3,2},{2,1},{7,6},{6,5},{11,10},{10,9},{15,14},{14,13},{19,18},{18... | collective-permute-start | bytes 2359304 | tf_op jit(solution)/shard_map/ppermute | solution.py:914
  282.6 24.9 %collective-permute-start.47 = (bf16[4,96,768]{2,1,0:T(8,128)(2,1)S(1)}, bf16[4,96,768]{2,1,0:T(8,128)(2,1)}, u32[]{:S(2)}, u32[]{:S(2)}) collective-permute-start(bf16[4,96,768]{2,1,0:T(8,128)(2,1)S(1)} %dynamic-slice_bitcast_fusion.2), channel_id=1, source_target_pairs={{0,8},{4,12},{8,0},{12,4},{16,24},{20,28},{24,16},{28,20},{1,9},{5... | collective-permute-start | bytes 1769480 | tf_op jit(solution)/shard_map/ppermute | solution.py:299
  284.3 24.4 %collective-permute-start.42 = (bf16[512,768]{1,0:T(8,128)(2,1)}, bf16[512,768]{1,0:T(8,128)(2,1)S(1)}, u32[]{:S(2)}, u32[]{:S(2)}) collective-permute-start(bf16[512,768]{1,0:T(8,128)(2,1)} %select_convert_fusion), channel_id=1, source_target_pairs={{0,1},{1,2},{2,3},{4,5},{5,6},{6,7},{8,9},{9,10},{10,11},{12,13},{... | collective-permute-start | bytes 2359304 | tf_op jit(solution)/shard_map/ppermute | solution.py:914
  285.7 23.1 %collective-permute-start.43 = (bf16[512,768]{1,0:T(8,128)(2,1)S(1)}, bf16[512,768]{1,0:T(8,128)(2,1)S(1)}, u32[]{:S(2)}, u32[]{:S(2)}) collective-permute-start(bf16[512,768]{1,0:T(8,128)(2,1)S(1)} %add_convert_fusion.4), channel_id=1, source_target_pairs={{3,2},{2,1},{1,0},{7,6},{6,5},{5,4},{11,10},{10,9},{9,8},{15,14},{... | collective-permute-start | bytes 2359304 | tf_op jit(solution)/shard_map/ppermute | solution.py:914
  288.2 36.6 %collective-permute-start.46 = (bf16[5,96,768]{2,1,0:T(8,128)(2,1)}, bf16[5,96,768]{2,1,0:T(8,128)(2,1)S(1)}, u32[]{:S(2)}, u32[]{:S(2)}) collective-permute-start(bf16[5,96,768]{2,1,0:T(8,128)(2,1)} %dynamic-slice_bitcast_fusion.1), channel_id=1, source_target_pairs={{0,16},{4,20},{8,24},{12,28},{16,0},{20,4},{24,8},{28,12},{1,17},{... | collective-permute-start | bytes 2211848 | tf_op jit(solution)/shard_map/ppermute | solution.py:299
  332.0 30.6 %collective-permute-start.53 = (bf16[2,192,768]{2,1,0:T(8,128)(2,1)}, bf16[2,192,768]{2,1,0:T(8,128)(2,1)}, u32[]{:S(2)}, u32[]{:S(2)}) collective-permute-start(bf16[2,192,768]{2,1,0:T(8,128)(2,1)} %fusion.11), channel_id=1, source_target_pairs={{0,2},{1,3},{2,0},{3,1},{4,6},{5,7},{6,4},{7,5},{8,10},{9,11},{10,... | collective-permute-start | bytes 1769480 | tf_op jit(solution)/shard_map/ppermute | solution.py:299
  354.5 27.5 %collective-permute-start.56 = (bf16[3,96,384]{2,1,0:T(8,128)(2,1)}, bf16[3,96,384]{2,1,0:T(8,128)(2,1)}, u32[]{:S(2)}, u32[]{:S(2)}) collective-permute-start(bf16[3,96,384]{2,1,0:T(8,128)(2,1)} %dynamic-slice_bitcast_fusion.4), channel_id=1, source_target_pairs={{0,16},{4,20},{8,24},{12,28},{16,0},{20,4},{24,8},{28,12},{1,17},{... | collective-permute-start | bytes 663560 | tf_op jit(solution)/shard_map/ppermute | solution.py:299
  356.0 26.1 %collective-permute-start.57 = (bf16[3,96,384]{2,1,0:T(8,128)(2,1)}, bf16[3,96,384]{2,1,0:T(8,128)(2,1)}, u32[]{:S(2)}, u32[]{:S(2)}) collective-permute-start(bf16[3,96,384]{2,1,0:T(8,128)(2,1)} %dynamic-slice_bitcast_fusion.3), channel_id=1, source_target_pairs={{0,8},{4,12},{8,0},{12,4},{16,24},{20,28},{24,16},{28,20},{1,9},{5... | collective-permute-start | bytes 663560 | tf_op jit(solution)/shard_map/ppermute | solution.py:299
  (98 other events, 1075.7 us)
where the time goes:
time: 416 us; the launch traced here: 408 us
  Pallas kernels  160 us (38%)
  waiting for transfers between devices  89 us (21%)
  starting transfers between devices  78.6 us (19%)
  other arithmetic  39 us (9%)
  local copies, waits for them, and re-layouts  32.7 us (8%)
  between operations  5.63 us (1%)
    ppermute x53, waiting for transfers between devices, swap(): return lax.ppermute(value, axis, [(i, i ^ bit) for i in range(count)])  72.6 us
    pallas_call x4, Pallas kernels, attend_backward(): pl.pallas_call(functools.partial(backward_kernel, number, first, last), o...  64.9 us
    ppermute x53, starting transfers between devices, swap(): return lax.ppermute(value, axis, [(i, i ^ bit) for i in range(count)])  62.8 us
    pallas_call x2, Pallas kernels, attend_forward(): pl.pallas_call(functools.partial(forward_kernel, numbers, first), out_sha...  39.5 us
    pallas_call x1, Pallas kernels, middle_call(): pl.pallas_call(functools.partial(middle_kernel, plan, block, len(arrays))...  27.4 us
    ppermute x10, waiting for transfers between devices, shards(): along = lambda value, pairs: lax.ppermute(value, 'mp', pairs)  16.4 us
    ppermute x10, starting transfers between devices, shards(): along = lambda value, pairs: lax.ppermute(value, 'mp', pairs)  15.8 us
    pallas_call x1, Pallas kernels, qkv_grads(): pl.pallas_call(functools.partial(qkv_grad_kernel, count), out_shape=[jax....  12.4 us
  transfers between devices with their start and end apart: 63, of which 23 were waited for; matrix products, arithmetic and copies ran while one was open for 16% of the time, Pallas kernels for 30%

commit v1 on v0

--- a/solution.py
+++ b/solution.py
@@ -56,7 +56,7 @@
     return lax.broadcasted_iota(jnp.int32, shape, len(shape) - 1) < HEAD_DIM
 
 
-def forward_kernel(numbers, first, scalars, *refs):
+def forward_kernel(numbers, first, final, scalars, *refs):
     count = len(numbers)
     chunk_refs = refs[:count]
     wk_ref, wv_ref, value_bias_ref = refs[count : count + 3]
@@ -71,7 +71,7 @@
     else:
         q_ref, top_in, sum_in, acc_in = refs[:4]
         key_outs, value_outs = refs[4 : 4 + count], refs[4 + count : 4 + 2 * count]
-        out_ref, log_ref = refs[4 + 2 * count :]
+        results = refs[4 + 2 * count :]
         q_pair = q_ref[...]
     weight = jnp.concatenate([wk_ref[...], wv_ref[...]], axis=1)
     keys = []
@@ -116,22 +116,29 @@
         here = jnp.exp(top - highest)
         before = jnp.exp(top_in[...] - highest)
         total = total * here + sum_in[...] * before
-        out_ref[...] = (mixed * here + acc_in[...] * before) / total
-        log_ref[...] = highest + jnp.log(total)
+        mixed = mixed * here + acc_in[...] * before
+        if final:
+            results[0][...] = mixed / total
+            results[1][...] = highest + jnp.log(total)
+        else:
+            results[0][...] = highest
+            results[1][...] = total
+            results[2][...] = mixed
 
 
 def attend_forward(chunks, numbers, scalars, query_weight, pair_weight, query_bias, value_bias, carried):
     rows = chunks[0].shape[0]
     count = len(chunks)
     first = carried is None
+    final = 3 in numbers
     column = lambda height, c: pl.BlockSpec((height, PAIR), lambda i, n: (0, c * PAIRS + i))
     whole = pl.BlockSpec((rows, D), lambda i, n: (0, 0))
     wide = jax.ShapeDtypeStruct((rows, D), full)
     narrow = jax.ShapeDtypeStruct((rows, D), low)
     extra = (query_weight, query_bias) if first else carried
-    results = (narrow, wide, wide, wide) if first else (wide, wide)
+    results = (narrow,) * first + (wide,) * (2 if final else 3)
     return pl.pallas_call(
-        functools.partial(forward_kernel, numbers, first),
+        functools.partial(forward_kernel, numbers, first, final),
         out_shape=(narrow,) * (2 * count) + results,
         grid_spec=pltpu.PrefetchScalarGridSpec(
             num_scalar_prefetch=1,
@@ -651,58 +658,90 @@
     )(limit, vectors, tokens, mixed, logs, cot, teach, *arrays)
 
 
-def feed_grad_kernel(
-    final_ref, act_ref, second_ref, pre_ref, middle_ref, attended_ref, *refs
-):
-    down_keep, down_send, up_keep, up_send, left, right = refs
-    block = down_keep.shape[2]
+def store_split(value, keep, send, index):
+    block = keep.shape[2]
+    even = lax.axis_index("dp") % 2 == 0
+    for outer in range(keep.shape[1]):
+        first = value[2 * outer * block : (2 * outer + 1) * block]
+        other = value[(2 * outer + 1) * block : (2 * outer + 2) * block]
+        keep[index, outer] = jnp.where(even, first, other).astype(low)
+        send[index, outer] = jnp.where(even, other, first).astype(low)
+
+
+def feed_grad_kernel(left_ref, right_ref, *refs):
+    keep, send, turned = refs[-3:]
     m = pl.program_id(0)
-    even = lax.axis_index("dp") % 2 == 0
 
     @pl.when(m == 0)
     def _():
-        left[...] = final_ref[...].T
-        right[...] = second_ref[...].T
-
-    def store(value, keep, send, index):
-        for outer in range(down_keep.shape[1]):
-            first = value[2 * outer * block : (2 * outer + 1) * block]
-            other = value[(2 * outer + 1) * block : (2 * outer + 2) * block]
-            keep[index, outer] = jnp.where(even, first, other).astype(low)
-            send[index, outer] = jnp.where(even, other, first).astype(low)
+        turned[...] = left_ref[...].T
 
     @pl.when(m < FF // D)
     def _():
-        store(dot_of(left[...], act_ref[0], 1, 0), down_keep, down_send, 0)
-        store(dot_of(right[...], pre_ref[0], 1, 0), up_keep, up_send, 0)
-
-    @pl.when(m == FF // D)
-    def _():
-        store(dot_of(middle_ref[...].T, attended_ref[...], 1, 0), up_keep, up_send, 0)
-
-
-def feed_grads(final_low, act, second, pre, middle_low, attended, dp):
-    rows = final_low.shape[0]
+        store_split(dot_of(turned[...], right_ref[0], 1, 0), keep, send, 0)
+
+    if len(refs) > 3:
+
+        @pl.when(m == FF // D)
+        def _():
+            store_split(dot_of(refs[0][...].T, refs[1][...], 1, 0), keep, send, 0)
+
+
+def feed_grads(left, right, more, dp):
+    rows = left.shape[0]
     hidden = FF // D
+    count = hidden + (1 if more else 0)
     whole = pl.BlockSpec((rows, D), lambda m: (0, 0))
-    last = hidden - 1
-    slice_of = pl.BlockSpec((1, rows, D), lambda m: (jnp.minimum(m, last), 0, 0))
-    shape = (hidden, dp // 2, D // dp, D)
-    longer = (hidden + 1,) + shape[1:]
-    down_spec = pl.BlockSpec((1,) + shape[1:], lambda m: (jnp.minimum(m, last), 0, 0, 0))
-    up_spec = pl.BlockSpec((1,) + shape[1:], lambda m: (m, 0, 0, 0))
+    shape = (count, dp // 2, D // dp, D)
     return pl.pallas_call(
         feed_grad_kernel,
-        out_shape=[jax.ShapeDtypeStruct(shape, low)] * 2
-        + [jax.ShapeDtypeStruct(longer, low)] * 2,
-        grid=(hidden + 1,),
-        in_specs=[whole, slice_of, whole, slice_of, whole, whole],
-        out_specs=[down_spec, down_spec, up_spec, up_spec],
-        scratch_shapes=[pltpu.VMEM((D, rows), low)] * 2,
+        out_shape=[jax.ShapeDtypeStruct(shape, low)] * 2,
+        grid=(count,),
+        in_specs=[
+            whole,
+            pl.BlockSpec((1, rows, D), lambda m: (jnp.minimum(m, hidden - 1), 0, 0)),
+        ]
+        + [whole] * len(more),
+        out_specs=[pl.BlockSpec((1,) + shape[1:], lambda m: (m, 0, 0, 0))] * 2,
+        scratch_shapes=[pltpu.VMEM((D, rows), low)],
         compiler_params=pltpu.CompilerParams(vmem_limit_bytes=VMEM_LIMIT),
         cost_estimate=SMALL_COST,
         name="feed_grads",
-    )(final_low, act, second, pre, middle_low, attended)
+    )(left, right, *more)
+
+
+def fold_kernel(bits, places, *refs):
+    count = len(bits)
+    me = lax.axis_index("dp")
+    for n in range(count):
+        keep, got = refs[2 * n : 2 * n + 2]
+        out_keep, out_send = refs[2 * count + 2 * n : 2 * count + 2 * n + 2]
+        step = 1 << places[n]
+        mine = (me // bits[n]) % 2 * step
+        for j in range(keep.shape[1] // 2):
+            base = (j // step) * 2 * step + j % step
+            for out, shift in ((out_keep, mine), (out_send, step - mine)):
+                value = keep[0, base + shift].astype(full) + got[0, base + shift].astype(full)
+                out[0, j] = value.astype(low)
+
+
+def fold(pairs, bits, places):
+    lead = pairs[0][0].shape[0]
+    block = lambda shape: pl.BlockSpec((1,) + shape[1:], lambda i: (i, 0, 0, 0))
+    halves = [
+        (keep.shape[0], keep.shape[1] // 2) + keep.shape[2:] for keep, _ in pairs for _ in range(2)
+    ]
+    outs = pl.pallas_call(
+        functools.partial(fold_kernel, bits, places),
+        out_shape=[jax.ShapeDtypeStruct(shape, low) for shape in halves],
+        grid=(lead,),
+        in_specs=[block(value.shape) for pair in pairs for value in pair],
+        out_specs=[block(shape) for shape in halves],
+        compiler_params=pltpu.CompilerParams(vmem_limit_bytes=VMEM_LIMIT),
+        cost_estimate=pl.CostEstimate(flops=0, bytes_accessed=16 << 20, transcendentals=0),
+        name="fold",
+    )(*[value for pair in pairs for value in pair])
+    return [(outs[2 * n], outs[2 * n + 1]) for n in range(len(pairs))]
 
 
 def qkv_grad_kernel(count, *refs):
@@ -710,19 +749,15 @@
     query_ref = refs[count]
     key_refs = refs[count + 1 : 2 * count + 1]
     value_refs = refs[2 * count + 1 : 3 * count + 1]
-    keep_ref, send_ref, sum_ref, turned = refs[3 * count + 1 :]
-    block = keep_ref.shape[2]
+    keeps, sends = refs[3 * count + 1 : 3 * count + 3], refs[3 * count + 3 : 3 * count + 5]
+    sum_ref, turned = refs[3 * count + 5 :]
     rows = query_ref.shape[0]
     c = pl.program_id(0)
-    even = lax.axis_index("dp") % 2 == 0
     ones = jnp.ones((16, rows), low)
 
     def store(value):
-        for outer in range(keep_ref.shape[1]):
-            first = value[2 * outer * block : (2 * outer + 1) * block]
-            other = value[(2 * outer + 1) * block : (2 * outer + 2) * block]
-            keep_ref[0, outer] = jnp.where(even, first, other).astype(low)
-            send_ref[0, outer] = jnp.where(even, other, first).astype(low)
+        for n in range(2):
+            store_split(value[:, n * D // 2 : (n + 1) * D // 2], keeps[n], sends[n], 0)
 
     @pl.when(c == 0)
     def _():
@@ -754,15 +789,15 @@
     rows = query_grad.shape[0]
     count = len(chunks)
     whole = pl.BlockSpec((rows, D), lambda c: (0, 0))
-    shape = (3, dp // 2, D // dp, D)
+    shape = (3, dp // 2, D // dp, D // 2)
     part = pl.BlockSpec((1,) + shape[1:], lambda c: (c, 0, 0, 0))
     return pl.pallas_call(
         functools.partial(qkv_grad_kernel, count),
-        out_shape=[jax.ShapeDtypeStruct(shape, low)] * 2
+        out_shape=[jax.ShapeDtypeStruct(shape, low)] * 4
         + [jax.ShapeDtypeStruct((16, D), full)],
         grid=(3,),
         in_specs=[whole] * (3 * count + 1),
-        out_specs=[part, part, pl.BlockSpec((16, D), lambda c: (0, 0))],
+        out_specs=[part] * 4 + [pl.BlockSpec((16, D), lambda c: (0, 0))],
         scratch_shapes=[pltpu.VMEM((count, D, rows), low)],
         compiler_params=pltpu.CompilerParams(vmem_limit_bytes=VMEM_LIMIT),
         cost_estimate=SMALL_COST,
@@ -776,35 +811,22 @@
     return keep, send.astype(low)
 
 
-def scatter_dp(parts):
+def scatter_dp(parts, turns):
     bits = outer_bits()
     half = len(bits) // 2
-    orders = [bits[half * (n % 2) :] + bits[: half * (n % 2)] for n in range(len(parts))]
-    me = lax.axis_index("dp")
-    sends = yield [send for _, send in parts]
-    held = [
-        (keep.astype(full) + swap(send, "dp", 1).astype(full)).astype(low)
-        for (keep, _), send in zip(parts, sends)
-    ]
-    held = [
-        value.reshape(value.shape[:1] + (2,) * len(bits) + value.shape[2:]) for value in held
-    ]
-    axes = [list(reversed(bits)) for _ in parts]
-    for step in range(len(bits)):
-        parts = []
-        for n, value in enumerate(held):
-            bit = orders[n][step]
-            axis = 1 + axes[n].index(bit)
-            axes[n].remove(bit)
-            parts.append(two_parts(value, axis, (me // bit) % 2))
+    orders = [[1] + bits[half * (turn % 2) :] + bits[: half * (turn % 2)] for turn in turns]
+    left = [list(bits) for _ in turns]
+    for step in range(len(bits) + 1):
         sends = yield [send for _, send in parts]
-        held = [
-            keep.astype(full) + swap(sends[n], "dp", orders[n][step]).astype(full)
-            for n, (keep, _) in enumerate(parts)
-        ]
-        if step < len(bits) - 1:
-            held = [value.astype(low) for value in held]
-    return held
+        got = [swap(send, "dp", turn[step]) for send, turn in zip(sends, orders)]
+        pairs = [(keep, other) for (keep, _), other in zip(parts, got)]
+        if step < len(bits):
+            places = []
+            for n, turn in enumerate(orders):
+                places.append(left[n].index(turn[step + 1]))
+                left[n].remove(turn[step + 1])
+            parts = fold(pairs, [turn[step + 1] for turn in orders], places)
+    return [(keep.astype(full) + other.astype(full))[:, 0] for keep, other in pairs]
 
 
 def scatter_mp(values):
@@ -822,9 +844,8 @@
     return [value[0] for value in values]
 
 
-def scatter_feed(up_parts, down_parts):
+def scatter_feed(up_own, down_own):
     mp = lax.axis_size("mp")
-    up_own, down_own = yield from scatter_dp([up_parts, down_parts])
     block = down_own.shape[1]
     out_own = up_own[mp].reshape(block, mp, -1).transpose(1, 0, 2)
     tall, out_grad = yield from scatter_mp(
@@ -833,10 +854,10 @@
     return tall[:block], tall[block:].T, out_grad.T
 
 
-def scatter_qkv(keep, send):
+def scatter_qkv(keep_left, keep_right, send_left, send_right):
     rank = lax.axis_index("mp")
     left_part, right_part = yield from scatter_dp(
-        [(keep[..., : D // 2], send[..., : D // 2]), (keep[..., D // 2 :], send[..., D // 2 :])]
+        [(keep_left, send_left), (keep_right, send_right)], (0, 1)
     )
     upper = rank >= 2
     odd = rank % 2 == 1
@@ -917,8 +938,8 @@
     aligned = block % 32 == 0
     narrow = order(jnp.concatenate([w_qkv.reshape(3 * block, -1), w_out.T]))
     first_swap = swap(narrow, "mp", 1)
-    up_own = order(w_up)
-    up_swap = swap(up_own, "mp", 1)
+    tall = order(jnp.concatenate([w_up, w_down.T]))
+    tall_swap = swap(tall, "mp", 1)
     pair = order(
         jnp.concatenate(
             [jnp.where(odd, first_swap, narrow), jnp.where(odd, narrow, first_swap)], axis=1
@@ -963,21 +984,23 @@
         split = 3 * block // 2
         qkv_gather = Gather([qkv_rows[:split], qkv_rows[split:]])
         qkv_gather.advance(order)
-    sent, up_pair = order(first_norm, jnp.concatenate([up_own, up_swap]))
-    from_left = along(sent, [(0, 1), (1, 2), (2, 3)])
-    from_right = along(sent, [(1, 0), (2, 1), (3, 2)])
-    down_own = order(w_down.T)
-    down_swap = swap(down_own, "mp", 1)
-    up_other = swap(up_pair, "mp", 2)
+    tall = order(jnp.concatenate([tall, tall_swap]))
+    tall_other = swap(tall, "mp", 2)
 
     if aligned:
         while qkv_gather.step < len(qkv_gather.bits):
             qkv_gather.advance(order)
-    hop_right, hop_left = order(from_left, from_right)
-    second_right = along(hop_right, [(1, 2), (2, 3)])
-    second_left = along(hop_left, [(1, 0), (2, 1)])
-    near = jnp.where(rank == 0, hop_left, hop_right)
+    sent = order(first_norm)
+    from_left = along(sent, [(0, 1), (1, 2), (2, 3)])
+    from_right = along(sent, [(1, 0), (2, 1), (3, 2)])
     if aligned:
+        feed_gather = Gather(
+            [
+                jnp.concatenate([tall, out_rows[: block // 2]]),
+                jnp.concatenate([tall_other, out_rows[block // 2 :]]),
+            ]
+        )
+        feed_gather.advance(order)
         qkv_gather.advance(order)
         arrays, plan = plan_of(
             qkv_gather.result,
@@ -989,79 +1012,50 @@
                 ],
             ],
         )
-        query_weight, pair_weight = place(arrays, plan, block, [(D, D), (D, 2 * D)])
+        query_weight, pair_weight = order(*place(arrays, plan, block, [(D, D), (D, 2 * D)]))
     else:
         weights = lax.all_gather(qkv_rows.reshape(3, block, D), "dp", axis=1, tiled=True)
         query_weight = weights[0]
         pair_weight = jnp.concatenate([weights[1], weights[2]], axis=1)
-    down_pair, up_other, query_weight, pair_weight = order(
-        jnp.concatenate([down_own, down_swap]), up_other, query_weight, pair_weight
-    )
-    down_other = swap(down_pair, "mp", 2)
-
+    hop_right, hop_left = order(from_left, from_right)
+    second_right = along(hop_right, [(1, 2), (2, 3)])
+    second_left = along(hop_left, [(1, 0), (2, 1)])
+    near = jnp.where(rank == 0, hop_left, hop_right)
     if aligned:
-        ups = Gather([up_pair, up_other])
-        ups.advance(order)
-    attend = lambda chunks, numbers, carried: order(
-        *attend_forward(
-            chunks,
-            numbers,
-            scalars,
-            query_weight,
-            pair_weight,
-            qv_bias[0:1],
-            qv_bias[1:2],
-            carried,
-        )
-    )
-    key_own, key_near, value_own, value_near, queries, *state = attend(
-        [first_norm, near], (0, 1), None
-    )
-    if aligned:
-        while ups.step < len(ups.bits):
-            ups.advance(order)
+        while feed_gather.step < len(feed_gather.bits):
+            feed_gather.advance(order)
+    attend = lambda chunks, numbers, carried: attend_forward(
+        chunks,
+        numbers,
+        scalars,
+        query_weight,
+        pair_weight,
+        qv_bias[0:1],
+        qv_bias[1:2],
+        carried,
+    )
+    key_own, key_near, value_own, value_near, queries, *state = order(
+        *attend(order(first_norm, near), (0, 1), None)
+    )
     second = order(jnp.where(upper, second_right, second_left))
     third = along(second, [(1, 0), (2, 3)])
+    key_second, value_second, *state = attend([second], (2,), (queries, *state))
+    key_second, value_second, *state = order(key_second, value_second, *state)
+    last = order(jnp.where(middle, hop_left, third))
     if aligned:
-        downs = Gather(
-            [
-                jnp.concatenate([down_pair, out_rows[: block // 2]]),
-                jnp.concatenate([down_other, out_rows[block // 2 :]]),
-            ]
+        feed_gather.advance(order)
+    key_last, value_last, mixed, logs = order(*attend([order(last)], (3,), (queries, *state)))
+    if aligned:
+        layout = lambda masks, shift: [
+            (0, block, 0, masks[0], D, 0),
+            (block, block, 1, masks[0], D, 0),
+            (2 * block, block, 0, masks[1], D, 0),
+            (3 * block, block, 1, masks[1], D, 0),
+            (4 * block, block // 2, 2, 0, 0, shift),
+        ]
+        arrays, plan = plan_of(
+            feed_gather.result, [layout((0, 1), 0), layout((2, 3), block // 2)]
         )
-        downs.advance(order)
-        ups.advance(order)
-        while downs.step < len(downs.bits):
-            downs.advance(order)
-    last = order(jnp.where(middle, hop_left, third))
-    key_second, key_last, value_second, value_last, mixed, logs = attend(
-        [second, last], (2, 3), (queries, *state)
-    )
-    if aligned:
-        downs.advance(order)
-        up_arrays, up_plan = plan_of(
-            ups.result,
-            [
-                [(0, block, 0, 0, D, 0), (block, block, 0, 1, D, 0)],
-                [(0, block, 0, 2, D, 0), (block, block, 0, 3, D, 0)],
-            ],
-        )
-        down_arrays, down_plan = plan_of(
-            downs.result,
-            [
-                [
-                    (0, block, 1, 0, D, 0),
-                    (block, block, 1, 1, D, 0),
-                    (2 * block, block // 2, 2, 0, 0, 0),
-                ],
-                [
-                    (0, block, 1, 2, D, 0),
-                    (block, block, 1, 3, D, 0),
-                    (2 * block, block // 2, 2, 0, 0, block // 2),
-                ],
-            ],
-        )
-        arrays, plan = up_arrays + down_arrays, up_plan + down_plan
     else:
         arrays = [
             lax.all_gather(w_up, ("mp", "dp"), axis=0, tiled=True),
@@ -1090,16 +1084,20 @@
         scalars, vectors, tokens, mixed, logs, cotangent, teacher, arrays, plan, block
     )
     gain_two, shift_two, middle_sum, final_sum = sums[0], sums[1], sums[2], sums[3]
-    down_keep, down_send, up_keep, up_send = feed_grads(
-        final_low, hidden_act, second_norm, pre_grad, middle_low, attended, dp
-    )
-
-    feed = Steps(scatter_feed((up_keep, up_send), (down_keep, down_send)))
+    down = Steps(scatter_dp([feed_grads(final_low, hidden_act, (), dp)], (1,)))
+    down.advance(order)
+    second_norm = order(second_norm)
+    up = Steps(
+        scatter_dp([feed_grads(second_norm, pre_grad, (middle_low, attended), dp)], (0,))
+    )
+    up.advance(order)
+    down.advance(order)
+    up.advance(order)
+
     key_grads = [None] * 4
     value_grads = [None] * 4
     firsts = [None] * 4
     query_grad = None
-    feed.advance(order)
     for n in (3, 2, 1, 0):
         query_grad, key_grads[n], value_grads[n], firsts[n] = attend_backward(
             n,
@@ -1118,26 +1116,30 @@
         firsts[n] = order(firsts[n])
         if n == 3:
             back_last = along(firsts[3], [(0, 1), (3, 2)]).astype(full)
-            feed.advance(order)
         elif n == 2:
+            down.advance(order)
+            up.advance(order)
             payload = order((firsts[2] + back_last).astype(low))
             back_right = along(payload, [(0, 1), (1, 2)]).astype(full)
             back_left = along(payload, [(3, 2), (2, 1)]).astype(full)
         elif n == 1:
-            feed.advance(order)
             to_right = jnp.where(
                 rank == 0, firsts[1], firsts[3].astype(full) + back_right
             ).astype(low)
             to_left = (firsts[1] + back_left).astype(low)
+            (up_own,) = up.finish(order)
+            (down_own,) = down.finish(order)
+            feed = Steps(scatter_feed(up_own, down_own))
+            feed.advance(order)
             to_right, to_left = order(to_right, to_left)
             final_right = along(to_right, [(0, 1), (1, 2), (2, 3)])
             final_left = along(to_left, [(3, 2), (2, 1), (1, 0)])
     query_grad, final_right, final_left = order(query_grad, final_right, final_left)
-    qkv_keep, qkv_send, bias_sums = qkv_grads(chunks, query_grad, key_grads, value_grads, dp)
-    qkv = Steps(scatter_qkv(qkv_keep, qkv_send))
+    *halves, bias_sums = qkv_grads(chunks, query_grad, key_grads, value_grads, dp)
+    qkv = Steps(scatter_qkv(*halves))
+    qkv.advance(order)
     qkv.advance(order)
     feed.advance(order)
-    qkv.advance(order)
     tokens, first_own = order(tokens, firsts[0])
     first_grad = first_own + final_right.astype(full) + final_left.astype(full)
     unit_one, inverse_one = norm_stats(tokens.astype(full) + table_row)
@@ -1158,10 +1160,10 @@
     )
     small = Steps(butterfly(packed))
     small.advance(order)
+    qkv.advance(order)
+    small.advance(order)
     small.advance(order)
     qkv.advance(order)
-    small.advance(order)
-    feed.advance(order)
     small.advance(order)
     qkv.advance(order)
     small.advance(order)

time: 416 us -> 410 us (0.986)
  Pallas kernels: 160 us -> 195 us
  starting transfers between devices: 78.6 us -> 56.6 us
  other arithmetic: 39 us -> 26.7 us
  local copies, waits for them, and re-layouts: 32.7 us -> 24.1 us
    pallas_call x2 -> x9, Pallas kernels: 39.5 us -> 72.2 us  [the longest x3 46.5 us: attend_forward(): pl.pallas_call(functools.partial(forward_kernel, numbers, first, final),...]
    ppermute x53 -> x43, starting transfers between devices: 62.8 us -> 37.3 us  [swap(): return lax.ppermute(value, axis, [(i, i ^ bit) for i in range(count)])]
    convert_element_type x7 -> x1, other arithmetic: 12.8 us -> 0.9 us  [two_parts(): return (keep, send.astype(low))]
    unnamed x119 -> x103, local copies, waits for them, and re-layouts: 6.39 us -> 10.9 us
    pallas_call x1 -> x2, Pallas kernels: 12 us -> 15 us  [feed_grads(): pl.pallas_call(feed_grad_kernel, out_shape=[jax.ShapeDtypeStruct(shape, l...]
    ppermute x53 -> x43, waiting for transfers between devices: 72.6 us -> 75.4 us  [swap(): return lax.ppermute(value, axis, [(i, i ^ bit) for i in range(count)])]
  transfers between devices with their start and end apart: 63 -> 53, of which waited for: 23 -> 20; matrix products, arithmetic and copies ran while one was open for 16% -> 10% of each run, Pallas kernels for 30% -> 35%
where the time goes in v1:
time: 410 us; the launch traced here: 403 us
  Pallas kernels  195 us (48%)
  waiting for transfers between devices  92.3 us (23%)
  starting transfers between devices  56.6 us (14%)
  other arithmetic  26.7 us (7%)
  local copies, waits for them, and re-layouts  24.1 us (6%)
  between operations  5.15 us (1%)
    ppermute x43, waiting for transfers between devices, swap(): return lax.ppermute(value, axis, [(i, i ^ bit) for i in range(count)])  75.4 us
    pallas_call x4, Pallas kernels, attend_backward(): pl.pallas_call(functools.partial(backward_kernel, number, first, last), o...  64.2 us
    pallas_call x3, Pallas kernels, attend_forward(): pl.pallas_call(functools.partial(forward_kernel, numbers, first, final),...  46.5 us
    ppermute x43, starting transfers between devices, swap(): return lax.ppermute(value, axis, [(i, i ^ bit) for i in range(count)])  37.3 us
    pallas_call x1, Pallas kernels, middle_call(): pl.pallas_call(functools.partial(middle_kernel, plan, block, len(arrays))...  27.4 us
    pallas_call x6, Pallas kernels, fold(): pl.pallas_call(functools.partial(fold_kernel, bits, places), out_shape=[j...  25.7 us
    ppermute x10, starting transfers between devices, shards(): along = lambda value, pairs: lax.ppermute(value, 'mp', pairs)  19.3 us
    ppermute x10, waiting for transfers between devices, shards(): along = lambda value, pairs: lax.ppermute(value, 'mp', pairs)  16.9 us
  transfers between devices with their start and end apart: 53, of which 20 were waited for; matrix products, arithmetic and copies ran while one was open for 10% of the time, Pallas kernels for 35%

profile of v1, /device:TPU:0, one launch (start us, length us, event | category | flops | bytes accessed | tf_op | source)
XLA Modules:
  0.0 402.6 jit_solution(11613050381121904848)
XLA Ops:
  38.3 15.4 %collective-permute-done.9 = bf16[384,768]{1,0:T(8,128)(2,1)S(1)} collective-permute-done((bf16[384,768]{1,0:T(8,128)(2,1)S(1)}, bf16[384,768]{1,0:T(8,128)(2,1)S(1)}, u32[]{:S(2)}, u32[]{:S(2)}) %collective-permute-start.9) | collective-permute-done | bytes 589856 | tf_op jit(solution)/shard_map/ppermute | solution.py:306
  55.2 4.6 %collective-permute-start.5 = (bf16[512,768]{1,0:T(8,128)(2,1)S(1)}, bf16[512,768]{1,0:T(8,128)(2,1)S(1)}, u32[]{:S(2)}, u32[]{:S(2)}) collective-permute-start(bf16[512,768]{1,0:T(8,128)(2,1)S(1)} %add_convert_fusion.2.refs_0_), channel_id=1, source_target_pairs={{0,1},{1,2},{2,3},{4,5},{5,6},{6,7},{8,9},{9,10},{10,11},{12,13},{... | collective-permute-start | bytes 2359304 | tf_op jit(solution)/shard_map/ppermute | solution.py:935
  68.1 7.7 %collective-permute-done.6 = bf16[512,768]{1,0:T(8,128)(2,1)S(1)} collective-permute-done((bf16[512,768]{1,0:T(8,128)(2,1)S(1)}, bf16[512,768]{1,0:T(8,128)(2,1)S(1)}, u32[]{:S(2)}, u32[]{:S(2)}) %collective-permute-start.6) | collective-permute-done | bytes 786464 | tf_op jit(solution)/shard_map/ppermute | solution.py:935
  82.7 20.2 %attend_forward.3 = (bf16[512,768]{1,0:T(8,128)(2,1)}, bf16[512,768]{1,0:T(8,128)(2,1)}, bf16[512,768]{1,0:T(8,128)(2,1)}, bf16[512,768]{1,0:T(8,128)(2,1)}, bf1...) custom-call(s32[6]{0:T(128)} %stack.33.scalars.refs_0_, ...), custom_call_target="tpu_custom_call" | custom-call | flops 1048576 | bytes 65536 | tf_op jit(solution)/shard_map/attend_forward/pallas_call | solution.py:140
  105.6 13.2 %attend_forward.4 = (bf16[512,768]{1,0:T(8,128)(2,1)}, bf16[512,768]{1,0:T(8,128)(2,1)}, f32[512,768]{1,0:T(8,128)}, f32[512,768]{1,0:T(8,128)}, f32[512,768]{1,0:T(8,128)}) custom-call(s32[6]{0:T(128)} %stack.33.scalars.refs_0_, bf16[512,768]{1,0:T(8,128)(2,1)} %copy-done.2, bf16[768,1536]{1,0:T(8,128)(2,1)} %get-tuple-element.212.refs_2_.refs_3_.refs_1_.wk_ref.wv_ref, ...), custom_call_target="tpu_custom_call" | custom-call | flops 1048576 | bytes 65536 | tf_op jit(solution)/shard_map/attend_forward/pallas_call | solution.py:140
  118.8 8.0 %collective-permute-done.18 = bf16[512,768]{1,0:T(8,128)(2,1)} collective-permute-done((bf16[512,768]{1,0:T(8,128)(2,1)S(1)}, bf16[512,768]{1,0:T(8,128)(2,1)}, u32[]{:S(2)}, u32[]{:S(2)}) %collective-permute-start.18) | collective-permute-done | bytes 786464 | tf_op jit(solution)/shard_map/ppermute | solution.py:935
  130.0 13.1 %attend_forward.5 = (bf16[512,768]{1,0:T(8,128)(2,1)}, bf16[512,768]{1,0:T(8,128)(2,1)}, f32[512,768]{1,0:T(8,128)}, f32[512,768]{1,0:T(8,128)}) custom-call(s32[6]{0:T(128)} %stack.33.scalars.refs_0_, bf16[512,768]{1,0:T(8,128)(2,1)} %broadcast_select_fusion.2.refs_0_.refs_3_, bf16[768,1536]{1,0:T(8,128)(2,1)} %get-tuple-element.212.refs_2_.refs_3_.refs_1_.wk_ref.wv_ref, ...), custom_call_target="tpu_custom_call" | custom-call | flops 1048576 | bytes 65536 | tf_op jit(solution)/shard_map/attend_forward/pallas_call | solution.py:140
  144.3 27.4 %middle.1 = (bf16[512,768]{1,0:T(8,128)(2,1)}, bf16[512,768]{1,0:T(8,128)(2,1)}, bf16[4,512,768]{2,1,0:T(8,128)(2,1)}, bf16[4,512,768]{2,1,0:T(8,128)(2,1)}, bf1...) custom-call(s32[6]{0:T(128)} %stack.33.scalars.refs_0_, ...), custom_call_target="tpu_custom_call" | custom-call | flops 1048576 | bytes 65536 | tf_op jit(solution)/shard_map/middle/pallas_call | solution.py:611
  171.7 6.9 %feed_grads.2 = (bf16[4,4,96,768]{3,2,1,0:T(8,128)(2,1)}, bf16[4,4,96,768]{3,2,1,0:T(8,128)(2,1)}) custom-call(bf16[512,768]{1,0:T(8,128)(2,1)} %get-tuple-element.264.left_ref, bf16[4,512,768]{2,1,0:T(8,128)(2,1)} %get-tuple-element.265.right_ref), custom_call_target="tpu_custom_call" | custom-call | flops 1048576 | bytes 65536 | tf_op jit(solution)/shard_map/feed_grads/pallas_call | solution.py:696
  178.6 8.1 %feed_grads.3 = (bf16[5,4,96,768]{3,2,1,0:T(8,128)(2,1)}, bf16[5,4,96,768]{3,2,1,0:T(8,128)(2,1)}) custom-call(bf16[512,768]{1,0:T(8,128)(2,1)} %get-tuple-element.268.left_ref, bf16[4,512,768]{2,1,0:T(8,128)(2,1)} %get-tuple-element.269.right_ref, bf16[512,768]{1,0:T(8,128)(2,1)} %get-tuple-element.270.refs_0_, bf16[512,768]{1,0:T(8,128)(2,1)} %get-tuple-element.271.refs_1_), custom_call_target="tpu_custom_call" | custom-call | flops 1048576 | bytes 65536 | tf_op jit(solution)/shard_map/feed_grads/pallas_call | solution.py:696
  187.2 8.5 %collective-permute-done.26.refs_1_ = bf16[4,4,96,768]{3,2,1,0:T(8,128)(2,1)S(1)} collective-permute-done((bf16[4,4,96,768]{3,2,1,0:T(8,128)(2,1)}, bf16[4,4,96,768]{3,2,1,0:T(8,128)(2,1)S(1)}, u32[]{:S(2)}, u32[]{:S(2)}) %collective-permute-start.26) | collective-permute-done | bytes 2359328 | tf_op jit(solution)/shard_map/ppermute | solution.py:306
  197.1 4.4 %fold.7 = (bf16[4,2,96,768]{3,2,1,0:T(8,128)(2,1)}, bf16[4,2,96,768]{3,2,1,0:T(8,128)(2,1)}) custom-call(bf16[4,4,96,768]{3,2,1,0:T(8,128)(2,1)} %get-tuple-element.276.refs_0_, bf16[4,4,96,768]{3,2,1,0:T(8,128)(2,1)} %copy-done.8), custom_call_target="tpu_custom_call" | custom-call | bytes 16777216 | tf_op jit(solution)/shard_map/fold/pallas_call | solution.py:734
  203.2 5.9 %fold.6 = (bf16[5,2,96,768]{3,2,1,0:T(8,128)(2,1)}, bf16[5,2,96,768]{3,2,1,0:T(8,128)(2,1)}) custom-call(bf16[5,4,96,768]{3,2,1,0:T(8,128)(2,1)} %get-tuple-element.272.refs_0_, bf16[5,4,96,768]{3,2,1,0:T(8,128)(2,1)} %copy-done.7), custom_call_target="tpu_custom_call" | custom-call | bytes 16777216 | tf_op jit(solution)/shard_map/fold/pallas_call | solution.py:734
  212.2 15.0 %attend_backward.4 = (f32[512,768]{1,0:T(8,128)}, bf16[512,768]{1,0:T(8,128)(2,1)}, bf16[512,768]{1,0:T(8,128)(2,1)}, bf16[512,768]{1,0:T(8,128)(2,1)}) custom-call(s32[6]{0:T(128)} %stack.33.scalars.refs_0_, bf16[512,768]{1,0:T(8,128)(2,1)} %get-tuple-element.231.refs_4_.q_ref, bf16[512,768]{1,0:T(8,128)(2,1)} %get-tuple-element.261.k_ref, ...), custom_call_target="tpu_custom_call" | custom-call | flops 1048576 | bytes 65536 | tf_op jit(solution)/shard_map/attend_backward/pallas_call | solution.py:257
  228.6 15.5 %attend_backward.5 = (f32[512,768]{1,0:T(8,128)}, bf16[512,768]{1,0:T(8,128)(2,1)}, bf16[512,768]{1,0:T(8,128)(2,1)}, f32[512,768]{1,0:T(8,128)}) custom-call(s32[6]{0:T(128)} %stack.33.scalars.refs_0_, bf16[512,768]{1,0:T(8,128)(2,1)} %get-tuple-element.231.refs_4_.q_ref, bf16[512,768]{1,0:T(8,128)(2,1)} %get-tuple-element.241.k_ref, ...), custom_call_target="tpu_custom_call" | custom-call | flops 1048576 | bytes 65536 | tf_op jit(solution)/shard_map/attend_backward/pallas_call | solution.py:257
  250.4 4.4 %fold.8 = (bf16[5,1,96,768]{3,2,1,0:T(8,128)(2,1)}, bf16[5,1,96,768]{3,2,1,0:T(8,128)(2,1)}) custom-call(bf16[5,2,96,768]{3,2,1,0:T(8,128)(2,1)} %get-tuple-element.289.refs_0_, bf16[5,2,96,768]{3,2,1,0:T(8,128)(2,1)} %copy-done.14), custom_call_target="tpu_custom_call" | custom-call | bytes 16777216 | tf_op jit(solution)/shard_map/fold/pallas_call | solution.py:734
  258.5 5.3 %collective-permute-done.33 = bf16[4,1,96,768]{3,2,1,0:T(8,128)(2,1)} collective-permute-done((bf16[4,1,96,768]{3,2,1,0:T(8,128)(2,1)}, bf16[4,1,96,768]{3,2,1,0:T(8,128)(2,1)}, u32[]{:S(2)}, u32[]{:S(2)}) %collective-permute-start.33) | collective-permute-done | bytes 589856 | tf_op jit(solution)/shard_map/ppermute | solution.py:306
  266.6 15.6 %attend_backward.6 = (f32[512,768]{1,0:T(8,128)}, bf16[512,768]{1,0:T(8,128)(2,1)}, bf16[512,768]{1,0:T(8,128)(2,1)}, f32[512,768]{1,0:T(8,128)}) custom-call(s32[6]{0:T(128)} %stack.33.scalars.refs_0_, bf16[512,768]{1,0:T(8,128)(2,1)} %get-tuple-element.231.refs_4_.q_ref, bf16[512,768]{1,0:T(8,128)(2,1)} %get-tuple-element.228.k_ref, ...), custom_call_target="tpu_custom_call" | custom-call | flops 1048576 | bytes 65536 | tf_op jit(solution)/shard_map/attend_backward/pallas_call | solution.py:257
  293.3 5.0 %collective-permute-start.34 = (bf16[2,192,768]{2,1,0:T(8,128)(2,1)}, bf16[2,192,768]{2,1,0:T(8,128)(2,1)}, u32[]{:S(2)}, u32[]{:S(2)}) collective-permute-start(bf16[2,192,768]{2,1,0:T(8,128)(2,1)} %fusion.14), channel_id=1, source_target_pairs={{0,2},{1,3},{2,0},{3,1},{4,6},{5,7},{6,4},{7,5},{8,10},{9,11},{10,... | collective-permute-start | bytes 1769480 | tf_op jit(solution)/shard_map/ppermute | solution.py:306
  300.7 18.1 %attend_backward.7 = (bf16[512,768]{1,0:T(8,128)(2,1)}, bf16[512,768]{1,0:T(8,128)(2,1)}, bf16[512,768]{1,0:T(8,128)(2,1)}, f32[512,768]{1,0:T(8,128)}) custom-call(s32[6]{0:T(128)} %stack.33.scalars.refs_0_, bf16[512,768]{1,0:T(8,128)(2,1)} %get-tuple-element.231.refs_4_.q_ref, bf16[512,768]{1,0:T(8,128)(2,1)} %get-tuple-element.227.k_ref, ...), custom_call_target="tpu_custom_call" | custom-call | flops 1048576 | bytes 65536 | tf_op jit(solution)/shard_map/attend_backward/pallas_call | solution.py:257
  318.8 11.7 %qkv_grads.1 = (bf16[3,4,96,384]{3,2,1,0:T(8,128)(2,1)}, bf16[3,4,96,384]{3,2,1,0:T(8,128)(2,1)}, bf16[3,4,96,384]{3,2,1,0:T(8,128)(2,1)}, bf16[3,4,96,384]{3,2,1,0:T(8,128)(2,1)}, f32[16,768]{1,0:T(8,128)}) custom-call(bf16[512,768]{1,0:T(8,128)(2,1)} %copy-done.3, bf16[512,768]{1,0:T(8,128)(2,1)} %broadcast_select_fusion.refs_1_, ...), custom_call_target="tpu_custom_call" | custom-call | flops 1048576 | bytes 65536 | tf_op jit(solution)/shard_map/qkv_grads/pallas_call | solution.py:794
  331.1 12.5 %collective-permute-done.35 = bf16[2,96,192]{1,2,0:T(8,128)(2,1)S(1)} collective-permute-done((bf16[2,96,192]{1,2,0:T(8,128)(2,1)S(1)}, bf16[2,96,192]{1,2,0:T(8,128)(2,1)S(1)}, u32[]{:S(2)}, u32[]{:S(2)}) %collective-permute-start.35) | collective-permute-done | bytes 73760 | tf_op jit(solution)/shard_map/ppermute | solution.py:306
  374.3 4.9 %collective-permute-done.44 = f32[20,768]{1,0:T(8,128)S(1)} collective-permute-done((f32[20,768]{1,0:T(8,128)S(1)}, f32[20,768]{1,0:T(8,128)S(1)}, u32[]{:S(2)}, u32[]{:S(2)}) %collective-permute-start.44) | collective-permute-done | bytes 61472 | tf_op jit(solution)/shard_map/ppermute | solution.py:306
  386.7 4.4 %collective-permute-done.48 = bf16[3,96,384]{2,1,0:T(8,128)(2,1)S(1)} collective-permute-done((bf16[3,96,384]{2,1,0:T(8,128)(2,1)S(1)}, bf16[3,96,384]{2,1,0:T(8,128)(2,1)S(1)}, u32[]{:S(2)}, u32[]{:S(2)}) %collective-permute-start.48) | collective-permute-done | bytes 221216 | tf_op jit(solution)/shard_map/ppermute | solution.py:306
  (287 shorter events, 141.6 us)
Async XLA Ops:
  6.7 22.6 %collective-permute-start.4 = (bf16[192,768]{1,0:T(8,128)(2,1)S(1)}, bf16[192,768]{1,0:T(8,128)(2,1)S(1)}, u32[]{:S(2)}, u32[]{:S(2)}) collective-permute-start(bf16[192,768]{1,0:T(8,128)(2,1)S(1)} %pad_maximum_fusion.7), channel_id=1, source_target_pairs={{0,1},{1,0},{2,3},{3,2},{4,5},{5,4},{6,7},{7,6},{8,9},{9,8},{10,11... | collective-permute-start | bytes 884744 | tf_op jit(solution)/shard_map/ppermute | solution.py:306
  29.3 24.4 %collective-permute-start.9 = (bf16[384,768]{1,0:T(8,128)(2,1)S(1)}, bf16[384,768]{1,0:T(8,128)(2,1)S(1)}, u32[]{:S(2)}, u32[]{:S(2)}) collective-permute-start(bf16[384,768]{1,0:T(8,128)(2,1)S(1)} %pad_maximum_fusion.3), channel_id=1, source_target_pairs={{0,2},{1,3},{2,0},{3,1},{4,6},{5,7},{6,4},{7,5},{8,10},{9,11},{10,... | collective-permute-start | bytes 1769480 | tf_op jit(solution)/shard_map/ppermute | solution.py:306
  36.1 17.7 %collective-permute-start.7 = (bf16[288,768]{1,0:T(8,128)(2,1)S(1)}, bf16[288,768]{1,0:T(8,128)(2,1)S(1)}, u32[]{:S(2)}, u32[]{:S(2)}) collective-permute-start(bf16[288,768]{1,0:T(8,128)(2,1)S(1)} %pad_maximum_fusion.4.refs_0_), channel_id=1, source_target_pairs={{0,16},{4,20},{8,24},{12,28},{16,0},{20,4},{24,8},{28,12},{1,17},{... | collective-permute-start | bytes 1327112 | tf_op jit(solution)/shard_map/ppermute | solution.py:306
  53.9 21.8 %collective-permute-start.6 = (bf16[512,768]{1,0:T(8,128)(2,1)S(1)}, bf16[512,768]{1,0:T(8,128)(2,1)S(1)}, u32[]{:S(2)}, u32[]{:S(2)}) collective-permute-start(bf16[512,768]{1,0:T(8,128)(2,1)S(1)} %add_convert_fusion.2.refs_0_), channel_id=1, source_target_pairs={{1,0},{2,1},{3,2},{5,4},{6,5},{7,6},{9,8},{10,9},{11,10},{13,12},{... | collective-permute-start | bytes 2359304 | tf_op jit(solution)/shard_map/ppermute | solution.py:935
  55.2 21.7 %collective-permute-start.5 = (bf16[512,768]{1,0:T(8,128)(2,1)S(1)}, bf16[512,768]{1,0:T(8,128)(2,1)S(1)}, u32[]{:S(2)}, u32[]{:S(2)}) collective-permute-start(bf16[512,768]{1,0:T(8,128)(2,1)S(1)} %add_convert_fusion.2.refs_0_), channel_id=1, source_target_pairs={{0,1},{1,2},{2,3},{4,5},{5,6},{6,7},{8,9},{9,10},{10,11},{12,13},{... | collective-permute-start | bytes 2359304 | tf_op jit(solution)/shard_map/ppermute | solution.py:935
  61.7 19.7 %collective-permute-start.16 = (bf16[432,768]{1,0:T(8,128)(2,1)S(1)}, bf16[432,768]{1,0:T(8,128)(2,1)S(1)}, u32[]{:S(2)}, u32[]{:S(2)}) collective-permute-start(bf16[432,768]{1,0:T(8,128)(2,1)S(1)} %pad_maximum_fusion.2), channel_id=1, source_target_pairs={{0,8},{4,12},{8,0},{12,4},{16,24},{20,28},{24,16},{28,20},{1,9},{5... | collective-permute-start | bytes 1990664 | tf_op jit(solution)/shard_map/ppermute | solution.py:306
  62.3 19.2 %collective-permute-start.17 = (bf16[432,768]{1,0:T(8,128)(2,1)S(1)}, bf16[432,768]{1,0:T(8,128)(2,1)S(1)}, u32[]{:S(2)}, u32[]{:S(2)}) collective-permute-start(bf16[432,768]{1,0:T(8,128)(2,1)S(1)} %fusion.13), channel_id=1, source_target_pairs={{0,16},{4,20},{8,24},{12,28},{16,0},{20,4},{24,8},{28,12},{1,17},{... | collective-permute-start | bytes 1990664 | tf_op jit(solution)/shard_map/ppermute | solution.py:306
  76.9 26.0 %collective-permute-start.14 = (bf16[512,768]{1,0:T(8,128)(2,1)S(1)}, bf16[512,768]{1,0:T(8,128)(2,1)}, u32[]{:S(2)}, u32[]{:S(2)}) collective-permute-start(bf16[512,768]{1,0:T(8,128)(2,1)S(1)} %collective-permute-done.5), channel_id=1, source_target_pairs={{1,2},{2,3},{5,6},{6,7},{9,10},{10,11},{13,14},{14,15},{17,18},{18... | collective-permute-start | bytes 2359304 | tf_op jit(solution)/shard_map/ppermute | solution.py:935
  78.5 24.4 %collective-permute-start.15 = (bf16[512,768]{1,0:T(8,128)(2,1)S(1)}, bf16[512,768]{1,0:T(8,128)(2,1)}, u32[]{:S(2)}, u32[]{:S(2)}) collective-permute-start(bf16[512,768]{1,0:T(8,128)(2,1)S(1)} %collective-permute-done.6), channel_id=1, source_target_pairs={{1,0},{2,1},{5,4},{6,5},{9,8},{10,9},{13,12},{14,13},{17,16},{18,1... | collective-permute-start | bytes 2359304 | tf_op jit(solution)/shard_map/ppermute | solution.py:935
  81.6 47.3 %collective-permute-start.19 = (bf16[864,768]{1,0:T(8,128)(2,1)S(1)}, bf16[864,768]{1,0:T(8,128)(2,1)S(1)}, u32[]{:S(2)}, u32[]{:S(2)}) collective-permute-start(bf16[864,768]{1,0:T(8,128)(2,1)S(1)} %pad_maximum_fusion.refs_7_), channel_id=1, source_target_pairs={{0,16},{4,20},{8,24},{12,28},{16,0},{20,4},{24,8},{28,12},{1,17},{... | collective-permute-start | bytes 3981320 | tf_op jit(solution)/shard_map/ppermute | solution.py:306
  82.2 46.8 %collective-permute-start.20 = (bf16[864,768]{1,0:T(8,128)(2,1)S(1)}, bf16[864,768]{1,0:T(8,128)(2,1)}, u32[]{:S(2)}, u32[]{:S(2)}) collective-permute-start(bf16[864,768]{1,0:T(8,128)(2,1)S(1)} %pad_maximum_fusion.1.refs_11_), channel_id=1, source_target_pairs={{0,8},{4,12},{8,0},{12,4},{16,24},{20,28},{24,16},{28,20},{1,9},{5... | collective-permute-start | bytes 3981320 | tf_op jit(solution)/shard_map/ppermute | solution.py:306
  104.1 22.7 %collective-permute-start.18 = (bf16[512,768]{1,0:T(8,128)(2,1)S(1)}, bf16[512,768]{1,0:T(8,128)(2,1)}, u32[]{:S(2)}, u32[]{:S(2)}) collective-permute-start(bf16[512,768]{1,0:T(8,128)(2,1)S(1)} %broadcast_select_fusion.1.refs_0_.refs_2_), channel_id=1, source_target_pairs={{1,0},{2,3},{5,4},{6,7},{9,8},{10,11},{13,12},{14,15},{17,16},{18,... | collective-permute-start | bytes 2359304 | tf_op jit(solution)/shard_map/ppermute | solution.py:935
  209.2 40.1 %collective-permute-start.28 = (bf16[5,2,96,768]{3,2,1,0:T(8,128)(2,1)}, bf16[5,2,96,768]{3,2,1,0:T(8,128)(2,1)S(1)}, u32[]{:S(2)}, u32[]{:S(2)}) collective-permute-start(bf16[5,2,96,768]{3,2,1,0:T(8,128)(2,1)} %get-tuple-element.279), channel_id=1, source_target_pairs={{0,8},{4,12},{8,0},{12,4},{16,24},{20,28},{24,16},{28,20},{1,9},{5... | collective-permute-start | bytes 4423688 | tf_op jit(solution)/shard_map/ppermute | solution.py:306
  210.7 33.4 %collective-permute-start.29 = (bf16[4,2,96,768]{3,2,1,0:T(8,128)(2,1)S(1)}, bf16[4,2,96,768]{3,2,1,0:T(8,128)(2,1)S(1)}, u32[]{:S(2)}, u32[]{:S(2)}) collective-permute-start(bf16[4,2,96,768]{3,2,1,0:T(8,128)(2,1)S(1)} %copy-done.49), channel_id=1, source_target_pairs={{0,16},{4,20},{8,24},{12,28},{16,0},{20,4},{24,8},{28,12},{1,17},{... | collective-permute-start | bytes 3538952 | tf_op jit(solution)/shard_map/ppermute | solution.py:306
  227.2 28.1 %collective-permute-start.27 = (bf16[512,768]{1,0:T(8,128)(2,1)}, bf16[512,768]{1,0:T(8,128)(2,1)S(1)}, u32[]{:S(2)}, u32[]{:S(2)}) collective-permute-start(bf16[512,768]{1,0:T(8,128)(2,1)} %get-tuple-element.284), channel_id=1, source_target_pairs={{0,1},{3,2},{4,5},{7,6},{8,9},{11,10},{12,13},{15,14},{16,17},{19,... | collective-permute-start | bytes 2359304 | tf_op jit(solution)/shard_map/ppermute | solution.py:935
  254.8 27.4 %collective-permute-start.32 = (bf16[5,1,96,768]{3,2,1,0:T(8,128)(2,1)}, bf16[5,1,96,768]{3,2,1,0:T(8,128)(2,1)S(1)}, u32[]{:S(2)}, u32[]{:S(2)}) collective-permute-start(bf16[5,1,96,768]{3,2,1,0:T(8,128)(2,1)} %get-tuple-element.294), channel_id=1, source_target_pairs={{0,16},{4,20},{8,24},{12,28},{16,0},{20,4},{24,8},{28,12},{1,17},{... | collective-permute-start | bytes 2211848 | tf_op jit(solution)/shard_map/ppermute | solution.py:306
  256.3 27.6 %collective-permute-start.30 = (bf16[512,768]{1,0:T(8,128)(2,1)}, bf16[512,768]{1,0:T(8,128)(2,1)}, u32[]{:S(2)}, u32[]{:S(2)}) collective-permute-start(bf16[512,768]{1,0:T(8,128)(2,1)} %add_convert_fusion.1), channel_id=1, source_target_pairs={{0,1},{1,2},{4,5},{5,6},{8,9},{9,10},{12,13},{13,14},{16,17},{17,1... | collective-permute-start | bytes 2359304 | tf_op jit(solution)/shard_map/ppermute | solution.py:935
  265.0 22.1 %collective-permute-start.31 = (bf16[512,768]{1,0:T(8,128)(2,1)}, bf16[512,768]{1,0:T(8,128)(2,1)}, u32[]{:S(2)}, u32[]{:S(2)}) collective-permute-start(bf16[512,768]{1,0:T(8,128)(2,1)} %add_convert_fusion.1), channel_id=1, source_target_pairs={{3,2},{2,1},{7,6},{6,5},{11,10},{10,9},{15,14},{14,13},{19,18},{18... | collective-permute-start | bytes 2359304 | tf_op jit(solution)/shard_map/ppermute | solution.py:935
  289.4 29.4 %collective-permute-start.36 = (bf16[512,768]{1,0:T(8,128)(2,1)}, bf16[512,768]{1,0:T(8,128)(2,1)}, u32[]{:S(2)}, u32[]{:S(2)}) collective-permute-start(bf16[512,768]{1,0:T(8,128)(2,1)} %select_convert_fusion), channel_id=1, source_target_pairs={{0,1},{1,2},{2,3},{4,5},{5,6},{6,7},{8,9},{9,10},{10,11},{12,13},{... | collective-permute-start | bytes 2359304 | tf_op jit(solution)/shard_map/ppermute | solution.py:935
  291.6 27.2 %collective-permute-start.37 = (bf16[512,768]{1,0:T(8,128)(2,1)}, bf16[512,768]{1,0:T(8,128)(2,1)}, u32[]{:S(2)}, u32[]{:S(2)}) collective-permute-start(bf16[512,768]{1,0:T(8,128)(2,1)} %add_convert_fusion), channel_id=1, source_target_pairs={{3,2},{2,1},{1,0},{7,6},{6,5},{5,4},{11,10},{10,9},{9,8},{15,14},{... | collective-permute-start | bytes 2359304 | tf_op jit(solution)/shard_map/ppermute | solution.py:935
  293.3 51.1 %collective-permute-start.34 = (bf16[2,192,768]{2,1,0:T(8,128)(2,1)}, bf16[2,192,768]{2,1,0:T(8,128)(2,1)}, u32[]{:S(2)}, u32[]{:S(2)}) collective-permute-start(bf16[2,192,768]{2,1,0:T(8,128)(2,1)} %fusion.14), channel_id=1, source_target_pairs={{0,2},{1,3},{2,0},{3,1},{4,6},{5,7},{6,4},{7,5},{8,10},{9,11},{10,... | collective-permute-start | bytes 1769480 | tf_op jit(solution)/shard_map/ppermute | solution.py:306
  298.9 44.8 %collective-permute-start.35 = (bf16[2,96,192]{1,2,0:T(8,128)(2,1)S(1)}, bf16[2,96,192]{1,2,0:T(8,128)(2,1)S(1)}, u32[]{:S(2)}, u32[]{:S(2)}) collective-permute-start(bf16[2,96,192]{1,2,0:T(8,128)(2,1)S(1)} %fusion.21), channel_id=1, source_target_pairs={{0,2},{1,3},{2,0},{3,1},{4,6},{5,7},{6,4},{7,5},{8,10},{9,11},{10,... | collective-permute-start | bytes 221192 | tf_op jit(solution)/shard_map/ppermute | solution.py:306
  330.5 16.5 %collective-permute-start.38 = (bf16[3,4,96,384]{3,2,1,0:T(8,128)(2,1)}, bf16[3,4,96,384]{3,2,1,0:T(8,128)(2,1)S(1)}, u32[]{:S(2)}, u32[]{:S(2)}) collective-permute-start(bf16[3,4,96,384]{3,2,1,0:T(8,128)(2,1)} %get-tuple-element.325), channel_id=1, source_target_pairs={{0,4},{4,0},{8,12},{12,8},{16,20},{20,16},{24,28},{28,24},{1,5},{5... | collective-permute-start | bytes 2654216 | tf_op jit(solution)/shard_map/ppermute | solution.py:306
  330.6 16.4 %collective-permute-start.39 = (bf16[3,4,96,384]{3,2,1,0:T(8,128)(2,1)}, bf16[3,4,96,384]{3,2,1,0:T(8,128)(2,1)S(1)}, u32[]{:S(2)}, u32[]{:S(2)}) collective-permute-start(bf16[3,4,96,384]{3,2,1,0:T(8,128)(2,1)} %get-tuple-element.327), channel_id=1, source_target_pairs={{0,4},{4,0},{8,12},{12,8},{16,20},{20,16},{24,28},{28,24},{1,5},{5... | collective-permute-start | bytes 2654216 | tf_op jit(solution)/shard_map/ppermute | solution.py:306
  (80 other events, 744.4 us)

commit v2 on v1

--- a/solution.py
+++ b/solution.py
@@ -30,17 +30,6 @@
     spread = jnp.mean(center * center, axis=-1, keepdims=True)
     inverse = lax.rsqrt(spread + epsilon)
     return center * inverse, inverse
-
-
-def norm_back(unit, inverse, gain_row, grad):
-    scaled = grad * gain_row
-    mean_scaled = jnp.mean(scaled, axis=-1, keepdims=True)
-    mean_unit = jnp.mean(scaled * unit, axis=-1, keepdims=True)
-    return (
-        inverse * (scaled - mean_scaled - unit * mean_unit),
-        jnp.sum(grad * unit, axis=0),
-        jnp.sum(grad, axis=0),
-    )
 
 
 def dot_of(left_side, right_side, left_dim, right_dim):
@@ -185,32 +174,28 @@
     k_pair = k_ref[...]
     v_pair = v_ref[...]
     lower = first_half((rows, PAIR))
-    lower_keys = first_half((keys, PAIR))
+    nothing = jnp.zeros((rows, PAIR), low)
+    two_halves = lambda pair: jnp.concatenate(
+        [jnp.where(lower, pair, nothing), jnp.where(lower, nothing, pair)]
+    )
+    queries = two_halves(q_pair)
+    grads_out = two_halves(g_pair)
+    row_of = lambda ref: jnp.concatenate([ref[0, 0:1, :], ref[0, 1:2, :]], axis=1)
     place = lax.broadcasted_iota(jnp.int32, (keys, 1), 0)
     bias = jnp.where(place < limit, 0.0, far_below)
-    dq = []
-    dk = []
-    dv = []
-    for half in range(2):
-        kept = lower if half == 0 else jnp.logical_not(lower)
-        q_half = jnp.where(kept, q_pair, jnp.zeros_like(q_pair))
-        g_half = jnp.where(kept, g_pair, jnp.zeros_like(g_pair))
-        log_row = log_ref[0, half : half + 1, :]
-        delta_row = delta_ref[0, half : half + 1, :]
-        scores = dot_of(k_pair, q_half, 1, 1) + bias
-        probs = jnp.exp(scores - log_row)
-        dv.append(dot_of(probs.astype(low), g_pair, 1, 0))
-        prob_grad = dot_of(v_pair, g_half, 1, 1)
-        score_grad = (probs * (prob_grad - delta_row)).astype(low)
-        dk.append(dot_of(score_grad, q_pair, 1, 0))
-        dq.append(dot_of(score_grad, k_pair, 0, 0))
-    dk_low = jnp.where(lower_keys, dk[0], dk[1]).astype(low)
-    dv_low = jnp.where(lower_keys, dv[0], dv[1]).astype(low)
+    scores = dot_of(k_pair, queries, 1, 1) + bias
+    prob_grad = dot_of(v_pair, grads_out, 1, 1)
+    probs = jnp.exp(scores - row_of(log_ref))
+    score_grad = (probs * (prob_grad - row_of(delta_ref))).astype(low)
+    dv_low = dot_of(probs.astype(low), grads_out, 1, 0).astype(low)
+    dk_low = dot_of(score_grad, queries, 1, 0).astype(low)
+    turned = dot_of(k_pair.T, score_grad, 1, 0)
+    upper_rows = lax.broadcasted_iota(jnp.int32, (PAIR, rows), 0) < HEAD_DIM
     dk_ref[...] = dk_low
     dv_ref[...] = dv_low
     grads = [dk_low, dv_low]
     weights = [wk_ref[...], wv_ref[...]]
-    dq_all = jnp.where(lower, dq[0], dq[1])
+    dq_all = jnp.where(upper_rows, turned[:, :rows], turned[:, rows:]).T
     if not first:
         dq_all = dq_all + dq_in[...]
     back = dot_of(jnp.concatenate(grads, axis=1), jnp.concatenate(weights, axis=1), 1, 1)
@@ -366,6 +351,8 @@
         return offset
     row = (me ^ mask) * block + offset
     if stride:
+        if rank_mask >= 2:
+            rank_mask = rank_mask ^ ((rank + 1) // 2 % 2)
         row = row + (rank ^ rank_mask) * stride
     return pl.multiple_of(row, 16)
 
@@ -420,24 +407,32 @@
     )(*arrays)
 
 
+def store_split(value, keep, send, index):
+    block = keep.shape[2]
+    even = lax.axis_index("dp") % 2 == 0
+    for outer in range(keep.shape[1]):
+        first = value[2 * outer * block : (2 * outer + 1) * block]
+        other = value[(2 * outer + 1) * block : (2 * outer + 2) * block]
+        keep[index, outer] = jnp.where(even, first, other).astype(low)
+        send[index, outer] = jnp.where(even, other, first).astype(low)
+
+
 def middle_kernel(plan, block, total, *refs):
     limit_ref, vector_ref = refs[:2]
     token_hbm, mixed_hbm, log_hbm, cot_hbm, teach_hbm = refs[2:7]
     pieces = refs[7 : 7 + total]
     (
         out_hbm,
-        final_hbm,
-        act_hbm,
-        pre_hbm,
-        second_hbm,
-        middle_low_hbm,
-        attended_hbm,
         middle_hbm,
         grad_hbm,
+        down_keep,
+        down_send,
+        up_keep,
+        up_send,
         delta_ref,
         log_ref,
         sum_ref,
-    ) = refs[7 + total : 19 + total]
+    ) = refs[7 + total : 17 + total]
     (
         token,
         mixed,
@@ -447,11 +442,9 @@
         up,
         down,
         proj,
-        act,
-        pre,
+        right,
         slope,
         second,
-        attended,
         middle,
         final,
         out,
@@ -459,10 +452,16 @@
         middle_low,
         grad,
         accum,
+        turned,
+        stage_keep,
+        stage_send,
         in_sems,
         weight_sems,
         out_sems,
-    ) = refs[19 + total :]
+        keep_sems,
+        send_sems,
+    ) = refs[17 + total :]
+    hidden = FF // D
     targets = (up, down, proj)
     rows = token.shape[0]
     me = lax.axis_index("dp")
@@ -510,16 +509,14 @@
     weight = vector_ref[5:6, :]
     gets[0].wait()
     gets[1].wait()
-    attended[...] = mixed[...].astype(low)
-    puts = [send(attended, attended_hbm, 0)]
+    right[2 * hidden] = mixed[...].astype(low)
     for copy in loads[2]:
         copy.wait()
     state = token[...].astype(full) + table_row + out_bias
-    state = state + dot_of(attended[...], proj[...], 1, 1)
+    state = state + dot_of(right[2 * hidden], proj[...], 1, 1)
     middle[...] = state
     unit, _ = norm_stats(state)
     second[...] = (unit * gain + shift).astype(low)
-    puts.append(send(second, second_hbm, 1))
     accum[...] = jnp.zeros((rows, D), full)
     for copy in loads[0]:
         copy.wait()
@@ -530,16 +527,15 @@
         place = pl.ds(pl.multiple_of(m * D, D), D)
         value = dot_of(second[...], up[place, :], 1, 0) + vector_ref[pl.ds(8 + m, 1), :]
         cumulative = 0.5 + 0.5 * lax.erf(value * (0.5**0.5))
-        act[m] = (value * cumulative).astype(low)
+        right[m] = (value * cumulative).astype(low)
         slope[m] = cumulative + value * jnp.exp(-0.5 * value * value) * 0.3989422804014327
-        accum[...] += dot_of(act[m], down[place, :], 1, 1)
+        accum[...] += dot_of(right[m], down[place, :], 1, 1)
         return 0
 
     lax.fori_loop(0, FF // D, forward, 0)
-    puts.append(send(act, act_hbm, 2))
     final_state = middle[...] + accum[...] + down_bias
     out[...] = final_state.astype(low)
-    puts.append(send(out, out_hbm, 3))
+    puts = [send(out, out_hbm, 0)]
     gets[3].wait()
     gets[4].wait()
     place = lax.broadcasted_iota(jnp.int32, (rows, 1), 0)
@@ -547,7 +543,6 @@
     grads = jnp.where(place < limit_ref[5], grads, 0.0)
     final[...] = grads
     final_low[...] = grads.astype(low)
-    puts.append(send(final_low, final_hbm, 4))
     sum_ref[3:4, :] = jnp.sum(grads, axis=0, keepdims=True)
     accum[...] = jnp.zeros((rows, D), full)
 
@@ -555,13 +550,12 @@
         place = pl.ds(pl.multiple_of(m * D, D), D)
         value = slope[m] * dot_of(final_low[...], down[place, :], 1, 0)
         value = value.astype(low)
-        pre[m] = value
+        right[hidden + m] = value
         sum_ref[pl.ds(8 + m, 1), :] = jnp.sum(value.astype(full), axis=0, keepdims=True)
         accum[...] += dot_of(value, up[place, :], 1, 1)
         return 0
 
     lax.fori_loop(0, FF // D, backward, 0)
-    puts.append(send(pre, pre_hbm, 5))
     unit, inverse = norm_stats(middle[...])
     second_grad = accum[...]
     sum_ref[0:1, :] = jnp.sum(second_grad * unit, axis=0, keepdims=True)
@@ -571,13 +565,12 @@
     mean_unit = jnp.mean(scaled * unit, axis=-1, keepdims=True)
     total_grad = final[...] + inverse * (scaled - mean_scaled - unit * mean_unit)
     middle[...] = total_grad
-    puts.append(send(middle, middle_hbm, 6))
+    puts.append(send(middle, middle_hbm, 1))
     middle_low[...] = total_grad.astype(low)
-    puts.append(send(middle_low, middle_low_hbm, 7))
     sum_ref[2:3, :] = jnp.sum(total_grad, axis=0, keepdims=True)
     attended_grad = dot_of(middle_low[...], proj[...], 1, 0).astype(low)
     grad[...] = attended_grad
-    puts.append(send(grad, grad_hbm, 8))
+    puts.append(send(grad, grad_hbm, 2))
     gets[2].wait()
     head = lax.broadcasted_iota(jnp.int32, (16, D), 0)
     lane = lax.broadcasted_iota(jnp.int32, (16, D), 1)
@@ -594,16 +587,45 @@
     for pair in range(PAIRS):
         delta_ref[pair] = deltas[2 * pair : 2 * pair + 2]
         log_ref[pair] = tops[2 * pair : 2 * pair + 2]
+    turned[0] = final_low[...].T
+    turned[1] = second[...].T
+    turned[2] = middle_low[...].T
+
+    def weights(i, _):
+        store_split(dot_of(turned[i // hidden], right[i], 1, 0), stage_keep, stage_send, i)
+
+        @pl.when(i < hidden)
+        def _():
+            pltpu.make_async_copy(stage_keep.at[i], down_keep.at[i], keep_sems.at[i]).start()
+            pltpu.make_async_copy(stage_send.at[i], down_send.at[i], send_sems.at[i]).start()
+
+        @pl.when(i >= hidden)
+        def _():
+            row = i - hidden
+            pltpu.make_async_copy(stage_keep.at[i], up_keep.at[row], keep_sems.at[i]).start()
+            pltpu.make_async_copy(stage_send.at[i], up_send.at[row], send_sems.at[i]).start()
+
+        return 0
+
+    lax.fori_loop(0, 2 * hidden + 1, weights, 0)
     for copy in puts:
         copy.wait()
-
-
-def middle_call(limit, vectors, tokens, mixed, logs, cot, teach, arrays, plan, block):
+    for i in range(2 * hidden + 1):
+        if i < hidden:
+            keep, gone, row = down_keep, down_send, i
+        else:
+            keep, gone, row = up_keep, up_send, i - hidden
+        pltpu.make_async_copy(stage_keep.at[i], keep.at[row], keep_sems.at[i]).wait()
+        pltpu.make_async_copy(stage_send.at[i], gone.at[row], send_sems.at[i]).wait()
+
+
+def middle_call(limit, vectors, tokens, mixed, logs, cot, teach, arrays, plan, block, dp):
     rows = tokens.shape[0]
     hidden = FF // D
     narrow = jax.ShapeDtypeStruct((rows, D), low)
     wide = jax.ShapeDtypeStruct((rows, D), full)
-    many = jax.ShapeDtypeStruct((hidden, rows, D), low)
+    shape = (dp // 2, D // dp, D)
+    parts = [jax.ShapeDtypeStruct((count,) + shape, low) for count in (hidden, hidden + 1)]
     stats = jax.ShapeDtypeStruct((PAIRS, 2, rows), full)
     anywhere = pl.BlockSpec(memory_space=pl.ANY)
     inside = pl.BlockSpec(memory_space=pltpu.VMEM)
@@ -612,21 +634,19 @@
         functools.partial(middle_kernel, plan, block, len(arrays)),
         out_shape=(
             narrow,
-            narrow,
-            many,
-            many,
-            narrow,
-            narrow,
-            narrow,
             wide,
             narrow,
+            parts[0],
+            parts[0],
+            parts[1],
+            parts[1],
             stats,
             stats,
             jax.ShapeDtypeStruct((8 + 8, D), full),
         ),
         in_specs=[pl.BlockSpec(memory_space=pltpu.SMEM), inside]
         + [anywhere] * (5 + len(arrays)),
-        out_specs=[anywhere] * 9 + [inside] * 3,
+        out_specs=[anywhere] * 7 + [inside] * 3,
         scratch_shapes=[
             pltpu.VMEM((rows, D), low),
             pltpu.VMEM((rows, D), full),
@@ -636,10 +656,8 @@
             pltpu.VMEM((FF, D), low),
             pltpu.VMEM((FF, D), low),
             pltpu.VMEM((D, D), low),
-            pltpu.VMEM((hidden, rows, D), low),
-            pltpu.VMEM((hidden, rows, D), low),
+            pltpu.VMEM((2 * hidden + 1, rows, D), low),
             pltpu.VMEM((hidden, rows, D), full),
-            pltpu.VMEM((rows, D), low),
             pltpu.VMEM((rows, D), low),
             pltpu.VMEM((rows, D), full),
             pltpu.VMEM((rows, D), full),
@@ -648,66 +666,19 @@
             pltpu.VMEM((rows, D), low),
             pltpu.VMEM((rows, D), low),
             pltpu.VMEM((rows, D), full),
+            pltpu.VMEM((3, D, rows), low),
+            pltpu.VMEM((2 * hidden + 1,) + shape, low),
+            pltpu.VMEM((2 * hidden + 1,) + shape, low),
             pltpu.SemaphoreType.DMA((5,)),
             pltpu.SemaphoreType.DMA((moves,)),
-            pltpu.SemaphoreType.DMA((9,)),
+            pltpu.SemaphoreType.DMA((3,)),
+            pltpu.SemaphoreType.DMA((2 * hidden + 1,)),
+            pltpu.SemaphoreType.DMA((2 * hidden + 1,)),
         ],
         compiler_params=pltpu.CompilerParams(vmem_limit_bytes=VMEM_LIMIT),
         cost_estimate=SMALL_COST,
         name="middle",
     )(limit, vectors, tokens, mixed, logs, cot, teach, *arrays)
-
-
-def store_split(value, keep, send, index):
-    block = keep.shape[2]
-    even = lax.axis_index("dp") % 2 == 0
-    for outer in range(keep.shape[1]):
-        first = value[2 * outer * block : (2 * outer + 1) * block]
-        other = value[(2 * outer + 1) * block : (2 * outer + 2) * block]
-        keep[index, outer] = jnp.where(even, first, other).astype(low)
-        send[index, outer] = jnp.where(even, other, first).astype(low)
-
-
-def feed_grad_kernel(left_ref, right_ref, *refs):
-    keep, send, turned = refs[-3:]
-    m = pl.program_id(0)
-
-    @pl.when(m == 0)
-    def _():
-        turned[...] = left_ref[...].T
-
-    @pl.when(m < FF // D)
-    def _():
-        store_split(dot_of(turned[...], right_ref[0], 1, 0), keep, send, 0)
-
-    if len(refs) > 3:
-
-        @pl.when(m == FF // D)
-        def _():
-            store_split(dot_of(refs[0][...].T, refs[1][...], 1, 0), keep, send, 0)
-
-
-def feed_grads(left, right, more, dp):
-    rows = left.shape[0]
-    hidden = FF // D
-    count = hidden + (1 if more else 0)
-    whole = pl.BlockSpec((rows, D), lambda m: (0, 0))
-    shape = (count, dp // 2, D // dp, D)
-    return pl.pallas_call(
-        feed_grad_kernel,
-        out_shape=[jax.ShapeDtypeStruct(shape, low)] * 2,
-        grid=(count,),
-        in_specs=[
-            whole,
-            pl.BlockSpec((1, rows, D), lambda m: (jnp.minimum(m, hidden - 1), 0, 0)),
-        ]
-        + [whole] * len(more),
-        out_specs=[pl.BlockSpec((1,) + shape[1:], lambda m: (m, 0, 0, 0))] * 2,
-        scratch_shapes=[pltpu.VMEM((D, rows), low)],
-        compiler_params=pltpu.CompilerParams(vmem_limit_bytes=VMEM_LIMIT),
-        cost_estimate=SMALL_COST,
-        name="feed_grads",
-    )(left, right, *more)
 
 
 def fold_kernel(bits, places, *refs):
@@ -745,64 +716,137 @@
 
 
 def qkv_grad_kernel(count, *refs):
-    chunk_refs = refs[:count]
-    query_ref = refs[count]
-    key_refs = refs[count + 1 : 2 * count + 1]
-    value_refs = refs[2 * count + 1 : 3 * count + 1]
-    keeps, sends = refs[3 * count + 1 : 3 * count + 3], refs[3 * count + 3 : 3 * count + 5]
-    sum_ref, turned = refs[3 * count + 5 :]
-    rows = query_ref.shape[0]
-    c = pl.program_id(0)
-    ones = jnp.ones((16, rows), low)
-
-    def store(value):
-        for n in range(2):
-            store_split(value[:, n * D // 2 : (n + 1) * D // 2], keeps[n], sends[n], 0)
-
-    @pl.when(c == 0)
-    def _():
-        for n in range(count):
-            turned[n] = chunk_refs[n][...].T
-        store(dot_of(turned[0], query_ref[...], 1, 0))
-        sum_ref[0:8, :] = dot_of(ones, query_ref[...], 1, 0)[0:8]
-
-    def many(sources):
-        value = dot_of(turned[0], sources[0][...], 1, 0)
-        for n in range(1, count):
-            value = value + dot_of(turned[n], sources[n][...], 1, 0)
-        store(value)
-
-    @pl.when(c == 1)
-    def _():
-        many(key_refs)
-
-    @pl.when(c == 2)
-    def _():
-        many(value_refs)
-        value = dot_of(ones, value_refs[0][...], 1, 0)
-        for n in range(1, count):
-            value = value + dot_of(ones, value_refs[n][...], 1, 0)
-        sum_ref[8:16, :] = value[0:8]
+    sources = refs[: 3 * count + 1]
+    outs = refs[3 * count + 1 : 3 * count + 5]
+    sum_ref, held, turned, total, stage, in_sems, out_sems = refs[3 * count + 5 :]
+    first_use = [0, count] + list(range(1, count)) + list(range(count + 1, 3 * count + 1))
+    for n in first_use:
+        pltpu.make_async_copy(sources[n], held.at[n], in_sems.at[n]).start()
+
+    def wait(n):
+        pltpu.make_async_copy(sources[0], held.at[n], in_sems.at[n]).wait()
+
+    def turn(n, _):
+        wait(n)
+        turned[n] = held[n].T
+        return 0
+
+    lax.fori_loop(0, count, turn, 0)
+    sum_ref[...] = jnp.zeros_like(sum_ref)
+
+    def step(i, _):
+        c = (i + count - 1) // count
+        n = jnp.where(i == 0, 0, (i + count - 1) % count)
+        wait(count + i)
+        right = held[count + i]
+        value = dot_of(turned[n], right, 1, 0)
+        total[...] = value + jnp.where(n == 0, jnp.zeros_like(value), total[...])
+
+        @pl.when(c != 1)
+        def _():
+            row = pl.ds(pl.multiple_of(c * 4, 8), 1)
+            sum_ref[row, :] += jnp.sum(right.astype(full), axis=0, keepdims=True)
+
+        @pl.when(i % count == 0)
+        def _():
+            for part in range(2):
+                store_split(
+                    total[:, part * D // 2 : (part + 1) * D // 2],
+                    stage.at[part],
+                    stage.at[2 + part],
+                    c,
+                )
+            for k in range(4):
+                pltpu.make_async_copy(
+                    stage.at[k, c], outs[k].at[c], out_sems.at[k * 3 + c]
+                ).start()
+
+        return 0
+
+    lax.fori_loop(0, 2 * count + 1, step, 0)
+    for k in range(4):
+        for c in range(3):
+            pltpu.make_async_copy(stage.at[k, c], outs[k].at[c], out_sems.at[k * 3 + c]).wait()
 
 
 def qkv_grads(chunks, query_grad, key_grads, value_grads, dp):
     rows = query_grad.shape[0]
     count = len(chunks)
-    whole = pl.BlockSpec((rows, D), lambda c: (0, 0))
     shape = (3, dp // 2, D // dp, D // 2)
-    part = pl.BlockSpec((1,) + shape[1:], lambda c: (c, 0, 0, 0))
+    anywhere = pl.BlockSpec(memory_space=pl.ANY)
     return pl.pallas_call(
         functools.partial(qkv_grad_kernel, count),
         out_shape=[jax.ShapeDtypeStruct(shape, low)] * 4
         + [jax.ShapeDtypeStruct((16, D), full)],
-        grid=(3,),
-        in_specs=[whole] * (3 * count + 1),
-        out_specs=[part] * 4 + [pl.BlockSpec((16, D), lambda c: (0, 0))],
-        scratch_shapes=[pltpu.VMEM((count, D, rows), low)],
+        in_specs=[anywhere] * (3 * count + 1),
+        out_specs=[anywhere] * 4 + [pl.BlockSpec(memory_space=pltpu.VMEM)],
+        scratch_shapes=[
+            pltpu.VMEM((3 * count + 1, rows, D), low),
+            pltpu.VMEM((count, D, rows), low),
+            pltpu.VMEM((D, D), full),
+            pltpu.VMEM((4,) + shape, low),
+            pltpu.SemaphoreType.DMA((3 * count + 1,)),
+            pltpu.SemaphoreType.DMA((12,)),
+        ],
         compiler_params=pltpu.CompilerParams(vmem_limit_bytes=VMEM_LIMIT),
         cost_estimate=SMALL_COST,
         name="qkv_grads",
     )(*chunks, query_grad, *key_grads, *value_grads)
+
+
+def last_kernel(
+    token_ref,
+    first_ref,
+    right_ref,
+    left_ref,
+    middle_ref,
+    vector_ref,
+    gain_ref,
+    bias_ref,
+    sum_ref,
+    out_ref,
+    pack_ref,
+):
+    @pl.when(pl.program_id(0) == 0)
+    def _():
+        pack_ref[...] = jnp.zeros_like(pack_ref)
+        pack_ref[1:2, :] = sum_ref[0:1, :]
+        pack_ref[3:4, :] = sum_ref[1:2, :]
+        pack_ref[4:5, :] = bias_ref[0:1, :]
+        pack_ref[5:6, :] = bias_ref[8:9, :]
+        pack_ref[6:8, :] = sum_ref[2:4, :]
+        pack_ref[8 : 8 + FF // D, :] = sum_ref[8 : 8 + FF // D, :]
+
+    unit, inverse = norm_stats(token_ref[...].astype(full) + vector_ref[0:1, :])
+    grad = first_ref[...] + right_ref[...].astype(full) + left_ref[...].astype(full)
+    scaled = grad * gain_ref[0:1, :]
+    mean_scaled = jnp.mean(scaled, axis=-1, keepdims=True)
+    mean_unit = jnp.mean(scaled * unit, axis=-1, keepdims=True)
+    result = middle_ref[...] + inverse * (scaled - mean_scaled - unit * mean_unit)
+    out_ref[...] = result
+    pack_ref[0:1, :] += jnp.sum(grad * unit, axis=0, keepdims=True)
+    pack_ref[2:3, :] += jnp.sum(grad, axis=0, keepdims=True)
+    pack_ref[pl.ds(16 + lax.axis_index("dp"), 1), :] += jnp.sum(result, axis=0, keepdims=True)
+
+
+def last_norm(tokens, first, right, left, middle_grad, vectors, gains, bias_sums, sums, dp):
+    rows = tokens.shape[0]
+    part = pl.BlockSpec((rows // 4, D), lambda i: (i, 0))
+    whole = lambda value: pl.BlockSpec(value.shape, lambda i: (0, 0))
+    small = (vectors, gains, bias_sums, sums)
+    return pl.pallas_call(
+        last_kernel,
+        out_shape=(
+            jax.ShapeDtypeStruct((rows, D), full),
+            jax.ShapeDtypeStruct((16 + dp, D), full),
+        ),
+        grid=(4,),
+        in_specs=[part] * 5 + [whole(value) for value in small],
+        out_specs=[part, pl.BlockSpec((16 + dp, D), lambda i: (0, 0))],
+        compiler_params=pltpu.CompilerParams(vmem_limit_bytes=VMEM_LIMIT),
+        cost_estimate=SMALL_COST,
+        name="last_norm",
+    )(tokens, first, right, left, middle_grad, *small)
 
 
 def two_parts(value, axis, mine):
@@ -826,57 +870,55 @@
                 places.append(left[n].index(turn[step + 1]))
                 left[n].remove(turn[step + 1])
             parts = fold(pairs, [turn[step + 1] for turn in orders], places)
-    return [(keep.astype(full) + other.astype(full))[:, 0] for keep, other in pairs]
-
-
-def scatter_mp(values):
+    got = yield [other for _, other in pairs]
+    return [
+        (keep.astype(full) + other.astype(full))[:, 0] for (keep, _), other in zip(pairs, got)
+    ]
+
+
+def scatter_mp(value):
     rank = lax.axis_index("mp")
-    for bit in (2, 1):
-        parts = []
-        for value in values:
-            pair = value.reshape((2, value.shape[0] // 2) + value.shape[1:])
-            parts.append(two_parts(pair, 0, (rank // bit) % 2))
-        sends = yield [send for _, send in parts]
-        values = [
-            keep.astype(full) + swap(send, "mp", bit).astype(full)
-            for (keep, _), send in zip(parts, sends)
-        ]
-    return [value[0] for value in values]
+    part = lambda index: lax.dynamic_index_in_dim(value, index, keepdims=False)
+    sends = yield [part(rank ^ bit).astype(low) for bit in (1, 2, 3)]
+    got = yield [swap(send, "mp", bit) for bit, send in zip((1, 2, 3), sends)]
+    got = [other.astype(full) for other in got]
+    return (part(rank) + got[0]) + (got[1] + got[2])
 
 
 def scatter_feed(up_own, down_own):
     mp = lax.axis_size("mp")
     block = down_own.shape[1]
     out_own = up_own[mp].reshape(block, mp, -1).transpose(1, 0, 2)
-    tall, out_grad = yield from scatter_mp(
-        [jnp.concatenate([up_own[:mp], down_own], axis=1), out_own]
-    )
-    return tall[:block], tall[block:].T, out_grad.T
+    own = yield from scatter_mp(
+        jnp.concatenate([up_own[:mp], down_own, out_own.reshape(mp, -1, D)], axis=1)
+    )
+    return own[:block], own[block : 2 * block].T, own[2 * block :].reshape(block, -1).T
 
 
 def scatter_qkv(keep_left, keep_right, send_left, send_right):
-    rank = lax.axis_index("mp")
     left_part, right_part = yield from scatter_dp(
         [(keep_left, send_left), (keep_right, send_right)], (0, 1)
     )
-    upper = rank >= 2
-    odd = rank % 2 == 1
-    (send,) = yield [jnp.where(upper, left_part, right_part).astype(low)]
-    keep = jnp.where(upper, right_part, left_part) + swap(send, "mp", 2).astype(full)
     width = D // lax.axis_size("mp")
-    (send,) = yield [jnp.where(odd, keep[..., :width], keep[..., width:]).astype(low)]
-    return jnp.where(odd, keep[..., width:], keep[..., :width]) + swap(
-        send, "mp", 1
-    ).astype(full)
-
-
-def butterfly(value):
-    for bit in [1] + outer_bits():
+    parts = [part[..., at : at + width] for part in (left_part, right_part) for at in (0, width)]
+    return (yield from scatter_mp(jnp.stack(parts)))
+
+
+def sum_small(value):
+    (value,) = yield [value]
+    value = value + swap(value, "dp", 1)
+    bits = outer_bits()
+    groups = [("dp", bits[n : n + 2]) for n in range(0, len(bits), 2)] + [("mp", [1, 2])]
+    for axis, pair in groups:
         (value,) = yield [value]
-        value = value + swap(value, "dp", bit)
-    for bit in (1, 2):
-        (value,) = yield [value]
-        value = value + swap(value, "mp", bit)
+        if len(pair) == 1:
+            value = value + swap(value, axis, pair[0])
+        else:
+            one, two = pair
+            got = [swap(value, axis, mask) for mask in (one, two, one + two)]
+            if axis == "mp":
+                got = yield got
+            value = (value + got[0]) + (got[1] + got[2])
     return value
 
 
@@ -985,11 +1027,13 @@
         qkv_gather = Gather([qkv_rows[:split], qkv_rows[split:]])
         qkv_gather.advance(order)
     tall = order(jnp.concatenate([tall, tall_swap]))
-    tall_other = swap(tall, "mp", 2)
+    tall_across = along(tall, [(1, 2), (2, 1)])
 
     if aligned:
         while qkv_gather.step < len(qkv_gather.bits):
             qkv_gather.advance(order)
+    tall_across = order(tall_across)
+    tall_other = jnp.where(middle, tall_across, along(tall_across, [(1, 0), (2, 3)]))
     sent = order(first_norm)
     from_left = along(sent, [(0, 1), (1, 2), (2, 3)])
     from_right = along(sent, [(1, 0), (2, 1), (3, 2)])
@@ -1000,7 +1044,6 @@
                 jnp.concatenate([tall_other, out_rows[block // 2 :]]),
             ]
         )
-        feed_gather.advance(order)
         qkv_gather.advance(order)
         arrays, plan = plan_of(
             qkv_gather.result,
@@ -1013,6 +1056,7 @@
             ],
         )
         query_weight, pair_weight = order(*place(arrays, plan, block, [(D, D), (D, 2 * D)]))
+        feed_gather.advance(order)
     else:
         weights = lax.all_gather(qkv_rows.reshape(3, block, D), "dp", axis=1, tiled=True)
         query_weight = weights[0]
@@ -1067,31 +1111,12 @@
     keys = [key_own, key_near, key_second, key_last]
     values = [value_own, value_near, value_second, value_last]
 
-    (
-        output,
-        final_low,
-        hidden_act,
-        pre_grad,
-        second_norm,
-        middle_low,
-        attended,
-        middle_grad,
-        attended_grad,
-        deltas,
-        log_rows,
-        sums,
-    ) = middle_call(
-        scalars, vectors, tokens, mixed, logs, cotangent, teacher, arrays, plan, block
-    )
-    gain_two, shift_two, middle_sum, final_sum = sums[0], sums[1], sums[2], sums[3]
-    down = Steps(scatter_dp([feed_grads(final_low, hidden_act, (), dp)], (1,)))
+    output, middle_grad, attended_grad, *parts, deltas, log_rows, sums = middle_call(
+        scalars, vectors, tokens, mixed, logs, cotangent, teacher, arrays, plan, block, dp
+    )
+    down = Steps(scatter_dp([(parts[0], parts[1])], (1,)))
     down.advance(order)
-    second_norm = order(second_norm)
-    up = Steps(
-        scatter_dp([feed_grads(second_norm, pre_grad, (middle_low, attended), dp)], (0,))
-    )
-    up.advance(order)
-    down.advance(order)
+    up = Steps(scatter_dp([(parts[2], parts[3])], (0,)))
     up.advance(order)
 
     key_grads = [None] * 4
@@ -1115,62 +1140,58 @@
         )
         firsts[n] = order(firsts[n])
         if n == 3:
+            down.advance(order)
+            up.advance(order)
             back_last = along(firsts[3], [(0, 1), (3, 2)]).astype(full)
         elif n == 2:
-            down.advance(order)
-            up.advance(order)
             payload = order((firsts[2] + back_last).astype(low))
             back_right = along(payload, [(0, 1), (1, 2)]).astype(full)
             back_left = along(payload, [(3, 2), (2, 1)]).astype(full)
         elif n == 1:
+            down.advance(order)
+            up.advance(order)
             to_right = jnp.where(
                 rank == 0, firsts[1], firsts[3].astype(full) + back_right
             ).astype(low)
             to_left = (firsts[1] + back_left).astype(low)
-            (up_own,) = up.finish(order)
-            (down_own,) = down.finish(order)
-            feed = Steps(scatter_feed(up_own, down_own))
-            feed.advance(order)
             to_right, to_left = order(to_right, to_left)
             final_right = along(to_right, [(0, 1), (1, 2), (2, 3)])
             final_left = along(to_left, [(3, 2), (2, 1), (1, 0)])
+    (up_own,) = up.finish(order)
+    (down_own,) = down.finish(order)
+    feed = Steps(scatter_feed(up_own, down_own))
+    feed.advance(order)
     query_grad, final_right, final_left = order(query_grad, final_right, final_left)
     *halves, bias_sums = qkv_grads(chunks, query_grad, key_grads, value_grads, dp)
     qkv = Steps(scatter_qkv(*halves))
     qkv.advance(order)
-    qkv.advance(order)
-    feed.advance(order)
     tokens, first_own = order(tokens, firsts[0])
-    first_grad = first_own + final_right.astype(full) + final_left.astype(full)
-    unit_one, inverse_one = norm_stats(tokens.astype(full) + table_row)
-    start_part, gain_one, shift_one = norm_back(
-        unit_one, inverse_one, norm_gains[0], first_grad
-    )
-    input_grad = middle_grad + start_part
-    sequence_sum = jnp.sum(input_grad, axis=0)
-    own_slot = (jnp.arange(dp) == data_rank).astype(full)
-    packed = jnp.concatenate(
-        [
-            jnp.stack([gain_one, gain_two, shift_one, shift_two]),
-            jnp.stack([bias_sums[0], bias_sums[8]]),
-            jnp.stack([middle_sum, final_sum]),
-            sums[8 : 8 + FF // D],
-            own_slot[:, None] * sequence_sum[None, :],
-        ]
-    )
-    small = Steps(butterfly(packed))
-    small.advance(order)
+    input_grad, packed = last_norm(
+        tokens,
+        first_own,
+        final_right,
+        final_left,
+        middle_grad,
+        vectors,
+        norm_gains,
+        bias_sums,
+        sums,
+        dp,
+    )
+    packed, input_grad = order(packed, input_grad)
+    small = Steps(sum_small(packed))
     qkv.advance(order)
     small.advance(order)
     small.advance(order)
+    feed.advance(order)
     qkv.advance(order)
     small.advance(order)
     qkv.advance(order)
-    small.advance(order)
+    qkv.advance(order)
+    total = small.finish(order)
     qkv_grad = qkv.finish(order)
-    total = small.finish(order)
     up_grad, down_grad, out_grad = feed.finish(order)
-    fixed = 8 + FF // D
+    fixed = 16
     chosen = (timesteps[None, :] == jnp.arange(time_table.shape[0])[:, None]).astype(full)
     table_grad = lax.dot_general(
         chosen,
@@ -1190,7 +1211,7 @@
         out_grad,
         total[6],
         up_grad,
-        total[8:fixed].reshape(FF),
+        total[8 : 8 + FF // D].reshape(FF),
         down_grad,
         total[7],
     )

time: 410 us -> 378 us (0.922)
  waiting for transfers between devices: 92.3 us -> 54.2 us
  starting transfers between devices: 56.6 us -> 71.2 us
    ppermute x43 -> x44, waiting for transfers between devices: 75.4 us -> 30.6 us  [swap(): return lax.ppermute(value, axis, [(i, i ^ bit) for i in range(count)])]
    ppermute x43 -> x44, starting transfers between devices: 37.3 us -> 47.6 us  [swap(): return lax.ppermute(value, axis, [(i, i ^ bit) for i in range(count)])]
    pallas_call x2 -> x1, Pallas kernels: 15 us -> 5.16 us  [last_norm(): pl.pallas_call(last_kernel, out_shape=(jax.ShapeDtypeStruct((rows, D), fu...]
    pallas_call x1, Pallas kernels: 27.4 us -> 35.7 us  [middle_call(): pl.pallas_call(functools.partial(middle_kernel, plan, block, len(arrays))...]
    ppermute x10 -> x12, waiting for transfers between devices: 16.9 us -> 23.6 us  [shards(): along = lambda value, pairs: lax.ppermute(value, 'mp', pairs)]
    ppermute x10 -> x12, starting transfers between devices: 19.3 us -> 23.6 us  [shards(): along = lambda value, pairs: lax.ppermute(value, 'mp', pairs)]
    reduce_sum x2 -> x0, other arithmetic: 4.33 us -> none  [the longest x1 2.55 us: norm_back(): jnp.sum(grad * unit, axis=0)]
    unnamed x103 -> x77, local copies, waits for them, and re-layouts: 10.9 us -> 11.3 us
  transfers between devices with their start and end apart: 53 -> 56, of which waited for: 20 -> 12; matrix products, arithmetic and copies ran while one was open for 10% -> 10% of each run, Pallas kernels for 35% -> 39%
where the time goes in v2:
time: 378 us; the launch traced here: 371 us
  Pallas kernels  192 us (51%)
  starting transfers between devices  71.2 us (19%)
  waiting for transfers between devices  54.2 us (14%)
  other arithmetic  22.9 us (6%)
  local copies, waits for them, and re-layouts  22.5 us (6%)
  between operations  5.33 us (1%)
    pallas_call x4, Pallas kernels, attend_backward(): pl.pallas_call(functools.partial(backward_kernel, number, first, last), o...  61.9 us
    ppermute x44, starting transfers between devices, swap(): return lax.ppermute(value, axis, [(i, i ^ bit) for i in range(count)])  47.6 us
    pallas_call x3, Pallas kernels, attend_forward(): pl.pallas_call(functools.partial(forward_kernel, numbers, first, final),...  46.5 us
    pallas_call x1, Pallas kernels, middle_call(): pl.pallas_call(functools.partial(middle_kernel, plan, block, len(arrays))...  35.7 us
    ppermute x44, waiting for transfers between devices, swap(): return lax.ppermute(value, axis, [(i, i ^ bit) for i in range(count)])  30.6 us
    pallas_call x6, Pallas kernels, fold(): pl.pallas_call(functools.partial(fold_kernel, bits, places), out_shape=[j...  25.7 us
    ppermute x12, starting transfers between devices, shards(): along = lambda value, pairs: lax.ppermute(value, 'mp', pairs)  23.6 us
    ppermute x12, waiting for transfers between devices, shards(): along = lambda value, pairs: lax.ppermute(value, 'mp', pairs)  23.6 us
  transfers between devices with their start and end apart: 56, of which 12 were waited for; matrix products, arithmetic and copies ran while one was open for 10% of the time, Pallas kernels for 39%

profile of v2, /device:TPU:0, one launch (start us, length us, event | category | flops | bytes accessed | tf_op | source)
XLA Modules:
  0.0 370.8 jit_solution(16577471407917251634)
XLA Ops:
  38.2 6.3 %collective-permute-done.10.refs_5_ = bf16[288,768]{1,0:T(8,128)(2,1)S(1)} collective-permute-done((bf16[288,768]{1,0:T(8,128)(2,1)S(1)}, bf16[288,768]{1,0:T(8,128)(2,1)S(1)}, u32[]{:S(2)}, u32[]{:S(2)}) %collective-permute-start.10) | collective-permute-done | bytes 442400 | tf_op jit(solution)/shard_map/ppermute | solution.py:291
  48.4 5.3 %collective-permute-start.6 = (bf16[512,768]{1,0:T(8,128)(2,1)S(1)}, bf16[512,768]{1,0:T(8,128)(2,1)S(1)}, u32[]{:S(2)}, u32[]{:S(2)}) collective-permute-start(bf16[512,768]{1,0:T(8,128)(2,1)S(1)} %add_convert_fusion.2.refs_0_), channel_id=1, source_target_pairs={{0,1},{1,2},{2,3},{4,5},{5,6},{6,7},{8,9},{9,10},{10,11},{12,13},{... | collective-permute-start | bytes 2359304 | tf_op jit(solution)/shard_map/ppermute | solution.py:977
  56.0 4.2 %place.1 = (bf16[768,768]{1,0:T(8,128)(2,1)}, bf16[768,1536]{1,0:T(8,128)(2,1)}) custom-call(bf16[288,768]{1,0:T(8,128)(2,1)} %copy-done.9, bf16[288,768]{1,0:T(8,128)(2,1)} %copy-done.23, bf16[288,768]{1,0:T(8,128)(2,1)} %copy-done.24, bf16[288,768]{1,0:T(8,128)(2,1)} %copy-done.25, bf16[288,768]{1,0:T(8,128)(2,1)} %copy-done.8, ...), custom_call_target="tpu_custom_call" | custom-call | flops 1048576 | bytes 65536 | tf_op jit(solution)/shard_map/place/pallas_call | solution.py:398
  60.2 4.7 %collective-permute-done.8 = bf16[384,768]{1,0:T(8,128)(2,1)} collective-permute-done((bf16[384,768]{1,0:T(8,128)(2,1)}, bf16[384,768]{1,0:T(8,128)(2,1)}, u32[]{:S(2)}, u32[]{:S(2)}) %collective-permute-start.8) | collective-permute-done | bytes 589856 | tf_op jit(solution)/shard_map/ppermute | solution.py:977
  70.6 10.0 %collective-permute-done.7 = bf16[512,768]{1,0:T(8,128)(2,1)S(1)} collective-permute-done((bf16[512,768]{1,0:T(8,128)(2,1)S(1)}, bf16[512,768]{1,0:T(8,128)(2,1)S(1)}, u32[]{:S(2)}, u32[]{:S(2)}) %collective-permute-start.7) | collective-permute-done | bytes 786464 | tf_op jit(solution)/shard_map/ppermute | solution.py:977
  85.8 20.2 %attend_forward.3 = (bf16[512,768]{1,0:T(8,128)(2,1)}, bf16[512,768]{1,0:T(8,128)(2,1)}, bf16[512,768]{1,0:T(8,128)(2,1)}, bf16[512,768]{1,0:T(8,128)(2,1)}, bf1...) custom-call(s32[6]{0:T(128)} %stack.42.scalars.refs_0_, ...), custom_call_target="tpu_custom_call" | custom-call | flops 1048576 | bytes 65536 | tf_op jit(solution)/shard_map/attend_forward/pallas_call | solution.py:129
  108.7 13.2 %attend_forward.4 = (bf16[512,768]{1,0:T(8,128)(2,1)}, bf16[512,768]{1,0:T(8,128)(2,1)}, f32[512,768]{1,0:T(8,128)}, f32[512,768]{1,0:T(8,128)}, f32[512,768]{1,0:T(8,128)}) custom-call(s32[6]{0:T(128)} %stack.42.scalars.refs_0_, bf16[512,768]{1,0:T(8,128)(2,1)} %copy-done.1, bf16[768,1536]{1,0:T(8,128)(2,1)} %get-tuple-element.220.refs_2_.refs_3_.refs_1_.wk_ref.wv_ref, ...), custom_call_target="tpu_custom_call" | custom-call | flops 1048576 | bytes 65536 | tf_op jit(solution)/shard_map/attend_forward/pallas_call | solution.py:129
  121.9 5.5 %collective-permute-done.19 = bf16[512,768]{1,0:T(8,128)(2,1)S(1)} collective-permute-done((bf16[512,768]{1,0:T(8,128)(2,1)S(1)}, bf16[512,768]{1,0:T(8,128)(2,1)S(1)}, u32[]{:S(2)}, u32[]{:S(2)}) %collective-permute-start.19) | collective-permute-done | bytes 786464 | tf_op jit(solution)/shard_map/ppermute | solution.py:977
  129.5 13.1 %attend_forward.5 = (bf16[512,768]{1,0:T(8,128)(2,1)}, bf16[512,768]{1,0:T(8,128)(2,1)}, f32[512,768]{1,0:T(8,128)}, f32[512,768]{1,0:T(8,128)}) custom-call(s32[6]{0:T(128)} %stack.42.scalars.refs_0_, bf16[512,768]{1,0:T(8,128)(2,1)} %broadcast_select_fusion.2.refs_0_.refs_3_, bf16[768,1536]{1,0:T(8,128)(2,1)} %get-tuple-element.220.refs_2_.refs_3_.refs_1_.wk_ref.wv_ref, ...), custom_call_target="tpu_custom_call" | custom-call | flops 1048576 | bytes 65536 | tf_op jit(solution)/shard_map/attend_forward/pallas_call | solution.py:129
  144.2 35.7 %middle.1 = (bf16[512,768]{1,0:T(8,128)(2,1)}, f32[512,768]{1,0:T(8,128)}, bf16[512,768]{1,0:T(8,128)(2,1)}, bf16[4,4,96,768]{3,2,1,0:T(8,128)(2,1)}, bf16[4,4,9...) custom-call(s32[6]{0:T(128)} %stack.42.scalars.refs_0_, ...), custom_call_target="tpu_custom_call" | custom-call | flops 1048576 | bytes 65536 | tf_op jit(solution)/shard_map/middle/pallas_call | solution.py:633
  180.4 14.3 %attend_backward.4 = (f32[512,768]{1,0:T(8,128)}, bf16[512,768]{1,0:T(8,128)(2,1)}, bf16[512,768]{1,0:T(8,128)(2,1)}, bf16[512,768]{1,0:T(8,128)(2,1)}) custom-call(s32[6]{0:T(128)} %stack.42.scalars.refs_0_, bf16[512,768]{1,0:T(8,128)(2,1)} %get-tuple-element.241.refs_4_.q_ref, bf16[512,768]{1,0:T(8,128)(2,1)} %get-tuple-element.273.k_ref, ...), custom_call_target="tpu_custom_call" | custom-call | flops 1048576 | bytes 65536 | tf_op jit(solution)/shard_map/attend_backward/pallas_call | solution.py:242
  197.6 4.5 %fold.7 = (bf16[4,2,96,768]{3,2,1,0:T(8,128)(2,1)}, bf16[4,2,96,768]{3,2,1,0:T(8,128)(2,1)}) custom-call(bf16[4,4,96,768]{3,2,1,0:T(8,128)(2,1)} %get-tuple-element.278.refs_0_, bf16[4,4,96,768]{3,2,1,0:T(8,128)(2,1)} %copy-done.7), custom_call_target="tpu_custom_call" | custom-call | bytes 16777216 | tf_op jit(solution)/shard_map/fold/pallas_call | solution.py:705
  203.6 6.0 %fold.6 = (bf16[5,2,96,768]{3,2,1,0:T(8,128)(2,1)}, bf16[5,2,96,768]{3,2,1,0:T(8,128)(2,1)}) custom-call(bf16[5,4,96,768]{3,2,1,0:T(8,128)(2,1)} %get-tuple-element.270.refs_0_, bf16[5,4,96,768]{3,2,1,0:T(8,128)(2,1)} %copy-done.6), custom_call_target="tpu_custom_call" | custom-call | bytes 16777216 | tf_op jit(solution)/shard_map/fold/pallas_call | solution.py:705
  212.3 14.6 %attend_backward.5 = (f32[512,768]{1,0:T(8,128)}, bf16[512,768]{1,0:T(8,128)(2,1)}, bf16[512,768]{1,0:T(8,128)(2,1)}, f32[512,768]{1,0:T(8,128)}) custom-call(s32[6]{0:T(128)} %stack.42.scalars.refs_0_, bf16[512,768]{1,0:T(8,128)(2,1)} %get-tuple-element.241.refs_4_.q_ref, bf16[512,768]{1,0:T(8,128)(2,1)} %get-tuple-element.251.k_ref, ...), custom_call_target="tpu_custom_call" | custom-call | flops 1048576 | bytes 65536 | tf_op jit(solution)/shard_map/attend_backward/pallas_call | solution.py:242
  231.4 14.6 %attend_backward.6 = (f32[512,768]{1,0:T(8,128)}, bf16[512,768]{1,0:T(8,128)(2,1)}, bf16[512,768]{1,0:T(8,128)(2,1)}, f32[512,768]{1,0:T(8,128)}) custom-call(s32[6]{0:T(128)} %stack.42.scalars.refs_0_, bf16[512,768]{1,0:T(8,128)(2,1)} %get-tuple-element.241.refs_4_.q_ref, bf16[512,768]{1,0:T(8,128)(2,1)} %get-tuple-element.238.k_ref, ...), custom_call_target="tpu_custom_call" | custom-call | flops 1048576 | bytes 65536 | tf_op jit(solution)/shard_map/attend_backward/pallas_call | solution.py:242
  251.8 4.4 %fold.8 = (bf16[5,1,96,768]{3,2,1,0:T(8,128)(2,1)}, bf16[5,1,96,768]{3,2,1,0:T(8,128)(2,1)}) custom-call(bf16[5,2,96,768]{3,2,1,0:T(8,128)(2,1)} %get-tuple-element.296.refs_0_, bf16[5,2,96,768]{3,2,1,0:T(8,128)(2,1)} %copy-done.10), custom_call_target="tpu_custom_call" | custom-call | bytes 16777216 | tf_op jit(solution)/shard_map/fold/pallas_call | solution.py:705
  261.0 5.1 %collective-permute-start.33 = (bf16[512,768]{1,0:T(8,128)(2,1)}, bf16[512,768]{1,0:T(8,128)(2,1)}, u32[]{:S(2)}, u32[]{:S(2)}) collective-permute-start(bf16[512,768]{1,0:T(8,128)(2,1)} %select_convert_fusion), channel_id=1, source_target_pairs={{0,1},{1,2},{2,3},{4,5},{5,6},{6,7},{8,9},{9,10},{10,11},{12,13},{... | collective-permute-start | bytes 2359304 | tf_op jit(solution)/shard_map/ppermute | solution.py:977
  267.5 18.4 %attend_backward.7 = (bf16[512,768]{1,0:T(8,128)(2,1)}, bf16[512,768]{1,0:T(8,128)(2,1)}, bf16[512,768]{1,0:T(8,128)(2,1)}, f32[512,768]{1,0:T(8,128)}) custom-call(s32[6]{0:T(128)} %stack.42.scalars.refs_0_, bf16[512,768]{1,0:T(8,128)(2,1)} %get-tuple-element.241.refs_4_.q_ref, bf16[512,768]{1,0:T(8,128)(2,1)} %get-tuple-element.237.k_ref, ...), custom_call_target="tpu_custom_call" | custom-call | flops 1048576 | bytes 65536 | tf_op jit(solution)/shard_map/attend_backward/pallas_call | solution.py:242
  291.3 12.6 %qkv_grads.1 = (bf16[3,4,96,384]{3,2,1,0:T(8,128)(2,1)}, bf16[3,4,96,384]{3,2,1,0:T(8,128)(2,1)}, bf16[3,4,96,384]{3,2,1,0:T(8,128)(2,1)}, bf16[3,4,96,384]{3,2,1,0:T(8,128)(2,1)}, f32[16,768]{1,0:T(8,128)}) custom-call(bf16[512,768]{1,0:T(8,128)(2,1)} %copy-done.2, bf16[512,768]{1,0:T(8,128)(2,1)} %broadcast_select_fusion.refs_1_, ...), custom_call_target="tpu_custom_call" | custom-call | flops 1048576 | bytes 65536 | tf_op jit(solution)/shard_map/qkv_grads/pallas_call | solution.py:777
  309.5 5.2 %last_norm.1 = (f32[512,768]{1,0:T(8,128)}, f32[24,768]{1,0:T(8,128)}) custom-call(bf16[512,768]{1,0:T(8,128)(2,1)} %token_ref, f32[512,768]{1,0:T(8,128)} %get-tuple-element.332.first_ref, bf16[512,768]{1,0:T(8,128)(2,1)} %collective-permute-done.33.right_ref, bf16[512,768]{1,0:T(8,128)(2,1)} %collective-permute-done.34.left_ref, ...), custom_call_target="tpu_custom_call" | custom-call | flops 1048576 | bytes 65536 | tf_op jit(solution)/shard_map/last_norm/pallas_call | solution.py:837
  315.9 4.0 %fold.10 = (bf16[3,2,96,384]{3,2,1,0:T(8,128)(2,1)}, bf16[3,2,96,384]{3,2,1,0:T(8,128)(2,1)}, bf16[3,2,96,384]{3,2,1,0:T(8,128)(2,1)}, bf16[3,2,96,384]{3,2,1,0:T(8,128)(2,1)}) custom-call(bf16[3,4,96,384]{3,2,1,0:T(8,128)(2,1)} %get-tuple-element.340.refs_0_, bf16[3,4,96,384]{3,2,1,0:T(8,128)(2,1)} %copy-done.14, ...), custom_call_target="tpu_custom_call" | custom-call | bytes 16777216 | tf_op jit(solution)/shard_map/fold/pallas_call | solution.py:705
  325.6 7.7 %collective-permute-done.46 = bf16[216,768]{1,0:T(8,128)(2,1)} collective-permute-done((bf16[216,768]{1,0:T(8,128)(2,1)}, bf16[216,768]{1,0:T(8,128)(2,1)}, u32[]{:S(2)}, u32[]{:S(2)}) %collective-permute-start.46) | collective-permute-done | bytes 331808 | tf_op jit(solution)/shard_map/ppermute | solution.py:291
  346.1 5.4 %collective-permute-start.48 = (f32[24,768]{1,0:T(8,128)S(1)}, f32[24,768]{1,0:T(8,128)S(1)}, u32[]{:S(2)}, u32[]{:S(2)}) collective-permute-start(f32[24,768]{1,0:T(8,128)S(1)} %add_add_fusion.1), channel_id=1, source_target_pairs={{0,1},{1,0},{2,3},{3,2},{4,5},{5,4},{6,7},{7,6},{8,9},{9,8},{10,11... | collective-permute-start | bytes 221192 | tf_op jit(solution)/shard_map/ppermute | solution.py:291
  365.0 4.6 %collective-permute-done.54 = bf16[3,96,192]{2,1,0:T(8,128)(2,1)S(1)} collective-permute-done((bf16[3,96,192]{2,1,0:T(8,128)(2,1)S(1)}, bf16[3,96,192]{2,1,0:T(8,128)(2,1)S(1)}, u32[]{:S(2)}, u32[]{:S(2)}) %collective-permute-start.54) | collective-permute-done | bytes 110624 | tf_op jit(solution)/shard_map/ppermute | solution.py:291
  (250 shorter events, 125.9 us)
Async XLA Ops:
  6.7 22.6 %collective-permute-start.1 = (bf16[192,768]{1,0:T(8,128)(2,1)S(1)}, bf16[192,768]{1,0:T(8,128)(2,1)S(1)}, u32[]{:S(2)}, u32[]{:S(2)}) collective-permute-start(bf16[192,768]{1,0:T(8,128)(2,1)S(1)} %pad_maximum_fusion.9), channel_id=1, source_target_pairs={{0,1},{1,0},{2,3},{3,2},{4,5},{5,4},{6,7},{7,6},{8,9},{9,8},{10,11... | collective-permute-start | bytes 884744 | tf_op jit(solution)/shard_map/ppermute | solution.py:291
  46.5 18.4 %collective-permute-start.8 = (bf16[384,768]{1,0:T(8,128)(2,1)}, bf16[384,768]{1,0:T(8,128)(2,1)}, u32[]{:S(2)}, u32[]{:S(2)}) collective-permute-start(bf16[384,768]{1,0:T(8,128)(2,1)} %collective-permute-done.3), channel_id=1, source_target_pairs={{1,0},{2,3},{5,4},{6,7},{9,8},{10,11},{13,12},{14,15},{17,16},{18,... | collective-permute-start | bytes 1769480 | tf_op jit(solution)/shard_map/ppermute | solution.py:977
  48.4 22.3 %collective-permute-start.6 = (bf16[512,768]{1,0:T(8,128)(2,1)S(1)}, bf16[512,768]{1,0:T(8,128)(2,1)S(1)}, u32[]{:S(2)}, u32[]{:S(2)}) collective-permute-start(bf16[512,768]{1,0:T(8,128)(2,1)S(1)} %add_convert_fusion.2.refs_0_), channel_id=1, source_target_pairs={{0,1},{1,2},{2,3},{4,5},{5,6},{6,7},{8,9},{9,10},{10,11},{12,13},{... | collective-permute-start | bytes 2359304 | tf_op jit(solution)/shard_map/ppermute | solution.py:977
  53.8 26.9 %collective-permute-start.7 = (bf16[512,768]{1,0:T(8,128)(2,1)S(1)}, bf16[512,768]{1,0:T(8,128)(2,1)S(1)}, u32[]{:S(2)}, u32[]{:S(2)}) collective-permute-start(bf16[512,768]{1,0:T(8,128)(2,1)S(1)} %add_convert_fusion.2.refs_0_), channel_id=1, source_target_pairs={{1,0},{2,1},{3,2},{5,4},{6,5},{7,6},{9,8},{10,9},{11,10},{13,12},{... | collective-permute-start | bytes 2359304 | tf_op jit(solution)/shard_map/ppermute | solution.py:977
  80.7 25.2 %collective-permute-start.15 = (bf16[512,768]{1,0:T(8,128)(2,1)S(1)}, bf16[512,768]{1,0:T(8,128)(2,1)S(1)}, u32[]{:S(2)}, u32[]{:S(2)}) collective-permute-start(bf16[512,768]{1,0:T(8,128)(2,1)S(1)} %collective-permute-done.6), channel_id=1, source_target_pairs={{1,2},{2,3},{5,6},{6,7},{9,10},{10,11},{13,14},{14,15},{17,18},{18... | collective-permute-start | bytes 2359304 | tf_op jit(solution)/shard_map/ppermute | solution.py:977
  81.4 24.6 %collective-permute-start.16 = (bf16[512,768]{1,0:T(8,128)(2,1)S(1)}, bf16[512,768]{1,0:T(8,128)(2,1)}, u32[]{:S(2)}, u32[]{:S(2)}) collective-permute-start(bf16[512,768]{1,0:T(8,128)(2,1)S(1)} %collective-permute-done.7), channel_id=1, source_target_pairs={{1,0},{2,1},{5,4},{6,5},{9,8},{10,9},{13,12},{14,13},{17,16},{18,1... | collective-permute-start | bytes 2359304 | tf_op jit(solution)/shard_map/ppermute | solution.py:977
  84.5 43.9 %collective-permute-start.20 = (bf16[864,768]{1,0:T(8,128)(2,1)S(1)}, bf16[864,768]{1,0:T(8,128)(2,1)}, u32[]{:S(2)}, u32[]{:S(2)}) collective-permute-start(bf16[864,768]{1,0:T(8,128)(2,1)S(1)} %pad_maximum_fusion.1.refs_7_), channel_id=1, source_target_pairs={{0,16},{4,20},{8,24},{12,28},{16,0},{20,4},{24,8},{28,12},{1,17},{... | collective-permute-start | bytes 3981320 | tf_op jit(solution)/shard_map/ppermute | solution.py:291
  85.1 43.3 %collective-permute-start.21 = (bf16[864,768]{1,0:T(8,128)(2,1)S(1)}, bf16[864,768]{1,0:T(8,128)(2,1)}, u32[]{:S(2)}, u32[]{:S(2)}) collective-permute-start(bf16[864,768]{1,0:T(8,128)(2,1)S(1)} %pad_maximum_fusion.2.refs_11_), channel_id=1, source_target_pairs={{0,8},{4,12},{8,0},{12,4},{16,24},{20,28},{24,16},{28,20},{1,9},{5... | collective-permute-start | bytes 3981320 | tf_op jit(solution)/shard_map/ppermute | solution.py:291
  107.2 20.2 %collective-permute-start.19 = (bf16[512,768]{1,0:T(8,128)(2,1)S(1)}, bf16[512,768]{1,0:T(8,128)(2,1)S(1)}, u32[]{:S(2)}, u32[]{:S(2)}) collective-permute-start(bf16[512,768]{1,0:T(8,128)(2,1)S(1)} %broadcast_select_fusion.1.refs_0_.refs_2_), channel_id=1, source_target_pairs={{1,0},{2,3},{5,4},{6,7},{9,8},{10,11},{13,12},{14,15},{17,16},{18,... | collective-permute-start | bytes 2359304 | tf_op jit(solution)/shard_map/ppermute | solution.py:977
  179.8 22.2 %collective-permute-start.26 = (bf16[5,4,96,768]{3,2,1,0:T(8,128)(2,1)}, bf16[5,4,96,768]{3,2,1,0:T(8,128)(2,1)S(1)}, u32[]{:S(2)}, u32[]{:S(2)}) collective-permute-start(bf16[5,4,96,768]{3,2,1,0:T(8,128)(2,1)} %get-tuple-element.276), channel_id=1, source_target_pairs={{0,4},{4,0},{8,12},{12,8},{16,20},{20,16},{24,28},{28,24},{1,5},{5... | collective-permute-start | bytes 8847368 | tf_op jit(solution)/shard_map/ppermute | solution.py:291
  194.7 32.3 %collective-permute-start.28 = (bf16[512,768]{1,0:T(8,128)(2,1)}, bf16[512,768]{1,0:T(8,128)(2,1)S(1)}, u32[]{:S(2)}, u32[]{:S(2)}) collective-permute-start(bf16[512,768]{1,0:T(8,128)(2,1)} %get-tuple-element.284), channel_id=1, source_target_pairs={{0,1},{3,2},{4,5},{7,6},{8,9},{11,10},{12,13},{15,14},{16,17},{19,... | collective-permute-start | bytes 2359304 | tf_op jit(solution)/shard_map/ppermute | solution.py:977
  209.6 41.1 %collective-permute-start.31 = (bf16[5,2,96,768]{3,2,1,0:T(8,128)(2,1)}, bf16[5,2,96,768]{3,2,1,0:T(8,128)(2,1)S(1)}, u32[]{:S(2)}, u32[]{:S(2)}) collective-permute-start(bf16[5,2,96,768]{3,2,1,0:T(8,128)(2,1)} %get-tuple-element.286), channel_id=1, source_target_pairs={{0,8},{4,12},{8,0},{12,4},{16,24},{20,28},{24,16},{28,20},{1,9},{5... | collective-permute-start | bytes 4423688 | tf_op jit(solution)/shard_map/ppermute | solution.py:291
  211.1 34.9 %collective-permute-start.32 = (bf16[4,2,96,768]{3,2,1,0:T(8,128)(2,1)S(1)}, bf16[4,2,96,768]{3,2,1,0:T(8,128)(2,1)S(1)}, u32[]{:S(2)}, u32[]{:S(2)}) collective-permute-start(bf16[4,2,96,768]{3,2,1,0:T(8,128)(2,1)S(1)} %copy-done.36), channel_id=1, source_target_pairs={{0,16},{4,20},{8,24},{12,28},{16,0},{20,4},{24,8},{28,12},{1,17},{... | collective-permute-start | bytes 3538952 | tf_op jit(solution)/shard_map/ppermute | solution.py:291
  228.5 29.1 %collective-permute-start.30 = (bf16[512,768]{1,0:T(8,128)(2,1)S(1)}, bf16[512,768]{1,0:T(8,128)(2,1)}, u32[]{:S(2)}, u32[]{:S(2)}) collective-permute-start(bf16[512,768]{1,0:T(8,128)(2,1)S(1)} %add_convert_fusion.1), channel_id=1, source_target_pairs={{3,2},{2,1},{7,6},{6,5},{11,10},{10,9},{15,14},{14,13},{19,18},{18... | collective-permute-start | bytes 2359304 | tf_op jit(solution)/shard_map/ppermute | solution.py:977
  230.0 29.8 %collective-permute-start.29 = (bf16[512,768]{1,0:T(8,128)(2,1)S(1)}, bf16[512,768]{1,0:T(8,128)(2,1)S(1)}, u32[]{:S(2)}, u32[]{:S(2)}) collective-permute-start(bf16[512,768]{1,0:T(8,128)(2,1)S(1)} %add_convert_fusion.1), channel_id=1, source_target_pairs={{0,1},{1,2},{4,5},{5,6},{8,9},{9,10},{12,13},{13,14},{16,17},{17,1... | collective-permute-start | bytes 2359304 | tf_op jit(solution)/shard_map/ppermute | solution.py:977
  256.2 29.6 %collective-permute-start.35 = (bf16[5,1,96,768]{3,2,0,1:T(8,128)(2,1)}, bf16[5,1,96,768]{3,2,0,1:T(8,128)(2,1)}, u32[]{:S(2)}, u32[]{:S(2)}) collective-permute-start(bf16[5,1,96,768]{3,2,0,1:T(8,128)(2,1)} %bitcast.68), channel_id=1, source_target_pairs={{0,16},{4,20},{8,24},{12,28},{16,0},{20,4},{24,8},{28,12},{1,17},{... | collective-permute-start | bytes 2211848 | tf_op jit(solution)/shard_map/ppermute | solution.py:291
  257.1 28.8 %collective-permute-start.36 = (bf16[4,1,96,768]{3,2,1,0:T(8,128)(2,1)}, bf16[4,1,96,768]{3,2,1,0:T(8,128)(2,1)S(1)}, u32[]{:S(2)}, u32[]{:S(2)}) collective-permute-start(bf16[4,1,96,768]{3,2,1,0:T(8,128)(2,1)} %get-tuple-element.300), channel_id=1, source_target_pairs={{0,8},{4,12},{8,0},{12,4},{16,24},{20,28},{24,16},{28,20},{1,9},{5... | collective-permute-start | bytes 1769480 | tf_op jit(solution)/shard_map/ppermute | solution.py:291
  261.0 30.3 %collective-permute-start.33 = (bf16[512,768]{1,0:T(8,128)(2,1)}, bf16[512,768]{1,0:T(8,128)(2,1)}, u32[]{:S(2)}, u32[]{:S(2)}) collective-permute-start(bf16[512,768]{1,0:T(8,128)(2,1)} %select_convert_fusion), channel_id=1, source_target_pairs={{0,1},{1,2},{2,3},{4,5},{5,6},{6,7},{8,9},{9,10},{10,11},{12,13},{... | collective-permute-start | bytes 2359304 | tf_op jit(solution)/shard_map/ppermute | solution.py:977
  266.2 25.1 %collective-permute-start.34 = (bf16[512,768]{1,0:T(8,128)(2,1)}, bf16[512,768]{1,0:T(8,128)(2,1)}, u32[]{:S(2)}, u32[]{:S(2)}) collective-permute-start(bf16[512,768]{1,0:T(8,128)(2,1)} %add_convert_fusion), channel_id=1, source_target_pairs={{3,2},{2,1},{1,0},{7,6},{6,5},{5,4},{11,10},{10,9},{9,8},{15,14},{... | collective-permute-start | bytes 2359304 | tf_op jit(solution)/shard_map/ppermute | solution.py:977
  304.5 19.8 %collective-permute-start.45 = (bf16[216,768]{1,0:T(8,128)(2,1)}, bf16[216,768]{1,0:T(8,128)(2,1)}, u32[]{:S(2)}, u32[]{:S(2)}) collective-permute-start(bf16[216,768]{1,0:T(8,128)(2,1)} %get-tuple-element.313), channel_id=1, source_target_pairs={{0,1},{1,0},{2,3},{3,2},{4,5},{5,4},{6,7},{7,6},{8,9},{9,8},{10,11... | collective-permute-start | bytes 995336 | tf_op jit(solution)/shard_map/ppermute | solution.py:291
  307.1 26.1 %collective-permute-start.46 = (bf16[216,768]{1,0:T(8,128)(2,1)}, bf16[216,768]{1,0:T(8,128)(2,1)}, u32[]{:S(2)}, u32[]{:S(2)}) collective-permute-start(bf16[216,768]{1,0:T(8,128)(2,1)} %get-tuple-element.314), channel_id=1, source_target_pairs={{0,2},{1,3},{2,0},{3,1},{4,6},{5,7},{6,4},{7,5},{8,10},{9,11},{10,... | collective-permute-start | bytes 995336 | tf_op jit(solution)/shard_map/ppermute | solution.py:291
  307.8 26.6 %collective-permute-start.47 = (bf16[216,768]{1,0:T(8,128)(2,1)}, bf16[216,768]{1,0:T(8,128)(2,1)}, u32[]{:S(2)}, u32[]{:S(2)}) collective-permute-start(bf16[216,768]{1,0:T(8,128)(2,1)} %get-tuple-element.315), channel_id=1, source_target_pairs={{0,3},{1,2},{2,1},{3,0},{4,7},{5,6},{6,5},{7,4},{8,11},{9,10},{10,... | collective-permute-start | bytes 995336 | tf_op jit(solution)/shard_map/ppermute | solution.py:291
  319.9 19.3 %collective-permute-start.43 = (bf16[3,2,96,384]{3,2,1,0:T(8,128)(2,1)}, bf16[3,2,96,384]{3,2,1,0:T(8,128)(2,1)S(1)}, u32[]{:S(2)}, u32[]{:S(2)}) collective-permute-start(bf16[3,2,96,384]{3,2,1,0:T(8,128)(2,1)} %get-tuple-element.344), channel_id=1, source_target_pairs={{0,8},{4,12},{8,0},{12,4},{16,24},{20,28},{24,16},{28,20},{1,9},{5... | collective-permute-start | bytes 1327112 | tf_op jit(solution)/shard_map/ppermute | solution.py:291
  324.3 20.8 %collective-permute-start.40 = (f32[24,768]{1,0:T(8,128)}, f32[24,768]{1,0:T(8,128)}, u32[]{:S(2)}, u32[]{:S(2)}) collective-permute-start(f32[24,768]{1,0:T(8,128)} %add.150), channel_id=1, source_target_pairs={{0,8},{4,12},{8,0},{12,4},{16,24},{20,28},{24,16},{28,20},{1,9},{5... | collective-permute-start | bytes 221192 | tf_op jit(solution)/shard_map/ppermute | solution.py:291
  (70 other events, 708.8 us)

commit v3 on v2

--- a/solution.py
+++ b/solution.py
@@ -147,6 +147,7 @@
     number,
     first,
     last,
+    folds,
     scalars,
     q_ref,
     k_ref,
@@ -164,8 +165,19 @@
     if not first:
         dq_in = refs[0]
         refs = refs[1:]
-    dq_ref, dk_ref, dv_ref, back_ref, accum = refs
+    count = len(folds)
+    fold_ins, refs = refs[: 2 * count], refs[2 * count :]
+    dq_ref, dk_ref, dv_ref, back_ref = refs[:4]
+    fold_outs, accum = refs[4:-1], refs[-1]
     step = pl.program_id(0)
+    for n, (lead, bit, at) in enumerate(folds):
+
+        @pl.when(step < lead)
+        def _():
+            fold_block(
+                *fold_ins[2 * n : 2 * n + 2], *fold_outs[2 * n : 2 * n + 2], bit, at
+            )
+
     rows = q_ref.shape[0]
     keys = k_ref.shape[0]
     limit = scalars[4] - scalars[number] * keys
@@ -232,20 +244,33 @@
     scalars,
     carried,
     last,
+    pairs,
+    bits,
+    places,
 ):
     rows, total = queries.shape[0], keys.shape[0]
     first = carried is None
+    folds = [(keep.shape[0], bit, at) for (keep, _), bit, at in zip(pairs, bits, places)]
+    halves = [
+        (keep.shape[0], keep.shape[1] // 2) + keep.shape[2:] for keep, _ in pairs for _ in range(2)
+    ]
+
+    def by_lead(shape):
+        end = shape[0] - 1
+        return pl.BlockSpec((1,) + shape[1:], lambda i, n: (jnp.minimum(i, end), 0, 0, 0))
+
     column = lambda count, c: pl.BlockSpec((count, PAIR), lambda i, n: (0, c * PAIRS + i))
     stats = pl.BlockSpec((1, 2, rows), lambda i, n: (i, 0, 0))
     extra = (query_weight,) * last + (() if first else (carried,))
     extra_specs = [column(D, 0)] * last + ([] if first else [column(rows, 0)])
     return pl.pallas_call(
-        functools.partial(backward_kernel, number, first, last),
+        functools.partial(backward_kernel, number, first, last, folds),
         out_shape=(
             jax.ShapeDtypeStruct((rows, D), low if last else full),
             jax.ShapeDtypeStruct((total, D), low),
             jax.ShapeDtypeStruct((total, D), low),
             jax.ShapeDtypeStruct((total, D), low if first else full),
+            *[jax.ShapeDtypeStruct(shape, low) for shape in halves],
         ),
         grid_spec=pltpu.PrefetchScalarGridSpec(
             num_scalar_prefetch=1,
@@ -260,13 +285,15 @@
                 column(D, 0),
                 column(D, 1),
             ]
-            + extra_specs,
+            + extra_specs
+            + [by_lead(value.shape) for pair in pairs for value in pair],
             out_specs=[
                 column(rows, 0),
                 column(total, 0),
                 column(total, 0),
                 pl.BlockSpec((total, D), lambda i, n: (0, 0)),
-            ],
+            ]
+            + [by_lead(shape) for shape in halves],
             scratch_shapes=[pltpu.VMEM((total, D), full)],
         ),
         compiler_params=pltpu.CompilerParams(vmem_limit_bytes=VMEM_LIMIT),
@@ -283,6 +310,7 @@
         pair_weight,
         pair_weight,
         *extra,
+        *[value for pair in pairs for value in pair],
     )
 
 
@@ -681,19 +709,25 @@
     )(limit, vectors, tokens, mixed, logs, cot, teach, *arrays)
 
 
+def fold_block(keep, got, out_keep, out_send, bit, place):
+    step = 1 << place
+    mine = (lax.axis_index("dp") // bit) % 2 * step
+    for j in range(keep.shape[1] // 2):
+        base = (j // step) * 2 * step + j % step
+        for out, shift in ((out_keep, mine), (out_send, step - mine)):
+            value = keep[0, base + shift].astype(full) + got[0, base + shift].astype(full)
+            out[0, j] = value.astype(low)
+
+
 def fold_kernel(bits, places, *refs):
     count = len(bits)
-    me = lax.axis_index("dp")
     for n in range(count):
-        keep, got = refs[2 * n : 2 * n + 2]
-        out_keep, out_send = refs[2 * count + 2 * n : 2 * count + 2 * n + 2]
-        step = 1 << places[n]
-        mine = (me // bits[n]) % 2 * step
-        for j in range(keep.shape[1] // 2):
-            base = (j // step) * 2 * step + j % step
-            for out, shift in ((out_keep, mine), (out_send, step - mine)):
-                value = keep[0, base + shift].astype(full) + got[0, base + shift].astype(full)
-                out[0, j] = value.astype(low)
+        fold_block(
+            *refs[2 * n : 2 * n + 2],
+            *refs[2 * count + 2 * n : 2 * count + 2 * n + 2],
+            bits[n],
+            places[n],
+        )
 
 
 def fold(pairs, bits, places):
@@ -855,24 +889,73 @@
     return keep, send.astype(low)
 
 
+class Scatter:
+    def __init__(self, parts, turns):
+        self.bits = outer_bits()
+        half = len(self.bits) // 2
+        self.orders = [
+            [1] + self.bits[half * (turn % 2) :] + self.bits[: half * (turn % 2)] for turn in turns
+        ]
+        self.left = [list(self.bits) for _ in turns]
+        self.step = 0
+        self.parts = parts
+
+    def sends(self):
+        return [send for _, send in self.parts]
+
+    def exchange(self, sends):
+        self.pairs = [
+            (keep, swap(send, "dp", turn[self.step]))
+            for (keep, _), send, turn in zip(self.parts, sends, self.orders)
+        ]
+        self.step += 1
+
+    def folds(self):
+        if self.step > len(self.bits):
+            return [], [], []
+        bits = [turn[self.step] for turn in self.orders]
+        places = []
+        for left, bit in zip(self.left, bits):
+            places.append(left.index(bit))
+            left.remove(bit)
+        return self.pairs, bits, places
+
+    def give(self, outs):
+        self.parts = [(outs[n], outs[n + 1]) for n in range(0, len(outs), 2)]
+
+    def fold(self):
+        outs = []
+        for pair, bit, at in zip(*self.folds()):
+            outs += fold([pair], [bit], [at])[0]
+        self.give(outs)
+
+    def advance(self, order):
+        sends = order(*self.sends())
+        self.exchange(list(sends) if len(self.parts) > 1 else [sends])
+
+    def finish(self, order):
+        while self.step <= len(self.bits):
+            self.fold()
+            self.advance(order)
+        got = order(*[other for _, other in self.pairs])
+        return [
+            (keep.astype(full) + other.astype(full))[:, 0]
+            for (keep, _), other in zip(self.pairs, got)
+        ]
+
+
 def scatter_dp(parts, turns):
-    bits = outer_bits()
-    half = len(bits) // 2
-    orders = [[1] + bits[half * (turn % 2) :] + bits[: half * (turn % 2)] for turn in turns]
-    left = [list(bits) for _ in turns]
-    for step in range(len(bits) + 1):
-        sends = yield [send for _, send in parts]
-        got = [swap(send, "dp", turn[step]) for send, turn in zip(sends, orders)]
-        pairs = [(keep, other) for (keep, _), other in zip(parts, got)]
-        if step < len(bits):
-            places = []
-            for n, turn in enumerate(orders):
-                places.append(left[n].index(turn[step + 1]))
-                left[n].remove(turn[step + 1])
-            parts = fold(pairs, [turn[step + 1] for turn in orders], places)
-    got = yield [other for _, other in pairs]
+    scatter = Scatter(parts, turns)
+    while True:
+        sends = yield scatter.sends()
+        scatter.exchange(sends)
+        if scatter.step > len(scatter.bits):
+            break
+        scatter.parts = fold(*scatter.folds())
+    got = yield [other for _, other in scatter.pairs]
     return [
-        (keep.astype(full) + other.astype(full))[:, 0] for (keep, _), other in zip(pairs, got)
+        (keep.astype(full) + other.astype(full))[:, 0]
+        for (keep, _), other in zip(scatter.pairs, got)
     ]
 
 
@@ -1114,17 +1197,16 @@
     output, middle_grad, attended_grad, *parts, deltas, log_rows, sums = middle_call(
         scalars, vectors, tokens, mixed, logs, cotangent, teacher, arrays, plan, block, dp
     )
-    down = Steps(scatter_dp([(parts[0], parts[1])], (1,)))
-    down.advance(order)
-    up = Steps(scatter_dp([(parts[2], parts[3])], (0,)))
-    up.advance(order)
+    scatter = Scatter([(parts[0], parts[1]), (parts[2], parts[3])], (1, 0))
+    scatter.advance(order)
 
     key_grads = [None] * 4
     value_grads = [None] * 4
     firsts = [None] * 4
     query_grad = None
     for n in (3, 2, 1, 0):
-        query_grad, key_grads[n], value_grads[n], firsts[n] = attend_backward(
+        pairs, bits, places = scatter.folds() if n % 2 == 0 else ([], [], [])
+        query_grad, key_grads[n], value_grads[n], firsts[n], *folded = attend_backward(
             n,
             queries,
             keys[n],
@@ -1137,19 +1219,21 @@
             scalars,
             query_grad,
             n == 0,
+            pairs,
+            bits,
+            places,
         )
         firsts[n] = order(firsts[n])
+        if folded:
+            scatter.give(folded)
         if n == 3:
-            down.advance(order)
-            up.advance(order)
             back_last = along(firsts[3], [(0, 1), (3, 2)]).astype(full)
         elif n == 2:
+            scatter.advance(order)
             payload = order((firsts[2] + back_last).astype(low))
             back_right = along(payload, [(0, 1), (1, 2)]).astype(full)
             back_left = along(payload, [(3, 2), (2, 1)]).astype(full)
         elif n == 1:
-            down.advance(order)
-            up.advance(order)
             to_right = jnp.where(
                 rank == 0, firsts[1], firsts[3].astype(full) + back_right
             ).astype(low)
@@ -1157,14 +1241,14 @@
             to_right, to_left = order(to_right, to_left)
             final_right = along(to_right, [(0, 1), (1, 2), (2, 3)])
             final_left = along(to_left, [(3, 2), (2, 1), (1, 0)])
-    (up_own,) = up.finish(order)
-    (down_own,) = down.finish(order)
-    feed = Steps(scatter_feed(up_own, down_own))
-    feed.advance(order)
+    scatter.advance(order)
     query_grad, final_right, final_left = order(query_grad, final_right, final_left)
     *halves, bias_sums = qkv_grads(chunks, query_grad, key_grads, value_grads, dp)
     qkv = Steps(scatter_qkv(*halves))
     qkv.advance(order)
+    down_own, up_own = scatter.finish(order)
+    feed = Steps(scatter_feed(up_own, down_own))
+    feed.advance(order)
     tokens, first_own = order(tokens, firsts[0])
     input_grad, packed = last_norm(
         tokens,

time: 378 us -> 368 us (0.974)
  Pallas kernels: 192 us -> 178 us
  waiting for transfers between devices: 54.2 us -> 64.9 us
    pallas_call x6 -> x2, Pallas kernels: 25.7 us -> 7.12 us  [fold(): pl.pallas_call(functools.partial(fold_kernel, bits, places), out_shape=[j...]
    ppermute x44, waiting for transfers between devices: 30.6 us -> 39.1 us  [swap(): return lax.ppermute(value, axis, [(i, i ^ bit) for i in range(count)])]
    pallas_call x4, Pallas kernels: 61.9 us -> 66.6 us  [attend_backward(): pl.pallas_call(functools.partial(backward_kernel, number, first, last, fo...]
    unnamed x77 -> x73, local copies, waits for them, and re-layouts: 11.3 us -> 6.82 us
  transfers between devices with their start and end apart: 56 -> 56, of which waited for: 12 -> 16; matrix products, arithmetic and copies ran while one was open for 10% -> 10% of each run, Pallas kernels for 39% -> 39%
where the time goes in v3:
time: 368 us; the launch traced here: 361 us
  Pallas kernels  178 us (48%)
  starting transfers between devices  69.4 us (19%)
  waiting for transfers between devices  64.9 us (18%)
  other arithmetic  21.4 us (6%)
  local copies, waits for them, and re-layouts  19.1 us (5%)
  between operations  5.28 us (1%)
    pallas_call x4, Pallas kernels, attend_backward(): pl.pallas_call(functools.partial(backward_kernel, number, first, last, fo...  66.6 us
    ppermute x44, starting transfers between devices, swap(): return lax.ppermute(value, axis, [(i, i ^ bit) for i in range(count)])  47 us
    pallas_call x3, Pallas kernels, attend_forward(): pl.pallas_call(functools.partial(forward_kernel, numbers, first, final),...  46.5 us
    ppermute x44, waiting for transfers between devices, swap(): return lax.ppermute(value, axis, [(i, i ^ bit) for i in range(count)])  39.1 us
    pallas_call x1, Pallas kernels, middle_call(): pl.pallas_call(functools.partial(middle_kernel, plan, block, len(arrays))...  35.7 us
    ppermute x12, waiting for transfers between devices, shards(): along = lambda value, pairs: lax.ppermute(value, 'mp', pairs)  25.9 us
    ppermute x12, starting transfers between devices, shards(): along = lambda value, pairs: lax.ppermute(value, 'mp', pairs)  22.4 us
    pallas_call x1, Pallas kernels, qkv_grads(): pl.pallas_call(functools.partial(qkv_grad_kernel, count), out_shape=[jax....  13.1 us
  transfers between devices with their start and end apart: 56, of which 16 were waited for; matrix products, arithmetic and copies ran while one was open for 10% of the time, Pallas kernels for 39%

profile of v3, /device:TPU:0, one launch (start us, length us, event | category | flops | bytes accessed | tf_op | source)
XLA Modules:
  0.0 361.4 jit_solution(10748641274518683231)
XLA Ops:
  38.2 6.3 %collective-permute-done.10.refs_5_ = bf16[288,768]{1,0:T(8,128)(2,1)S(1)} collective-permute-done((bf16[288,768]{1,0:T(8,128)(2,1)S(1)}, bf16[288,768]{1,0:T(8,128)(2,1)S(1)}, u32[]{:S(2)}, u32[]{:S(2)}) %collective-permute-start.10) | collective-permute-done | bytes 442400 | tf_op jit(solution)/shard_map/ppermute | solution.py:319
  48.4 5.5 %collective-permute-start.6 = (bf16[512,768]{1,0:T(8,128)(2,1)S(1)}, bf16[512,768]{1,0:T(8,128)(2,1)}, u32[]{:S(2)}, u32[]{:S(2)}) collective-permute-start(bf16[512,768]{1,0:T(8,128)(2,1)S(1)} %add_convert_fusion.2.refs_0_), channel_id=1, source_target_pairs={{0,1},{1,2},{2,3},{4,5},{5,6},{6,7},{8,9},{9,10},{10,11},{12,13},{... | collective-permute-start | bytes 2359304 | tf_op jit(solution)/shard_map/ppermute | solution.py:1060
  56.1 4.2 %place.1 = (bf16[768,768]{1,0:T(8,128)(2,1)}, bf16[768,1536]{1,0:T(8,128)(2,1)}) custom-call(bf16[288,768]{1,0:T(8,128)(2,1)} %copy-done.10, bf16[288,768]{1,0:T(8,128)(2,1)} %copy-done.22, bf16[288,768]{1,0:T(8,128)(2,1)} %copy-done.23, bf16[288,768]{1,0:T(8,128)(2,1)} %copy-done.24, bf16[288,768]{1,0:T(8,128)(2,1)} %copy-done.9, ...), custom_call_target="tpu_custom_call" | custom-call | flops 1048576 | bytes 65536 | tf_op jit(solution)/shard_map/place/pallas_call | solution.py:426
  60.3 4.3 %collective-permute-done.8 = bf16[384,768]{1,0:T(8,128)(2,1)S(1)} collective-permute-done((bf16[384,768]{1,0:T(8,128)(2,1)S(1)}, bf16[384,768]{1,0:T(8,128)(2,1)S(1)}, u32[]{:S(2)}, u32[]{:S(2)}) %collective-permute-start.8) | collective-permute-done | bytes 589856 | tf_op jit(solution)/shard_map/ppermute | solution.py:1060
  66.0 4.0 %collective-permute-done.6 = bf16[512,768]{1,0:T(8,128)(2,1)} collective-permute-done((bf16[512,768]{1,0:T(8,128)(2,1)S(1)}, bf16[512,768]{1,0:T(8,128)(2,1)}, u32[]{:S(2)}, u32[]{:S(2)}) %collective-permute-start.6) | collective-permute-done | bytes 786464 | tf_op jit(solution)/shard_map/ppermute | solution.py:1060
  70.0 10.5 %collective-permute-done.7 = bf16[512,768]{1,0:T(8,128)(2,1)S(1)} collective-permute-done((bf16[512,768]{1,0:T(8,128)(2,1)S(1)}, bf16[512,768]{1,0:T(8,128)(2,1)S(1)}, u32[]{:S(2)}, u32[]{:S(2)}) %collective-permute-start.7) | collective-permute-done | bytes 786464 | tf_op jit(solution)/shard_map/ppermute | solution.py:1060
  86.5 20.2 %attend_forward.3 = (bf16[512,768]{1,0:T(8,128)(2,1)}, bf16[512,768]{1,0:T(8,128)(2,1)}, bf16[512,768]{1,0:T(8,128)(2,1)}, bf16[512,768]{1,0:T(8,128)(2,1)}, bf1...) custom-call(s32[6]{0:T(128)} %stack.42.scalars.refs_0_, ...), custom_call_target="tpu_custom_call" | custom-call | flops 1048576 | bytes 65536 | tf_op jit(solution)/shard_map/attend_forward/pallas_call | solution.py:129
  109.4 13.2 %attend_forward.4 = (bf16[512,768]{1,0:T(8,128)(2,1)}, bf16[512,768]{1,0:T(8,128)(2,1)}, f32[512,768]{1,0:T(8,128)}, f32[512,768]{1,0:T(8,128)}, f32[512,768]{1,0:T(8,128)}) custom-call(s32[6]{0:T(128)} %stack.42.scalars.refs_0_, bf16[512,768]{1,0:T(8,128)(2,1)} %copy-done.1, bf16[768,1536]{1,0:T(8,128)(2,1)} %get-tuple-element.220.refs_2_.refs_3_.refs_1_.wk_ref.wv_ref, ...), custom_call_target="tpu_custom_call" | custom-call | flops 1048576 | bytes 65536 | tf_op jit(solution)/shard_map/attend_forward/pallas_call | solution.py:129
  122.6 6.8 %collective-permute-done.19 = bf16[512,768]{1,0:T(8,128)(2,1)} collective-permute-done((bf16[512,768]{1,0:T(8,128)(2,1)S(1)}, bf16[512,768]{1,0:T(8,128)(2,1)}, u32[]{:S(2)}, u32[]{:S(2)}) %collective-permute-start.19) | collective-permute-done | bytes 786464 | tf_op jit(solution)/shard_map/ppermute | solution.py:1060
  132.6 13.1 %attend_forward.5 = (bf16[512,768]{1,0:T(8,128)(2,1)}, bf16[512,768]{1,0:T(8,128)(2,1)}, f32[512,768]{1,0:T(8,128)}, f32[512,768]{1,0:T(8,128)}) custom-call(s32[6]{0:T(128)} %stack.42.scalars.refs_0_, bf16[512,768]{1,0:T(8,128)(2,1)} %broadcast_select_fusion.2.refs_0_.refs_3_, bf16[768,1536]{1,0:T(8,128)(2,1)} %get-tuple-element.220.refs_2_.refs_3_.refs_1_.wk_ref.wv_ref, ...), custom_call_target="tpu_custom_call" | custom-call | flops 1048576 | bytes 65536 | tf_op jit(solution)/shard_map/attend_forward/pallas_call | solution.py:129
  145.8 35.7 %middle.1 = (bf16[512,768]{1,0:T(8,128)(2,1)}, f32[512,768]{1,0:T(8,128)}, bf16[512,768]{1,0:T(8,128)(2,1)}, bf16[4,4,96,768]{3,2,1,0:T(8,128)(2,1)}, bf16[4,4,9...) custom-call(s32[6]{0:T(128)} %stack.42.scalars.refs_0_, ...), custom_call_target="tpu_custom_call" | custom-call | flops 1048576 | bytes 65536 | tf_op jit(solution)/shard_map/middle/pallas_call | solution.py:661
  182.1 14.2 %attend_backward.4 = (f32[512,768]{1,0:T(8,128)}, bf16[512,768]{1,0:T(8,128)(2,1)}, bf16[512,768]{1,0:T(8,128)(2,1)}, bf16[512,768]{1,0:T(8,128)(2,1)}) custom-call(s32[6]{0:T(128)} %stack.42.scalars.refs_0_, bf16[512,768]{1,0:T(8,128)(2,1)} %get-tuple-element.241.refs_4_.q_ref, bf16[512,768]{1,0:T(8,128)(2,1)} %get-tuple-element.270.k_ref, ...), custom_call_target="tpu_custom_call" | custom-call | flops 1048576 | bytes 65536 | tf_op jit(solution)/shard_map/attend_backward/pallas_call | solution.py:266
  200.0 17.8 %attend_backward.5 = (f32[512,768]{1,0:T(8,128)}, bf16[512,768]{1,0:T(8,128)(2,1)}, bf16[512,768]{1,0:T(8,128)(2,1)}, f32[512,768]{1,0:T(8,128)}, bf16[4,2,96,76...) custom-call(s32[6]{0:T(128)} %stack.42.scalars.refs_0_, ...), custom_call_target="tpu_custom_call" | custom-call | flops 1048576 | bytes 65536 | tf_op jit(solution)/shard_map/attend_backward/pallas_call | solution.py:266
  224.3 14.6 %attend_backward.6 = (f32[512,768]{1,0:T(8,128)}, bf16[512,768]{1,0:T(8,128)(2,1)}, bf16[512,768]{1,0:T(8,128)(2,1)}, f32[512,768]{1,0:T(8,128)}) custom-call(s32[6]{0:T(128)} %stack.42.scalars.refs_0_, bf16[512,768]{1,0:T(8,128)(2,1)} %get-tuple-element.241.refs_4_.q_ref, bf16[512,768]{1,0:T(8,128)(2,1)} %get-tuple-element.238.k_ref, ...), custom_call_target="tpu_custom_call" | custom-call | flops 1048576 | bytes 65536 | tf_op jit(solution)/shard_map/attend_backward/pallas_call | solution.py:266
  241.3 4.6 %collective-permute-start.35 = (bf16[512,768]{1,0:T(8,128)(2,1)S(1)}, bf16[512,768]{1,0:T(8,128)(2,1)S(1)}, u32[]{:S(2)}, u32[]{:S(2)}) collective-permute-start(bf16[512,768]{1,0:T(8,128)(2,1)S(1)} %select_convert_fusion), channel_id=1, source_target_pairs={{0,1},{1,2},{2,3},{4,5},{5,6},{6,7},{8,9},{9,10},{10,11},{12,13},{... | collective-permute-start | bytes 2359304 | tf_op jit(solution)/shard_map/ppermute | solution.py:1060
  253.6 19.9 %attend_backward.7 = (bf16[512,768]{1,0:T(8,128)(2,1)}, bf16[512,768]{1,0:T(8,128)(2,1)}, bf16[512,768]{1,0:T(8,128)(2,1)}, f32[512,768]{1,0:T(8,128)}, bf16[4,1...) custom-call(s32[6]{0:T(128)} %stack.42.scalars.refs_0_, ...), custom_call_target="tpu_custom_call" | custom-call | flops 1048576 | bytes 65536 | tf_op jit(solution)/shard_map/attend_backward/pallas_call | solution.py:266
  276.3 13.1 %qkv_grads.1 = (bf16[3,4,96,384]{3,2,1,0:T(8,128)(2,1)}, bf16[3,4,96,384]{3,2,1,0:T(8,128)(2,1)}, bf16[3,4,96,384]{3,2,1,0:T(8,128)(2,1)}, bf16[3,4,96,384]{3,2,1,0:T(8,128)(2,1)}, f32[16,768]{1,0:T(8,128)}) custom-call(bf16[512,768]{1,0:T(8,128)(2,1)} %copy-done.2, bf16[512,768]{1,0:T(8,128)(2,1)} %broadcast_select_fusion.refs_1_, ...), custom_call_target="tpu_custom_call" | custom-call | flops 1048576 | bytes 65536 | tf_op jit(solution)/shard_map/qkv_grads/pallas_call | solution.py:811
  297.4 4.1 %collective-permute-start.46 = (bf16[216,768]{1,0:T(8,128)(2,1)}, bf16[216,768]{1,0:T(8,128)(2,1)}, u32[]{:S(2)}, u32[]{:S(2)}) collective-permute-start(bf16[216,768]{1,0:T(8,128)(2,1)} %get-tuple-element.329), channel_id=1, source_target_pairs={{0,2},{1,3},{2,0},{3,1},{4,6},{5,7},{6,4},{7,5},{8,10},{9,11},{10,... | collective-permute-start | bytes 995336 | tf_op jit(solution)/shard_map/ppermute | solution.py:319
  301.8 5.2 %last_norm.1 = (f32[512,768]{1,0:T(8,128)}, f32[24,768]{1,0:T(8,128)}) custom-call(bf16[512,768]{1,0:T(8,128)(2,1)} %token_ref, f32[512,768]{1,0:T(8,128)} %get-tuple-element.332.first_ref, bf16[512,768]{1,0:T(8,128)(2,1)} %copy-done.15, bf16[512,768]{1,0:T(8,128)(2,1)} %copy-done.16, f32[512,768]{1,0:T(8,128)} %get-tuple-element.333.middle_ref, ...), custom_call_target="tpu_custom_call" | custom-call | flops 1048576 | bytes 65536 | tf_op jit(solution)/shard_map/last_norm/pallas_call | solution.py:871
  307.0 3.9 %fold.2 = (bf16[3,2,96,384]{3,2,1,0:T(8,128)(2,1)}, bf16[3,2,96,384]{3,2,1,0:T(8,128)(2,1)}, bf16[3,2,96,384]{3,2,1,0:T(8,128)(2,1)}, bf16[3,2,96,384]{3,2,1,0:T(8,128)(2,1)}) custom-call(bf16[3,4,96,384]{3,2,1,0:T(8,128)(2,1)} %get-tuple-element.340.refs_0_, bf16[3,4,96,384]{3,2,1,0:T(8,128)(2,1)} %collective-permute-done.37.refs_1_, ...), custom_call_target="tpu_custom_call" | custom-call | bytes 16777216 | tf_op jit(solution)/shard_map/fold/pallas_call | solution.py:739
  316.6 8.2 %collective-permute-done.46 = bf16[216,768]{1,0:T(8,128)(2,1)} collective-permute-done((bf16[216,768]{1,0:T(8,128)(2,1)}, bf16[216,768]{1,0:T(8,128)(2,1)}, u32[]{:S(2)}, u32[]{:S(2)}) %collective-permute-start.46) | collective-permute-done | bytes 331808 | tf_op jit(solution)/shard_map/ppermute | solution.py:319
  331.6 3.2 fold.3
  337.6 4.2 %collective-permute-start.48 = (f32[24,768]{1,0:T(8,128)S(1)}, f32[24,768]{1,0:T(8,128)S(1)}, u32[]{:S(2)}, u32[]{:S(2)}) collective-permute-start(f32[24,768]{1,0:T(8,128)S(1)} %add_add_fusion.1), channel_id=1, source_target_pairs={{0,1},{1,0},{2,3},{3,2},{4,5},{5,4},{6,7},{7,6},{8,9},{9,8},{10,11... | collective-permute-start | bytes 221192 | tf_op jit(solution)/shard_map/ppermute | solution.py:319
  355.1 5.1 %collective-permute-done.54 = bf16[3,96,192]{2,1,0:T(8,128)(2,1)S(1)} collective-permute-done((bf16[3,96,192]{2,1,0:T(8,128)(2,1)S(1)}, bf16[3,96,192]{2,1,0:T(8,128)(2,1)S(1)}, u32[]{:S(2)}, u32[]{:S(2)}) %collective-permute-start.54) | collective-permute-done | bytes 110624 | tf_op jit(solution)/shard_map/ppermute | solution.py:319
  (242 shorter events, 114.3 us)
Async XLA Ops:
  6.7 22.6 %collective-permute-start.1 = (bf16[192,768]{1,0:T(8,128)(2,1)S(1)}, bf16[192,768]{1,0:T(8,128)(2,1)S(1)}, u32[]{:S(2)}, u32[]{:S(2)}) collective-permute-start(bf16[192,768]{1,0:T(8,128)(2,1)S(1)} %pad_maximum_fusion.9), channel_id=1, source_target_pairs={{0,1},{1,0},{2,3},{3,2},{4,5},{5,4},{6,7},{7,6},{8,9},{9,8},{10,11... | collective-permute-start | bytes 884744 | tf_op jit(solution)/shard_map/ppermute | solution.py:319
  46.5 18.1 %collective-permute-start.8 = (bf16[384,768]{1,0:T(8,128)(2,1)S(1)}, bf16[384,768]{1,0:T(8,128)(2,1)S(1)}, u32[]{:S(2)}, u32[]{:S(2)}) collective-permute-start(bf16[384,768]{1,0:T(8,128)(2,1)S(1)} %collective-permute-done.3), channel_id=1, source_target_pairs={{1,0},{2,3},{5,4},{6,7},{9,8},{10,11},{13,12},{14,15},{17,16},{18,... | collective-permute-start | bytes 1769480 | tf_op jit(solution)/shard_map/ppermute | solution.py:1060
  48.4 21.6 %collective-permute-start.6 = (bf16[512,768]{1,0:T(8,128)(2,1)S(1)}, bf16[512,768]{1,0:T(8,128)(2,1)}, u32[]{:S(2)}, u32[]{:S(2)}) collective-permute-start(bf16[512,768]{1,0:T(8,128)(2,1)S(1)} %add_convert_fusion.2.refs_0_), channel_id=1, source_target_pairs={{0,1},{1,2},{2,3},{4,5},{5,6},{6,7},{8,9},{9,10},{10,11},{12,13},{... | collective-permute-start | bytes 2359304 | tf_op jit(solution)/shard_map/ppermute | solution.py:1060
  53.9 26.6 %collective-permute-start.7 = (bf16[512,768]{1,0:T(8,128)(2,1)S(1)}, bf16[512,768]{1,0:T(8,128)(2,1)S(1)}, u32[]{:S(2)}, u32[]{:S(2)}) collective-permute-start(bf16[512,768]{1,0:T(8,128)(2,1)S(1)} %add_convert_fusion.2.refs_0_), channel_id=1, source_target_pairs={{1,0},{2,1},{3,2},{5,4},{6,5},{7,6},{9,8},{10,9},{11,10},{13,12},{... | collective-permute-start | bytes 2359304 | tf_op jit(solution)/shard_map/ppermute | solution.py:1060
  64.7 20.3 %collective-permute-start.18 = (bf16[432,768]{1,0:T(8,128)(2,1)S(1)}, bf16[432,768]{1,0:T(8,128)(2,1)S(1)}, u32[]{:S(2)}, u32[]{:S(2)}) collective-permute-start(bf16[432,768]{1,0:T(8,128)(2,1)S(1)} %fusion.5), channel_id=1, source_target_pairs={{0,16},{4,20},{8,24},{12,28},{16,0},{20,4},{24,8},{28,12},{1,17},{... | collective-permute-start | bytes 1990664 | tf_op jit(solution)/shard_map/ppermute | solution.py:319
  65.3 19.8 %collective-permute-start.17 = (bf16[432,768]{1,0:T(8,128)(2,1)S(1)}, bf16[432,768]{1,0:T(8,128)(2,1)S(1)}, u32[]{:S(2)}, u32[]{:S(2)}) collective-permute-start(bf16[432,768]{1,0:T(8,128)(2,1)S(1)} %pad_maximum_fusion.4), channel_id=1, source_target_pairs={{0,8},{4,12},{8,0},{12,4},{16,24},{20,28},{24,16},{28,20},{1,9},{5... | collective-permute-start | bytes 1990664 | tf_op jit(solution)/shard_map/ppermute | solution.py:319
  80.5 26.2 %collective-permute-start.15 = (bf16[512,768]{1,0:T(8,128)(2,1)}, bf16[512,768]{1,0:T(8,128)(2,1)}, u32[]{:S(2)}, u32[]{:S(2)}) collective-permute-start(bf16[512,768]{1,0:T(8,128)(2,1)} %collective-permute-done.6), channel_id=1, source_target_pairs={{1,2},{2,3},{5,6},{6,7},{9,10},{10,11},{13,14},{14,15},{17,18},{18... | collective-permute-start | bytes 2359304 | tf_op jit(solution)/shard_map/ppermute | solution.py:1060
  82.1 24.6 %collective-permute-start.16 = (bf16[512,768]{1,0:T(8,128)(2,1)S(1)}, bf16[512,768]{1,0:T(8,128)(2,1)}, u32[]{:S(2)}, u32[]{:S(2)}) collective-permute-start(bf16[512,768]{1,0:T(8,128)(2,1)S(1)} %collective-permute-done.7), channel_id=1, source_target_pairs={{1,0},{2,1},{5,4},{6,5},{9,8},{10,9},{13,12},{14,13},{17,16},{18,1... | collective-permute-start | bytes 2359304 | tf_op jit(solution)/shard_map/ppermute | solution.py:1060
  85.2 46.3 %collective-permute-start.20 = (bf16[864,768]{1,0:T(8,128)(2,1)S(1)}, bf16[864,768]{1,0:T(8,128)(2,1)S(1)}, u32[]{:S(2)}, u32[]{:S(2)}) collective-permute-start(bf16[864,768]{1,0:T(8,128)(2,1)S(1)} %pad_maximum_fusion.1.refs_7_), channel_id=1, source_target_pairs={{0,16},{4,20},{8,24},{12,28},{16,0},{20,4},{24,8},{28,12},{1,17},{... | collective-permute-start | bytes 3981320 | tf_op jit(solution)/shard_map/ppermute | solution.py:319
  85.8 45.8 %collective-permute-start.21 = (bf16[864,768]{1,0:T(8,128)(2,1)S(1)}, bf16[864,768]{1,0:T(8,128)(2,1)}, u32[]{:S(2)}, u32[]{:S(2)}) collective-permute-start(bf16[864,768]{1,0:T(8,128)(2,1)S(1)} %pad_maximum_fusion.2.refs_11_), channel_id=1, source_target_pairs={{0,8},{4,12},{8,0},{12,4},{16,24},{20,28},{24,16},{28,20},{1,9},{5... | collective-permute-start | bytes 3981320 | tf_op jit(solution)/shard_map/ppermute | solution.py:319
  107.9 21.4 %collective-permute-start.19 = (bf16[512,768]{1,0:T(8,128)(2,1)S(1)}, bf16[512,768]{1,0:T(8,128)(2,1)}, u32[]{:S(2)}, u32[]{:S(2)}) collective-permute-start(bf16[512,768]{1,0:T(8,128)(2,1)S(1)} %broadcast_select_fusion.1.refs_0_.refs_2_), channel_id=1, source_target_pairs={{1,0},{2,3},{5,4},{6,7},{9,8},{10,11},{13,12},{14,15},{17,16},{18,... | collective-permute-start | bytes 2359304 | tf_op jit(solution)/shard_map/ppermute | solution.py:1060
  196.3 23.1 %collective-permute-start.28 = (bf16[512,768]{1,0:T(8,128)(2,1)}, bf16[512,768]{1,0:T(8,128)(2,1)S(1)}, u32[]{:S(2)}, u32[]{:S(2)}) collective-permute-start(bf16[512,768]{1,0:T(8,128)(2,1)} %get-tuple-element.280), channel_id=1, source_target_pairs={{0,1},{3,2},{4,5},{7,6},{8,9},{11,10},{12,13},{15,14},{16,17},{19,... | collective-permute-start | bytes 2359304 | tf_op jit(solution)/shard_map/ppermute | solution.py:1060
  217.8 34.5 %collective-permute-start.32 = (bf16[5,2,96,768]{3,2,1,0:T(8,128)(2,1)}, bf16[5,2,96,768]{3,2,1,0:T(8,128)(2,1)S(1)}, u32[]{:S(2)}, u32[]{:S(2)}) collective-permute-start(bf16[5,2,96,768]{3,2,1,0:T(8,128)(2,1)} %get-tuple-element.290), channel_id=1, source_target_pairs={{0,8},{4,12},{8,0},{12,4},{16,24},{20,28},{24,16},{28,20},{1,9},{5... | collective-permute-start | bytes 4423688 | tf_op jit(solution)/shard_map/ppermute | solution.py:319
  221.0 18.0 %collective-permute-start.30 = (bf16[512,768]{1,0:T(8,128)(2,1)S(1)}, bf16[512,768]{1,0:T(8,128)(2,1)S(1)}, u32[]{:S(2)}, u32[]{:S(2)}) collective-permute-start(bf16[512,768]{1,0:T(8,128)(2,1)S(1)} %add_convert_fusion.1), channel_id=1, source_target_pairs={{3,2},{2,1},{7,6},{6,5},{11,10},{10,9},{15,14},{14,13},{19,18},{18... | collective-permute-start | bytes 2359304 | tf_op jit(solution)/shard_map/ppermute | solution.py:1060
  221.7 27.9 %collective-permute-start.31 = (bf16[4,2,96,768]{3,2,1,0:T(8,128)(2,1)}, bf16[4,2,96,768]{3,2,1,0:T(8,128)(2,1)S(1)}, u32[]{:S(2)}, u32[]{:S(2)}) collective-permute-start(bf16[4,2,96,768]{3,2,1,0:T(8,128)(2,1)} %get-tuple-element.289), channel_id=1, source_target_pairs={{0,16},{4,20},{8,24},{12,28},{16,0},{20,4},{24,8},{28,12},{1,17},{... | collective-permute-start | bytes 3538952 | tf_op jit(solution)/shard_map/ppermute | solution.py:319
  222.9 18.0 %collective-permute-start.29 = (bf16[512,768]{1,0:T(8,128)(2,1)S(1)}, bf16[512,768]{1,0:T(8,128)(2,1)S(1)}, u32[]{:S(2)}, u32[]{:S(2)}) collective-permute-start(bf16[512,768]{1,0:T(8,128)(2,1)S(1)} %add_convert_fusion.1), channel_id=1, source_target_pairs={{0,1},{1,2},{4,5},{5,6},{8,9},{9,10},{12,13},{13,14},{16,17},{17,1... | collective-permute-start | bytes 2359304 | tf_op jit(solution)/shard_map/ppermute | solution.py:1060
  241.3 35.0 %collective-permute-start.35 = (bf16[512,768]{1,0:T(8,128)(2,1)S(1)}, bf16[512,768]{1,0:T(8,128)(2,1)S(1)}, u32[]{:S(2)}, u32[]{:S(2)}) collective-permute-start(bf16[512,768]{1,0:T(8,128)(2,1)S(1)} %select_convert_fusion), channel_id=1, source_target_pairs={{0,1},{1,2},{2,3},{4,5},{5,6},{6,7},{8,9},{9,10},{10,11},{12,13},{... | collective-permute-start | bytes 2359304 | tf_op jit(solution)/shard_map/ppermute | solution.py:1060
  245.9 30.3 %collective-permute-start.36 = (bf16[512,768]{1,0:T(8,128)(2,1)S(1)}, bf16[512,768]{1,0:T(8,128)(2,1)S(1)}, u32[]{:S(2)}, u32[]{:S(2)}) collective-permute-start(bf16[512,768]{1,0:T(8,128)(2,1)S(1)} %add_convert_fusion), channel_id=1, source_target_pairs={{3,2},{2,1},{1,0},{7,6},{6,5},{5,4},{11,10},{10,9},{9,8},{15,14},{... | collective-permute-start | bytes 2359304 | tf_op jit(solution)/shard_map/ppermute | solution.py:1060
  273.5 18.0 %collective-permute-start.34 = (bf16[5,1,96,768]{3,2,1,0:T(8,128)(2,1)}, bf16[5,1,96,768]{3,2,1,0:T(8,128)(2,1)}, u32[]{:S(2)}, u32[]{:S(2)}) collective-permute-start(bf16[5,1,96,768]{3,2,1,0:T(8,128)(2,1)} %get-tuple-element.308), channel_id=1, source_target_pairs={{0,16},{4,20},{8,24},{12,28},{16,0},{20,4},{24,8},{28,12},{1,17},{... | collective-permute-start | bytes 2211848 | tf_op jit(solution)/shard_map/ppermute | solution.py:319
  297.4 27.4 %collective-permute-start.46 = (bf16[216,768]{1,0:T(8,128)(2,1)}, bf16[216,768]{1,0:T(8,128)(2,1)}, u32[]{:S(2)}, u32[]{:S(2)}) collective-permute-start(bf16[216,768]{1,0:T(8,128)(2,1)} %get-tuple-element.329), channel_id=1, source_target_pairs={{0,2},{1,3},{2,0},{3,1},{4,6},{5,7},{6,4},{7,5},{8,10},{9,11},{10,... | collective-permute-start | bytes 995336 | tf_op jit(solution)/shard_map/ppermute | solution.py:319
  301.5 24.4 %collective-permute-start.47 = (bf16[216,768]{1,0:T(8,128)(2,1)}, bf16[216,768]{1,0:T(8,128)(2,1)}, u32[]{:S(2)}, u32[]{:S(2)}) collective-permute-start(bf16[216,768]{1,0:T(8,128)(2,1)} %get-tuple-element.330), channel_id=1, source_target_pairs={{0,3},{1,2},{2,1},{3,0},{4,7},{5,6},{6,5},{7,4},{8,11},{9,10},{10,... | collective-permute-start | bytes 995336 | tf_op jit(solution)/shard_map/ppermute | solution.py:319
  311.0 19.7 %collective-permute-start.43 = (bf16[3,2,96,384]{3,2,1,0:T(8,128)(2,1)}, bf16[3,2,96,384]{3,2,1,0:T(8,128)(2,1)S(1)}, u32[]{:S(2)}, u32[]{:S(2)}) collective-permute-start(bf16[3,2,96,384]{3,2,1,0:T(8,128)(2,1)} %get-tuple-element.344), channel_id=1, source_target_pairs={{0,8},{4,12},{8,0},{12,4},{16,24},{20,28},{24,16},{28,20},{1,9},{5... | collective-permute-start | bytes 1327112 | tf_op jit(solution)/shard_map/ppermute | solution.py:319
  312.5 18.2 %collective-permute-start.44 = (bf16[3,2,96,384]{3,2,1,0:T(8,128)(2,1)}, bf16[3,2,96,384]{3,2,1,0:T(8,128)(2,1)S(1)}, u32[]{:S(2)}, u32[]{:S(2)}) collective-permute-start(bf16[3,2,96,384]{3,2,1,0:T(8,128)(2,1)} %get-tuple-element.345), channel_id=1, source_target_pairs={{0,16},{4,20},{8,24},{12,28},{16,0},{20,4},{24,8},{28,12},{1,17},{... | collective-permute-start | bytes 1327112 | tf_op jit(solution)/shard_map/ppermute | solution.py:319
  315.3 21.3 %collective-permute-start.40 = (f32[24,768]{1,0:T(8,128)}, f32[24,768]{1,0:T(8,128)}, u32[]{:S(2)}, u32[]{:S(2)}) collective-permute-start(f32[24,768]{1,0:T(8,128)} %add.150), channel_id=1, source_target_pairs={{0,8},{4,12},{8,0},{12,4},{16,24},{20,28},{24,16},{28,20},{1,9},{5... | collective-permute-start | bytes 221192 | tf_op jit(solution)/shard_map/ppermute | solution.py:319
  (68 other events, 743.3 us)

commit v4 on v3

--- a/solution.py
+++ b/solution.py
@@ -968,11 +968,23 @@
     return (part(rank) + got[0]) + (got[1] + got[2])
 
 
+def halve_mp(value):
+    rank = lax.axis_index("mp")
+    pairs = value.reshape((2, 2) + value.shape[1:])
+    keep, send = two_parts(pairs, 1, rank % 2)
+    (send,) = yield [send]
+    (got,) = yield [swap(send, "mp", 1)]
+    keep, send = two_parts(keep.astype(full) + got.astype(full), 0, rank // 2)
+    (send,) = yield [send]
+    (got,) = yield [swap(send, "mp", 2)]
+    return keep + got.astype(full)
+
+
 def scatter_feed(up_own, down_own):
     mp = lax.axis_size("mp")
     block = down_own.shape[1]
     out_own = up_own[mp].reshape(block, mp, -1).transpose(1, 0, 2)
-    own = yield from scatter_mp(
+    own = yield from halve_mp(
         jnp.concatenate([up_own[:mp], down_own, out_own.reshape(mp, -1, D)], axis=1)
     )
     return own[:block], own[block : 2 * block].T, own[2 * block :].reshape(block, -1).T
@@ -1249,6 +1261,7 @@
     down_own, up_own = scatter.finish(order)
     feed = Steps(scatter_feed(up_own, down_own))
     feed.advance(order)
+    qkv.advance(order)
     tokens, first_own = order(tokens, firsts[0])
     input_grad, packed = last_norm(
         tokens,
@@ -1264,14 +1277,15 @@
     )
     packed, input_grad = order(packed, input_grad)
     small = Steps(sum_small(packed))
+    feed.advance(order)
+    feed.advance(order)
+    small.advance(order)
     qkv.advance(order)
-    small.advance(order)
-    small.advance(order)
-    feed.advance(order)
     qkv.advance(order)
     small.advance(order)
     qkv.advance(order)
-    qkv.advance(order)
+    small.advance(order)
+    feed.advance(order)
     total = small.finish(order)
     qkv_grad = qkv.finish(order)
     up_grad, down_grad, out_grad = feed.finish(order)

time: 368 us -> 362 us (0.984)
  the two profiles are of different devices: /device:TPU:0 before, /device:TPU:17 now
where the time goes in v4:
time: 362 us; the launch traced here: 355 us
  Pallas kernels  178 us (49%)
  starting transfers between devices  73.5 us (20%)
  waiting for transfers between devices  58.5 us (16%)
  local copies, waits for them, and re-layouts  18.9 us (5%)
  other arithmetic  17.5 us (5%)
  between operations  5.29 us (1%)
    pallas_call x4, Pallas kernels, attend_backward(): pl.pallas_call(functools.partial(backward_kernel, number, first, last, fo...  66.6 us
    pallas_call x3, Pallas kernels, attend_forward(): pl.pallas_call(functools.partial(forward_kernel, numbers, first, final),...  46.5 us
    ppermute x43, starting transfers between devices, swap(): return lax.ppermute(value, axis, [(i, i ^ bit) for i in range(count)])  40.9 us
    pallas_call x1, Pallas kernels, middle_call(): pl.pallas_call(functools.partial(middle_kernel, plan, block, len(arrays))...  35.7 us
    ppermute x12, starting transfers between devices, shards(): along = lambda value, pairs: lax.ppermute(value, 'mp', pairs)  32.6 us
    ppermute x43, waiting for transfers between devices, swap(): return lax.ppermute(value, axis, [(i, i ^ bit) for i in range(count)])  31.2 us
    ppermute x12, waiting for transfers between devices, shards(): along = lambda value, pairs: lax.ppermute(value, 'mp', pairs)  27.3 us
    pallas_call x1, Pallas kernels, qkv_grads(): pl.pallas_call(functools.partial(qkv_grad_kernel, count), out_shape=[jax....  13.1 us
  transfers between devices with their start and end apart: 55, of which 15 were waited for; matrix products, arithmetic and copies ran while one was open for 8% of the time, Pallas kernels for 39%

profile of v4, /device:TPU:17, one launch (start us, length us, event | category | flops | bytes accessed | tf_op | source)
XLA Modules:
  0.0 355.0 jit_solution(8443277115044097068)
XLA Ops:
  17.1 3.9 %collective-permute-done.2 = bf16[384,384]{1,0:T(8,128)(2,1)S(1)} collective-permute-done((bf16[384,384]{1,0:T(8,128)(2,1)S(1)}, bf16[384,384]{1,0:T(8,128)(2,1)S(1)}, u32[]{:S(2)}, u32[]{:S(2)}) %collective-permute-start.2) | collective-permute-done | bytes 294944 | tf_op jit(solution)/shard_map/ppermute | solution.py:319
  23.6 3.2 collective-permute-start.3
  29.1 8.8 %collective-permute-done.3 = bf16[384,768]{1,0:T(8,128)(2,1)} collective-permute-done((bf16[384,768]{1,0:T(8,128)(2,1)S(1)}, bf16[384,768]{1,0:T(8,128)(2,1)}, u32[]{:S(2)}, u32[]{:S(2)}) %collective-permute-start.3) | collective-permute-done | bytes 589856 | tf_op jit(solution)/shard_map/ppermute | solution.py:1072
  37.9 3.5 collective-permute-start.11
  41.6 6.3 %collective-permute-start.8 = (bf16[384,768]{1,0:T(8,128)(2,1)}, bf16[384,768]{1,0:T(8,128)(2,1)}, u32[]{:S(2)}, u32[]{:S(2)}) collective-permute-start(bf16[384,768]{1,0:T(8,128)(2,1)} %collective-permute-done.3), channel_id=1, source_target_pairs={{1,0},{2,3},{5,4},{6,7},{9,8},{10,11},{13,12},{14,15},{17,16},{18,... | collective-permute-start | bytes 1769480 | tf_op jit(solution)/shard_map/ppermute | solution.py:1072
  50.6 3.4 collective-permute-start.7
  54.9 4.2 %place.1 = (bf16[768,768]{1,0:T(8,128)(2,1)}, bf16[768,1536]{1,0:T(8,128)(2,1)}) custom-call(bf16[288,768]{1,0:T(8,128)(2,1)} %copy-done.12, bf16[288,768]{1,0:T(8,128)(2,1)} %copy-done.23, bf16[288,768]{1,0:T(8,128)(2,1)} %copy-done.24, bf16[288,768]{1,0:T(8,128)(2,1)} %copy-done.25, bf16[288,768]{1,0:T(8,128)(2,1)} %copy-done.11, ...), custom_call_target="tpu_custom_call" | custom-call | flops 1048576 | bytes 65536 | tf_op jit(solution)/shard_map/place/pallas_call | solution.py:426
  61.6 14.7 %collective-permute-done.6 = bf16[512,768]{1,0:T(8,128)(2,1)S(1)} collective-permute-done((bf16[512,768]{1,0:T(8,128)(2,1)S(1)}, bf16[512,768]{1,0:T(8,128)(2,1)S(1)}, u32[]{:S(2)}, u32[]{:S(2)}) %collective-permute-start.6) | collective-permute-done | bytes 786464 | tf_op jit(solution)/shard_map/ppermute | solution.py:1072
  76.3 4.1 %collective-permute-start.15 = (bf16[512,768]{1,0:T(8,128)(2,1)S(1)}, bf16[512,768]{1,0:T(8,128)(2,1)S(1)}, u32[]{:S(2)}, u32[]{:S(2)}) collective-permute-start(bf16[512,768]{1,0:T(8,128)(2,1)S(1)} %collective-permute-done.6), channel_id=1, source_target_pairs={{1,2},{2,3},{5,6},{6,7},{9,10},{10,11},{13,14},{14,15},{17,18},{18... | collective-permute-start | bytes 2359304 | tf_op jit(solution)/shard_map/ppermute | solution.py:1072
  85.2 20.2 %attend_forward.3 = (bf16[512,768]{1,0:T(8,128)(2,1)}, bf16[512,768]{1,0:T(8,128)(2,1)}, bf16[512,768]{1,0:T(8,128)(2,1)}, bf16[512,768]{1,0:T(8,128)(2,1)}, bf1...) custom-call(s32[6]{0:T(128)} %stack.42.scalars.refs_0_, ...), custom_call_target="tpu_custom_call" | custom-call | flops 1048576 | bytes 65536 | tf_op jit(solution)/shard_map/attend_forward/pallas_call | solution.py:129
  107.1 13.2 %attend_forward.4 = (bf16[512,768]{1,0:T(8,128)(2,1)}, bf16[512,768]{1,0:T(8,128)(2,1)}, f32[512,768]{1,0:T(8,128)}, f32[512,768]{1,0:T(8,128)}, f32[512,768]{1,0:T(8,128)}) custom-call(s32[6]{0:T(128)} %stack.42.scalars.refs_0_, bf16[512,768]{1,0:T(8,128)(2,1)} %copy-done.1, bf16[768,1536]{1,0:T(8,128)(2,1)} %get-tuple-element.218.refs_2_.refs_3_.refs_1_.wk_ref.wv_ref, ...), custom_call_target="tpu_custom_call" | custom-call | flops 1048576 | bytes 65536 | tf_op jit(solution)/shard_map/attend_forward/pallas_call | solution.py:129
  126.2 13.1 %attend_forward.5 = (bf16[512,768]{1,0:T(8,128)(2,1)}, bf16[512,768]{1,0:T(8,128)(2,1)}, f32[512,768]{1,0:T(8,128)}, f32[512,768]{1,0:T(8,128)}) custom-call(s32[6]{0:T(128)} %stack.42.scalars.refs_0_, bf16[512,768]{1,0:T(8,128)(2,1)} %broadcast_select_fusion.2.refs_0_.refs_3_, bf16[768,1536]{1,0:T(8,128)(2,1)} %get-tuple-element.218.refs_2_.refs_3_.refs_1_.wk_ref.wv_ref, ...), custom_call_target="tpu_custom_call" | custom-call | flops 1048576 | bytes 65536 | tf_op jit(solution)/shard_map/attend_forward/pallas_call | solution.py:129
  140.9 35.7 %middle.1 = (bf16[512,768]{1,0:T(8,128)(2,1)}, f32[512,768]{1,0:T(8,128)}, bf16[512,768]{1,0:T(8,128)(2,1)}, bf16[4,4,96,768]{3,2,1,0:T(8,128)(2,1)}, bf16[4,4,9...) custom-call(s32[6]{0:T(128)} %stack.42.scalars.refs_0_, ...), custom_call_target="tpu_custom_call" | custom-call | flops 1048576 | bytes 65536 | tf_op jit(solution)/shard_map/middle/pallas_call | solution.py:661
  177.1 14.2 %attend_backward.4 = (f32[512,768]{1,0:T(8,128)}, bf16[512,768]{1,0:T(8,128)(2,1)}, bf16[512,768]{1,0:T(8,128)(2,1)}, bf16[512,768]{1,0:T(8,128)(2,1)}) custom-call(s32[6]{0:T(128)} %stack.42.scalars.refs_0_, bf16[512,768]{1,0:T(8,128)(2,1)} %get-tuple-element.239.refs_4_.q_ref, bf16[512,768]{1,0:T(8,128)(2,1)} %get-tuple-element.268.k_ref, ...), custom_call_target="tpu_custom_call" | custom-call | flops 1048576 | bytes 65536 | tf_op jit(solution)/shard_map/attend_backward/pallas_call | solution.py:266
  195.0 17.8 %attend_backward.5 = (f32[512,768]{1,0:T(8,128)}, bf16[512,768]{1,0:T(8,128)(2,1)}, bf16[512,768]{1,0:T(8,128)(2,1)}, f32[512,768]{1,0:T(8,128)}, bf16[4,2,96,76...) custom-call(s32[6]{0:T(128)} %stack.42.scalars.refs_0_, ...), custom_call_target="tpu_custom_call" | custom-call | flops 1048576 | bytes 65536 | tf_op jit(solution)/shard_map/attend_backward/pallas_call | solution.py:266
  220.0 14.6 %attend_backward.6 = (f32[512,768]{1,0:T(8,128)}, bf16[512,768]{1,0:T(8,128)(2,1)}, bf16[512,768]{1,0:T(8,128)(2,1)}, f32[512,768]{1,0:T(8,128)}) custom-call(s32[6]{0:T(128)} %stack.42.scalars.refs_0_, bf16[512,768]{1,0:T(8,128)(2,1)} %get-tuple-element.239.refs_4_.q_ref, bf16[512,768]{1,0:T(8,128)(2,1)} %get-tuple-element.236.k_ref, ...), custom_call_target="tpu_custom_call" | custom-call | flops 1048576 | bytes 65536 | tf_op jit(solution)/shard_map/attend_backward/pallas_call | solution.py:266
  240.6 3.4 collective-permute-start.34
  247.6 19.9 %attend_backward.7 = (bf16[512,768]{1,0:T(8,128)(2,1)}, bf16[512,768]{1,0:T(8,128)(2,1)}, bf16[512,768]{1,0:T(8,128)(2,1)}, f32[512,768]{1,0:T(8,128)}, bf16[4,1...) custom-call(s32[6]{0:T(128)} %stack.42.scalars.refs_0_, ...), custom_call_target="tpu_custom_call" | custom-call | flops 1048576 | bytes 65536 | tf_op jit(solution)/shard_map/attend_backward/pallas_call | solution.py:266
  269.8 13.1 %qkv_grads.1 = (bf16[3,4,96,384]{3,2,1,0:T(8,128)(2,1)}, bf16[3,4,96,384]{3,2,1,0:T(8,128)(2,1)}, bf16[3,4,96,384]{3,2,1,0:T(8,128)(2,1)}, bf16[3,4,96,384]{3,2,1,0:T(8,128)(2,1)}, f32[16,768]{1,0:T(8,128)}) custom-call(bf16[512,768]{1,0:T(8,128)(2,1)} %copy-done.2, bf16[512,768]{1,0:T(8,128)(2,1)} %broadcast_select_fusion.refs_1_, ...), custom_call_target="tpu_custom_call" | custom-call | flops 1048576 | bytes 65536 | tf_op jit(solution)/shard_map/qkv_grads/pallas_call | solution.py:811
  291.6 3.9 %fold.2 = (bf16[3,2,96,384]{3,2,1,0:T(8,128)(2,1)}, bf16[3,2,96,384]{3,2,1,0:T(8,128)(2,1)}, bf16[3,2,96,384]{3,2,1,0:T(8,128)(2,1)}, bf16[3,2,96,384]{3,2,1,0:T(8,128)(2,1)}) custom-call(bf16[3,4,96,384]{3,2,1,0:T(8,128)(2,1)} %get-tuple-element.316.refs_0_, bf16[3,4,96,384]{3,2,1,0:T(8,128)(2,1)} %collective-permute-done.35.refs_1_, ...), custom_call_target="tpu_custom_call" | custom-call | bytes 16777216 | tf_op jit(solution)/shard_map/fold/pallas_call | solution.py:739
  297.0 5.2 %last_norm.1 = (f32[512,768]{1,0:T(8,128)}, f32[24,768]{1,0:T(8,128)}) custom-call(bf16[512,768]{1,0:T(8,128)(2,1)} %token_ref, f32[512,768]{1,0:T(8,128)} %get-tuple-element.334.first_ref, bf16[512,768]{1,0:T(8,128)(2,1)} %copy-done.18, bf16[512,768]{1,0:T(8,128)(2,1)} %copy-done.19, f32[512,768]{1,0:T(8,128)} %get-tuple-element.335.middle_ref, ...), custom_call_target="tpu_custom_call" | custom-call | flops 1048576 | bytes 65536 | tf_op jit(solution)/shard_map/last_norm/pallas_call | solution.py:871
  311.7 3.6 %collective-permute-start.40 = (f32[24,768]{1,0:T(8,128)S(1)}, f32[24,768]{1,0:T(8,128)S(1)}, u32[]{:S(2)}, u32[]{:S(2)}) collective-permute-start(f32[24,768]{1,0:T(8,128)S(1)} %copy-done.28), channel_id=1, source_target_pairs={{0,4},{4,0},{8,12},{12,8},{16,20},{20,16},{24,28},{28,24},{1,5},{5... | collective-permute-start | bytes 221192 | tf_op jit(solution)/shard_map/ppermute | solution.py:319
  325.2 10.8 %collective-permute-done.51 = bf16[216,768]{1,0:T(8,128)(2,1)S(1)} collective-permute-done((bf16[216,768]{1,0:T(8,128)(2,1)S(1)}, bf16[216,768]{1,0:T(8,128)(2,1)S(1)}, u32[]{:S(2)}, u32[]{:S(2)}) %collective-permute-start.51) | collective-permute-done | bytes 331808 | tf_op jit(solution)/shard_map/ppermute | solution.py:319
  340.7 8.2 %collective-permute-done.50 = f32[24,768]{1,0:T(8,128)S(1)} collective-permute-done((f32[24,768]{1,0:T(8,128)S(1)}, f32[24,768]{1,0:T(8,128)S(1)}, u32[]{:S(2)}, u32[]{:S(2)}) %collective-permute-start.50) | collective-permute-done | bytes 73760 | tf_op jit(solution)/shard_map/ppermute | solution.py:319
  (245 shorter events, 100.8 us)
Async XLA Ops:
  4.9 18.7 %collective-permute-start.1 = (bf16[192,768]{1,0:T(8,128)(2,1)S(1)}, bf16[192,768]{1,0:T(8,128)(2,1)S(1)}, u32[]{:S(2)}, u32[]{:S(2)}) collective-permute-start(bf16[192,768]{1,0:T(8,128)(2,1)S(1)} %pad_maximum_fusion.9), channel_id=1, source_target_pairs={{0,1},{1,0},{2,3},{3,2},{4,5},{5,4},{6,7},{7,6},{8,9},{9,8},{10,11... | collective-permute-start | bytes 884744 | tf_op jit(solution)/shard_map/ppermute | solution.py:319
  41.6 18.0 %collective-permute-start.8 = (bf16[384,768]{1,0:T(8,128)(2,1)}, bf16[384,768]{1,0:T(8,128)(2,1)}, u32[]{:S(2)}, u32[]{:S(2)}) collective-permute-start(bf16[384,768]{1,0:T(8,128)(2,1)} %collective-permute-done.3), channel_id=1, source_target_pairs={{1,0},{2,3},{5,4},{6,7},{9,8},{10,11},{13,12},{14,15},{17,16},{18,... | collective-permute-start | bytes 1769480 | tf_op jit(solution)/shard_map/ppermute | solution.py:1072
  48.7 27.6 %collective-permute-start.6 = (bf16[512,768]{1,0:T(8,128)(2,1)S(1)}, bf16[512,768]{1,0:T(8,128)(2,1)S(1)}, u32[]{:S(2)}, u32[]{:S(2)}) collective-permute-start(bf16[512,768]{1,0:T(8,128)(2,1)S(1)} %add_convert_fusion.2.refs_0_), channel_id=1, source_target_pairs={{0,1},{1,2},{2,3},{4,5},{5,6},{6,7},{8,9},{9,10},{10,11},{12,13},{... | collective-permute-start | bytes 2359304 | tf_op jit(solution)/shard_map/ppermute | solution.py:1072
  50.6 25.6 %collective-permute-start.7 = (bf16[512,768]{1,0:T(8,128)(2,1)S(1)}, bf16[512,768]{1,0:T(8,128)(2,1)S(1)}, u32[]{:S(2)}, u32[]{:S(2)}) collective-permute-start(bf16[512,768]{1,0:T(8,128)(2,1)S(1)} %add_convert_fusion.2.refs_0_), channel_id=1, source_target_pairs={{1,0},{2,1},{3,2},{5,4},{6,5},{7,6},{9,8},{10,9},{11,10},{13,12},{... | collective-permute-start | bytes 2359304 | tf_op jit(solution)/shard_map/ppermute | solution.py:1072
  60.7 23.4 %collective-permute-start.18 = (bf16[432,768]{1,0:T(8,128)(2,1)S(1)}, bf16[432,768]{1,0:T(8,128)(2,1)S(1)}, u32[]{:S(2)}, u32[]{:S(2)}) collective-permute-start(bf16[432,768]{1,0:T(8,128)(2,1)S(1)} %fusion.6), channel_id=1, source_target_pairs={{0,16},{4,20},{8,24},{12,28},{16,0},{20,4},{24,8},{28,12},{1,17},{... | collective-permute-start | bytes 1990664 | tf_op jit(solution)/shard_map/ppermute | solution.py:319
  61.4 22.9 %collective-permute-start.17 = (bf16[432,768]{1,0:T(8,128)(2,1)S(1)}, bf16[432,768]{1,0:T(8,128)(2,1)S(1)}, u32[]{:S(2)}, u32[]{:S(2)}) collective-permute-start(bf16[432,768]{1,0:T(8,128)(2,1)S(1)} %pad_maximum_fusion.4), channel_id=1, source_target_pairs={{0,8},{4,12},{8,0},{12,4},{16,24},{20,28},{24,16},{28,20},{1,9},{5... | collective-permute-start | bytes 1990664 | tf_op jit(solution)/shard_map/ppermute | solution.py:319
  76.3 29.1 %collective-permute-start.15 = (bf16[512,768]{1,0:T(8,128)(2,1)S(1)}, bf16[512,768]{1,0:T(8,128)(2,1)S(1)}, u32[]{:S(2)}, u32[]{:S(2)}) collective-permute-start(bf16[512,768]{1,0:T(8,128)(2,1)S(1)} %collective-permute-done.6), channel_id=1, source_target_pairs={{1,2},{2,3},{5,6},{6,7},{9,10},{10,11},{13,14},{14,15},{17,18},{18... | collective-permute-start | bytes 2359304 | tf_op jit(solution)/shard_map/ppermute | solution.py:1072
  80.4 25.0 %collective-permute-start.16 = (bf16[512,768]{1,0:T(8,128)(2,1)S(1)}, bf16[512,768]{1,0:T(8,128)(2,1)}, u32[]{:S(2)}, u32[]{:S(2)}) collective-permute-start(bf16[512,768]{1,0:T(8,128)(2,1)S(1)} %collective-permute-done.7), channel_id=1, source_target_pairs={{1,0},{2,1},{5,4},{6,5},{9,8},{10,9},{13,12},{14,13},{17,16},{18,1... | collective-permute-start | bytes 2359304 | tf_op jit(solution)/shard_map/ppermute | solution.py:1072
  84.3 38.2 %collective-permute-start.20 = (bf16[864,768]{1,0:T(8,128)(2,1)S(1)}, bf16[864,768]{1,0:T(8,128)(2,1)}, u32[]{:S(2)}, u32[]{:S(2)}) collective-permute-start(bf16[864,768]{1,0:T(8,128)(2,1)S(1)} %pad_maximum_fusion.1.refs_7_), channel_id=1, source_target_pairs={{0,16},{4,20},{8,24},{12,28},{16,0},{20,4},{24,8},{28,12},{1,17},{... | collective-permute-start | bytes 3981320 | tf_op jit(solution)/shard_map/ppermute | solution.py:319
  85.0 37.5 %collective-permute-start.21 = (bf16[864,768]{1,0:T(8,128)(2,1)S(1)}, bf16[864,768]{1,0:T(8,128)(2,1)}, u32[]{:S(2)}, u32[]{:S(2)}) collective-permute-start(bf16[864,768]{1,0:T(8,128)(2,1)S(1)} %pad_maximum_fusion.2.refs_11_), channel_id=1, source_target_pairs={{0,8},{4,12},{8,0},{12,4},{16,24},{20,28},{24,16},{28,20},{1,9},{5... | collective-permute-start | bytes 3981320 | tf_op jit(solution)/shard_map/ppermute | solution.py:319
  122.5 16.8 %collective-permute-start.22 = (bf16[864,768]{1,0:T(8,128)(2,1)S(1)}, bf16[864,768]{1,0:T(8,128)(2,1)S(1)}, u32[]{:S(2)}, u32[]{:S(2)}) collective-permute-start(bf16[864,768]{1,0:T(8,128)(2,1)S(1)} %pad_maximum_fusion.1.refs_7_), channel_id=1, source_target_pairs={{0,4},{4,0},{8,12},{12,8},{16,20},{20,16},{24,28},{28,24},{1,5},{5... | collective-permute-start | bytes 3981320 | tf_op jit(solution)/shard_map/ppermute | solution.py:319
  191.4 22.7 %collective-permute-start.28 = (bf16[512,768]{1,0:T(8,128)(2,1)}, bf16[512,768]{1,0:T(8,128)(2,1)S(1)}, u32[]{:S(2)}, u32[]{:S(2)}) collective-permute-start(bf16[512,768]{1,0:T(8,128)(2,1)} %get-tuple-element.278), channel_id=1, source_target_pairs={{0,1},{3,2},{4,5},{7,6},{8,9},{11,10},{12,13},{15,14},{16,17},{19,... | collective-permute-start | bytes 2359304 | tf_op jit(solution)/shard_map/ppermute | solution.py:1072
  212.8 33.7 %collective-permute-start.32 = (bf16[5,2,96,768]{3,2,1,0:T(8,128)(2,1)}, bf16[5,2,96,768]{3,2,1,0:T(8,128)(2,1)S(1)}, u32[]{:S(2)}, u32[]{:S(2)}) collective-permute-start(bf16[5,2,96,768]{3,2,1,0:T(8,128)(2,1)} %get-tuple-element.288), channel_id=1, source_target_pairs={{0,8},{4,12},{8,0},{12,4},{16,24},{20,28},{24,16},{28,20},{1,9},{5... | collective-permute-start | bytes 4423688 | tf_op jit(solution)/shard_map/ppermute | solution.py:319
  215.6 20.6 %collective-permute-start.30 = (bf16[512,768]{1,0:T(8,128)(2,1)S(1)}, bf16[512,768]{1,0:T(8,128)(2,1)S(1)}, u32[]{:S(2)}, u32[]{:S(2)}) collective-permute-start(bf16[512,768]{1,0:T(8,128)(2,1)S(1)} %add_convert_fusion.1), channel_id=1, source_target_pairs={{3,2},{2,1},{7,6},{6,5},{11,10},{10,9},{15,14},{14,13},{19,18},{18... | collective-permute-start | bytes 2359304 | tf_op jit(solution)/shard_map/ppermute | solution.py:1072
  217.8 26.8 %collective-permute-start.31 = (bf16[4,2,96,768]{3,2,1,0:T(8,128)(2,1)}, bf16[4,2,96,768]{3,2,1,0:T(8,128)(2,1)S(1)}, u32[]{:S(2)}, u32[]{:S(2)}) collective-permute-start(bf16[4,2,96,768]{3,2,1,0:T(8,128)(2,1)} %get-tuple-element.287), channel_id=1, source_target_pairs={{0,16},{4,20},{8,24},{12,28},{16,0},{20,4},{24,8},{28,12},{1,17},{... | collective-permute-start | bytes 3538952 | tf_op jit(solution)/shard_map/ppermute | solution.py:319
  218.7 19.6 %collective-permute-start.29 = (bf16[512,768]{1,0:T(8,128)(2,1)S(1)}, bf16[512,768]{1,0:T(8,128)(2,1)S(1)}, u32[]{:S(2)}, u32[]{:S(2)}) collective-permute-start(bf16[512,768]{1,0:T(8,128)(2,1)S(1)} %add_convert_fusion.1), channel_id=1, source_target_pairs={{0,1},{1,2},{4,5},{5,6},{8,9},{9,10},{12,13},{13,14},{16,17},{17,1... | collective-permute-start | bytes 2359304 | tf_op jit(solution)/shard_map/ppermute | solution.py:1072
  238.7 31.0 %collective-permute-start.33 = (bf16[512,768]{1,0:T(8,128)(2,1)S(1)}, bf16[512,768]{1,0:T(8,128)(2,1)S(1)}, u32[]{:S(2)}, u32[]{:S(2)}) collective-permute-start(bf16[512,768]{1,0:T(8,128)(2,1)S(1)} %select_convert_fusion), channel_id=1, source_target_pairs={{0,1},{1,2},{2,3},{4,5},{5,6},{6,7},{8,9},{9,10},{10,11},{12,13},{... | collective-permute-start | bytes 2359304 | tf_op jit(solution)/shard_map/ppermute | solution.py:1072
  240.6 29.1 %collective-permute-start.34 = (bf16[512,768]{1,0:T(8,128)(2,1)S(1)}, bf16[512,768]{1,0:T(8,128)(2,1)S(1)}, u32[]{:S(2)}, u32[]{:S(2)}) collective-permute-start(bf16[512,768]{1,0:T(8,128)(2,1)S(1)} %add_convert_fusion), channel_id=1, source_target_pairs={{3,2},{2,1},{1,0},{7,6},{6,5},{5,4},{11,10},{10,9},{9,8},{15,14},{... | collective-permute-start | bytes 2359304 | tf_op jit(solution)/shard_map/ppermute | solution.py:1072
  267.5 17.3 %collective-permute-start.38 = (bf16[5,1,96,768]{3,2,1,0:T(8,128)(2,1)}, bf16[5,1,96,768]{3,2,1,0:T(8,128)(2,1)}, u32[]{:S(2)}, u32[]{:S(2)}) collective-permute-start(bf16[5,1,96,768]{3,2,1,0:T(8,128)(2,1)} %get-tuple-element.306), channel_id=1, source_target_pairs={{0,16},{4,20},{8,24},{12,28},{16,0},{20,4},{24,8},{28,12},{1,17},{... | collective-permute-start | bytes 2211848 | tf_op jit(solution)/shard_map/ppermute | solution.py:319
  268.5 16.4 %collective-permute-start.37 = (bf16[4,1,96,768]{3,2,1,0:T(8,128)(2,1)}, bf16[4,1,96,768]{3,2,1,0:T(8,128)(2,1)}, u32[]{:S(2)}, u32[]{:S(2)}) collective-permute-start(bf16[4,1,96,768]{3,2,1,0:T(8,128)(2,1)} %get-tuple-element.305), channel_id=1, source_target_pairs={{0,8},{4,12},{8,0},{12,4},{16,24},{20,28},{24,16},{28,20},{1,9},{5... | collective-permute-start | bytes 1769480 | tf_op jit(solution)/shard_map/ppermute | solution.py:319
  315.3 20.7 %collective-permute-start.51 = (bf16[216,768]{1,0:T(8,128)(2,1)S(1)}, bf16[216,768]{1,0:T(8,128)(2,1)S(1)}, u32[]{:S(2)}, u32[]{:S(2)}) collective-permute-start(bf16[216,768]{1,0:T(8,128)(2,1)S(1)} %fusion.8), channel_id=1, source_target_pairs={{0,2},{1,3},{2,0},{3,1},{4,6},{5,7},{6,4},{7,5},{8,10},{9,11},{10,... | collective-permute-start | bytes 995336 | tf_op jit(solution)/shard_map/ppermute | solution.py:319
  320.9 32.2 %collective-permute-start.52 = (bf16[3,96,192]{2,1,0:T(8,128)(2,1)S(1)}, bf16[3,96,192]{2,1,0:T(8,128)(2,1)S(1)}, u32[]{:S(2)}, u32[]{:S(2)}) collective-permute-start(bf16[3,96,192]{2,1,0:T(8,128)(2,1)S(1)} %get-tuple-element.356), channel_id=1, source_target_pairs={{0,1},{1,0},{2,3},{3,2},{4,5},{5,4},{6,7},{7,6},{8,9},{9,8},{10,11... | collective-permute-start | bytes 331784 | tf_op jit(solution)/shard_map/ppermute | solution.py:319
  322.0 31.1 %collective-permute-start.53 = (bf16[3,96,192]{2,1,0:T(8,128)(2,1)S(1)}, bf16[3,96,192]{2,1,0:T(8,128)(2,1)S(1)}, u32[]{:S(2)}, u32[]{:S(2)}) collective-permute-start(bf16[3,96,192]{2,1,0:T(8,128)(2,1)S(1)} %get-tuple-element.357), channel_id=1, source_target_pairs={{0,2},{1,3},{2,0},{3,1},{4,6},{5,7},{6,4},{7,5},{8,10},{9,11},{10,... | collective-permute-start | bytes 331784 | tf_op jit(solution)/shard_map/ppermute | solution.py:319
  323.8 17.0 %collective-permute-start.49 = (f32[24,768]{1,0:T(8,128)S(1)}, f32[24,768]{1,0:T(8,128)S(1)}, u32[]{:S(2)}, u32[]{:S(2)}) collective-permute-start(f32[24,768]{1,0:T(8,128)S(1)} %add_add_fusion.1), channel_id=1, source_target_pairs={{0,2},{1,3},{2,0},{3,1},{4,6},{5,7},{6,4},{7,5},{8,10},{9,11},{10,... | collective-permute-start | bytes 221192 | tf_op jit(solution)/shard_map/ppermute | solution.py:319
  (69 other events, 716.8 us)

commit v5 on v4

--- a/solution.py
+++ b/solution.py
@@ -1127,19 +1127,17 @@
     if aligned:
         while qkv_gather.step < len(qkv_gather.bits):
             qkv_gather.advance(order)
-    tall_across = order(tall_across)
-    tall_other = jnp.where(middle, tall_across, along(tall_across, [(1, 0), (2, 3)]))
     sent = order(first_norm)
     from_left = along(sent, [(0, 1), (1, 2), (2, 3)])
     from_right = along(sent, [(1, 0), (2, 1), (3, 2)])
+    tall_across = order(tall_across)
+    tall_other = jnp.where(middle, tall_across, along(tall_across, [(1, 0), (2, 3)]))
     if aligned:
-        feed_gather = Gather(
-            [
-                jnp.concatenate([tall, out_rows[: block // 2]]),
-                jnp.concatenate([tall_other, out_rows[block // 2 :]]),
-            ]
-        )
         qkv_gather.advance(order)
+    hop_right, hop_left = order(from_left, from_right)
+    second_right = along(hop_right, [(1, 2), (2, 3)])
+    second_left = along(hop_left, [(1, 0), (2, 1)])
+    if aligned:
         arrays, plan = plan_of(
             qkv_gather.result,
             [
@@ -1151,39 +1149,43 @@
             ],
         )
         query_weight, pair_weight = order(*place(arrays, plan, block, [(D, D), (D, 2 * D)]))
+        feed_gather = Gather(
+            [
+                jnp.concatenate([tall, out_rows[: block // 2]]),
+                jnp.concatenate([tall_other, out_rows[block // 2 :]]),
+            ]
+        )
         feed_gather.advance(order)
     else:
         weights = lax.all_gather(qkv_rows.reshape(3, block, D), "dp", axis=1, tiled=True)
         query_weight = weights[0]
         pair_weight = jnp.concatenate([weights[1], weights[2]], axis=1)
-    hop_right, hop_left = order(from_left, from_right)
-    second_right = along(hop_right, [(1, 2), (2, 3)])
-    second_left = along(hop_left, [(1, 0), (2, 1)])
     near = jnp.where(rank == 0, hop_left, hop_right)
+    attend = lambda chunk, number, carried: order(
+        *attend_forward(
+            [order(chunk)],
+            (number,),
+            scalars,
+            query_weight,
+            pair_weight,
+            qv_bias[0:1],
+            qv_bias[1:2],
+            carried,
+        )
+    )
+    key_own, value_own, queries, *state = attend(first_norm, 0, None)
     if aligned:
         while feed_gather.step < len(feed_gather.bits):
             feed_gather.advance(order)
-    attend = lambda chunks, numbers, carried: attend_forward(
-        chunks,
-        numbers,
-        scalars,
-        query_weight,
-        pair_weight,
-        qv_bias[0:1],
-        qv_bias[1:2],
-        carried,
-    )
-    key_own, key_near, value_own, value_near, queries, *state = order(
-        *attend(order(first_norm, near), (0, 1), None)
-    )
+    key_near, value_near, *state = attend(near, 1, (queries, *state))
+    second_right, second_left = order(second_right, second_left)
     second = order(jnp.where(upper, second_right, second_left))
     third = along(second, [(1, 0), (2, 3)])
-    key_second, value_second, *state = attend([second], (2,), (queries, *state))
-    key_second, value_second, *state = order(key_second, value_second, *state)
+    key_second, value_second, *state = attend(second, 2, (queries, *state))
     last = order(jnp.where(middle, hop_left, third))
     if aligned:
         feed_gather.advance(order)
-    key_last, value_last, mixed, logs = order(*attend([order(last)], (3,), (queries, *state)))
+    key_last, value_last, mixed, logs = attend(last, 3, (queries, *state))
     if aligned:
         layout = lambda masks, shift: [
             (0, block, 0, masks[0], D, 0),

time: 362 us -> 371 us (1.025)
  the two profiles are of different devices: /device:TPU:17 before, /device:TPU:19 now
where the time goes in v5:
time: 371 us; the launch traced here: 364 us
  Pallas kernels  185 us (50%)
  waiting for transfers between devices  66.5 us (18%)
  starting transfers between devices  66.1 us (18%)
  local copies, waits for them, and re-layouts  20 us (5%)
  other arithmetic  19.1 us (5%)
  between operations  5.25 us (1%)
    pallas_call x4, Pallas kernels, attend_backward(): pl.pallas_call(functools.partial(backward_kernel, number, first, last, fo...  66.6 us
    pallas_call x4, Pallas kernels, attend_forward(): pl.pallas_call(functools.partial(forward_kernel, numbers, first, final),...  52.6 us
    ppermute x43, waiting for transfers between devices, swap(): return lax.ppermute(value, axis, [(i, i ^ bit) for i in range(count)])  39.8 us
    ppermute x43, starting transfers between devices, swap(): return lax.ppermute(value, axis, [(i, i ^ bit) for i in range(count)])  37.6 us
    pallas_call x1, Pallas kernels, middle_call(): pl.pallas_call(functools.partial(middle_kernel, plan, block, len(arrays))...  35.7 us
    ppermute x12, starting transfers between devices, shards(): along = lambda value, pairs: lax.ppermute(value, 'mp', pairs)  28.5 us
    ppermute x12, waiting for transfers between devices, shards(): along = lambda value, pairs: lax.ppermute(value, 'mp', pairs)  26.7 us
    pallas_call x1, Pallas kernels, qkv_grads(): pl.pallas_call(functools.partial(qkv_grad_kernel, count), out_shape=[jax....  13.1 us
  transfers between devices with their start and end apart: 55, of which 17 were waited for; matrix products, arithmetic and copies ran while one was open for 8% of the time, Pallas kernels for 40%

profile of v5, /device:TPU:19, one launch (start us, length us, event | category | flops | bytes accessed | tf_op | source)
XLA Modules:
  0.0 364.4 jit_solution(588162825317380217)
XLA Ops:
  17.0 4.0 %collective-permute-done.1 = bf16[384,384]{1,0:T(8,128)(2,1)S(1)} collective-permute-done((bf16[384,384]{1,0:T(8,128)(2,1)S(1)}, bf16[384,384]{1,0:T(8,128)(2,1)S(1)}, u32[]{:S(2)}, u32[]{:S(2)}) %collective-permute-start.1) | collective-permute-done | bytes 294944 | tf_op jit(solution)/shard_map/ppermute | solution.py:319
  22.7 3.8 %collective-permute-done.3 = bf16[144,768]{1,0:T(8,128)(2,1)S(1)} collective-permute-done((bf16[144,768]{1,0:T(8,128)(2,1)S(1)}, bf16[144,768]{1,0:T(8,128)(2,1)S(1)}, u32[]{:S(2)}, u32[]{:S(2)}) %collective-permute-start.3) | collective-permute-done | bytes 221216 | tf_op jit(solution)/shard_map/ppermute | solution.py:319
  27.5 4.4 %collective-permute-start.5 = (bf16[512,768]{1,0:T(8,128)(2,1)S(1)}, bf16[512,768]{1,0:T(8,128)(2,1)S(1)}, u32[]{:S(2)}, u32[]{:S(2)}) collective-permute-start(bf16[512,768]{1,0:T(8,128)(2,1)S(1)} %add_convert_fusion.2.refs_0_), channel_id=1, source_target_pairs={{0,1},{1,2},{2,3},{4,5},{5,6},{6,7},{8,9},{9,10},{10,11},{12,13},{... | collective-permute-start | bytes 2359304 | tf_op jit(solution)/shard_map/ppermute | solution.py:1072
  36.5 22.6 %collective-permute-done.9 = bf16[384,768]{1,0:T(8,128)(2,1)S(1)} collective-permute-done((bf16[384,768]{1,0:T(8,128)(2,1)S(1)}, bf16[384,768]{1,0:T(8,128)(2,1)S(1)}, u32[]{:S(2)}, u32[]{:S(2)}) %collective-permute-start.9) | collective-permute-done | bytes 589856 | tf_op jit(solution)/shard_map/ppermute | solution.py:1072
  61.2 5.2 %collective-permute-start.13 = (bf16[288,768]{1,0:T(8,128)(2,1)S(1)}, bf16[288,768]{1,0:T(8,128)(2,1)S(1)}, u32[]{:S(2)}, u32[]{:S(2)}) collective-permute-start(bf16[288,768]{1,0:T(8,128)(2,1)S(1)} %pad_maximum_fusion.6.refs_0_), channel_id=1, source_target_pairs={{0,4},{4,0},{8,12},{12,8},{16,20},{20,16},{24,28},{28,24},{1,5},{5... | collective-permute-start | bytes 1327112 | tf_op jit(solution)/shard_map/ppermute | solution.py:319
  70.8 4.2 %place.1 = (bf16[768,768]{1,0:T(8,128)(2,1)}, bf16[768,1536]{1,0:T(8,128)(2,1)}) custom-call(bf16[288,768]{1,0:T(8,128)(2,1)} %copy-done.12, bf16[288,768]{1,0:T(8,128)(2,1)} %copy-done.23, bf16[288,768]{1,0:T(8,128)(2,1)} %copy-done.25, bf16[288,768]{1,0:T(8,128)(2,1)} %copy-done.26, bf16[288,768]{1,0:T(8,128)(2,1)} %copy-done.11, ...), custom_call_target="tpu_custom_call" | custom-call | flops 1048576 | bytes 65536 | tf_op jit(solution)/shard_map/place/pallas_call | solution.py:426
  78.6 4.4 %collective-permute-start.11 = (bf16[512,768]{1,0:T(8,128)(2,1)S(1)}, bf16[512,768]{1,0:T(8,128)(2,1)}, u32[]{:S(2)}, u32[]{:S(2)}) collective-permute-start(bf16[512,768]{1,0:T(8,128)(2,1)S(1)} %collective-permute-done.6), channel_id=1, source_target_pairs={{1,0},{2,1},{5,4},{6,5},{9,8},{10,9},{13,12},{14,13},{17,16},{18,1... | collective-permute-start | bytes 2359304 | tf_op jit(solution)/shard_map/ppermute | solution.py:1072
  84.5 13.1 %attend_forward.4 = (bf16[512,768]{1,0:T(8,128)(2,1)}, bf16[512,768]{1,0:T(8,128)(2,1)}, bf16[512,768]{1,0:T(8,128)(2,1)}, f32[512,768]{1,0:T(8,128)}, f32[512,768]{1,0:T(8,128)}, /*index=5*/f32[512,768]{1,0:T(8,128)}) custom-call(s32[6]{0:T(128)} %stack.42.scalars.refs_0_, bf16[512,768]{1,0:T(8,128)(2,1)} %copy-done.2, ...), custom_call_target="tpu_custom_call" | custom-call | flops 1048576 | bytes 65536 | tf_op jit(solution)/shard_map/attend_forward/pallas_call | solution.py:129
  102.1 13.2 %attend_forward.5 = (bf16[512,768]{1,0:T(8,128)(2,1)}, bf16[512,768]{1,0:T(8,128)(2,1)}, f32[512,768]{1,0:T(8,128)}, f32[512,768]{1,0:T(8,128)}, f32[512,768]{1,0:T(8,128)}) custom-call(s32[6]{0:T(128)} %stack.42.scalars.refs_0_, bf16[512,768]{1,0:T(8,128)(2,1)} %broadcast_select_fusion.refs_0_.refs_1_, ...), custom_call_target="tpu_custom_call" | custom-call | flops 1048576 | bytes 65536 | tf_op jit(solution)/shard_map/attend_forward/pallas_call | solution.py:129
  116.9 13.2 %attend_forward.6 = (bf16[512,768]{1,0:T(8,128)(2,1)}, bf16[512,768]{1,0:T(8,128)(2,1)}, f32[512,768]{1,0:T(8,128)}, f32[512,768]{1,0:T(8,128)}, f32[512,768]{1,0:T(8,128)}) custom-call(s32[6]{0:T(128)} %stack.42.scalars.refs_0_, bf16[512,768]{1,0:T(8,128)(2,1)} %copy-done.1, bf16[768,1536]{1,0:T(8,128)(2,1)} %get-tuple-element.229.refs_1_.refs_2_.wk_ref.wv_ref, ...), custom_call_target="tpu_custom_call" | custom-call | flops 1048576 | bytes 65536 | tf_op jit(solution)/shard_map/attend_forward/pallas_call | solution.py:129
  136.1 13.2 %attend_forward.7 = (bf16[512,768]{1,0:T(8,128)(2,1)}, bf16[512,768]{1,0:T(8,128)(2,1)}, f32[512,768]{1,0:T(8,128)}, f32[512,768]{1,0:T(8,128)}) custom-call(s32[6]{0:T(128)} %stack.42.scalars.refs_0_, bf16[512,768]{1,0:T(8,128)(2,1)} %broadcast_select_fusion.2.refs_0_.refs_3_, bf16[768,1536]{1,0:T(8,128)(2,1)} %get-tuple-element.229.refs_1_.refs_2_.wk_ref.wv_ref, ...), custom_call_target="tpu_custom_call" | custom-call | flops 1048576 | bytes 65536 | tf_op jit(solution)/shard_map/attend_forward/pallas_call | solution.py:129
  150.9 35.7 %middle.1 = (bf16[512,768]{1,0:T(8,128)(2,1)}, f32[512,768]{1,0:T(8,128)}, bf16[512,768]{1,0:T(8,128)(2,1)}, bf16[4,4,96,768]{3,2,1,0:T(8,128)(2,1)}, bf16[4,4,9...) custom-call(s32[6]{0:T(128)} %stack.42.scalars.refs_0_, ...), custom_call_target="tpu_custom_call" | custom-call | flops 1048576 | bytes 65536 | tf_op jit(solution)/shard_map/middle/pallas_call | solution.py:661
  187.1 14.2 %attend_backward.4 = (f32[512,768]{1,0:T(8,128)}, bf16[512,768]{1,0:T(8,128)(2,1)}, bf16[512,768]{1,0:T(8,128)(2,1)}, bf16[512,768]{1,0:T(8,128)(2,1)}) custom-call(s32[6]{0:T(128)} %stack.42.scalars.refs_0_, bf16[512,768]{1,0:T(8,128)(2,1)} %get-tuple-element.241.refs_4_.q_ref, bf16[512,768]{1,0:T(8,128)(2,1)} %get-tuple-element.286.k_ref, ...), custom_call_target="tpu_custom_call" | custom-call | flops 1048576 | bytes 65536 | tf_op jit(solution)/shard_map/attend_backward/pallas_call | solution.py:266
  205.0 17.8 %attend_backward.5 = (f32[512,768]{1,0:T(8,128)}, bf16[512,768]{1,0:T(8,128)(2,1)}, bf16[512,768]{1,0:T(8,128)(2,1)}, f32[512,768]{1,0:T(8,128)}, bf16[4,2,96,76...) custom-call(s32[6]{0:T(128)} %stack.42.scalars.refs_0_, ...), custom_call_target="tpu_custom_call" | custom-call | flops 1048576 | bytes 65536 | tf_op jit(solution)/shard_map/attend_backward/pallas_call | solution.py:266
  228.3 14.6 %attend_backward.6 = (f32[512,768]{1,0:T(8,128)}, bf16[512,768]{1,0:T(8,128)(2,1)}, bf16[512,768]{1,0:T(8,128)(2,1)}, f32[512,768]{1,0:T(8,128)}) custom-call(s32[6]{0:T(128)} %stack.42.scalars.refs_0_, bf16[512,768]{1,0:T(8,128)(2,1)} %get-tuple-element.241.refs_4_.q_ref, bf16[512,768]{1,0:T(8,128)(2,1)} %get-tuple-element.253.k_ref, ...), custom_call_target="tpu_custom_call" | custom-call | flops 1048576 | bytes 65536 | tf_op jit(solution)/shard_map/attend_backward/pallas_call | solution.py:266
  249.1 3.4 collective-permute-start.34
  257.6 19.9 %attend_backward.7 = (bf16[512,768]{1,0:T(8,128)(2,1)}, bf16[512,768]{1,0:T(8,128)(2,1)}, bf16[512,768]{1,0:T(8,128)(2,1)}, f32[512,768]{1,0:T(8,128)}, bf16[4,1...) custom-call(s32[6]{0:T(128)} %stack.42.scalars.refs_0_, ...), custom_call_target="tpu_custom_call" | custom-call | flops 1048576 | bytes 65536 | tf_op jit(solution)/shard_map/attend_backward/pallas_call | solution.py:266
  278.0 13.1 %qkv_grads.1 = (bf16[3,4,96,384]{3,2,1,0:T(8,128)(2,1)}, bf16[3,4,96,384]{3,2,1,0:T(8,128)(2,1)}, bf16[3,4,96,384]{3,2,1,0:T(8,128)(2,1)}, bf16[3,4,96,384]{3,2,1,0:T(8,128)(2,1)}, f32[16,768]{1,0:T(8,128)}) custom-call(bf16[512,768]{1,0:T(8,128)(2,1)} %copy-done.2, bf16[512,768]{1,0:T(8,128)(2,1)} %broadcast_select_fusion.refs_0_.refs_1_, ...), custom_call_target="tpu_custom_call" | custom-call | flops 1048576 | bytes 65536 | tf_op jit(solution)/shard_map/qkv_grads/pallas_call | solution.py:811
  301.1 3.9 %fold.2 = (bf16[3,2,96,384]{3,2,1,0:T(8,128)(2,1)}, bf16[3,2,96,384]{3,2,1,0:T(8,128)(2,1)}, bf16[3,2,96,384]{3,2,1,0:T(8,128)(2,1)}, bf16[3,2,96,384]{3,2,1,0:T(8,128)(2,1)}) custom-call(bf16[3,4,96,384]{3,2,1,0:T(8,128)(2,1)} %get-tuple-element.334.refs_0_, bf16[3,4,96,384]{3,2,1,0:T(8,128)(2,1)} %collective-permute-done.35.refs_1_, ...), custom_call_target="tpu_custom_call" | custom-call | bytes 16777216 | tf_op jit(solution)/shard_map/fold/pallas_call | solution.py:739
  306.4 5.2 %last_norm.1 = (f32[512,768]{1,0:T(8,128)}, f32[24,768]{1,0:T(8,128)}) custom-call(bf16[512,768]{1,0:T(8,128)(2,1)} %token_ref, f32[512,768]{1,0:T(8,128)} %get-tuple-element.352.first_ref, bf16[512,768]{1,0:T(8,128)(2,1)} %copy-done.18, bf16[512,768]{1,0:T(8,128)(2,1)} %copy-done.19, f32[512,768]{1,0:T(8,128)} %get-tuple-element.353.middle_ref, ...), custom_call_target="tpu_custom_call" | custom-call | flops 1048576 | bytes 65536 | tf_op jit(solution)/shard_map/last_norm/pallas_call | solution.py:871
  316.4 3.2 fold.3
  334.6 10.8 %collective-permute-done.51 = bf16[216,768]{1,0:T(8,128)(2,1)S(1)} collective-permute-done((bf16[216,768]{1,0:T(8,128)(2,1)S(1)}, bf16[216,768]{1,0:T(8,128)(2,1)S(1)}, u32[]{:S(2)}, u32[]{:S(2)}) %collective-permute-start.51) | collective-permute-done | bytes 331808 | tf_op jit(solution)/shard_map/ppermute | solution.py:319
  350.1 8.1 %collective-permute-done.50 = f32[24,768]{1,0:T(8,128)S(1)} collective-permute-done((f32[24,768]{1,0:T(8,128)S(1)}, f32[24,768]{1,0:T(8,128)S(1)}, u32[]{:S(2)}, u32[]{:S(2)}) %collective-permute-start.50) | collective-permute-done | bytes 73760 | tf_op jit(solution)/shard_map/ppermute | solution.py:319
  358.3 3.0 fusion.7
  (250 shorter events, 104.9 us)
Async XLA Ops:
  4.9 17.7 %collective-permute-start.4 = (bf16[192,768]{1,0:T(8,128)(2,1)S(1)}, bf16[192,768]{1,0:T(8,128)(2,1)S(1)}, u32[]{:S(2)}, u32[]{:S(2)}) collective-permute-start(bf16[192,768]{1,0:T(8,128)(2,1)S(1)} %pad_maximum_fusion.9), channel_id=1, source_target_pairs={{0,1},{1,0},{2,3},{3,2},{4,5},{5,4},{6,7},{7,6},{8,9},{9,8},{10,11... | collective-permute-start | bytes 884744 | tf_op jit(solution)/shard_map/ppermute | solution.py:319
  27.5 39.0 %collective-permute-start.5 = (bf16[512,768]{1,0:T(8,128)(2,1)S(1)}, bf16[512,768]{1,0:T(8,128)(2,1)S(1)}, u32[]{:S(2)}, u32[]{:S(2)}) collective-permute-start(bf16[512,768]{1,0:T(8,128)(2,1)S(1)} %add_convert_fusion.2.refs_0_), channel_id=1, source_target_pairs={{0,1},{1,2},{2,3},{4,5},{5,6},{6,7},{8,9},{9,10},{10,11},{12,13},{... | collective-permute-start | bytes 2359304 | tf_op jit(solution)/shard_map/ppermute | solution.py:1072
  32.0 35.0 %collective-permute-start.6 = (bf16[512,768]{1,0:T(8,128)(2,1)S(1)}, bf16[512,768]{1,0:T(8,128)(2,1)S(1)}, u32[]{:S(2)}, u32[]{:S(2)}) collective-permute-start(bf16[512,768]{1,0:T(8,128)(2,1)S(1)} %add_convert_fusion.2.refs_0_), channel_id=1, source_target_pairs={{1,0},{2,1},{3,2},{5,4},{6,5},{7,6},{9,8},{10,9},{11,10},{13,12},{... | collective-permute-start | bytes 2359304 | tf_op jit(solution)/shard_map/ppermute | solution.py:1072
  33.9 25.2 %collective-permute-start.9 = (bf16[384,768]{1,0:T(8,128)(2,1)S(1)}, bf16[384,768]{1,0:T(8,128)(2,1)S(1)}, u32[]{:S(2)}, u32[]{:S(2)}) collective-permute-start(bf16[384,768]{1,0:T(8,128)(2,1)S(1)} %pad_maximum_fusion.5), channel_id=1, source_target_pairs={{1,2},{2,1},{5,6},{6,5},{9,10},{10,9},{13,14},{14,13},{17,18},{18,... | collective-permute-start | bytes 1769480 | tf_op jit(solution)/shard_map/ppermute | solution.py:1072
  36.1 25.1 %collective-permute-start.7 = (bf16[288,768]{1,0:T(8,128)(2,1)S(1)}, bf16[288,768]{1,0:T(8,128)(2,1)S(1)}, u32[]{:S(2)}, u32[]{:S(2)}) collective-permute-start(bf16[288,768]{1,0:T(8,128)(2,1)S(1)} %pad_maximum_fusion.6.refs_0_), channel_id=1, source_target_pairs={{0,16},{4,20},{8,24},{12,28},{16,0},{20,4},{24,8},{28,12},{1,17},{... | collective-permute-start | bytes 1327112 | tf_op jit(solution)/shard_map/ppermute | solution.py:319
  36.2 25.1 %collective-permute-start.8 = (bf16[288,768]{1,0:T(8,128)(2,1)S(1)}, bf16[288,768]{1,0:T(8,128)(2,1)S(1)}, u32[]{:S(2)}, u32[]{:S(2)}) collective-permute-start(bf16[288,768]{1,0:T(8,128)(2,1)S(1)} %pad_maximum_fusion.7.refs_4_), channel_id=1, source_target_pairs={{0,8},{4,12},{8,0},{12,4},{16,24},{20,28},{24,16},{28,20},{1,9},{5... | collective-permute-start | bytes 1327112 | tf_op jit(solution)/shard_map/ppermute | solution.py:319
  76.2 21.4 %collective-permute-start.18 = (bf16[432,768]{1,0:T(8,128)(2,1)S(1)}, bf16[432,768]{1,0:T(8,128)(2,1)S(1)}, u32[]{:S(2)}, u32[]{:S(2)}) collective-permute-start(bf16[432,768]{1,0:T(8,128)(2,1)S(1)} %fusion.6), channel_id=1, source_target_pairs={{0,16},{4,20},{8,24},{12,28},{16,0},{20,4},{24,8},{28,12},{1,17},{... | collective-permute-start | bytes 1990664 | tf_op jit(solution)/shard_map/ppermute | solution.py:319
  76.3 21.4 %collective-permute-start.17 = (bf16[432,768]{1,0:T(8,128)(2,1)S(1)}, bf16[432,768]{1,0:T(8,128)(2,1)}, u32[]{:S(2)}, u32[]{:S(2)}) collective-permute-start(bf16[432,768]{1,0:T(8,128)(2,1)S(1)} %pad_maximum_fusion.4), channel_id=1, source_target_pairs={{0,8},{4,12},{8,0},{12,4},{16,24},{20,28},{24,16},{28,20},{1,9},{5... | collective-permute-start | bytes 1990664 | tf_op jit(solution)/shard_map/ppermute | solution.py:319
  76.6 38.6 %collective-permute-start.10 = (bf16[512,768]{1,0:T(8,128)(2,1)S(1)}, bf16[512,768]{1,0:T(8,128)(2,1)S(1)}, u32[]{:S(2)}, u32[]{:S(2)}) collective-permute-start(bf16[512,768]{1,0:T(8,128)(2,1)S(1)} %collective-permute-done.5), channel_id=1, source_target_pairs={{1,2},{2,3},{5,6},{6,7},{9,10},{10,11},{13,14},{14,15},{17,18},{18... | collective-permute-start | bytes 2359304 | tf_op jit(solution)/shard_map/ppermute | solution.py:1072
  78.6 36.7 %collective-permute-start.11 = (bf16[512,768]{1,0:T(8,128)(2,1)S(1)}, bf16[512,768]{1,0:T(8,128)(2,1)}, u32[]{:S(2)}, u32[]{:S(2)}) collective-permute-start(bf16[512,768]{1,0:T(8,128)(2,1)S(1)} %collective-permute-done.6), channel_id=1, source_target_pairs={{1,0},{2,1},{5,4},{6,5},{9,8},{10,9},{13,12},{14,13},{17,16},{18,1... | collective-permute-start | bytes 2359304 | tf_op jit(solution)/shard_map/ppermute | solution.py:1072
  99.4 33.4 %collective-permute-start.20 = (bf16[864,768]{1,0:T(8,128)(2,1)S(1)}, bf16[864,768]{1,0:T(8,128)(2,1)}, u32[]{:S(2)}, u32[]{:S(2)}) collective-permute-start(bf16[864,768]{1,0:T(8,128)(2,1)S(1)} %pad_maximum_fusion.1.refs_7_), channel_id=1, source_target_pairs={{0,16},{4,20},{8,24},{12,28},{16,0},{20,4},{24,8},{28,12},{1,17},{... | collective-permute-start | bytes 3981320 | tf_op jit(solution)/shard_map/ppermute | solution.py:319
  100.9 32.0 %collective-permute-start.21 = (bf16[864,768]{1,0:T(8,128)(2,1)S(1)}, bf16[864,768]{1,0:T(8,128)(2,1)}, u32[]{:S(2)}, u32[]{:S(2)}) collective-permute-start(bf16[864,768]{1,0:T(8,128)(2,1)S(1)} %pad_maximum_fusion.2.refs_11_), channel_id=1, source_target_pairs={{0,8},{4,12},{8,0},{12,4},{16,24},{20,28},{24,16},{28,20},{1,9},{5... | collective-permute-start | bytes 3981320 | tf_op jit(solution)/shard_map/ppermute | solution.py:319
  201.4 21.8 %collective-permute-start.28 = (bf16[512,768]{1,0:T(8,128)(2,1)}, bf16[512,768]{1,0:T(8,128)(2,1)S(1)}, u32[]{:S(2)}, u32[]{:S(2)}) collective-permute-start(bf16[512,768]{1,0:T(8,128)(2,1)} %get-tuple-element.296), channel_id=1, source_target_pairs={{0,1},{3,2},{4,5},{7,6},{8,9},{11,10},{12,13},{15,14},{16,17},{19,... | collective-permute-start | bytes 2359304 | tf_op jit(solution)/shard_map/ppermute | solution.py:1072
  222.8 33.7 %collective-permute-start.32 = (bf16[5,2,96,768]{3,2,1,0:T(8,128)(2,1)}, bf16[5,2,96,768]{3,2,1,0:T(8,128)(2,1)S(1)}, u32[]{:S(2)}, u32[]{:S(2)}) collective-permute-start(bf16[5,2,96,768]{3,2,1,0:T(8,128)(2,1)} %get-tuple-element.306), channel_id=1, source_target_pairs={{0,8},{4,12},{8,0},{12,4},{16,24},{20,28},{24,16},{28,20},{1,9},{5... | collective-permute-start | bytes 4423688 | tf_op jit(solution)/shard_map/ppermute | solution.py:319
  224.7 20.6 %collective-permute-start.30 = (bf16[512,768]{1,0:T(8,128)(2,1)S(1)}, bf16[512,768]{1,0:T(8,128)(2,1)S(1)}, u32[]{:S(2)}, u32[]{:S(2)}) collective-permute-start(bf16[512,768]{1,0:T(8,128)(2,1)S(1)} %add_convert_fusion.1), channel_id=1, source_target_pairs={{3,2},{2,1},{7,6},{6,5},{11,10},{10,9},{15,14},{14,13},{19,18},{18... | collective-permute-start | bytes 2359304 | tf_op jit(solution)/shard_map/ppermute | solution.py:1072
  226.9 26.8 %collective-permute-start.31 = (bf16[4,2,96,768]{3,2,1,0:T(8,128)(2,1)}, bf16[4,2,96,768]{3,2,1,0:T(8,128)(2,1)S(1)}, u32[]{:S(2)}, u32[]{:S(2)}) collective-permute-start(bf16[4,2,96,768]{3,2,1,0:T(8,128)(2,1)} %get-tuple-element.305), channel_id=1, source_target_pairs={{0,16},{4,20},{8,24},{12,28},{16,0},{20,4},{24,8},{28,12},{1,17},{... | collective-permute-start | bytes 3538952 | tf_op jit(solution)/shard_map/ppermute | solution.py:319
  227.0 19.8 %collective-permute-start.29 = (bf16[512,768]{1,0:T(8,128)(2,1)S(1)}, bf16[512,768]{1,0:T(8,128)(2,1)S(1)}, u32[]{:S(2)}, u32[]{:S(2)}) collective-permute-start(bf16[512,768]{1,0:T(8,128)(2,1)S(1)} %add_convert_fusion.1), channel_id=1, source_target_pairs={{0,1},{1,2},{4,5},{5,6},{8,9},{9,10},{12,13},{13,14},{16,17},{17,1... | collective-permute-start | bytes 2359304 | tf_op jit(solution)/shard_map/ppermute | solution.py:1072
  247.2 30.8 %collective-permute-start.33 = (bf16[512,768]{1,0:T(8,128)(2,1)S(1)}, bf16[512,768]{1,0:T(8,128)(2,1)S(1)}, u32[]{:S(2)}, u32[]{:S(2)}) collective-permute-start(bf16[512,768]{1,0:T(8,128)(2,1)S(1)} %select_convert_fusion), channel_id=1, source_target_pairs={{0,1},{1,2},{2,3},{4,5},{5,6},{6,7},{8,9},{9,10},{10,11},{12,13},{... | collective-permute-start | bytes 2359304 | tf_op jit(solution)/shard_map/ppermute | solution.py:1072
  249.1 28.9 %collective-permute-start.34 = (bf16[512,768]{1,0:T(8,128)(2,1)S(1)}, bf16[512,768]{1,0:T(8,128)(2,1)S(1)}, u32[]{:S(2)}, u32[]{:S(2)}) collective-permute-start(bf16[512,768]{1,0:T(8,128)(2,1)S(1)} %add_convert_fusion), channel_id=1, source_target_pairs={{3,2},{2,1},{1,0},{7,6},{6,5},{5,4},{11,10},{10,9},{9,8},{15,14},{... | collective-permute-start | bytes 2359304 | tf_op jit(solution)/shard_map/ppermute | solution.py:1072
  277.5 17.1 %collective-permute-start.38 = (bf16[5,1,96,768]{3,2,1,0:T(8,128)(2,1)}, bf16[5,1,96,768]{3,2,1,0:T(8,128)(2,1)}, u32[]{:S(2)}, u32[]{:S(2)}) collective-permute-start(bf16[5,1,96,768]{3,2,1,0:T(8,128)(2,1)} %get-tuple-element.324), channel_id=1, source_target_pairs={{0,16},{4,20},{8,24},{12,28},{16,0},{20,4},{24,8},{28,12},{1,17},{... | collective-permute-start | bytes 2211848 | tf_op jit(solution)/shard_map/ppermute | solution.py:319
  324.6 20.8 %collective-permute-start.51 = (bf16[216,768]{1,0:T(8,128)(2,1)S(1)}, bf16[216,768]{1,0:T(8,128)(2,1)S(1)}, u32[]{:S(2)}, u32[]{:S(2)}) collective-permute-start(bf16[216,768]{1,0:T(8,128)(2,1)S(1)} %fusion.8), channel_id=1, source_target_pairs={{0,2},{1,3},{2,0},{3,1},{4,6},{5,7},{6,4},{7,5},{8,10},{9,11},{10,... | collective-permute-start | bytes 995336 | tf_op jit(solution)/shard_map/ppermute | solution.py:319
  330.4 32.1 %collective-permute-start.52 = (bf16[3,96,192]{2,1,0:T(8,128)(2,1)S(1)}, bf16[3,96,192]{2,1,0:T(8,128)(2,1)S(1)}, u32[]{:S(2)}, u32[]{:S(2)}) collective-permute-start(bf16[3,96,192]{2,1,0:T(8,128)(2,1)S(1)} %get-tuple-element.374), channel_id=1, source_target_pairs={{0,1},{1,0},{2,3},{3,2},{4,5},{5,4},{6,7},{7,6},{8,9},{9,8},{10,11... | collective-permute-start | bytes 331784 | tf_op jit(solution)/shard_map/ppermute | solution.py:319
  331.5 31.1 %collective-permute-start.53 = (bf16[3,96,192]{2,1,0:T(8,128)(2,1)S(1)}, bf16[3,96,192]{2,1,0:T(8,128)(2,1)S(1)}, u32[]{:S(2)}, u32[]{:S(2)}) collective-permute-start(bf16[3,96,192]{2,1,0:T(8,128)(2,1)S(1)} %get-tuple-element.375), channel_id=1, source_target_pairs={{0,2},{1,3},{2,0},{3,1},{4,6},{5,7},{6,4},{7,5},{8,10},{9,11},{10,... | collective-permute-start | bytes 331784 | tf_op jit(solution)/shard_map/ppermute | solution.py:319
  333.2 16.9 %collective-permute-start.49 = (f32[24,768]{1,0:T(8,128)S(1)}, f32[24,768]{1,0:T(8,128)S(1)}, u32[]{:S(2)}, u32[]{:S(2)}) collective-permute-start(f32[24,768]{1,0:T(8,128)S(1)} %add_add_fusion.1), channel_id=1, source_target_pairs={{0,2},{1,3},{2,0},{3,1},{4,6},{5,7},{6,4},{7,5},{8,10},{9,11},{10,... | collective-permute-start | bytes 221192 | tf_op jit(solution)/shard_map/ppermute | solution.py:319
  (71 other events, 701.0 us)

commit v6 on v5

--- a/solution.py
+++ b/solution.py
@@ -1124,15 +1124,14 @@
     tall = order(jnp.concatenate([tall, tall_swap]))
     tall_across = along(tall, [(1, 2), (2, 1)])
 
-    if aligned:
-        while qkv_gather.step < len(qkv_gather.bits):
-            qkv_gather.advance(order)
     sent = order(first_norm)
     from_left = along(sent, [(0, 1), (1, 2), (2, 3)])
     from_right = along(sent, [(1, 0), (2, 1), (3, 2)])
     tall_across = order(tall_across)
-    tall_other = jnp.where(middle, tall_across, along(tall_across, [(1, 0), (2, 3)]))
+    tall_far = along(tall_across, [(1, 0), (2, 3)])
     if aligned:
+        while qkv_gather.step < len(qkv_gather.bits):
+            qkv_gather.advance(order)
         qkv_gather.advance(order)
     hop_right, hop_left = order(from_left, from_right)
     second_right = along(hop_right, [(1, 2), (2, 3)])
@@ -1149,6 +1148,7 @@
             ],
         )
         query_weight, pair_weight = order(*place(arrays, plan, block, [(D, D), (D, 2 * D)]))
+        tall_other = jnp.where(middle, tall_across, order(tall_far))
         feed_gather = Gather(
             [
                 jnp.concatenate([tall, out_rows[: block // 2]]),
@@ -1161,10 +1161,10 @@
         query_weight = weights[0]
         pair_weight = jnp.concatenate([weights[1], weights[2]], axis=1)
     near = jnp.where(rank == 0, hop_left, hop_right)
-    attend = lambda chunk, number, carried: order(
+    attend = lambda parts, numbers, carried: order(
         *attend_forward(
-            [order(chunk)],
-            (number,),
+            parts,
+            numbers,
             scalars,
             query_weight,
             pair_weight,
@@ -1173,19 +1173,21 @@
             carried,
         )
     )
-    key_own, value_own, queries, *state = attend(first_norm, 0, None)
+    key_own, value_own, queries, *state = attend([order(first_norm)], (0,), None)
+    second_right, second_left = order(second_right, second_left)
+    second = order(jnp.where(upper, second_right, second_left))
+    third = along(second, [(1, 0), (2, 3)])
     if aligned:
         while feed_gather.step < len(feed_gather.bits):
             feed_gather.advance(order)
-    key_near, value_near, *state = attend(near, 1, (queries, *state))
-    second_right, second_left = order(second_right, second_left)
-    second = order(jnp.where(upper, second_right, second_left))
-    third = along(second, [(1, 0), (2, 3)])
-    key_second, value_second, *state = attend(second, 2, (queries, *state))
-    last = order(jnp.where(middle, hop_left, third))
+    near, second = order(near, second)
+    key_near, key_second, value_near, value_second, *state = attend(
+        [near, second], (1, 2), (queries, *state)
+    )
+    last = order(jnp.where(middle, hop_left, order(third)))
     if aligned:
         feed_gather.advance(order)
-    key_last, value_last, mixed, logs = attend(last, 3, (queries, *state))
+    key_last, value_last, mixed, logs = attend([order(last)], (3,), (queries, *state))
     if aligned:
         layout = lambda masks, shift: [
             (0, block, 0, masks[0], D, 0),

time: 371 us -> 356 us (0.960)
  the two profiles are of different devices: /device:TPU:19 before, /device:TPU:17 now
where the time goes in v6:
time: 356 us; the launch traced here: 350 us
  Pallas kernels  177 us (50%)
  starting transfers between devices  77.2 us (22%)
  waiting for transfers between devices  46.9 us (13%)
  local copies, waits for them, and re-layouts  20.6 us (6%)
  other arithmetic  20.4 us (6%)
  between operations  5.31 us (1%)
    pallas_call x4, Pallas kernels, attend_backward(): pl.pallas_call(functools.partial(backward_kernel, number, first, last, fo...  66.6 us
    ppermute x43, starting transfers between devices, swap(): return lax.ppermute(value, axis, [(i, i ^ bit) for i in range(count)])  48.3 us
    pallas_call x3, Pallas kernels, attend_forward(): pl.pallas_call(functools.partial(forward_kernel, numbers, first, final),...  45.2 us
    ppermute x43, waiting for transfers between devices, swap(): return lax.ppermute(value, axis, [(i, i ^ bit) for i in range(count)])  39.6 us
    pallas_call x1, Pallas kernels, middle_call(): pl.pallas_call(functools.partial(middle_kernel, plan, block, len(arrays))...  35.7 us
    ppermute x12, starting transfers between devices, shards(): along = lambda value, pairs: lax.ppermute(value, 'mp', pairs)  28.9 us
    pallas_call x1, Pallas kernels, qkv_grads(): pl.pallas_call(functools.partial(qkv_grad_kernel, count), out_shape=[jax....  13.1 us
    unnamed x81, local copies, waits for them, and re-layouts  10.3 us
  transfers between devices with their start and end apart: 55, of which 19 were waited for; matrix products, arithmetic and copies ran while one was open for 8% of the time, Pallas kernels for 39%

profile of v6, /device:TPU:17, one launch (start us, length us, event | category | flops | bytes accessed | tf_op | source)
XLA Modules:
  0.0 350.4 jit_solution(2733558799165042066)
XLA Ops:
  17.3 3.7 %collective-permute-done.2 = bf16[384,384]{1,0:T(8,128)(2,1)S(1)} collective-permute-done((bf16[384,384]{1,0:T(8,128)(2,1)S(1)}, bf16[384,384]{1,0:T(8,128)(2,1)S(1)}, u32[]{:S(2)}, u32[]{:S(2)}) %collective-permute-start.2) | collective-permute-done | bytes 294944 | tf_op jit(solution)/shard_map/ppermute | solution.py:319
  21.1 3.2 collective-permute-start.7
  32.2 3.7 %collective-permute-done.7 = bf16[384,768]{1,0:T(8,128)(2,1)} collective-permute-done((bf16[384,768]{1,0:T(8,128)(2,1)S(1)}, bf16[384,768]{1,0:T(8,128)(2,1)}, u32[]{:S(2)}, u32[]{:S(2)}) %collective-permute-start.7) | collective-permute-done | bytes 589856 | tf_op jit(solution)/shard_map/ppermute | solution.py:1072
  44.6 6.6 %collective-permute-start.13 = (bf16[288,768]{1,0:T(8,128)(2,1)S(1)}, bf16[288,768]{1,0:T(8,128)(2,1)S(1)}, u32[]{:S(2)}, u32[]{:S(2)}) collective-permute-start(bf16[288,768]{1,0:T(8,128)(2,1)S(1)} %pad_maximum_fusion.6.refs_0_), channel_id=1, source_target_pairs={{0,4},{4,0},{8,12},{12,8},{16,20},{20,16},{24,28},{28,24},{1,5},{5... | collective-permute-start | bytes 1327112 | tf_op jit(solution)/shard_map/ppermute | solution.py:319
  58.4 5.2 %collective-permute-start.11 = (bf16[512,768]{1,0:T(8,128)(2,1)S(1)}, bf16[512,768]{1,0:T(8,128)(2,1)}, u32[]{:S(2)}, u32[]{:S(2)}) collective-permute-start(bf16[512,768]{1,0:T(8,128)(2,1)S(1)} %collective-permute-done.4), channel_id=1, source_target_pairs={{1,0},{2,1},{5,4},{6,5},{9,8},{10,9},{13,12},{14,13},{17,16},{18,1... | collective-permute-start | bytes 2359304 | tf_op jit(solution)/shard_map/ppermute | solution.py:1072
  65.2 4.1 %place.1 = (bf16[768,768]{1,0:T(8,128)(2,1)}, bf16[768,1536]{1,0:T(8,128)(2,1)}) custom-call(bf16[288,768]{1,0:T(8,128)(2,1)} %copy-done.12, bf16[288,768]{1,0:T(8,128)(2,1)} %copy-done.24, bf16[288,768]{1,0:T(8,128)(2,1)} %copy-done.26, bf16[288,768]{1,0:T(8,128)(2,1)} %copy-done.27, bf16[288,768]{1,0:T(8,128)(2,1)} %copy-done.11, ...), custom_call_target="tpu_custom_call" | custom-call | flops 1048576 | bytes 65536 | tf_op jit(solution)/shard_map/place/pallas_call | solution.py:426
  73.7 13.1 %attend_forward.3 = (bf16[512,768]{1,0:T(8,128)(2,1)}, bf16[512,768]{1,0:T(8,128)(2,1)}, bf16[512,768]{1,0:T(8,128)(2,1)}, f32[512,768]{1,0:T(8,128)}, f32[512,768]{1,0:T(8,128)}, /*index=5*/f32[512,768]{1,0:T(8,128)}) custom-call(s32[6]{0:T(128)} %stack.42.scalars.refs_0_, bf16[512,768]{1,0:T(8,128)(2,1)} %copy-done.1, ...), custom_call_target="tpu_custom_call" | custom-call | flops 1048576 | bytes 65536 | tf_op jit(solution)/shard_map/attend_forward/pallas_call | solution.py:129
  93.1 18.9 %attend_forward.4 = (bf16[512,768]{1,0:T(8,128)(2,1)}, bf16[512,768]{1,0:T(8,128)(2,1)}, bf16[512,768]{1,0:T(8,128)(2,1)}, bf16[512,768]{1,0:T(8,128)(2,1)}, f32...) custom-call(s32[6]{0:T(128)} %stack.42.scalars.refs_0_, ...), custom_call_target="tpu_custom_call" | custom-call | flops 1048576 | bytes 65536 | tf_op jit(solution)/shard_map/attend_forward/pallas_call | solution.py:129
  113.0 6.2 %collective-permute-done.20.refs_8_ = bf16[864,768]{1,0:T(8,128)(2,1)} collective-permute-done((bf16[864,768]{1,0:T(8,128)(2,1)S(1)}, bf16[864,768]{1,0:T(8,128)(2,1)}, u32[]{:S(2)}, u32[]{:S(2)}) %collective-permute-start.20) | collective-permute-done | bytes 1327136 | tf_op jit(solution)/shard_map/ppermute | solution.py:319
  122.5 13.1 %attend_forward.5 = (bf16[512,768]{1,0:T(8,128)(2,1)}, bf16[512,768]{1,0:T(8,128)(2,1)}, f32[512,768]{1,0:T(8,128)}, f32[512,768]{1,0:T(8,128)}) custom-call(s32[6]{0:T(128)} %stack.42.scalars.refs_0_, bf16[512,768]{1,0:T(8,128)(2,1)} %broadcast_select_fusion.2.refs_0_.refs_3_, bf16[768,1536]{1,0:T(8,128)(2,1)} %get-tuple-element.225.refs_1_.refs_2_.refs_3_.wk_ref.wv_ref, ...), custom_call_target="tpu_custom_call" | custom-call | flops 1048576 | bytes 65536 | tf_op jit(solution)/shard_map/attend_forward/pallas_call | solution.py:129
  137.2 35.7 %middle.1 = (bf16[512,768]{1,0:T(8,128)(2,1)}, f32[512,768]{1,0:T(8,128)}, bf16[512,768]{1,0:T(8,128)(2,1)}, bf16[4,4,96,768]{3,2,1,0:T(8,128)(2,1)}, bf16[4,4,9...) custom-call(s32[6]{0:T(128)} %stack.42.scalars.refs_0_, ...), custom_call_target="tpu_custom_call" | custom-call | flops 1048576 | bytes 65536 | tf_op jit(solution)/shard_map/middle/pallas_call | solution.py:661
  173.5 14.2 %attend_backward.4 = (f32[512,768]{1,0:T(8,128)}, bf16[512,768]{1,0:T(8,128)(2,1)}, bf16[512,768]{1,0:T(8,128)(2,1)}, bf16[512,768]{1,0:T(8,128)(2,1)}) custom-call(s32[6]{0:T(128)} %stack.42.scalars.refs_0_, bf16[512,768]{1,0:T(8,128)(2,1)} %get-tuple-element.238.refs_5_.refs_4_.q_ref, bf16[512,768]{1,0:T(8,128)(2,1)} %get-tuple-element.278.k_ref, ...), custom_call_target="tpu_custom_call" | custom-call | flops 1048576 | bytes 65536 | tf_op jit(solution)/shard_map/attend_backward/pallas_call | solution.py:266
  191.4 17.8 %attend_backward.5 = (f32[512,768]{1,0:T(8,128)}, bf16[512,768]{1,0:T(8,128)(2,1)}, bf16[512,768]{1,0:T(8,128)(2,1)}, f32[512,768]{1,0:T(8,128)}, bf16[4,2,96,76...) custom-call(s32[6]{0:T(128)} %stack.42.scalars.refs_0_, ...), custom_call_target="tpu_custom_call" | custom-call | flops 1048576 | bytes 65536 | tf_op jit(solution)/shard_map/attend_backward/pallas_call | solution.py:266
  215.6 14.9 %attend_backward.6 = (f32[512,768]{1,0:T(8,128)}, bf16[512,768]{1,0:T(8,128)(2,1)}, bf16[512,768]{1,0:T(8,128)(2,1)}, f32[512,768]{1,0:T(8,128)}) custom-call(s32[6]{0:T(128)} %stack.42.scalars.refs_0_, bf16[512,768]{1,0:T(8,128)(2,1)} %get-tuple-element.238.refs_5_.refs_4_.q_ref, bf16[512,768]{1,0:T(8,128)(2,1)} %get-tuple-element.256.k_ref, ...), custom_call_target="tpu_custom_call" | custom-call | flops 1048576 | bytes 65536 | tf_op jit(solution)/shard_map/attend_backward/pallas_call | solution.py:266
  236.5 3.4 collective-permute-start.34
  244.1 19.7 %attend_backward.7 = (bf16[512,768]{1,0:T(8,128)(2,1)}, bf16[512,768]{1,0:T(8,128)(2,1)}, bf16[512,768]{1,0:T(8,128)(2,1)}, f32[512,768]{1,0:T(8,128)}, bf16[4,1...) custom-call(s32[6]{0:T(128)} %stack.42.scalars.refs_0_, ...), custom_call_target="tpu_custom_call" | custom-call | flops 1048576 | bytes 65536 | tf_op jit(solution)/shard_map/attend_backward/pallas_call | solution.py:266
  265.3 13.1 %qkv_grads.1 = (bf16[3,4,96,384]{3,2,1,0:T(8,128)(2,1)}, bf16[3,4,96,384]{3,2,1,0:T(8,128)(2,1)}, bf16[3,4,96,384]{3,2,1,0:T(8,128)(2,1)}, bf16[3,4,96,384]{3,2,1,0:T(8,128)(2,1)}, f32[16,768]{1,0:T(8,128)}) custom-call(bf16[512,768]{1,0:T(8,128)(2,1)} %copy-done.1, bf16[512,768]{1,0:T(8,128)(2,1)} %broadcast_select_fusion.refs_0_.refs_1_, ...), custom_call_target="tpu_custom_call" | custom-call | flops 1048576 | bytes 65536 | tf_op jit(solution)/shard_map/qkv_grads/pallas_call | solution.py:811
  287.1 3.9 %fold.2 = (bf16[3,2,96,384]{3,2,1,0:T(8,128)(2,1)}, bf16[3,2,96,384]{3,2,1,0:T(8,128)(2,1)}, bf16[3,2,96,384]{3,2,1,0:T(8,128)(2,1)}, bf16[3,2,96,384]{3,2,1,0:T(8,128)(2,1)}) custom-call(bf16[3,4,96,384]{3,2,1,0:T(8,128)(2,1)} %get-tuple-element.326.refs_0_, bf16[3,4,96,384]{3,2,1,0:T(8,128)(2,1)} %collective-permute-done.35.refs_1_, ...), custom_call_target="tpu_custom_call" | custom-call | bytes 16777216 | tf_op jit(solution)/shard_map/fold/pallas_call | solution.py:739
  292.5 5.2 %last_norm.1 = (f32[512,768]{1,0:T(8,128)}, f32[24,768]{1,0:T(8,128)}) custom-call(bf16[512,768]{1,0:T(8,128)(2,1)} %token_ref, f32[512,768]{1,0:T(8,128)} %get-tuple-element.344.first_ref, bf16[512,768]{1,0:T(8,128)(2,1)} %copy-done.20, bf16[512,768]{1,0:T(8,128)(2,1)} %copy-done.21, f32[512,768]{1,0:T(8,128)} %get-tuple-element.345.middle_ref, ...), custom_call_target="tpu_custom_call" | custom-call | flops 1048576 | bytes 65536 | tf_op jit(solution)/shard_map/last_norm/pallas_call | solution.py:871
  302.5 3.2 fold.3
  321.2 8.0 %collective-permute-done.51 = bf16[216,768]{1,0:T(8,128)(2,1)S(1)} collective-permute-done((bf16[216,768]{1,0:T(8,128)(2,1)S(1)}, bf16[216,768]{1,0:T(8,128)(2,1)S(1)}, u32[]{:S(2)}, u32[]{:S(2)}) %collective-permute-start.51) | collective-permute-done | bytes 331808 | tf_op jit(solution)/shard_map/ppermute | solution.py:319
  329.2 3.3 collective-permute-start.50
  334.8 9.4 %collective-permute-done.50 = f32[24,768]{1,0:T(8,128)S(1)} collective-permute-done((f32[24,768]{1,0:T(8,128)S(1)}, f32[24,768]{1,0:T(8,128)S(1)}, u32[]{:S(2)}, u32[]{:S(2)}) %collective-permute-start.50) | collective-permute-done | bytes 73760 | tf_op jit(solution)/shard_map/ppermute | solution.py:319
  344.3 3.0 fusion.7
  (251 shorter events, 112.6 us)
Async XLA Ops:
  26.8 25.8 %collective-permute-start.3 = (bf16[512,768]{1,0:T(8,128)(2,1)S(1)}, bf16[512,768]{1,0:T(8,128)(2,1)S(1)}, u32[]{:S(2)}, u32[]{:S(2)}) collective-permute-start(bf16[512,768]{1,0:T(8,128)(2,1)S(1)} %add_convert_fusion.2.refs_0_), channel_id=1, source_target_pairs={{0,1},{1,2},{2,3},{4,5},{5,6},{6,7},{8,9},{9,10},{10,11},{12,13},{... | collective-permute-start | bytes 2359304 | tf_op jit(solution)/shard_map/ppermute | solution.py:1072
  29.4 26.1 %collective-permute-start.4 = (bf16[512,768]{1,0:T(8,128)(2,1)S(1)}, bf16[512,768]{1,0:T(8,128)(2,1)S(1)}, u32[]{:S(2)}, u32[]{:S(2)}) collective-permute-start(bf16[512,768]{1,0:T(8,128)(2,1)S(1)} %add_convert_fusion.2.refs_0_), channel_id=1, source_target_pairs={{1,0},{2,1},{3,2},{5,4},{6,5},{7,6},{9,8},{10,9},{11,10},{13,12},{... | collective-permute-start | bytes 2359304 | tf_op jit(solution)/shard_map/ppermute | solution.py:1072
  38.4 31.0 %collective-permute-start.12 = (bf16[384,768]{1,0:T(8,128)(2,1)}, bf16[384,768]{1,0:T(8,128)(2,1)}, u32[]{:S(2)}, u32[]{:S(2)}) collective-permute-start(bf16[384,768]{1,0:T(8,128)(2,1)} %collective-permute-done.7), channel_id=1, source_target_pairs={{1,0},{2,3},{5,4},{6,7},{9,8},{10,11},{13,12},{14,15},{17,16},{18,... | collective-permute-start | bytes 1769480 | tf_op jit(solution)/shard_map/ppermute | solution.py:1072
  55.7 31.1 %collective-permute-start.10 = (bf16[512,768]{1,0:T(8,128)(2,1)S(1)}, bf16[512,768]{1,0:T(8,128)(2,1)}, u32[]{:S(2)}, u32[]{:S(2)}) collective-permute-start(bf16[512,768]{1,0:T(8,128)(2,1)S(1)} %collective-permute-done.3), channel_id=1, source_target_pairs={{1,2},{2,3},{5,6},{6,7},{9,10},{10,11},{13,14},{14,15},{17,18},{18... | collective-permute-start | bytes 2359304 | tf_op jit(solution)/shard_map/ppermute | solution.py:1072
  58.4 28.4 %collective-permute-start.11 = (bf16[512,768]{1,0:T(8,128)(2,1)S(1)}, bf16[512,768]{1,0:T(8,128)(2,1)}, u32[]{:S(2)}, u32[]{:S(2)}) collective-permute-start(bf16[512,768]{1,0:T(8,128)(2,1)S(1)} %collective-permute-done.4), channel_id=1, source_target_pairs={{1,0},{2,1},{5,4},{6,5},{9,8},{10,9},{13,12},{14,13},{17,16},{18,1... | collective-permute-start | bytes 2359304 | tf_op jit(solution)/shard_map/ppermute | solution.py:1072
  70.6 17.5 %collective-permute-start.19 = (bf16[432,768]{1,0:T(8,128)(2,1)S(1)}, bf16[432,768]{1,0:T(8,128)(2,1)S(1)}, u32[]{:S(2)}, u32[]{:S(2)}) collective-permute-start(bf16[432,768]{1,0:T(8,128)(2,1)S(1)} %fusion.6), channel_id=1, source_target_pairs={{0,16},{4,20},{8,24},{12,28},{16,0},{20,4},{24,8},{28,12},{1,17},{... | collective-permute-start | bytes 1990664 | tf_op jit(solution)/shard_map/ppermute | solution.py:319
  71.9 16.3 %collective-permute-start.18 = (bf16[432,768]{1,0:T(8,128)(2,1)S(1)}, bf16[432,768]{1,0:T(8,128)(2,1)}, u32[]{:S(2)}, u32[]{:S(2)}) collective-permute-start(bf16[432,768]{1,0:T(8,128)(2,1)S(1)} %pad_maximum_fusion.4), channel_id=1, source_target_pairs={{0,8},{4,12},{8,0},{12,4},{16,24},{20,28},{24,16},{28,20},{1,9},{5... | collective-permute-start | bytes 1990664 | tf_op jit(solution)/shard_map/ppermute | solution.py:319
  90.0 29.2 %collective-permute-start.20 = (bf16[864,768]{1,0:T(8,128)(2,1)S(1)}, bf16[864,768]{1,0:T(8,128)(2,1)}, u32[]{:S(2)}, u32[]{:S(2)}) collective-permute-start(bf16[864,768]{1,0:T(8,128)(2,1)S(1)} %pad_maximum_fusion.1.refs_7_), channel_id=1, source_target_pairs={{0,16},{4,20},{8,24},{12,28},{16,0},{20,4},{24,8},{28,12},{1,17},{... | collective-permute-start | bytes 3981320 | tf_op jit(solution)/shard_map/ppermute | solution.py:319
  90.3 28.9 %collective-permute-start.21 = (bf16[864,768]{1,0:T(8,128)(2,1)S(1)}, bf16[864,768]{1,0:T(8,128)(2,1)}, u32[]{:S(2)}, u32[]{:S(2)}) collective-permute-start(bf16[864,768]{1,0:T(8,128)(2,1)S(1)} %pad_maximum_fusion.2.refs_11_), channel_id=1, source_target_pairs={{0,8},{4,12},{8,0},{12,4},{16,24},{20,28},{24,16},{28,20},{1,9},{5... | collective-permute-start | bytes 3981320 | tf_op jit(solution)/shard_map/ppermute | solution.py:319
  90.6 21.5 %collective-permute-start.17 = (bf16[512,768]{1,0:T(8,128)(2,1)S(1)}, bf16[512,768]{1,0:T(8,128)(2,1)S(1)}, u32[]{:S(2)}, u32[]{:S(2)}) collective-permute-start(bf16[512,768]{1,0:T(8,128)(2,1)S(1)} %broadcast_select_fusion.1.refs_1_.refs_2_), channel_id=1, source_target_pairs={{1,0},{2,3},{5,4},{6,7},{9,8},{10,11},{13,12},{14,15},{17,16},{18,... | collective-permute-start | bytes 2359304 | tf_op jit(solution)/shard_map/ppermute | solution.py:1072
  119.2 16.4 %collective-permute-start.22 = (bf16[864,768]{1,0:T(8,128)(2,1)S(1)}, bf16[864,768]{1,0:T(8,128)(2,1)S(1)}, u32[]{:S(2)}, u32[]{:S(2)}) collective-permute-start(bf16[864,768]{1,0:T(8,128)(2,1)S(1)} %pad_maximum_fusion.1.refs_7_), channel_id=1, source_target_pairs={{0,4},{4,0},{8,12},{12,8},{16,20},{20,16},{24,28},{28,24},{1,5},{5... | collective-permute-start | bytes 3981320 | tf_op jit(solution)/shard_map/ppermute | solution.py:319
  172.8 16.2 %collective-permute-start.27 = (bf16[5,4,96,768]{3,2,1,0:T(8,128)(2,1)}, bf16[5,4,96,768]{3,2,1,0:T(8,128)(2,1)S(1)}, u32[]{:S(2)}, u32[]{:S(2)}) collective-permute-start(bf16[5,4,96,768]{3,2,1,0:T(8,128)(2,1)} %get-tuple-element.283), channel_id=1, source_target_pairs={{0,4},{4,0},{8,12},{12,8},{16,20},{20,16},{24,28},{28,24},{1,5},{5... | collective-permute-start | bytes 8847368 | tf_op jit(solution)/shard_map/ppermute | solution.py:319
  173.4 15.6 %collective-permute-start.26 = (bf16[4,4,96,768]{3,2,1,0:T(8,128)(2,1)}, bf16[4,4,96,768]{3,2,1,0:T(8,128)(2,1)S(1)}, u32[]{:S(2)}, u32[]{:S(2)}) collective-permute-start(bf16[4,4,96,768]{3,2,1,0:T(8,128)(2,1)} %get-tuple-element.282), channel_id=1, source_target_pairs={{0,4},{4,0},{8,12},{12,8},{16,20},{20,16},{24,28},{28,24},{1,5},{5... | collective-permute-start | bytes 7077896 | tf_op jit(solution)/shard_map/ppermute | solution.py:319
  187.7 21.8 %collective-permute-start.28 = (bf16[512,768]{1,0:T(8,128)(2,1)}, bf16[512,768]{1,0:T(8,128)(2,1)S(1)}, u32[]{:S(2)}, u32[]{:S(2)}) collective-permute-start(bf16[512,768]{1,0:T(8,128)(2,1)} %get-tuple-element.288), channel_id=1, source_target_pairs={{0,1},{3,2},{4,5},{7,6},{8,9},{11,10},{12,13},{15,14},{16,17},{19,... | collective-permute-start | bytes 2359304 | tf_op jit(solution)/shard_map/ppermute | solution.py:1072
  209.2 33.7 %collective-permute-start.32 = (bf16[5,2,96,768]{3,2,1,0:T(8,128)(2,1)}, bf16[5,2,96,768]{3,2,1,0:T(8,128)(2,1)S(1)}, u32[]{:S(2)}, u32[]{:S(2)}) collective-permute-start(bf16[5,2,96,768]{3,2,1,0:T(8,128)(2,1)} %get-tuple-element.298), channel_id=1, source_target_pairs={{0,8},{4,12},{8,0},{12,4},{16,24},{20,28},{24,16},{28,20},{1,9},{5... | collective-permute-start | bytes 4423688 | tf_op jit(solution)/shard_map/ppermute | solution.py:319
  211.1 20.3 %collective-permute-start.30 = (bf16[512,768]{1,0:T(8,128)(2,1)S(1)}, bf16[512,768]{1,0:T(8,128)(2,1)S(1)}, u32[]{:S(2)}, u32[]{:S(2)}) collective-permute-start(bf16[512,768]{1,0:T(8,128)(2,1)S(1)} %add_convert_fusion.1), channel_id=1, source_target_pairs={{3,2},{2,1},{7,6},{6,5},{11,10},{10,9},{15,14},{14,13},{19,18},{18... | collective-permute-start | bytes 2359304 | tf_op jit(solution)/shard_map/ppermute | solution.py:1072
  213.1 27.1 %collective-permute-start.31 = (bf16[4,2,96,768]{3,2,1,0:T(8,128)(2,1)}, bf16[4,2,96,768]{3,2,1,0:T(8,128)(2,1)S(1)}, u32[]{:S(2)}, u32[]{:S(2)}) collective-permute-start(bf16[4,2,96,768]{3,2,1,0:T(8,128)(2,1)} %get-tuple-element.297), channel_id=1, source_target_pairs={{0,16},{4,20},{8,24},{12,28},{16,0},{20,4},{24,8},{28,12},{1,17},{... | collective-permute-start | bytes 3538952 | tf_op jit(solution)/shard_map/ppermute | solution.py:319
  214.3 19.9 %collective-permute-start.29 = (bf16[512,768]{1,0:T(8,128)(2,1)S(1)}, bf16[512,768]{1,0:T(8,128)(2,1)S(1)}, u32[]{:S(2)}, u32[]{:S(2)}) collective-permute-start(bf16[512,768]{1,0:T(8,128)(2,1)S(1)} %add_convert_fusion.1), channel_id=1, source_target_pairs={{0,1},{1,2},{4,5},{5,6},{8,9},{9,10},{12,13},{13,14},{16,17},{17,1... | collective-permute-start | bytes 2359304 | tf_op jit(solution)/shard_map/ppermute | solution.py:1072
  234.6 30.7 %collective-permute-start.33 = (bf16[512,768]{1,0:T(8,128)(2,1)S(1)}, bf16[512,768]{1,0:T(8,128)(2,1)S(1)}, u32[]{:S(2)}, u32[]{:S(2)}) collective-permute-start(bf16[512,768]{1,0:T(8,128)(2,1)S(1)} %select_convert_fusion), channel_id=1, source_target_pairs={{0,1},{1,2},{2,3},{4,5},{5,6},{6,7},{8,9},{9,10},{10,11},{12,13},{... | collective-permute-start | bytes 2359304 | tf_op jit(solution)/shard_map/ppermute | solution.py:1072
  236.5 28.8 %collective-permute-start.34 = (bf16[512,768]{1,0:T(8,128)(2,1)S(1)}, bf16[512,768]{1,0:T(8,128)(2,1)S(1)}, u32[]{:S(2)}, u32[]{:S(2)}) collective-permute-start(bf16[512,768]{1,0:T(8,128)(2,1)S(1)} %add_convert_fusion), channel_id=1, source_target_pairs={{3,2},{2,1},{1,0},{7,6},{6,5},{5,4},{11,10},{10,9},{9,8},{15,14},{... | collective-permute-start | bytes 2359304 | tf_op jit(solution)/shard_map/ppermute | solution.py:1072
  263.7 17.1 %collective-permute-start.38 = (bf16[5,1,96,768]{3,2,1,0:T(8,128)(2,1)}, bf16[5,1,96,768]{3,2,1,0:T(8,128)(2,1)}, u32[]{:S(2)}, u32[]{:S(2)}) collective-permute-start(bf16[5,1,96,768]{3,2,1,0:T(8,128)(2,1)} %get-tuple-element.316), channel_id=1, source_target_pairs={{0,16},{4,20},{8,24},{12,28},{16,0},{20,4},{24,8},{28,12},{1,17},{... | collective-permute-start | bytes 2211848 | tf_op jit(solution)/shard_map/ppermute | solution.py:319
  310.7 18.5 %collective-permute-start.51 = (bf16[216,768]{1,0:T(8,128)(2,1)S(1)}, bf16[216,768]{1,0:T(8,128)(2,1)S(1)}, u32[]{:S(2)}, u32[]{:S(2)}) collective-permute-start(bf16[216,768]{1,0:T(8,128)(2,1)S(1)} %fusion.8), channel_id=1, source_target_pairs={{0,2},{1,3},{2,0},{3,1},{4,6},{5,7},{6,4},{7,5},{8,10},{9,11},{10,... | collective-permute-start | bytes 995336 | tf_op jit(solution)/shard_map/ppermute | solution.py:319
  316.1 32.4 %collective-permute-start.52 = (bf16[3,96,192]{2,1,0:T(8,128)(2,1)S(1)}, bf16[3,96,192]{2,1,0:T(8,128)(2,1)S(1)}, u32[]{:S(2)}, u32[]{:S(2)}) collective-permute-start(bf16[3,96,192]{2,1,0:T(8,128)(2,1)S(1)} %get-tuple-element.366), channel_id=1, source_target_pairs={{0,1},{1,0},{2,3},{3,2},{4,5},{5,4},{6,7},{7,6},{8,9},{9,8},{10,11... | collective-permute-start | bytes 331784 | tf_op jit(solution)/shard_map/ppermute | solution.py:319
  317.5 31.1 %collective-permute-start.53 = (bf16[3,96,192]{2,1,0:T(8,128)(2,1)S(1)}, bf16[3,96,192]{2,1,0:T(8,128)(2,1)S(1)}, u32[]{:S(2)}, u32[]{:S(2)}) collective-permute-start(bf16[3,96,192]{2,1,0:T(8,128)(2,1)S(1)} %get-tuple-element.367), channel_id=1, source_target_pairs={{0,2},{1,3},{2,0},{3,1},{4,6},{5,7},{6,4},{7,5},{8,10},{9,11},{10,... | collective-permute-start | bytes 331784 | tf_op jit(solution)/shard_map/ppermute | solution.py:319
  (72 other events, 693.3 us)

commit v7 on v6

--- a/solution.py
+++ b/solution.py
@@ -347,6 +347,7 @@
         ]
         self.result = [[([0], part)] for part in parts]
         self.step = 0
+        self.early = []
 
     def advance(self, order):
         held = self.result
@@ -363,15 +364,22 @@
                 for mask, block, bit in zip(masks, blocks, bits)
             ]
         else:
-            arrays = order(*[array for pieces in held for _, array in pieces])
-            arrays = iter(arrays)
+            rest = [pieces[1:] if self.early else pieces for pieces in held]
+            arrays = iter(order(*[array for pieces in rest for _, array in pieces]))
             self.result = []
-            for pieces in held:
+            for n, pieces in enumerate(rest):
                 kept = [(masks, next(arrays)) for masks, _ in pieces]
-                self.result.append(
-                    kept + [([m ^ 1 for m in masks], swap(array, "dp", 1)) for masks, array in kept]
-                )
+                ours = held[n][:1] + kept if self.early else kept
+                theirs = [([m ^ 1 for m in masks], swap(array, "dp", 1)) for masks, array in kept]
+                self.result.append(ours + self.early[n : n + 1] + theirs)
         self.step += 1
+
+    def send_early(self, order):
+        arrays = order(*[pieces[0][1] for pieces in self.result])
+        self.early = [
+            ([m ^ 1 for m in pieces[0][0]], swap(array, "dp", 1))
+            for pieces, array in zip(self.result, arrays)
+        ]
 
 
 def canonical_row(me, rank, block, mask, rank_mask, stride, offset):
@@ -1173,22 +1181,21 @@
             carried,
         )
     )
-    key_own, value_own, queries, *state = attend([order(first_norm)], (0,), None)
+    key_own, key_near, value_own, value_near, queries, *state = attend(
+        list(order(first_norm, near)), (0, 1), None
+    )
     second_right, second_left = order(second_right, second_left)
     second = order(jnp.where(upper, second_right, second_left))
     third = along(second, [(1, 0), (2, 3)])
     if aligned:
         while feed_gather.step < len(feed_gather.bits):
             feed_gather.advance(order)
-    near, second = order(near, second)
-    key_near, key_second, value_near, value_second, *state = attend(
-        [near, second], (1, 2), (queries, *state)
-    )
+        feed_gather.send_early(order)
+    key_second, value_second, *state = attend([order(second)], (2,), (queries, *state))
     last = order(jnp.where(middle, hop_left, order(third)))
+    key_last, value_last, mixed, logs = attend([order(last)], (3,), (queries, *state))
     if aligned:
         feed_gather.advance(order)
-    key_last, value_last, mixed, logs = attend([order(last)], (3,), (queries, *state))
-    if aligned:
         layout = lambda masks, shift: [
             (0, block, 0, masks[0], D, 0),
             (block, block, 1, masks[0], D, 0),
@@ -1289,10 +1296,9 @@
     small.advance(order)
     qkv.advance(order)
     small.advance(order)
-    feed.advance(order)
     total = small.finish(order)
+    up_grad, down_grad, out_grad = feed.finish(order)
     qkv_grad = qkv.finish(order)
-    up_grad, down_grad, out_grad = feed.finish(order)
     fixed = 16
     chosen = (timesteps[None, :] == jnp.arange(time_table.shape[0])[:, None]).astype(full)
     table_grad = lax.dot_general(

time: 356 us -> 359 us (level)
  the two profiles are of different devices: /device:TPU:17 before, /device:TPU:0 now
where the time goes in v7:
time: 359 us; the launch traced here: 352 us
  Pallas kernels  178 us (50%)
  starting transfers between devices  66.7 us (19%)
  waiting for transfers between devices  56.1 us (16%)
  other arithmetic  22.3 us (6%)
  local copies, waits for them, and re-layouts  20.4 us (6%)
  between operations  5.35 us (1%)
    pallas_call x4, Pallas kernels, attend_backward(): pl.pallas_call(functools.partial(backward_kernel, number, first, last, fo...  66.7 us
    pallas_call x3, Pallas kernels, attend_forward(): pl.pallas_call(functools.partial(forward_kernel, numbers, first, final),...  46.5 us
    ppermute x43, starting transfers between devices, swap(): return lax.ppermute(value, axis, [(i, i ^ bit) for i in range(count)])  44.6 us
    ppermute x43, waiting for transfers between devices, swap(): return lax.ppermute(value, axis, [(i, i ^ bit) for i in range(count)])  37.4 us
    pallas_call x1, Pallas kernels, middle_call(): pl.pallas_call(functools.partial(middle_kernel, plan, block, len(arrays))...  35.7 us
    ppermute x12, starting transfers between devices, shards(): along = lambda value, pairs: lax.ppermute(value, 'mp', pairs)  22.1 us
    ppermute x12, waiting for transfers between devices, shards(): along = lambda value, pairs: lax.ppermute(value, 'mp', pairs)  18.7 us
    pallas_call x1, Pallas kernels, qkv_grads(): pl.pallas_call(functools.partial(qkv_grad_kernel, count), out_shape=[jax....  13.1 us
  transfers between devices with their start and end apart: 55, of which 21 were waited for; matrix products, arithmetic and copies ran while one was open for 9% of the time, Pallas kernels for 40%

profile of v7, /device:TPU:0, one launch (start us, length us, event | category | flops | bytes accessed | tf_op | source)
XLA Modules:
  0.0 352.2 jit_solution(5380510465738686752)
XLA Ops:
  2.6 3.1 collective-permute-start
  11.6 3.1 collective-permute-start.2
  23.1 3.2 collective-permute-done.2
  30.7 3.2 collective-permute-start.3
  38.6 6.4 %collective-permute-done.8.refs_1_ = bf16[288,768]{1,0:T(8,128)(2,1)S(1)} collective-permute-done((bf16[288,768]{1,0:T(8,128)(2,1)S(1)}, bf16[288,768]{1,0:T(8,128)(2,1)S(1)}, u32[]{:S(2)}, u32[]{:S(2)}) %collective-permute-start.8) | collective-permute-done | bytes 442400 | tf_op jit(solution)/shard_map/ppermute | solution.py:319
  48.5 7.8 %collective-permute-done.4 = bf16[512,768]{1,0:T(8,128)(2,1)S(1)} collective-permute-done((bf16[512,768]{1,0:T(8,128)(2,1)S(1)}, bf16[512,768]{1,0:T(8,128)(2,1)S(1)}, u32[]{:S(2)}, u32[]{:S(2)}) %collective-permute-start.4) | collective-permute-done | bytes 786464 | tf_op jit(solution)/shard_map/ppermute | solution.py:1080
  60.9 4.1 %place.1 = (bf16[768,768]{1,0:T(8,128)(2,1)}, bf16[768,1536]{1,0:T(8,128)(2,1)}) custom-call(bf16[288,768]{1,0:T(8,128)(2,1)} %copy-done.12, bf16[288,768]{1,0:T(8,128)(2,1)} %copy-done.22, bf16[288,768]{1,0:T(8,128)(2,1)} %copy-done.24, bf16[288,768]{1,0:T(8,128)(2,1)} %copy-done.25, bf16[288,768]{1,0:T(8,128)(2,1)} %copy-done.11, ...), custom_call_target="tpu_custom_call" | custom-call | flops 1048576 | bytes 65536 | tf_op jit(solution)/shard_map/place/pallas_call | solution.py:434
  69.3 20.2 %attend_forward.3 = (bf16[512,768]{1,0:T(8,128)(2,1)}, bf16[512,768]{1,0:T(8,128)(2,1)}, bf16[512,768]{1,0:T(8,128)(2,1)}, bf16[512,768]{1,0:T(8,128)(2,1)}, bf1...) custom-call(s32[6]{0:T(128)} %stack.42.scalars.refs_0_, ...), custom_call_target="tpu_custom_call" | custom-call | flops 1048576 | bytes 65536 | tf_op jit(solution)/shard_map/attend_forward/pallas_call | solution.py:129
  97.7 13.2 %attend_forward.4 = (bf16[512,768]{1,0:T(8,128)(2,1)}, bf16[512,768]{1,0:T(8,128)(2,1)}, f32[512,768]{1,0:T(8,128)}, f32[512,768]{1,0:T(8,128)}, f32[512,768]{1,0:T(8,128)}) custom-call(s32[6]{0:T(128)} %stack.42.scalars.refs_0_, bf16[512,768]{1,0:T(8,128)(2,1)} %copy-done.1, bf16[768,1536]{1,0:T(8,128)(2,1)} %get-tuple-element.225.refs_2_.refs_3_.refs_1_.wk_ref.wv_ref, ...), custom_call_target="tpu_custom_call" | custom-call | flops 1048576 | bytes 65536 | tf_op jit(solution)/shard_map/attend_forward/pallas_call | solution.py:129
  110.9 7.6 %collective-permute-done.17 = bf16[512,768]{1,0:T(8,128)(2,1)S(1)} collective-permute-done((bf16[512,768]{1,0:T(8,128)(2,1)S(1)}, bf16[512,768]{1,0:T(8,128)(2,1)S(1)}, u32[]{:S(2)}, u32[]{:S(2)}) %collective-permute-start.17) | collective-permute-done | bytes 786464 | tf_op jit(solution)/shard_map/ppermute | solution.py:1080
  119.5 13.1 %attend_forward.5 = (bf16[512,768]{1,0:T(8,128)(2,1)}, bf16[512,768]{1,0:T(8,128)(2,1)}, f32[512,768]{1,0:T(8,128)}, f32[512,768]{1,0:T(8,128)}) custom-call(s32[6]{0:T(128)} %stack.42.scalars.refs_0_, bf16[512,768]{1,0:T(8,128)(2,1)} %broadcast_select_fusion.2.refs_0_.refs_3_, bf16[768,1536]{1,0:T(8,128)(2,1)} %get-tuple-element.225.refs_2_.refs_3_.refs_1_.wk_ref.wv_ref, ...), custom_call_target="tpu_custom_call" | custom-call | flops 1048576 | bytes 65536 | tf_op jit(solution)/shard_map/attend_forward/pallas_call | solution.py:129
  139.0 35.7 %middle.1 = (bf16[512,768]{1,0:T(8,128)(2,1)}, f32[512,768]{1,0:T(8,128)}, bf16[512,768]{1,0:T(8,128)(2,1)}, bf16[4,4,96,768]{3,2,1,0:T(8,128)(2,1)}, bf16[4,4,9...) custom-call(s32[6]{0:T(128)} %stack.42.scalars.refs_0_, ...), custom_call_target="tpu_custom_call" | custom-call | flops 1048576 | bytes 65536 | tf_op jit(solution)/shard_map/middle/pallas_call | solution.py:669
  175.3 14.3 %attend_backward.4 = (f32[512,768]{1,0:T(8,128)}, bf16[512,768]{1,0:T(8,128)(2,1)}, bf16[512,768]{1,0:T(8,128)(2,1)}, bf16[512,768]{1,0:T(8,128)(2,1)}) custom-call(s32[6]{0:T(128)} %stack.42.scalars.refs_0_, bf16[512,768]{1,0:T(8,128)(2,1)} %get-tuple-element.243.refs_4_.q_ref, bf16[512,768]{1,0:T(8,128)(2,1)} %get-tuple-element.274.k_ref, ...), custom_call_target="tpu_custom_call" | custom-call | flops 1048576 | bytes 65536 | tf_op jit(solution)/shard_map/attend_backward/pallas_call | solution.py:266
  193.3 17.8 %attend_backward.5 = (f32[512,768]{1,0:T(8,128)}, bf16[512,768]{1,0:T(8,128)(2,1)}, bf16[512,768]{1,0:T(8,128)(2,1)}, f32[512,768]{1,0:T(8,128)}, bf16[4,2,96,76...) custom-call(s32[6]{0:T(128)} %stack.42.scalars.refs_0_, ...), custom_call_target="tpu_custom_call" | custom-call | flops 1048576 | bytes 65536 | tf_op jit(solution)/shard_map/attend_backward/pallas_call | solution.py:266
  218.5 14.6 %attend_backward.6 = (f32[512,768]{1,0:T(8,128)}, bf16[512,768]{1,0:T(8,128)(2,1)}, bf16[512,768]{1,0:T(8,128)(2,1)}, f32[512,768]{1,0:T(8,128)}) custom-call(s32[6]{0:T(128)} %stack.42.scalars.refs_0_, bf16[512,768]{1,0:T(8,128)(2,1)} %get-tuple-element.243.refs_4_.q_ref, bf16[512,768]{1,0:T(8,128)(2,1)} %get-tuple-element.240.k_ref, ...), custom_call_target="tpu_custom_call" | custom-call | flops 1048576 | bytes 65536 | tf_op jit(solution)/shard_map/attend_backward/pallas_call | solution.py:266
  235.5 5.1 %collective-permute-start.33 = (bf16[512,768]{1,0:T(8,128)(2,1)S(1)}, bf16[512,768]{1,0:T(8,128)(2,1)S(1)}, u32[]{:S(2)}, u32[]{:S(2)}) collective-permute-start(bf16[512,768]{1,0:T(8,128)(2,1)S(1)} %select_convert_fusion), channel_id=1, source_target_pairs={{0,1},{1,2},{2,3},{4,5},{5,6},{6,7},{8,9},{9,10},{10,11},{12,13},{... | collective-permute-start | bytes 2359304 | tf_op jit(solution)/shard_map/ppermute | solution.py:1080
  246.8 19.9 %attend_backward.7 = (bf16[512,768]{1,0:T(8,128)(2,1)}, bf16[512,768]{1,0:T(8,128)(2,1)}, bf16[512,768]{1,0:T(8,128)(2,1)}, f32[512,768]{1,0:T(8,128)}, bf16[4,1...) custom-call(s32[6]{0:T(128)} %stack.42.scalars.refs_0_, ...), custom_call_target="tpu_custom_call" | custom-call | flops 1048576 | bytes 65536 | tf_op jit(solution)/shard_map/attend_backward/pallas_call | solution.py:266
  269.9 13.1 %qkv_grads.1 = (bf16[3,4,96,384]{3,2,1,0:T(8,128)(2,1)}, bf16[3,4,96,384]{3,2,1,0:T(8,128)(2,1)}, bf16[3,4,96,384]{3,2,1,0:T(8,128)(2,1)}, bf16[3,4,96,384]{3,2,1,0:T(8,128)(2,1)}, f32[16,768]{1,0:T(8,128)}) custom-call(bf16[512,768]{1,0:T(8,128)(2,1)} %copy-done.2, bf16[512,768]{1,0:T(8,128)(2,1)} %broadcast_select_fusion.refs_1_, ...), custom_call_target="tpu_custom_call" | custom-call | flops 1048576 | bytes 65536 | tf_op jit(solution)/shard_map/qkv_grads/pallas_call | solution.py:819
  289.2 3.9 %fold.2 = (bf16[3,2,96,384]{3,2,1,0:T(8,128)(2,1)}, bf16[3,2,96,384]{3,2,1,0:T(8,128)(2,1)}, bf16[3,2,96,384]{3,2,1,0:T(8,128)(2,1)}, bf16[3,2,96,384]{3,2,1,0:T(8,128)(2,1)}) custom-call(bf16[3,4,96,384]{3,2,1,0:T(8,128)(2,1)} %get-tuple-element.326.refs_0_, bf16[3,4,96,384]{3,2,1,0:T(8,128)(2,1)} %collective-permute-done.35.refs_1_, ...), custom_call_target="tpu_custom_call" | custom-call | bytes 16777216 | tf_op jit(solution)/shard_map/fold/pallas_call | solution.py:747
  296.2 5.2 %last_norm.1 = (f32[512,768]{1,0:T(8,128)}, f32[24,768]{1,0:T(8,128)}) custom-call(bf16[512,768]{1,0:T(8,128)(2,1)} %token_ref, f32[512,768]{1,0:T(8,128)} %get-tuple-element.344.first_ref, bf16[512,768]{1,0:T(8,128)(2,1)} %copy-done.18, bf16[512,768]{1,0:T(8,128)(2,1)} %copy-done.19, f32[512,768]{1,0:T(8,128)} %get-tuple-element.345.middle_ref, ...), custom_call_target="tpu_custom_call" | custom-call | flops 1048576 | bytes 65536 | tf_op jit(solution)/shard_map/last_norm/pallas_call | solution.py:879
  301.3 3.8 %collective-permute-done.39 = bf16[2,216,768]{2,1,0:T(8,128)(2,1)} collective-permute-done((bf16[2,216,768]{2,1,0:T(8,128)(2,1)S(1)}, bf16[2,216,768]{2,1,0:T(8,128)(2,1)}, u32[]{:S(2)}, u32[]{:S(2)}) %collective-permute-start.39) | collective-permute-done | bytes 663584 | tf_op jit(solution)/shard_map/ppermute | solution.py:319
  307.5 3.2 fold.3
  325.3 4.4 %collective-permute-start.49 = (f32[24,768]{1,0:T(8,128)S(1)}, f32[24,768]{1,0:T(8,128)}, u32[]{:S(2)}, u32[]{:S(2)}) collective-permute-start(f32[24,768]{1,0:T(8,128)S(1)} %add_add_fusion.1), channel_id=1, source_target_pairs={{0,2},{1,3},{2,0},{3,1},{4,6},{5,7},{6,4},{7,5},{8,10},{9,11},{10,... | collective-permute-start | bytes 221192 | tf_op jit(solution)/shard_map/ppermute | solution.py:319
  334.1 5.6 %collective-permute-done.49 = f32[24,768]{1,0:T(8,128)} collective-permute-done((f32[24,768]{1,0:T(8,128)S(1)}, f32[24,768]{1,0:T(8,128)}, u32[]{:S(2)}, u32[]{:S(2)}) %collective-permute-start.49) | collective-permute-done | bytes 73760 | tf_op jit(solution)/shard_map/ppermute | solution.py:319
  (247 shorter events, 115.2 us)
Async XLA Ops:
  30.7 17.8 %collective-permute-start.3 = (bf16[512,768]{1,0:T(8,128)(2,1)S(1)}, bf16[512,768]{1,0:T(8,128)(2,1)S(1)}, u32[]{:S(2)}, u32[]{:S(2)}) collective-permute-start(bf16[512,768]{1,0:T(8,128)(2,1)S(1)} %add_convert_fusion.2.refs_0_), channel_id=1, source_target_pairs={{0,1},{1,2},{2,3},{4,5},{5,6},{6,7},{8,9},{9,10},{10,11},{12,13},{... | collective-permute-start | bytes 2359304 | tf_op jit(solution)/shard_map/ppermute | solution.py:1080
  34.0 22.4 %collective-permute-start.4 = (bf16[512,768]{1,0:T(8,128)(2,1)S(1)}, bf16[512,768]{1,0:T(8,128)(2,1)S(1)}, u32[]{:S(2)}, u32[]{:S(2)}) collective-permute-start(bf16[512,768]{1,0:T(8,128)(2,1)S(1)} %add_convert_fusion.2.refs_0_), channel_id=1, source_target_pairs={{1,0},{2,1},{3,2},{5,4},{6,5},{7,6},{9,8},{10,9},{11,10},{13,12},{... | collective-permute-start | bytes 2359304 | tf_op jit(solution)/shard_map/ppermute | solution.py:1080
  37.3 28.2 %collective-permute-start.12 = (bf16[384,768]{1,0:T(8,128)(2,1)}, bf16[384,768]{1,0:T(8,128)(2,1)}, u32[]{:S(2)}, u32[]{:S(2)}) collective-permute-start(bf16[384,768]{1,0:T(8,128)(2,1)} %collective-permute-done.7), channel_id=1, source_target_pairs={{1,0},{2,3},{5,4},{6,7},{9,8},{10,11},{13,12},{14,15},{17,16},{18,... | collective-permute-start | bytes 1769480 | tf_op jit(solution)/shard_map/ppermute | solution.py:1080
  56.4 33.1 %collective-permute-start.10 = (bf16[512,768]{1,0:T(8,128)(2,1)S(1)}, bf16[512,768]{1,0:T(8,128)(2,1)}, u32[]{:S(2)}, u32[]{:S(2)}) collective-permute-start(bf16[512,768]{1,0:T(8,128)(2,1)S(1)} %collective-permute-done.3), channel_id=1, source_target_pairs={{1,2},{2,3},{5,6},{6,7},{9,10},{10,11},{13,14},{14,15},{17,18},{18... | collective-permute-start | bytes 2359304 | tf_op jit(solution)/shard_map/ppermute | solution.py:1080
  58.0 31.5 %collective-permute-start.11 = (bf16[512,768]{1,0:T(8,128)(2,1)S(1)}, bf16[512,768]{1,0:T(8,128)(2,1)}, u32[]{:S(2)}, u32[]{:S(2)}) collective-permute-start(bf16[512,768]{1,0:T(8,128)(2,1)S(1)} %collective-permute-done.4), channel_id=1, source_target_pairs={{1,0},{2,1},{5,4},{6,5},{9,8},{10,9},{13,12},{14,13},{17,16},{18,1... | collective-permute-start | bytes 2359304 | tf_op jit(solution)/shard_map/ppermute | solution.py:1080
  66.6 24.1 %collective-permute-start.19 = (bf16[432,768]{1,0:T(8,128)(2,1)S(1)}, bf16[432,768]{1,0:T(8,128)(2,1)S(1)}, u32[]{:S(2)}, u32[]{:S(2)}) collective-permute-start(bf16[432,768]{1,0:T(8,128)(2,1)S(1)} %fusion.6), channel_id=1, source_target_pairs={{0,16},{4,20},{8,24},{12,28},{16,0},{20,4},{24,8},{28,12},{1,17},{... | collective-permute-start | bytes 1990664 | tf_op jit(solution)/shard_map/ppermute | solution.py:319
  67.8 23.1 %collective-permute-start.18 = (bf16[432,768]{1,0:T(8,128)(2,1)S(1)}, bf16[432,768]{1,0:T(8,128)(2,1)}, u32[]{:S(2)}, u32[]{:S(2)}) collective-permute-start(bf16[432,768]{1,0:T(8,128)(2,1)S(1)} %pad_maximum_fusion.4), channel_id=1, source_target_pairs={{0,8},{4,12},{8,0},{12,4},{16,24},{20,28},{24,16},{28,20},{1,9},{5... | collective-permute-start | bytes 1990664 | tf_op jit(solution)/shard_map/ppermute | solution.py:319
  92.6 40.0 %collective-permute-start.20 = (bf16[864,768]{1,0:T(8,128)(2,1)S(1)}, bf16[864,768]{1,0:T(8,128)(2,1)}, u32[]{:S(2)}, u32[]{:S(2)}) collective-permute-start(bf16[864,768]{1,0:T(8,128)(2,1)S(1)} %pad_maximum_fusion.1.refs_7_), channel_id=1, source_target_pairs={{0,16},{4,20},{8,24},{12,28},{16,0},{20,4},{24,8},{28,12},{1,17},{... | collective-permute-start | bytes 3981320 | tf_op jit(solution)/shard_map/ppermute | solution.py:319
  94.2 38.5 %collective-permute-start.21 = (bf16[864,768]{1,0:T(8,128)(2,1)S(1)}, bf16[864,768]{1,0:T(8,128)(2,1)}, u32[]{:S(2)}, u32[]{:S(2)}) collective-permute-start(bf16[864,768]{1,0:T(8,128)(2,1)S(1)} %pad_maximum_fusion.2.refs_11_), channel_id=1, source_target_pairs={{0,8},{4,12},{8,0},{12,4},{16,24},{20,28},{24,16},{28,20},{1,9},{5... | collective-permute-start | bytes 3981320 | tf_op jit(solution)/shard_map/ppermute | solution.py:319
  95.7 22.8 %collective-permute-start.17 = (bf16[512,768]{1,0:T(8,128)(2,1)S(1)}, bf16[512,768]{1,0:T(8,128)(2,1)S(1)}, u32[]{:S(2)}, u32[]{:S(2)}) collective-permute-start(bf16[512,768]{1,0:T(8,128)(2,1)S(1)} %broadcast_select_fusion.1.refs_0_.refs_2_), channel_id=1, source_target_pairs={{1,0},{2,3},{5,4},{6,7},{9,8},{10,11},{13,12},{14,15},{17,16},{18,... | collective-permute-start | bytes 2359304 | tf_op jit(solution)/shard_map/ppermute | solution.py:1080
  97.1 36.1 %collective-permute-start.22 = (bf16[864,768]{1,0:T(8,128)(2,1)S(1)}, bf16[864,768]{1,0:T(8,128)(2,1)}, u32[]{:S(2)}, u32[]{:S(2)}) collective-permute-start(bf16[864,768]{1,0:T(8,128)(2,1)S(1)} %pad_maximum_fusion.1.refs_7_), channel_id=1, source_target_pairs={{0,4},{4,0},{8,12},{12,8},{16,20},{20,16},{24,28},{28,24},{1,5},{5... | collective-permute-start | bytes 3981320 | tf_op jit(solution)/shard_map/ppermute | solution.py:319
  97.2 36.0 %collective-permute-start.24 = (bf16[864,768]{1,0:T(8,128)(2,1)S(1)}, bf16[864,768]{1,0:T(8,128)(2,1)}, u32[]{:S(2)}, u32[]{:S(2)}) collective-permute-start(bf16[864,768]{1,0:T(8,128)(2,1)S(1)} %pad_maximum_fusion.2.refs_11_), channel_id=1, source_target_pairs={{0,4},{4,0},{8,12},{12,8},{16,20},{20,16},{24,28},{28,24},{1,5},{5... | collective-permute-start | bytes 3981320 | tf_op jit(solution)/shard_map/ppermute | solution.py:319
  174.7 16.4 %collective-permute-start.27 = (bf16[5,4,96,768]{3,2,1,0:T(8,128)(2,1)}, bf16[5,4,96,768]{3,2,1,0:T(8,128)(2,1)S(1)}, u32[]{:S(2)}, u32[]{:S(2)}) collective-permute-start(bf16[5,4,96,768]{3,2,1,0:T(8,128)(2,1)} %get-tuple-element.283), channel_id=1, source_target_pairs={{0,4},{4,0},{8,12},{12,8},{16,20},{20,16},{24,28},{28,24},{1,5},{5... | collective-permute-start | bytes 8847368 | tf_op jit(solution)/shard_map/ppermute | solution.py:319
  189.5 23.2 %collective-permute-start.28 = (bf16[512,768]{1,0:T(8,128)(2,1)}, bf16[512,768]{1,0:T(8,128)(2,1)S(1)}, u32[]{:S(2)}, u32[]{:S(2)}) collective-permute-start(bf16[512,768]{1,0:T(8,128)(2,1)} %get-tuple-element.288), channel_id=1, source_target_pairs={{0,1},{3,2},{4,5},{7,6},{8,9},{11,10},{12,13},{15,14},{16,17},{19,... | collective-permute-start | bytes 2359304 | tf_op jit(solution)/shard_map/ppermute | solution.py:1080
  211.2 34.4 %collective-permute-start.32 = (bf16[5,2,96,768]{3,2,1,0:T(8,128)(2,1)}, bf16[5,2,96,768]{3,2,1,0:T(8,128)(2,1)S(1)}, u32[]{:S(2)}, u32[]{:S(2)}) collective-permute-start(bf16[5,2,96,768]{3,2,1,0:T(8,128)(2,1)} %get-tuple-element.298), channel_id=1, source_target_pairs={{0,8},{4,12},{8,0},{12,4},{16,24},{20,28},{24,16},{28,20},{1,9},{5... | collective-permute-start | bytes 4423688 | tf_op jit(solution)/shard_map/ppermute | solution.py:319
  214.3 18.8 %collective-permute-start.30 = (bf16[512,768]{1,0:T(8,128)(2,1)S(1)}, bf16[512,768]{1,0:T(8,128)(2,1)S(1)}, u32[]{:S(2)}, u32[]{:S(2)}) collective-permute-start(bf16[512,768]{1,0:T(8,128)(2,1)S(1)} %add_convert_fusion.1), channel_id=1, source_target_pairs={{3,2},{2,1},{7,6},{6,5},{11,10},{10,9},{15,14},{14,13},{19,18},{18... | collective-permute-start | bytes 2359304 | tf_op jit(solution)/shard_map/ppermute | solution.py:1080
  215.0 27.9 %collective-permute-start.31 = (bf16[4,2,96,768]{3,2,1,0:T(8,128)(2,1)}, bf16[4,2,96,768]{3,2,1,0:T(8,128)(2,1)S(1)}, u32[]{:S(2)}, u32[]{:S(2)}) collective-permute-start(bf16[4,2,96,768]{3,2,1,0:T(8,128)(2,1)} %get-tuple-element.297), channel_id=1, source_target_pairs={{0,16},{4,20},{8,24},{12,28},{16,0},{20,4},{24,8},{28,12},{1,17},{... | collective-permute-start | bytes 3538952 | tf_op jit(solution)/shard_map/ppermute | solution.py:319
  216.6 18.4 %collective-permute-start.29 = (bf16[512,768]{1,0:T(8,128)(2,1)S(1)}, bf16[512,768]{1,0:T(8,128)(2,1)S(1)}, u32[]{:S(2)}, u32[]{:S(2)}) collective-permute-start(bf16[512,768]{1,0:T(8,128)(2,1)S(1)} %add_convert_fusion.1), channel_id=1, source_target_pairs={{0,1},{1,2},{4,5},{5,6},{8,9},{9,10},{12,13},{13,14},{16,17},{17,1... | collective-permute-start | bytes 2359304 | tf_op jit(solution)/shard_map/ppermute | solution.py:1080
  235.5 34.3 %collective-permute-start.33 = (bf16[512,768]{1,0:T(8,128)(2,1)S(1)}, bf16[512,768]{1,0:T(8,128)(2,1)S(1)}, u32[]{:S(2)}, u32[]{:S(2)}) collective-permute-start(bf16[512,768]{1,0:T(8,128)(2,1)S(1)} %select_convert_fusion), channel_id=1, source_target_pairs={{0,1},{1,2},{2,3},{4,5},{5,6},{6,7},{8,9},{9,10},{10,11},{12,13},{... | collective-permute-start | bytes 2359304 | tf_op jit(solution)/shard_map/ppermute | solution.py:1080
  240.7 29.2 %collective-permute-start.34 = (bf16[512,768]{1,0:T(8,128)(2,1)S(1)}, bf16[512,768]{1,0:T(8,128)(2,1)S(1)}, u32[]{:S(2)}, u32[]{:S(2)}) collective-permute-start(bf16[512,768]{1,0:T(8,128)(2,1)S(1)} %add_convert_fusion), channel_id=1, source_target_pairs={{3,2},{2,1},{1,0},{7,6},{6,5},{5,4},{11,10},{10,9},{9,8},{15,14},{... | collective-permute-start | bytes 2359304 | tf_op jit(solution)/shard_map/ppermute | solution.py:1080
  266.8 17.9 %collective-permute-start.38 = (bf16[5,1,96,768]{3,2,1,0:T(8,128)(2,1)}, bf16[5,1,96,768]{3,2,1,0:T(8,128)(2,1)}, u32[]{:S(2)}, u32[]{:S(2)}) collective-permute-start(bf16[5,1,96,768]{3,2,1,0:T(8,128)(2,1)} %get-tuple-element.316), channel_id=1, source_target_pairs={{0,16},{4,20},{8,24},{12,28},{16,0},{20,4},{24,8},{28,12},{1,17},{... | collective-permute-start | bytes 2211848 | tf_op jit(solution)/shard_map/ppermute | solution.py:319
  313.0 29.6 %collective-permute-start.54 = (bf16[216,768]{1,0:T(8,128)(2,1)S(1)}, bf16[216,768]{1,0:T(8,128)(2,1)S(1)}, u32[]{:S(2)}, u32[]{:S(2)}) collective-permute-start(bf16[216,768]{1,0:T(8,128)(2,1)S(1)} %fusion.8), channel_id=1, source_target_pairs={{0,2},{1,3},{2,0},{3,1},{4,6},{5,7},{6,4},{7,5},{8,10},{9,11},{10,... | collective-permute-start | bytes 995336 | tf_op jit(solution)/shard_map/ppermute | solution.py:319
  329.7 19.8 %collective-permute-start.51 = (bf16[3,96,192]{2,1,0:T(8,128)(2,1)}, bf16[3,96,192]{2,1,0:T(8,128)(2,1)S(1)}, u32[]{:S(2)}, u32[]{:S(2)}) collective-permute-start(bf16[3,96,192]{2,1,0:T(8,128)(2,1)} %get-tuple-element.366), channel_id=1, source_target_pairs={{0,1},{1,0},{2,3},{3,2},{4,5},{5,4},{6,7},{7,6},{8,9},{9,8},{10,11... | collective-permute-start | bytes 331784 | tf_op jit(solution)/shard_map/ppermute | solution.py:319
  333.1 16.4 %collective-permute-start.52 = (bf16[3,96,192]{2,1,0:T(8,128)(2,1)}, bf16[3,96,192]{2,1,0:T(8,128)(2,1)S(1)}, u32[]{:S(2)}, u32[]{:S(2)}) collective-permute-start(bf16[3,96,192]{2,1,0:T(8,128)(2,1)} %get-tuple-element.367), channel_id=1, source_target_pairs={{0,2},{1,3},{2,0},{3,1},{4,6},{5,7},{6,4},{7,5},{8,10},{9,11},{10,... | collective-permute-start | bytes 331784 | tf_op jit(solution)/shard_map/ppermute | solution.py:319
  (70 other events, 626.2 us)

commit v8 on v7

--- a/solution.py
+++ b/solution.py
@@ -1181,9 +1181,7 @@
             carried,
         )
     )
-    key_own, key_near, value_own, value_near, queries, *state = attend(
-        list(order(first_norm, near)), (0, 1), None
-    )
+    key_own, value_own, queries, *state = attend([order(first_norm)], (0,), None)
     second_right, second_left = order(second_right, second_left)
     second = order(jnp.where(upper, second_right, second_left))
     third = along(second, [(1, 0), (2, 3)])
@@ -1191,7 +1189,10 @@
         while feed_gather.step < len(feed_gather.bits):
             feed_gather.advance(order)
         feed_gather.send_early(order)
-    key_second, value_second, *state = attend([order(second)], (2,), (queries, *state))
+    near, second = order(near, second)
+    key_near, key_second, value_near, value_second, *state = attend(
+        [near, second], (1, 2), (queries, *state)
+    )
     last = order(jnp.where(middle, hop_left, order(third)))
     key_last, value_last, mixed, logs = attend([order(last)], (3,), (queries, *state))
     if aligned:

time: 359 us -> 356 us (level)
  waiting for transfers between devices: 56.1 us -> 48 us
  starting transfers between devices: 66.7 us -> 72.6 us
    ppermute x12, waiting for transfers between devices: 18.7 us -> 12.3 us  [shards(): along = lambda value, pairs: lax.ppermute(value, 'mp', pairs)]
    ppermute x12, starting transfers between devices: 22.1 us -> 27.6 us  [shards(): along = lambda value, pairs: lax.ppermute(value, 'mp', pairs)]
    unnamed x77 -> x81, local copies, waits for them, and re-layouts: 9.47 us -> 10.3 us
  transfers between devices with their start and end apart: 55 -> 55, of which waited for: 21 -> 20; matrix products, arithmetic and copies ran while one was open for 9% -> 9% of each run, Pallas kernels for 40% -> 40%
where the time goes in v8:
time: 356 us; the launch traced here: 349 us
  Pallas kernels  177 us (50%)
  starting transfers between devices  72.6 us (20%)
  waiting for transfers between devices  48 us (13%)
  other arithmetic  22.4 us (6%)
  local copies, waits for them, and re-layouts  21.2 us (6%)
  between operations  5.33 us (1%)
    pallas_call x4, Pallas kernels, attend_backward(): pl.pallas_call(functools.partial(backward_kernel, number, first, last, fo...  66.7 us
    pallas_call x3, Pallas kernels, attend_forward(): pl.pallas_call(functools.partial(forward_kernel, numbers, first, final),...  45.1 us
    ppermute x43, starting transfers between devices, swap(): return lax.ppermute(value, axis, [(i, i ^ bit) for i in range(count)])  45 us
    ppermute x43, waiting for transfers between devices, swap(): return lax.ppermute(value, axis, [(i, i ^ bit) for i in range(count)])  35.7 us
    pallas_call x1, Pallas kernels, middle_call(): pl.pallas_call(functools.partial(middle_kernel, plan, block, len(arrays))...  35.7 us
    ppermute x12, starting transfers between devices, shards(): along = lambda value, pairs: lax.ppermute(value, 'mp', pairs)  27.6 us
    pallas_call x1, Pallas kernels, qkv_grads(): pl.pallas_call(functools.partial(qkv_grad_kernel, count), out_shape=[jax....  13.1 us
    ppermute x12, waiting for transfers between devices, shards(): along = lambda value, pairs: lax.ppermute(value, 'mp', pairs)  12.3 us
  transfers between devices with their start and end apart: 55, of which 20 were waited for; matrix products, arithmetic and copies ran while one was open for 9% of the time, Pallas kernels for 40%

profile of v8, /device:TPU:0, one launch (start us, length us, event | category | flops | bytes accessed | tf_op | source)
XLA Modules:
  0.0 349.4 jit_solution(10900985932108670294)
XLA Ops:
  23.0 3.2 collective-permute-done.2
  30.7 3.2 collective-permute-start.3
  38.5 6.4 %collective-permute-done.8.refs_1_ = bf16[288,768]{1,0:T(8,128)(2,1)S(1)} collective-permute-done((bf16[288,768]{1,0:T(8,128)(2,1)S(1)}, bf16[288,768]{1,0:T(8,128)(2,1)S(1)}, u32[]{:S(2)}, u32[]{:S(2)}) %collective-permute-start.8) | collective-permute-done | bytes 442400 | tf_op jit(solution)/shard_map/ppermute | solution.py:319
  48.5 7.8 %collective-permute-done.4 = bf16[512,768]{1,0:T(8,128)(2,1)S(1)} collective-permute-done((bf16[512,768]{1,0:T(8,128)(2,1)S(1)}, bf16[512,768]{1,0:T(8,128)(2,1)S(1)}, u32[]{:S(2)}, u32[]{:S(2)}) %collective-permute-start.4) | collective-permute-done | bytes 786464 | tf_op jit(solution)/shard_map/ppermute | solution.py:1080
  61.6 4.1 %place.1 = (bf16[768,768]{1,0:T(8,128)(2,1)}, bf16[768,1536]{1,0:T(8,128)(2,1)}) custom-call(bf16[288,768]{1,0:T(8,128)(2,1)} %copy-done.12, bf16[288,768]{1,0:T(8,128)(2,1)} %copy-done.24, bf16[288,768]{1,0:T(8,128)(2,1)} %copy-done.26, bf16[288,768]{1,0:T(8,128)(2,1)} %copy-done.27, bf16[288,768]{1,0:T(8,128)(2,1)} %copy-done.11, ...), custom_call_target="tpu_custom_call" | custom-call | flops 1048576 | bytes 65536 | tf_op jit(solution)/shard_map/place/pallas_call | solution.py:434
  68.7 13.1 %attend_forward.3 = (bf16[512,768]{1,0:T(8,128)(2,1)}, bf16[512,768]{1,0:T(8,128)(2,1)}, bf16[512,768]{1,0:T(8,128)(2,1)}, f32[512,768]{1,0:T(8,128)}, f32[512,768]{1,0:T(8,128)}, /*index=5*/f32[512,768]{1,0:T(8,128)}) custom-call(s32[6]{0:T(128)} %stack.42.scalars.refs_0_, bf16[512,768]{1,0:T(8,128)(2,1)} %copy-done.1, ...), custom_call_target="tpu_custom_call" | custom-call | flops 1048576 | bytes 65536 | tf_op jit(solution)/shard_map/attend_forward/pallas_call | solution.py:129
  92.4 18.8 %attend_forward.4 = (bf16[512,768]{1,0:T(8,128)(2,1)}, bf16[512,768]{1,0:T(8,128)(2,1)}, bf16[512,768]{1,0:T(8,128)(2,1)}, bf16[512,768]{1,0:T(8,128)(2,1)}, f32...) custom-call(s32[6]{0:T(128)} %stack.42.scalars.refs_0_, ...), custom_call_target="tpu_custom_call" | custom-call | flops 1048576 | bytes 65536 | tf_op jit(solution)/shard_map/attend_forward/pallas_call | solution.py:129
  112.5 13.1 %attend_forward.5 = (bf16[512,768]{1,0:T(8,128)(2,1)}, bf16[512,768]{1,0:T(8,128)(2,1)}, f32[512,768]{1,0:T(8,128)}, f32[512,768]{1,0:T(8,128)}) custom-call(s32[6]{0:T(128)} %stack.42.scalars.refs_0_, bf16[512,768]{1,0:T(8,128)(2,1)} %broadcast_select_fusion.2.refs_0_.refs_3_, bf16[768,1536]{1,0:T(8,128)(2,1)} %get-tuple-element.225.refs_1_.refs_2_.refs_3_.wk_ref.wv_ref, ...), custom_call_target="tpu_custom_call" | custom-call | flops 1048576 | bytes 65536 | tf_op jit(solution)/shard_map/attend_forward/pallas_call | solution.py:129
  132.0 35.7 %middle.1 = (bf16[512,768]{1,0:T(8,128)(2,1)}, f32[512,768]{1,0:T(8,128)}, bf16[512,768]{1,0:T(8,128)(2,1)}, bf16[4,4,96,768]{3,2,1,0:T(8,128)(2,1)}, bf16[4,4,9...) custom-call(s32[6]{0:T(128)} %stack.42.scalars.refs_0_, ...), custom_call_target="tpu_custom_call" | custom-call | flops 1048576 | bytes 65536 | tf_op jit(solution)/shard_map/middle/pallas_call | solution.py:669
  168.3 14.2 %attend_backward.4 = (f32[512,768]{1,0:T(8,128)}, bf16[512,768]{1,0:T(8,128)(2,1)}, bf16[512,768]{1,0:T(8,128)(2,1)}, bf16[512,768]{1,0:T(8,128)(2,1)}) custom-call(s32[6]{0:T(128)} %stack.42.scalars.refs_0_, bf16[512,768]{1,0:T(8,128)(2,1)} %get-tuple-element.238.refs_5_.refs_4_.q_ref, bf16[512,768]{1,0:T(8,128)(2,1)} %get-tuple-element.274.k_ref, ...), custom_call_target="tpu_custom_call" | custom-call | flops 1048576 | bytes 65536 | tf_op jit(solution)/shard_map/attend_backward/pallas_call | solution.py:266
  182.5 6.7 %collective-permute-start.28 = (bf16[512,768]{1,0:T(8,128)(2,1)}, bf16[512,768]{1,0:T(8,128)(2,1)S(1)}, u32[]{:S(2)}, u32[]{:S(2)}) collective-permute-start(bf16[512,768]{1,0:T(8,128)(2,1)} %get-tuple-element.288), channel_id=1, source_target_pairs={{0,1},{3,2},{4,5},{7,6},{8,9},{11,10},{12,13},{15,14},{16,17},{19,... | collective-permute-start | bytes 2359304 | tf_op jit(solution)/shard_map/ppermute | solution.py:1080
  191.5 17.8 %attend_backward.5 = (f32[512,768]{1,0:T(8,128)}, bf16[512,768]{1,0:T(8,128)(2,1)}, bf16[512,768]{1,0:T(8,128)(2,1)}, f32[512,768]{1,0:T(8,128)}, bf16[4,2,96,76...) custom-call(s32[6]{0:T(128)} %stack.42.scalars.refs_0_, ...), custom_call_target="tpu_custom_call" | custom-call | flops 1048576 | bytes 65536 | tf_op jit(solution)/shard_map/attend_backward/pallas_call | solution.py:266
  216.0 14.9 %attend_backward.6 = (f32[512,768]{1,0:T(8,128)}, bf16[512,768]{1,0:T(8,128)(2,1)}, bf16[512,768]{1,0:T(8,128)(2,1)}, f32[512,768]{1,0:T(8,128)}) custom-call(s32[6]{0:T(128)} %stack.42.scalars.refs_0_, bf16[512,768]{1,0:T(8,128)(2,1)} %get-tuple-element.238.refs_5_.refs_4_.q_ref, bf16[512,768]{1,0:T(8,128)(2,1)} %get-tuple-element.258.k_ref, ...), custom_call_target="tpu_custom_call" | custom-call | flops 1048576 | bytes 65536 | tf_op jit(solution)/shard_map/attend_backward/pallas_call | solution.py:266
  233.2 5.5 %collective-permute-start.33 = (bf16[512,768]{1,0:T(8,128)(2,1)S(1)}, bf16[512,768]{1,0:T(8,128)(2,1)S(1)}, u32[]{:S(2)}, u32[]{:S(2)}) collective-permute-start(bf16[512,768]{1,0:T(8,128)(2,1)S(1)} %select_convert_fusion), channel_id=1, source_target_pairs={{0,1},{1,2},{2,3},{4,5},{5,6},{6,7},{8,9},{9,10},{10,11},{12,13},{... | collective-permute-start | bytes 2359304 | tf_op jit(solution)/shard_map/ppermute | solution.py:1080
  240.3 3.4 collective-permute-done.32.refs_5_
  244.8 19.7 %attend_backward.7 = (bf16[512,768]{1,0:T(8,128)(2,1)}, bf16[512,768]{1,0:T(8,128)(2,1)}, bf16[512,768]{1,0:T(8,128)(2,1)}, f32[512,768]{1,0:T(8,128)}, bf16[4,1...) custom-call(s32[6]{0:T(128)} %stack.42.scalars.refs_0_, ...), custom_call_target="tpu_custom_call" | custom-call | flops 1048576 | bytes 65536 | tf_op jit(solution)/shard_map/attend_backward/pallas_call | solution.py:266
  267.0 13.1 %qkv_grads.1 = (bf16[3,4,96,384]{3,2,1,0:T(8,128)(2,1)}, bf16[3,4,96,384]{3,2,1,0:T(8,128)(2,1)}, bf16[3,4,96,384]{3,2,1,0:T(8,128)(2,1)}, bf16[3,4,96,384]{3,2,1,0:T(8,128)(2,1)}, f32[16,768]{1,0:T(8,128)}) custom-call(bf16[512,768]{1,0:T(8,128)(2,1)} %copy-done.1, bf16[512,768]{1,0:T(8,128)(2,1)} %broadcast_select_fusion.refs_0_.refs_1_, ...), custom_call_target="tpu_custom_call" | custom-call | flops 1048576 | bytes 65536 | tf_op jit(solution)/shard_map/qkv_grads/pallas_call | solution.py:819
  286.8 3.9 %fold.2 = (bf16[3,2,96,384]{3,2,1,0:T(8,128)(2,1)}, bf16[3,2,96,384]{3,2,1,0:T(8,128)(2,1)}, bf16[3,2,96,384]{3,2,1,0:T(8,128)(2,1)}, bf16[3,2,96,384]{3,2,1,0:T(8,128)(2,1)}) custom-call(bf16[3,4,96,384]{3,2,1,0:T(8,128)(2,1)} %get-tuple-element.326.refs_0_, bf16[3,4,96,384]{3,2,1,0:T(8,128)(2,1)} %collective-permute-done.35.refs_1_, ...), custom_call_target="tpu_custom_call" | custom-call | bytes 16777216 | tf_op jit(solution)/shard_map/fold/pallas_call | solution.py:747
  293.1 5.2 %last_norm.1 = (f32[512,768]{1,0:T(8,128)}, f32[24,768]{1,0:T(8,128)}) custom-call(bf16[512,768]{1,0:T(8,128)(2,1)} %token_ref, f32[512,768]{1,0:T(8,128)} %get-tuple-element.344.first_ref, bf16[512,768]{1,0:T(8,128)(2,1)} %copy-done.20, bf16[512,768]{1,0:T(8,128)(2,1)} %copy-done.21, f32[512,768]{1,0:T(8,128)} %get-tuple-element.345.middle_ref, ...), custom_call_target="tpu_custom_call" | custom-call | flops 1048576 | bytes 65536 | tf_op jit(solution)/shard_map/last_norm/pallas_call | solution.py:879
  298.3 3.9 %collective-permute-done.39 = bf16[2,216,768]{2,1,0:T(8,128)(2,1)} collective-permute-done((bf16[2,216,768]{2,1,0:T(8,128)(2,1)S(1)}, bf16[2,216,768]{2,1,0:T(8,128)(2,1)}, u32[]{:S(2)}, u32[]{:S(2)}) %collective-permute-start.39) | collective-permute-done | bytes 663584 | tf_op jit(solution)/shard_map/ppermute | solution.py:319
  304.5 3.2 fold.3
  322.4 4.8 %collective-permute-start.49 = (f32[24,768]{1,0:T(8,128)S(1)}, f32[24,768]{1,0:T(8,128)}, u32[]{:S(2)}, u32[]{:S(2)}) collective-permute-start(f32[24,768]{1,0:T(8,128)S(1)} %add_add_fusion.1), channel_id=1, source_target_pairs={{0,2},{1,3},{2,0},{3,1},{4,6},{5,7},{6,4},{7,5},{8,10},{9,11},{10,... | collective-permute-start | bytes 221192 | tf_op jit(solution)/shard_map/ppermute | solution.py:319
  331.6 3.3 collective-permute-done.49
  334.9 4.8 %collective-permute-start.53 = (bf16[3,96,192]{2,1,0:T(8,128)(2,1)}, bf16[3,96,192]{2,1,0:T(8,128)(2,1)}, u32[]{:S(2)}, u32[]{:S(2)}) collective-permute-start(bf16[3,96,192]{2,1,0:T(8,128)(2,1)} %get-tuple-element.368), channel_id=1, source_target_pairs={{0,3},{1,2},{2,1},{3,0},{4,7},{5,6},{6,5},{7,4},{8,11},{9,10},{10,... | collective-permute-start | bytes 331784 | tf_op jit(solution)/shard_map/ppermute | solution.py:319
  (251 shorter events, 114.2 us)
Async XLA Ops:
  30.7 17.8 %collective-permute-start.3 = (bf16[512,768]{1,0:T(8,128)(2,1)S(1)}, bf16[512,768]{1,0:T(8,128)(2,1)S(1)}, u32[]{:S(2)}, u32[]{:S(2)}) collective-permute-start(bf16[512,768]{1,0:T(8,128)(2,1)S(1)} %add_convert_fusion.2.refs_0_), channel_id=1, source_target_pairs={{0,1},{1,2},{2,3},{4,5},{5,6},{6,7},{8,9},{9,10},{10,11},{12,13},{... | collective-permute-start | bytes 2359304 | tf_op jit(solution)/shard_map/ppermute | solution.py:1080
  34.0 22.4 %collective-permute-start.4 = (bf16[512,768]{1,0:T(8,128)(2,1)S(1)}, bf16[512,768]{1,0:T(8,128)(2,1)S(1)}, u32[]{:S(2)}, u32[]{:S(2)}) collective-permute-start(bf16[512,768]{1,0:T(8,128)(2,1)S(1)} %add_convert_fusion.2.refs_0_), channel_id=1, source_target_pairs={{1,0},{2,1},{3,2},{5,4},{6,5},{7,6},{9,8},{10,9},{11,10},{13,12},{... | collective-permute-start | bytes 2359304 | tf_op jit(solution)/shard_map/ppermute | solution.py:1080
  37.3 28.5 %collective-permute-start.12 = (bf16[384,768]{1,0:T(8,128)(2,1)}, bf16[384,768]{1,0:T(8,128)(2,1)}, u32[]{:S(2)}, u32[]{:S(2)}) collective-permute-start(bf16[384,768]{1,0:T(8,128)(2,1)} %collective-permute-done.7), channel_id=1, source_target_pairs={{1,0},{2,3},{5,4},{6,7},{9,8},{10,11},{13,12},{14,15},{17,16},{18,... | collective-permute-start | bytes 1769480 | tf_op jit(solution)/shard_map/ppermute | solution.py:1080
  56.4 25.4 %collective-permute-start.10 = (bf16[512,768]{1,0:T(8,128)(2,1)S(1)}, bf16[512,768]{1,0:T(8,128)(2,1)}, u32[]{:S(2)}, u32[]{:S(2)}) collective-permute-start(bf16[512,768]{1,0:T(8,128)(2,1)S(1)} %collective-permute-done.3), channel_id=1, source_target_pairs={{1,2},{2,3},{5,6},{6,7},{9,10},{10,11},{13,14},{14,15},{17,18},{18... | collective-permute-start | bytes 2359304 | tf_op jit(solution)/shard_map/ppermute | solution.py:1080
  58.7 24.4 %collective-permute-start.11 = (bf16[512,768]{1,0:T(8,128)(2,1)S(1)}, bf16[512,768]{1,0:T(8,128)(2,1)}, u32[]{:S(2)}, u32[]{:S(2)}) collective-permute-start(bf16[512,768]{1,0:T(8,128)(2,1)S(1)} %collective-permute-done.4), channel_id=1, source_target_pairs={{1,0},{2,1},{5,4},{6,5},{9,8},{10,9},{13,12},{14,13},{17,16},{18,1... | collective-permute-start | bytes 2359304 | tf_op jit(solution)/shard_map/ppermute | solution.py:1080
  67.0 17.4 %collective-permute-start.19 = (bf16[432,768]{1,0:T(8,128)(2,1)S(1)}, bf16[432,768]{1,0:T(8,128)(2,1)S(1)}, u32[]{:S(2)}, u32[]{:S(2)}) collective-permute-start(bf16[432,768]{1,0:T(8,128)(2,1)S(1)} %fusion.6), channel_id=1, source_target_pairs={{0,16},{4,20},{8,24},{12,28},{16,0},{20,4},{24,8},{28,12},{1,17},{... | collective-permute-start | bytes 1990664 | tf_op jit(solution)/shard_map/ppermute | solution.py:319
  67.6 17.1 %collective-permute-start.18 = (bf16[432,768]{1,0:T(8,128)(2,1)S(1)}, bf16[432,768]{1,0:T(8,128)(2,1)}, u32[]{:S(2)}, u32[]{:S(2)}) collective-permute-start(bf16[432,768]{1,0:T(8,128)(2,1)S(1)} %pad_maximum_fusion.4), channel_id=1, source_target_pairs={{0,8},{4,12},{8,0},{12,4},{16,24},{20,28},{24,16},{28,20},{1,9},{5... | collective-permute-start | bytes 1990664 | tf_op jit(solution)/shard_map/ppermute | solution.py:319
  86.6 39.1 %collective-permute-start.20 = (bf16[864,768]{1,0:T(8,128)(2,1)S(1)}, bf16[864,768]{1,0:T(8,128)(2,1)}, u32[]{:S(2)}, u32[]{:S(2)}) collective-permute-start(bf16[864,768]{1,0:T(8,128)(2,1)S(1)} %pad_maximum_fusion.1.refs_7_), channel_id=1, source_target_pairs={{0,16},{4,20},{8,24},{12,28},{16,0},{20,4},{24,8},{28,12},{1,17},{... | collective-permute-start | bytes 3981320 | tf_op jit(solution)/shard_map/ppermute | solution.py:319
  88.2 37.5 %collective-permute-start.21 = (bf16[864,768]{1,0:T(8,128)(2,1)S(1)}, bf16[864,768]{1,0:T(8,128)(2,1)}, u32[]{:S(2)}, u32[]{:S(2)}) collective-permute-start(bf16[864,768]{1,0:T(8,128)(2,1)S(1)} %pad_maximum_fusion.2.refs_11_), channel_id=1, source_target_pairs={{0,8},{4,12},{8,0},{12,4},{16,24},{20,28},{24,16},{28,20},{1,9},{5... | collective-permute-start | bytes 3981320 | tf_op jit(solution)/shard_map/ppermute | solution.py:319
  89.4 22.1 %collective-permute-start.17 = (bf16[512,768]{1,0:T(8,128)(2,1)S(1)}, bf16[512,768]{1,0:T(8,128)(2,1)S(1)}, u32[]{:S(2)}, u32[]{:S(2)}) collective-permute-start(bf16[512,768]{1,0:T(8,128)(2,1)S(1)} %broadcast_select_fusion.1.refs_1_.refs_2_), channel_id=1, source_target_pairs={{1,0},{2,3},{5,4},{6,7},{9,8},{10,11},{13,12},{14,15},{17,16},{18,... | collective-permute-start | bytes 2359304 | tf_op jit(solution)/shard_map/ppermute | solution.py:1080
  91.9 34.4 %collective-permute-start.22 = (bf16[864,768]{1,0:T(8,128)(2,1)S(1)}, bf16[864,768]{1,0:T(8,128)(2,1)}, u32[]{:S(2)}, u32[]{:S(2)}) collective-permute-start(bf16[864,768]{1,0:T(8,128)(2,1)S(1)} %pad_maximum_fusion.1.refs_7_), channel_id=1, source_target_pairs={{0,4},{4,0},{8,12},{12,8},{16,20},{20,16},{24,28},{28,24},{1,5},{5... | collective-permute-start | bytes 3981320 | tf_op jit(solution)/shard_map/ppermute | solution.py:319
  91.9 34.3 %collective-permute-start.24 = (bf16[864,768]{1,0:T(8,128)(2,1)S(1)}, bf16[864,768]{1,0:T(8,128)(2,1)}, u32[]{:S(2)}, u32[]{:S(2)}) collective-permute-start(bf16[864,768]{1,0:T(8,128)(2,1)S(1)} %pad_maximum_fusion.2.refs_11_), channel_id=1, source_target_pairs={{0,4},{4,0},{8,12},{12,8},{16,20},{20,16},{24,28},{28,24},{1,5},{5... | collective-permute-start | bytes 3981320 | tf_op jit(solution)/shard_map/ppermute | solution.py:319
  167.7 21.5 %collective-permute-start.27 = (bf16[5,4,96,768]{3,2,1,0:T(8,128)(2,1)}, bf16[5,4,96,768]{3,2,1,0:T(8,128)(2,1)S(1)}, u32[]{:S(2)}, u32[]{:S(2)}) collective-permute-start(bf16[5,4,96,768]{3,2,1,0:T(8,128)(2,1)} %get-tuple-element.283), channel_id=1, source_target_pairs={{0,4},{4,0},{8,12},{12,8},{16,20},{20,16},{24,28},{28,24},{1,5},{5... | collective-permute-start | bytes 8847368 | tf_op jit(solution)/shard_map/ppermute | solution.py:319
  167.9 21.3 %collective-permute-start.26 = (bf16[4,4,96,768]{3,2,1,0:T(8,128)(2,1)}, bf16[4,4,96,768]{3,2,1,0:T(8,128)(2,1)S(1)}, u32[]{:S(2)}, u32[]{:S(2)}) collective-permute-start(bf16[4,4,96,768]{3,2,1,0:T(8,128)(2,1)} %get-tuple-element.282), channel_id=1, source_target_pairs={{0,4},{4,0},{8,12},{12,8},{16,20},{20,16},{24,28},{28,24},{1,5},{5... | collective-permute-start | bytes 7077896 | tf_op jit(solution)/shard_map/ppermute | solution.py:319
  182.5 27.7 %collective-permute-start.28 = (bf16[512,768]{1,0:T(8,128)(2,1)}, bf16[512,768]{1,0:T(8,128)(2,1)S(1)}, u32[]{:S(2)}, u32[]{:S(2)}) collective-permute-start(bf16[512,768]{1,0:T(8,128)(2,1)} %get-tuple-element.288), channel_id=1, source_target_pairs={{0,1},{3,2},{4,5},{7,6},{8,9},{11,10},{12,13},{15,14},{16,17},{19,... | collective-permute-start | bytes 2359304 | tf_op jit(solution)/shard_map/ppermute | solution.py:1080
  209.3 34.3 %collective-permute-start.32 = (bf16[5,2,96,768]{3,2,1,0:T(8,128)(2,1)}, bf16[5,2,96,768]{3,2,1,0:T(8,128)(2,1)S(1)}, u32[]{:S(2)}, u32[]{:S(2)}) collective-permute-start(bf16[5,2,96,768]{3,2,1,0:T(8,128)(2,1)} %get-tuple-element.298), channel_id=1, source_target_pairs={{0,8},{4,12},{8,0},{12,4},{16,24},{20,28},{24,16},{28,20},{1,9},{5... | collective-permute-start | bytes 4423688 | tf_op jit(solution)/shard_map/ppermute | solution.py:319
  211.8 19.1 %collective-permute-start.30 = (bf16[512,768]{1,0:T(8,128)(2,1)S(1)}, bf16[512,768]{1,0:T(8,128)(2,1)S(1)}, u32[]{:S(2)}, u32[]{:S(2)}) collective-permute-start(bf16[512,768]{1,0:T(8,128)(2,1)S(1)} %add_convert_fusion.1), channel_id=1, source_target_pairs={{3,2},{2,1},{7,6},{6,5},{11,10},{10,9},{15,14},{14,13},{19,18},{18... | collective-permute-start | bytes 2359304 | tf_op jit(solution)/shard_map/ppermute | solution.py:1080
  212.5 27.7 %collective-permute-start.31 = (bf16[4,2,96,768]{3,2,1,0:T(8,128)(2,1)}, bf16[4,2,96,768]{3,2,1,0:T(8,128)(2,1)S(1)}, u32[]{:S(2)}, u32[]{:S(2)}) collective-permute-start(bf16[4,2,96,768]{3,2,1,0:T(8,128)(2,1)} %get-tuple-element.297), channel_id=1, source_target_pairs={{0,16},{4,20},{8,24},{12,28},{16,0},{20,4},{24,8},{28,12},{1,17},{... | collective-permute-start | bytes 3538952 | tf_op jit(solution)/shard_map/ppermute | solution.py:319
  214.1 18.5 %collective-permute-start.29 = (bf16[512,768]{1,0:T(8,128)(2,1)S(1)}, bf16[512,768]{1,0:T(8,128)(2,1)S(1)}, u32[]{:S(2)}, u32[]{:S(2)}) collective-permute-start(bf16[512,768]{1,0:T(8,128)(2,1)S(1)} %add_convert_fusion.1), channel_id=1, source_target_pairs={{0,1},{1,2},{4,5},{5,6},{8,9},{9,10},{12,13},{13,14},{16,17},{17,1... | collective-permute-start | bytes 2359304 | tf_op jit(solution)/shard_map/ppermute | solution.py:1080
  233.2 33.7 %collective-permute-start.33 = (bf16[512,768]{1,0:T(8,128)(2,1)S(1)}, bf16[512,768]{1,0:T(8,128)(2,1)S(1)}, u32[]{:S(2)}, u32[]{:S(2)}) collective-permute-start(bf16[512,768]{1,0:T(8,128)(2,1)S(1)} %select_convert_fusion), channel_id=1, source_target_pairs={{0,1},{1,2},{2,3},{4,5},{5,6},{6,7},{8,9},{9,10},{10,11},{12,13},{... | collective-permute-start | bytes 2359304 | tf_op jit(solution)/shard_map/ppermute | solution.py:1080
  238.7 28.2 %collective-permute-start.34 = (bf16[512,768]{1,0:T(8,128)(2,1)S(1)}, bf16[512,768]{1,0:T(8,128)(2,1)S(1)}, u32[]{:S(2)}, u32[]{:S(2)}) collective-permute-start(bf16[512,768]{1,0:T(8,128)(2,1)S(1)} %add_convert_fusion), channel_id=1, source_target_pairs={{3,2},{2,1},{1,0},{7,6},{6,5},{5,4},{11,10},{10,9},{9,8},{15,14},{... | collective-permute-start | bytes 2359304 | tf_op jit(solution)/shard_map/ppermute | solution.py:1080
  264.5 17.8 %collective-permute-start.38 = (bf16[5,1,96,768]{3,2,1,0:T(8,128)(2,1)}, bf16[5,1,96,768]{3,2,1,0:T(8,128)(2,1)}, u32[]{:S(2)}, u32[]{:S(2)}) collective-permute-start(bf16[5,1,96,768]{3,2,1,0:T(8,128)(2,1)} %get-tuple-element.316), channel_id=1, source_target_pairs={{0,16},{4,20},{8,24},{12,28},{16,0},{20,4},{24,8},{28,12},{1,17},{... | collective-permute-start | bytes 2211848 | tf_op jit(solution)/shard_map/ppermute | solution.py:319
  309.8 29.9 %collective-permute-start.54 = (bf16[216,768]{1,0:T(8,128)(2,1)S(1)}, bf16[216,768]{1,0:T(8,128)(2,1)S(1)}, u32[]{:S(2)}, u32[]{:S(2)}) collective-permute-start(bf16[216,768]{1,0:T(8,128)(2,1)S(1)} %fusion.8), channel_id=1, source_target_pairs={{0,2},{1,3},{2,0},{3,1},{4,6},{5,7},{6,4},{7,5},{8,10},{9,11},{10,... | collective-permute-start | bytes 995336 | tf_op jit(solution)/shard_map/ppermute | solution.py:319
  327.3 19.4 %collective-permute-start.51 = (bf16[3,96,192]{2,1,0:T(8,128)(2,1)}, bf16[3,96,192]{2,1,0:T(8,128)(2,1)S(1)}, u32[]{:S(2)}, u32[]{:S(2)}) collective-permute-start(bf16[3,96,192]{2,1,0:T(8,128)(2,1)} %get-tuple-element.366), channel_id=1, source_target_pairs={{0,1},{1,0},{2,3},{3,2},{4,5},{5,4},{6,7},{7,6},{8,9},{9,8},{10,11... | collective-permute-start | bytes 331784 | tf_op jit(solution)/shard_map/ppermute | solution.py:319
  (72 other events, 646.9 us)

commit v9 on v8

--- a/solution.py
+++ b/solution.py
@@ -1293,6 +1293,7 @@
     feed.advance(order)
     small.advance(order)
     qkv.advance(order)
+    feed.advance(order)
     qkv.advance(order)
     small.advance(order)
     qkv.advance(order)

time: 356 us -> 355 us (level)
  waiting for transfers between devices: 48 us -> 53 us
    ppermute x43, waiting for transfers between devices: 35.7 us -> 40.7 us  [swap(): return lax.ppermute(value, axis, [(i, i ^ bit) for i in range(count)])]
    unnamed x81 -> x87, local copies, waits for them, and re-layouts: 10.3 us -> 11.2 us
  transfers between devices with their start and end apart: 55 -> 55, of which waited for: 20 -> 22; matrix products, arithmetic and copies ran while one was open for 9% -> 8% of each run, Pallas kernels for 40% -> 40%
where the time goes in v9:
time: 355 us; the launch traced here: 349 us
  Pallas kernels  177 us (50%)
  starting transfers between devices  69.6 us (20%)
  waiting for transfers between devices  53 us (15%)
  local copies, waits for them, and re-layouts  21.5 us (6%)
  other arithmetic  19.6 us (6%)
  between operations  5.39 us (2%)
    pallas_call x4, Pallas kernels, attend_backward(): pl.pallas_call(functools.partial(backward_kernel, number, first, last, fo...  66.7 us
    pallas_call x3, Pallas kernels, attend_forward(): pl.pallas_call(functools.partial(forward_kernel, numbers, first, final),...  45.1 us
    ppermute x43, starting transfers between devices, swap(): return lax.ppermute(value, axis, [(i, i ^ bit) for i in range(count)])  42.1 us
    ppermute x43, waiting for transfers between devices, swap(): return lax.ppermute(value, axis, [(i, i ^ bit) for i in range(count)])  40.7 us
    pallas_call x1, Pallas kernels, middle_call(): pl.pallas_call(functools.partial(middle_kernel, plan, block, len(arrays))...  35.7 us
    ppermute x12, starting transfers between devices, shards(): along = lambda value, pairs: lax.ppermute(value, 'mp', pairs)  27.5 us
    pallas_call x1, Pallas kernels, qkv_grads(): pl.pallas_call(functools.partial(qkv_grad_kernel, count), out_shape=[jax....  13.1 us
    ppermute x12, waiting for transfers between devices, shards(): along = lambda value, pairs: lax.ppermute(value, 'mp', pairs)  12.3 us
  transfers between devices with their start and end apart: 55, of which 22 were waited for; matrix products, arithmetic and copies ran while one was open for 8% of the time, Pallas kernels for 40%

profile of v9, /device:TPU:0, one launch (start us, length us, event | category | flops | bytes accessed | tf_op | source)
XLA Modules:
  0.0 349.0 jit_solution(9486018567192249033)
XLA Ops:
  30.7 3.2 collective-permute-start.3
  38.6 6.4 %collective-permute-done.8.refs_1_ = bf16[288,768]{1,0:T(8,128)(2,1)S(1)} collective-permute-done((bf16[288,768]{1,0:T(8,128)(2,1)S(1)}, bf16[288,768]{1,0:T(8,128)(2,1)S(1)}, u32[]{:S(2)}, u32[]{:S(2)}) %collective-permute-start.8) | collective-permute-done | bytes 442400 | tf_op jit(solution)/shard_map/ppermute | solution.py:319
  48.5 7.8 %collective-permute-done.4 = bf16[512,768]{1,0:T(8,128)(2,1)S(1)} collective-permute-done((bf16[512,768]{1,0:T(8,128)(2,1)S(1)}, bf16[512,768]{1,0:T(8,128)(2,1)S(1)}, u32[]{:S(2)}, u32[]{:S(2)}) %collective-permute-start.4) | collective-permute-done | bytes 786464 | tf_op jit(solution)/shard_map/ppermute | solution.py:1080
  61.6 4.1 %place.1 = (bf16[768,768]{1,0:T(8,128)(2,1)}, bf16[768,1536]{1,0:T(8,128)(2,1)}) custom-call(bf16[288,768]{1,0:T(8,128)(2,1)} %copy-done.12, bf16[288,768]{1,0:T(8,128)(2,1)} %copy-done.26, bf16[288,768]{1,0:T(8,128)(2,1)} %copy-done.28, bf16[288,768]{1,0:T(8,128)(2,1)} %copy-done.29, bf16[288,768]{1,0:T(8,128)(2,1)} %copy-done.11, ...), custom_call_target="tpu_custom_call" | custom-call | flops 1048576 | bytes 65536 | tf_op jit(solution)/shard_map/place/pallas_call | solution.py:434
  68.7 13.1 %attend_forward.3 = (bf16[512,768]{1,0:T(8,128)(2,1)}, bf16[512,768]{1,0:T(8,128)(2,1)}, bf16[512,768]{1,0:T(8,128)(2,1)}, f32[512,768]{1,0:T(8,128)}, f32[512,768]{1,0:T(8,128)}, /*index=5*/f32[512,768]{1,0:T(8,128)}) custom-call(s32[6]{0:T(128)} %stack.42.scalars.refs_0_, bf16[512,768]{1,0:T(8,128)(2,1)} %copy-done.1, ...), custom_call_target="tpu_custom_call" | custom-call | flops 1048576 | bytes 65536 | tf_op jit(solution)/shard_map/attend_forward/pallas_call | solution.py:129
  92.4 18.8 %attend_forward.4 = (bf16[512,768]{1,0:T(8,128)(2,1)}, bf16[512,768]{1,0:T(8,128)(2,1)}, bf16[512,768]{1,0:T(8,128)(2,1)}, bf16[512,768]{1,0:T(8,128)(2,1)}, f32...) custom-call(s32[6]{0:T(128)} %stack.42.scalars.refs_0_, ...), custom_call_target="tpu_custom_call" | custom-call | flops 1048576 | bytes 65536 | tf_op jit(solution)/shard_map/attend_forward/pallas_call | solution.py:129
  112.5 13.1 %attend_forward.5 = (bf16[512,768]{1,0:T(8,128)(2,1)}, bf16[512,768]{1,0:T(8,128)(2,1)}, f32[512,768]{1,0:T(8,128)}, f32[512,768]{1,0:T(8,128)}) custom-call(s32[6]{0:T(128)} %stack.42.scalars.refs_0_, bf16[512,768]{1,0:T(8,128)(2,1)} %broadcast_select_fusion.2.refs_0_.refs_3_, bf16[768,1536]{1,0:T(8,128)(2,1)} %get-tuple-element.225.refs_1_.refs_2_.refs_3_.wk_ref.wv_ref, ...), custom_call_target="tpu_custom_call" | custom-call | flops 1048576 | bytes 65536 | tf_op jit(solution)/shard_map/attend_forward/pallas_call | solution.py:129
  132.0 35.7 %middle.1 = (bf16[512,768]{1,0:T(8,128)(2,1)}, f32[512,768]{1,0:T(8,128)}, bf16[512,768]{1,0:T(8,128)(2,1)}, bf16[4,4,96,768]{3,2,1,0:T(8,128)(2,1)}, bf16[4,4,9...) custom-call(s32[6]{0:T(128)} %stack.42.scalars.refs_0_, ...), custom_call_target="tpu_custom_call" | custom-call | flops 1048576 | bytes 65536 | tf_op jit(solution)/shard_map/middle/pallas_call | solution.py:669
  168.3 14.2 %attend_backward.4 = (f32[512,768]{1,0:T(8,128)}, bf16[512,768]{1,0:T(8,128)(2,1)}, bf16[512,768]{1,0:T(8,128)(2,1)}, bf16[512,768]{1,0:T(8,128)(2,1)}) custom-call(s32[6]{0:T(128)} %stack.42.scalars.refs_0_, bf16[512,768]{1,0:T(8,128)(2,1)} %get-tuple-element.238.refs_5_.refs_4_.q_ref, bf16[512,768]{1,0:T(8,128)(2,1)} %get-tuple-element.274.k_ref, ...), custom_call_target="tpu_custom_call" | custom-call | flops 1048576 | bytes 65536 | tf_op jit(solution)/shard_map/attend_backward/pallas_call | solution.py:266
  182.5 6.6 %collective-permute-start.28 = (bf16[512,768]{1,0:T(8,128)(2,1)}, bf16[512,768]{1,0:T(8,128)(2,1)S(1)}, u32[]{:S(2)}, u32[]{:S(2)}) collective-permute-start(bf16[512,768]{1,0:T(8,128)(2,1)} %get-tuple-element.288), channel_id=1, source_target_pairs={{0,1},{3,2},{4,5},{7,6},{8,9},{11,10},{12,13},{15,14},{16,17},{19,... | collective-permute-start | bytes 2359304 | tf_op jit(solution)/shard_map/ppermute | solution.py:1080
  191.5 17.9 %attend_backward.5 = (f32[512,768]{1,0:T(8,128)}, bf16[512,768]{1,0:T(8,128)(2,1)}, bf16[512,768]{1,0:T(8,128)(2,1)}, f32[512,768]{1,0:T(8,128)}, bf16[4,2,96,76...) custom-call(s32[6]{0:T(128)} %stack.42.scalars.refs_0_, ...), custom_call_target="tpu_custom_call" | custom-call | flops 1048576 | bytes 65536 | tf_op jit(solution)/shard_map/attend_backward/pallas_call | solution.py:266
  216.0 14.9 %attend_backward.6 = (f32[512,768]{1,0:T(8,128)}, bf16[512,768]{1,0:T(8,128)(2,1)}, bf16[512,768]{1,0:T(8,128)(2,1)}, f32[512,768]{1,0:T(8,128)}) custom-call(s32[6]{0:T(128)} %stack.42.scalars.refs_0_, bf16[512,768]{1,0:T(8,128)(2,1)} %get-tuple-element.238.refs_5_.refs_4_.q_ref, bf16[512,768]{1,0:T(8,128)(2,1)} %get-tuple-element.258.k_ref, ...), custom_call_target="tpu_custom_call" | custom-call | flops 1048576 | bytes 65536 | tf_op jit(solution)/shard_map/attend_backward/pallas_call | solution.py:266
  233.3 5.4 %collective-permute-start.33 = (bf16[512,768]{1,0:T(8,128)(2,1)S(1)}, bf16[512,768]{1,0:T(8,128)(2,1)S(1)}, u32[]{:S(2)}, u32[]{:S(2)}) collective-permute-start(bf16[512,768]{1,0:T(8,128)(2,1)S(1)} %select_convert_fusion), channel_id=1, source_target_pairs={{0,1},{1,2},{2,3},{4,5},{5,6},{6,7},{8,9},{9,10},{10,11},{12,13},{... | collective-permute-start | bytes 2359304 | tf_op jit(solution)/shard_map/ppermute | solution.py:1080
  240.3 3.4 collective-permute-done.32.refs_5_
  244.8 19.7 %attend_backward.7 = (bf16[512,768]{1,0:T(8,128)(2,1)}, bf16[512,768]{1,0:T(8,128)(2,1)}, bf16[512,768]{1,0:T(8,128)(2,1)}, f32[512,768]{1,0:T(8,128)}, bf16[4,1...) custom-call(s32[6]{0:T(128)} %stack.42.scalars.refs_0_, ...), custom_call_target="tpu_custom_call" | custom-call | flops 1048576 | bytes 65536 | tf_op jit(solution)/shard_map/attend_backward/pallas_call | solution.py:266
  266.9 13.1 %qkv_grads.1 = (bf16[3,4,96,384]{3,2,1,0:T(8,128)(2,1)}, bf16[3,4,96,384]{3,2,1,0:T(8,128)(2,1)}, bf16[3,4,96,384]{3,2,1,0:T(8,128)(2,1)}, bf16[3,4,96,384]{3,2,1,0:T(8,128)(2,1)}, f32[16,768]{1,0:T(8,128)}) custom-call(bf16[512,768]{1,0:T(8,128)(2,1)} %copy-done.1, bf16[512,768]{1,0:T(8,128)(2,1)} %broadcast_select_fusion.refs_0_.refs_1_, ...), custom_call_target="tpu_custom_call" | custom-call | flops 1048576 | bytes 65536 | tf_op jit(solution)/shard_map/qkv_grads/pallas_call | solution.py:819
  286.8 4.0 %fold.2 = (bf16[3,2,96,384]{3,2,1,0:T(8,128)(2,1)}, bf16[3,2,96,384]{3,2,1,0:T(8,128)(2,1)}, bf16[3,2,96,384]{3,2,1,0:T(8,128)(2,1)}, bf16[3,2,96,384]{3,2,1,0:T(8,128)(2,1)}) custom-call(bf16[3,4,96,384]{3,2,1,0:T(8,128)(2,1)} %get-tuple-element.326.refs_0_, bf16[3,4,96,384]{3,2,1,0:T(8,128)(2,1)} %collective-permute-done.35.refs_1_, ...), custom_call_target="tpu_custom_call" | custom-call | bytes 16777216 | tf_op jit(solution)/shard_map/fold/pallas_call | solution.py:747
  293.1 5.2 %last_norm.1 = (f32[512,768]{1,0:T(8,128)}, f32[24,768]{1,0:T(8,128)}) custom-call(bf16[512,768]{1,0:T(8,128)(2,1)} %token_ref, f32[512,768]{1,0:T(8,128)} %get-tuple-element.344.first_ref, bf16[512,768]{1,0:T(8,128)(2,1)} %copy-done.20, bf16[512,768]{1,0:T(8,128)(2,1)} %copy-done.21, f32[512,768]{1,0:T(8,128)} %get-tuple-element.345.middle_ref, ...), custom_call_target="tpu_custom_call" | custom-call | flops 1048576 | bytes 65536 | tf_op jit(solution)/shard_map/last_norm/pallas_call | solution.py:879
  298.3 3.9 %collective-permute-done.39 = bf16[2,216,768]{2,1,0:T(8,128)(2,1)} collective-permute-done((bf16[2,216,768]{2,1,0:T(8,128)(2,1)S(1)}, bf16[2,216,768]{2,1,0:T(8,128)(2,1)}, u32[]{:S(2)}, u32[]{:S(2)}) %collective-permute-start.39) | collective-permute-done | bytes 663584 | tf_op jit(solution)/shard_map/ppermute | solution.py:319
  308.1 3.2 fold.3
  314.6 5.7 %collective-permute-done.45 = bf16[216,768]{1,0:T(8,128)(2,1)S(1)} collective-permute-done((bf16[216,768]{1,0:T(8,128)(2,1)S(1)}, bf16[216,768]{1,0:T(8,128)(2,1)S(1)}, u32[]{:S(2)}, u32[]{:S(2)}) %collective-permute-start.45) | collective-permute-done | bytes 331808 | tf_op jit(solution)/shard_map/ppermute | solution.py:319
  327.7 3.4 collective-permute-start.50
  332.5 3.8 %collective-permute-start.53 = (bf16[3,96,192]{2,1,0:T(8,128)(2,1)S(1)}, bf16[3,96,192]{2,1,0:T(8,128)(2,1)S(1)}, u32[]{:S(2)}, u32[]{:S(2)}) collective-permute-start(bf16[3,96,192]{2,1,0:T(8,128)(2,1)S(1)} %get-tuple-element.368), channel_id=1, source_target_pairs={{0,2},{1,3},{2,0},{3,1},{4,6},{5,7},{6,4},{7,5},{8,10},{9,11},{10,... | collective-permute-start | bytes 331784 | tf_op jit(solution)/shard_map/ppermute | solution.py:319
  342.4 4.8 %collective-permute-done.53 = bf16[3,96,192]{2,1,0:T(8,128)(2,1)S(1)} collective-permute-done((bf16[3,96,192]{2,1,0:T(8,128)(2,1)S(1)}, bf16[3,96,192]{2,1,0:T(8,128)(2,1)S(1)}, u32[]{:S(2)}, u32[]{:S(2)}) %collective-permute-start.53) | collective-permute-done | bytes 110624 | tf_op jit(solution)/shard_map/ppermute | solution.py:319
  (257 shorter events, 112.2 us)
Async XLA Ops:
  6.7 16.4 %collective-permute-start.1 = (bf16[192,768]{1,0:T(8,128)(2,1)S(1)}, bf16[192,768]{1,0:T(8,128)(2,1)S(1)}, u32[]{:S(2)}, u32[]{:S(2)}) collective-permute-start(bf16[192,768]{1,0:T(8,128)(2,1)S(1)} %pad_maximum_fusion.9), channel_id=1, source_target_pairs={{0,1},{1,0},{2,3},{3,2},{4,5},{5,4},{6,7},{7,6},{8,9},{9,8},{10,11... | collective-permute-start | bytes 884744 | tf_op jit(solution)/shard_map/ppermute | solution.py:319
  30.7 17.8 %collective-permute-start.3 = (bf16[512,768]{1,0:T(8,128)(2,1)S(1)}, bf16[512,768]{1,0:T(8,128)(2,1)S(1)}, u32[]{:S(2)}, u32[]{:S(2)}) collective-permute-start(bf16[512,768]{1,0:T(8,128)(2,1)S(1)} %add_convert_fusion.2.refs_0_), channel_id=1, source_target_pairs={{0,1},{1,2},{2,3},{4,5},{5,6},{6,7},{8,9},{9,10},{10,11},{12,13},{... | collective-permute-start | bytes 2359304 | tf_op jit(solution)/shard_map/ppermute | solution.py:1080
  34.0 22.4 %collective-permute-start.4 = (bf16[512,768]{1,0:T(8,128)(2,1)S(1)}, bf16[512,768]{1,0:T(8,128)(2,1)S(1)}, u32[]{:S(2)}, u32[]{:S(2)}) collective-permute-start(bf16[512,768]{1,0:T(8,128)(2,1)S(1)} %add_convert_fusion.2.refs_0_), channel_id=1, source_target_pairs={{1,0},{2,1},{3,2},{5,4},{6,5},{7,6},{9,8},{10,9},{11,10},{13,12},{... | collective-permute-start | bytes 2359304 | tf_op jit(solution)/shard_map/ppermute | solution.py:1080
  37.3 28.5 %collective-permute-start.12 = (bf16[384,768]{1,0:T(8,128)(2,1)}, bf16[384,768]{1,0:T(8,128)(2,1)}, u32[]{:S(2)}, u32[]{:S(2)}) collective-permute-start(bf16[384,768]{1,0:T(8,128)(2,1)} %collective-permute-done.7), channel_id=1, source_target_pairs={{1,0},{2,3},{5,4},{6,7},{9,8},{10,11},{13,12},{14,15},{17,16},{18,... | collective-permute-start | bytes 1769480 | tf_op jit(solution)/shard_map/ppermute | solution.py:1080
  56.4 25.4 %collective-permute-start.10 = (bf16[512,768]{1,0:T(8,128)(2,1)S(1)}, bf16[512,768]{1,0:T(8,128)(2,1)}, u32[]{:S(2)}, u32[]{:S(2)}) collective-permute-start(bf16[512,768]{1,0:T(8,128)(2,1)S(1)} %collective-permute-done.3), channel_id=1, source_target_pairs={{1,2},{2,3},{5,6},{6,7},{9,10},{10,11},{13,14},{14,15},{17,18},{18... | collective-permute-start | bytes 2359304 | tf_op jit(solution)/shard_map/ppermute | solution.py:1080
  58.7 24.4 %collective-permute-start.11 = (bf16[512,768]{1,0:T(8,128)(2,1)S(1)}, bf16[512,768]{1,0:T(8,128)(2,1)}, u32[]{:S(2)}, u32[]{:S(2)}) collective-permute-start(bf16[512,768]{1,0:T(8,128)(2,1)S(1)} %collective-permute-done.4), channel_id=1, source_target_pairs={{1,0},{2,1},{5,4},{6,5},{9,8},{10,9},{13,12},{14,13},{17,16},{18,1... | collective-permute-start | bytes 2359304 | tf_op jit(solution)/shard_map/ppermute | solution.py:1080
  67.0 17.4 %collective-permute-start.19 = (bf16[432,768]{1,0:T(8,128)(2,1)S(1)}, bf16[432,768]{1,0:T(8,128)(2,1)S(1)}, u32[]{:S(2)}, u32[]{:S(2)}) collective-permute-start(bf16[432,768]{1,0:T(8,128)(2,1)S(1)} %fusion.6), channel_id=1, source_target_pairs={{0,16},{4,20},{8,24},{12,28},{16,0},{20,4},{24,8},{28,12},{1,17},{... | collective-permute-start | bytes 1990664 | tf_op jit(solution)/shard_map/ppermute | solution.py:319
  67.6 17.1 %collective-permute-start.18 = (bf16[432,768]{1,0:T(8,128)(2,1)S(1)}, bf16[432,768]{1,0:T(8,128)(2,1)}, u32[]{:S(2)}, u32[]{:S(2)}) collective-permute-start(bf16[432,768]{1,0:T(8,128)(2,1)S(1)} %pad_maximum_fusion.4), channel_id=1, source_target_pairs={{0,8},{4,12},{8,0},{12,4},{16,24},{20,28},{24,16},{28,20},{1,9},{5... | collective-permute-start | bytes 1990664 | tf_op jit(solution)/shard_map/ppermute | solution.py:319
  86.6 39.1 %collective-permute-start.20 = (bf16[864,768]{1,0:T(8,128)(2,1)S(1)}, bf16[864,768]{1,0:T(8,128)(2,1)}, u32[]{:S(2)}, u32[]{:S(2)}) collective-permute-start(bf16[864,768]{1,0:T(8,128)(2,1)S(1)} %pad_maximum_fusion.1.refs_7_), channel_id=1, source_target_pairs={{0,16},{4,20},{8,24},{12,28},{16,0},{20,4},{24,8},{28,12},{1,17},{... | collective-permute-start | bytes 3981320 | tf_op jit(solution)/shard_map/ppermute | solution.py:319
  88.2 37.5 %collective-permute-start.21 = (bf16[864,768]{1,0:T(8,128)(2,1)S(1)}, bf16[864,768]{1,0:T(8,128)(2,1)}, u32[]{:S(2)}, u32[]{:S(2)}) collective-permute-start(bf16[864,768]{1,0:T(8,128)(2,1)S(1)} %pad_maximum_fusion.2.refs_11_), channel_id=1, source_target_pairs={{0,8},{4,12},{8,0},{12,4},{16,24},{20,28},{24,16},{28,20},{1,9},{5... | collective-permute-start | bytes 3981320 | tf_op jit(solution)/shard_map/ppermute | solution.py:319
  89.4 22.1 %collective-permute-start.17 = (bf16[512,768]{1,0:T(8,128)(2,1)S(1)}, bf16[512,768]{1,0:T(8,128)(2,1)S(1)}, u32[]{:S(2)}, u32[]{:S(2)}) collective-permute-start(bf16[512,768]{1,0:T(8,128)(2,1)S(1)} %broadcast_select_fusion.1.refs_1_.refs_2_), channel_id=1, source_target_pairs={{1,0},{2,3},{5,4},{6,7},{9,8},{10,11},{13,12},{14,15},{17,16},{18,... | collective-permute-start | bytes 2359304 | tf_op jit(solution)/shard_map/ppermute | solution.py:1080
  91.9 34.4 %collective-permute-start.22 = (bf16[864,768]{1,0:T(8,128)(2,1)S(1)}, bf16[864,768]{1,0:T(8,128)(2,1)}, u32[]{:S(2)}, u32[]{:S(2)}) collective-permute-start(bf16[864,768]{1,0:T(8,128)(2,1)S(1)} %pad_maximum_fusion.1.refs_7_), channel_id=1, source_target_pairs={{0,4},{4,0},{8,12},{12,8},{16,20},{20,16},{24,28},{28,24},{1,5},{5... | collective-permute-start | bytes 3981320 | tf_op jit(solution)/shard_map/ppermute | solution.py:319
  91.9 34.4 %collective-permute-start.24 = (bf16[864,768]{1,0:T(8,128)(2,1)S(1)}, bf16[864,768]{1,0:T(8,128)(2,1)}, u32[]{:S(2)}, u32[]{:S(2)}) collective-permute-start(bf16[864,768]{1,0:T(8,128)(2,1)S(1)} %pad_maximum_fusion.2.refs_11_), channel_id=1, source_target_pairs={{0,4},{4,0},{8,12},{12,8},{16,20},{20,16},{24,28},{28,24},{1,5},{5... | collective-permute-start | bytes 3981320 | tf_op jit(solution)/shard_map/ppermute | solution.py:319
  167.7 21.5 %collective-permute-start.27 = (bf16[5,4,96,768]{3,2,1,0:T(8,128)(2,1)}, bf16[5,4,96,768]{3,2,1,0:T(8,128)(2,1)S(1)}, u32[]{:S(2)}, u32[]{:S(2)}) collective-permute-start(bf16[5,4,96,768]{3,2,1,0:T(8,128)(2,1)} %get-tuple-element.283), channel_id=1, source_target_pairs={{0,4},{4,0},{8,12},{12,8},{16,20},{20,16},{24,28},{28,24},{1,5},{5... | collective-permute-start | bytes 8847368 | tf_op jit(solution)/shard_map/ppermute | solution.py:319
  167.9 21.3 %collective-permute-start.26 = (bf16[4,4,96,768]{3,2,1,0:T(8,128)(2,1)}, bf16[4,4,96,768]{3,2,1,0:T(8,128)(2,1)S(1)}, u32[]{:S(2)}, u32[]{:S(2)}) collective-permute-start(bf16[4,4,96,768]{3,2,1,0:T(8,128)(2,1)} %get-tuple-element.282), channel_id=1, source_target_pairs={{0,4},{4,0},{8,12},{12,8},{16,20},{20,16},{24,28},{28,24},{1,5},{5... | collective-permute-start | bytes 7077896 | tf_op jit(solution)/shard_map/ppermute | solution.py:319
  182.5 27.7 %collective-permute-start.28 = (bf16[512,768]{1,0:T(8,128)(2,1)}, bf16[512,768]{1,0:T(8,128)(2,1)S(1)}, u32[]{:S(2)}, u32[]{:S(2)}) collective-permute-start(bf16[512,768]{1,0:T(8,128)(2,1)} %get-tuple-element.288), channel_id=1, source_target_pairs={{0,1},{3,2},{4,5},{7,6},{8,9},{11,10},{12,13},{15,14},{16,17},{19,... | collective-permute-start | bytes 2359304 | tf_op jit(solution)/shard_map/ppermute | solution.py:1080
  209.3 34.3 %collective-permute-start.32 = (bf16[5,2,96,768]{3,2,1,0:T(8,128)(2,1)}, bf16[5,2,96,768]{3,2,1,0:T(8,128)(2,1)S(1)}, u32[]{:S(2)}, u32[]{:S(2)}) collective-permute-start(bf16[5,2,96,768]{3,2,1,0:T(8,128)(2,1)} %get-tuple-element.298), channel_id=1, source_target_pairs={{0,8},{4,12},{8,0},{12,4},{16,24},{20,28},{24,16},{28,20},{1,9},{5... | collective-permute-start | bytes 4423688 | tf_op jit(solution)/shard_map/ppermute | solution.py:319
  211.8 19.1 %collective-permute-start.30 = (bf16[512,768]{1,0:T(8,128)(2,1)S(1)}, bf16[512,768]{1,0:T(8,128)(2,1)S(1)}, u32[]{:S(2)}, u32[]{:S(2)}) collective-permute-start(bf16[512,768]{1,0:T(8,128)(2,1)S(1)} %add_convert_fusion.1), channel_id=1, source_target_pairs={{3,2},{2,1},{7,6},{6,5},{11,10},{10,9},{15,14},{14,13},{19,18},{18... | collective-permute-start | bytes 2359304 | tf_op jit(solution)/shard_map/ppermute | solution.py:1080
  212.5 27.7 %collective-permute-start.31 = (bf16[4,2,96,768]{3,2,1,0:T(8,128)(2,1)}, bf16[4,2,96,768]{3,2,1,0:T(8,128)(2,1)S(1)}, u32[]{:S(2)}, u32[]{:S(2)}) collective-permute-start(bf16[4,2,96,768]{3,2,1,0:T(8,128)(2,1)} %get-tuple-element.297), channel_id=1, source_target_pairs={{0,16},{4,20},{8,24},{12,28},{16,0},{20,4},{24,8},{28,12},{1,17},{... | collective-permute-start | bytes 3538952 | tf_op jit(solution)/shard_map/ppermute | solution.py:319
  214.1 18.5 %collective-permute-start.29 = (bf16[512,768]{1,0:T(8,128)(2,1)S(1)}, bf16[512,768]{1,0:T(8,128)(2,1)S(1)}, u32[]{:S(2)}, u32[]{:S(2)}) collective-permute-start(bf16[512,768]{1,0:T(8,128)(2,1)S(1)} %add_convert_fusion.1), channel_id=1, source_target_pairs={{0,1},{1,2},{4,5},{5,6},{8,9},{9,10},{12,13},{13,14},{16,17},{17,1... | collective-permute-start | bytes 2359304 | tf_op jit(solution)/shard_map/ppermute | solution.py:1080
  233.3 33.7 %collective-permute-start.33 = (bf16[512,768]{1,0:T(8,128)(2,1)S(1)}, bf16[512,768]{1,0:T(8,128)(2,1)S(1)}, u32[]{:S(2)}, u32[]{:S(2)}) collective-permute-start(bf16[512,768]{1,0:T(8,128)(2,1)S(1)} %select_convert_fusion), channel_id=1, source_target_pairs={{0,1},{1,2},{2,3},{4,5},{5,6},{6,7},{8,9},{9,10},{10,11},{12,13},{... | collective-permute-start | bytes 2359304 | tf_op jit(solution)/shard_map/ppermute | solution.py:1080
  238.7 28.2 %collective-permute-start.34 = (bf16[512,768]{1,0:T(8,128)(2,1)S(1)}, bf16[512,768]{1,0:T(8,128)(2,1)S(1)}, u32[]{:S(2)}, u32[]{:S(2)}) collective-permute-start(bf16[512,768]{1,0:T(8,128)(2,1)S(1)} %add_convert_fusion), channel_id=1, source_target_pairs={{3,2},{2,1},{1,0},{7,6},{6,5},{5,4},{11,10},{10,9},{9,8},{15,14},{... | collective-permute-start | bytes 2359304 | tf_op jit(solution)/shard_map/ppermute | solution.py:1080
  264.5 17.8 %collective-permute-start.38 = (bf16[5,1,96,768]{3,2,1,0:T(8,128)(2,1)}, bf16[5,1,96,768]{3,2,1,0:T(8,128)(2,1)}, u32[]{:S(2)}, u32[]{:S(2)}) collective-permute-start(bf16[5,1,96,768]{3,2,1,0:T(8,128)(2,1)} %get-tuple-element.316), channel_id=1, source_target_pairs={{0,16},{4,20},{8,24},{12,28},{16,0},{20,4},{24,8},{28,12},{1,17},{... | collective-permute-start | bytes 2211848 | tf_op jit(solution)/shard_map/ppermute | solution.py:319
  290.8 16.4 %collective-permute-start.41 = (bf16[3,2,96,384]{3,2,1,0:T(8,128)(2,1)}, bf16[3,2,96,384]{3,2,1,0:T(8,128)(2,1)S(1)}, u32[]{:S(2)}, u32[]{:S(2)}) collective-permute-start(bf16[3,2,96,384]{3,2,1,0:T(8,128)(2,1)} %get-tuple-element.341), channel_id=1, source_target_pairs={{0,8},{4,12},{8,0},{12,4},{16,24},{20,28},{24,16},{28,20},{1,9},{5... | collective-permute-start | bytes 1327112 | tf_op jit(solution)/shard_map/ppermute | solution.py:319
  (75 other events, 653.0 us)

commit v10 on v9

--- a/solution.py
+++ b/solution.py
@@ -1298,9 +1298,9 @@
     small.advance(order)
     qkv.advance(order)
     small.advance(order)
+    qkv_grad = qkv.finish(order)
+    up_grad, down_grad, out_grad = feed.finish(order)
     total = small.finish(order)
-    up_grad, down_grad, out_grad = feed.finish(order)
-    qkv_grad = qkv.finish(order)
     fixed = 16
     chosen = (timesteps[None, :] == jnp.arange(time_table.shape[0])[:, None]).astype(full)
     table_grad = lax.dot_general(

time: 355 us -> 360 us (1.014)
    unnamed x87 -> x83, local copies, waits for them, and re-layouts: 11.2 us -> 10.3 us
  transfers between devices with their start and end apart: 55 -> 55, of which waited for: 22 -> 18; matrix products, arithmetic and copies ran while one was open for 8% -> 7% of each run, Pallas kernels for 40% -> 40%
where the time goes in v10:
time: 360 us; the launch traced here: 354 us
  Pallas kernels  177 us (49%)
  starting transfers between devices  73.1 us (20%)
  waiting for transfers between devices  55.1 us (15%)
  local copies, waits for them, and re-layouts  20.6 us (6%)
  other arithmetic  19.6 us (5%)
  between operations  5.41 us (2%)
    pallas_call x4, Pallas kernels, attend_backward(): pl.pallas_call(functools.partial(backward_kernel, number, first, last, fo...  66.7 us
    ppermute x43, starting transfers between devices, swap(): return lax.ppermute(value, axis, [(i, i ^ bit) for i in range(count)])  45.5 us
    pallas_call x3, Pallas kernels, attend_forward(): pl.pallas_call(functools.partial(forward_kernel, numbers, first, final),...  45.2 us
    ppermute x43, waiting for transfers between devices, swap(): return lax.ppermute(value, axis, [(i, i ^ bit) for i in range(count)])  42.9 us
    pallas_call x1, Pallas kernels, middle_call(): pl.pallas_call(functools.partial(middle_kernel, plan, block, len(arrays))...  35.7 us
    ppermute x12, starting transfers between devices, shards(): along = lambda value, pairs: lax.ppermute(value, 'mp', pairs)  27.6 us
    pallas_call x1, Pallas kernels, qkv_grads(): pl.pallas_call(functools.partial(qkv_grad_kernel, count), out_shape=[jax....  13.1 us
    ppermute x12, waiting for transfers between devices, shards(): along = lambda value, pairs: lax.ppermute(value, 'mp', pairs)  12.2 us
  transfers between devices with their start and end apart: 55, of which 18 were waited for; matrix products, arithmetic and copies ran while one was open for 7% of the time, Pallas kernels for 40%

profile of v10, /device:TPU:0, one launch (start us, length us, event | category | flops | bytes accessed | tf_op | source)
XLA Modules:
  0.0 353.8 jit_solution(9763612555333637387)
XLA Ops:
  30.7 3.2 collective-permute-start.3
  38.6 6.4 %collective-permute-done.8.refs_1_ = bf16[288,768]{1,0:T(8,128)(2,1)S(1)} collective-permute-done((bf16[288,768]{1,0:T(8,128)(2,1)S(1)}, bf16[288,768]{1,0:T(8,128)(2,1)S(1)}, u32[]{:S(2)}, u32[]{:S(2)}) %collective-permute-start.8) | collective-permute-done | bytes 442400 | tf_op jit(solution)/shard_map/ppermute | solution.py:319
  48.5 7.8 %collective-permute-done.4 = bf16[512,768]{1,0:T(8,128)(2,1)S(1)} collective-permute-done((bf16[512,768]{1,0:T(8,128)(2,1)S(1)}, bf16[512,768]{1,0:T(8,128)(2,1)S(1)}, u32[]{:S(2)}, u32[]{:S(2)}) %collective-permute-start.4) | collective-permute-done | bytes 786464 | tf_op jit(solution)/shard_map/ppermute | solution.py:1080
  61.6 4.1 %place.1 = (bf16[768,768]{1,0:T(8,128)(2,1)}, bf16[768,1536]{1,0:T(8,128)(2,1)}) custom-call(bf16[288,768]{1,0:T(8,128)(2,1)} %copy-done.12, bf16[288,768]{1,0:T(8,128)(2,1)} %copy-done.24, bf16[288,768]{1,0:T(8,128)(2,1)} %copy-done.26, bf16[288,768]{1,0:T(8,128)(2,1)} %copy-done.27, bf16[288,768]{1,0:T(8,128)(2,1)} %copy-done.11, ...), custom_call_target="tpu_custom_call" | custom-call | flops 1048576 | bytes 65536 | tf_op jit(solution)/shard_map/place/pallas_call | solution.py:434
  68.7 13.1 %attend_forward.3 = (bf16[512,768]{1,0:T(8,128)(2,1)}, bf16[512,768]{1,0:T(8,128)(2,1)}, bf16[512,768]{1,0:T(8,128)(2,1)}, f32[512,768]{1,0:T(8,128)}, f32[512,768]{1,0:T(8,128)}, /*index=5*/f32[512,768]{1,0:T(8,128)}) custom-call(s32[6]{0:T(128)} %stack.42.scalars.refs_0_, bf16[512,768]{1,0:T(8,128)(2,1)} %copy-done.1, ...), custom_call_target="tpu_custom_call" | custom-call | flops 1048576 | bytes 65536 | tf_op jit(solution)/shard_map/attend_forward/pallas_call | solution.py:129
  92.4 18.9 %attend_forward.4 = (bf16[512,768]{1,0:T(8,128)(2,1)}, bf16[512,768]{1,0:T(8,128)(2,1)}, bf16[512,768]{1,0:T(8,128)(2,1)}, bf16[512,768]{1,0:T(8,128)(2,1)}, f32...) custom-call(s32[6]{0:T(128)} %stack.42.scalars.refs_0_, ...), custom_call_target="tpu_custom_call" | custom-call | flops 1048576 | bytes 65536 | tf_op jit(solution)/shard_map/attend_forward/pallas_call | solution.py:129
  112.5 13.1 %attend_forward.5 = (bf16[512,768]{1,0:T(8,128)(2,1)}, bf16[512,768]{1,0:T(8,128)(2,1)}, f32[512,768]{1,0:T(8,128)}, f32[512,768]{1,0:T(8,128)}) custom-call(s32[6]{0:T(128)} %stack.42.scalars.refs_0_, bf16[512,768]{1,0:T(8,128)(2,1)} %broadcast_select_fusion.2.refs_0_.refs_3_, bf16[768,1536]{1,0:T(8,128)(2,1)} %get-tuple-element.225.refs_1_.refs_2_.refs_3_.wk_ref.wv_ref, ...), custom_call_target="tpu_custom_call" | custom-call | flops 1048576 | bytes 65536 | tf_op jit(solution)/shard_map/attend_forward/pallas_call | solution.py:129
  132.0 35.7 %middle.1 = (bf16[512,768]{1,0:T(8,128)(2,1)}, f32[512,768]{1,0:T(8,128)}, bf16[512,768]{1,0:T(8,128)(2,1)}, bf16[4,4,96,768]{3,2,1,0:T(8,128)(2,1)}, bf16[4,4,9...) custom-call(s32[6]{0:T(128)} %stack.42.scalars.refs_0_, ...), custom_call_target="tpu_custom_call" | custom-call | flops 1048576 | bytes 65536 | tf_op jit(solution)/shard_map/middle/pallas_call | solution.py:669
  168.3 14.3 %attend_backward.4 = (f32[512,768]{1,0:T(8,128)}, bf16[512,768]{1,0:T(8,128)(2,1)}, bf16[512,768]{1,0:T(8,128)(2,1)}, bf16[512,768]{1,0:T(8,128)(2,1)}) custom-call(s32[6]{0:T(128)} %stack.42.scalars.refs_0_, bf16[512,768]{1,0:T(8,128)(2,1)} %get-tuple-element.238.refs_5_.refs_4_.q_ref, bf16[512,768]{1,0:T(8,128)(2,1)} %get-tuple-element.274.k_ref, ...), custom_call_target="tpu_custom_call" | custom-call | flops 1048576 | bytes 65536 | tf_op jit(solution)/shard_map/attend_backward/pallas_call | solution.py:266
  182.6 6.7 %collective-permute-start.28 = (bf16[512,768]{1,0:T(8,128)(2,1)}, bf16[512,768]{1,0:T(8,128)(2,1)S(1)}, u32[]{:S(2)}, u32[]{:S(2)}) collective-permute-start(bf16[512,768]{1,0:T(8,128)(2,1)} %get-tuple-element.288), channel_id=1, source_target_pairs={{0,1},{3,2},{4,5},{7,6},{8,9},{11,10},{12,13},{15,14},{16,17},{19,... | collective-permute-start | bytes 2359304 | tf_op jit(solution)/shard_map/ppermute | solution.py:1080
  191.6 17.8 %attend_backward.5 = (f32[512,768]{1,0:T(8,128)}, bf16[512,768]{1,0:T(8,128)(2,1)}, bf16[512,768]{1,0:T(8,128)(2,1)}, f32[512,768]{1,0:T(8,128)}, bf16[4,2,96,76...) custom-call(s32[6]{0:T(128)} %stack.42.scalars.refs_0_, ...), custom_call_target="tpu_custom_call" | custom-call | flops 1048576 | bytes 65536 | tf_op jit(solution)/shard_map/attend_backward/pallas_call | solution.py:266
  216.1 14.9 %attend_backward.6 = (f32[512,768]{1,0:T(8,128)}, bf16[512,768]{1,0:T(8,128)(2,1)}, bf16[512,768]{1,0:T(8,128)(2,1)}, f32[512,768]{1,0:T(8,128)}) custom-call(s32[6]{0:T(128)} %stack.42.scalars.refs_0_, bf16[512,768]{1,0:T(8,128)(2,1)} %get-tuple-element.238.refs_5_.refs_4_.q_ref, bf16[512,768]{1,0:T(8,128)(2,1)} %get-tuple-element.258.k_ref, ...), custom_call_target="tpu_custom_call" | custom-call | flops 1048576 | bytes 65536 | tf_op jit(solution)/shard_map/attend_backward/pallas_call | solution.py:266
  233.4 5.5 %collective-permute-start.33 = (bf16[512,768]{1,0:T(8,128)(2,1)S(1)}, bf16[512,768]{1,0:T(8,128)(2,1)S(1)}, u32[]{:S(2)}, u32[]{:S(2)}) collective-permute-start(bf16[512,768]{1,0:T(8,128)(2,1)S(1)} %select_convert_fusion), channel_id=1, source_target_pairs={{0,1},{1,2},{2,3},{4,5},{5,6},{6,7},{8,9},{9,10},{10,11},{12,13},{... | collective-permute-start | bytes 2359304 | tf_op jit(solution)/shard_map/ppermute | solution.py:1080
  240.4 3.4 collective-permute-done.32.refs_5_
  244.9 19.7 %attend_backward.7 = (bf16[512,768]{1,0:T(8,128)(2,1)}, bf16[512,768]{1,0:T(8,128)(2,1)}, bf16[512,768]{1,0:T(8,128)(2,1)}, f32[512,768]{1,0:T(8,128)}, bf16[4,1...) custom-call(s32[6]{0:T(128)} %stack.42.scalars.refs_0_, ...), custom_call_target="tpu_custom_call" | custom-call | flops 1048576 | bytes 65536 | tf_op jit(solution)/shard_map/attend_backward/pallas_call | solution.py:266
  267.0 13.1 %qkv_grads.1 = (bf16[3,4,96,384]{3,2,1,0:T(8,128)(2,1)}, bf16[3,4,96,384]{3,2,1,0:T(8,128)(2,1)}, bf16[3,4,96,384]{3,2,1,0:T(8,128)(2,1)}, bf16[3,4,96,384]{3,2,1,0:T(8,128)(2,1)}, f32[16,768]{1,0:T(8,128)}) custom-call(bf16[512,768]{1,0:T(8,128)(2,1)} %copy-done.1, bf16[512,768]{1,0:T(8,128)(2,1)} %broadcast_select_fusion.refs_0_.refs_1_, ...), custom_call_target="tpu_custom_call" | custom-call | flops 1048576 | bytes 65536 | tf_op jit(solution)/shard_map/qkv_grads/pallas_call | solution.py:819
  286.9 3.9 %fold.2 = (bf16[3,2,96,384]{3,2,1,0:T(8,128)(2,1)}, bf16[3,2,96,384]{3,2,1,0:T(8,128)(2,1)}, bf16[3,2,96,384]{3,2,1,0:T(8,128)(2,1)}, bf16[3,2,96,384]{3,2,1,0:T(8,128)(2,1)}) custom-call(bf16[3,4,96,384]{3,2,1,0:T(8,128)(2,1)} %get-tuple-element.326.refs_0_, bf16[3,4,96,384]{3,2,1,0:T(8,128)(2,1)} %collective-permute-done.35.refs_1_, ...), custom_call_target="tpu_custom_call" | custom-call | bytes 16777216 | tf_op jit(solution)/shard_map/fold/pallas_call | solution.py:747
  293.2 5.2 %last_norm.1 = (f32[512,768]{1,0:T(8,128)}, f32[24,768]{1,0:T(8,128)}) custom-call(bf16[512,768]{1,0:T(8,128)(2,1)} %token_ref, f32[512,768]{1,0:T(8,128)} %get-tuple-element.344.first_ref, bf16[512,768]{1,0:T(8,128)(2,1)} %copy-done.20, bf16[512,768]{1,0:T(8,128)(2,1)} %copy-done.21, f32[512,768]{1,0:T(8,128)} %get-tuple-element.345.middle_ref, ...), custom_call_target="tpu_custom_call" | custom-call | flops 1048576 | bytes 65536 | tf_op jit(solution)/shard_map/last_norm/pallas_call | solution.py:879
  298.4 3.9 %collective-permute-done.39 = bf16[2,216,768]{2,1,0:T(8,128)(2,1)} collective-permute-done((bf16[2,216,768]{2,1,0:T(8,128)(2,1)S(1)}, bf16[2,216,768]{2,1,0:T(8,128)(2,1)}, u32[]{:S(2)}, u32[]{:S(2)}) %collective-permute-start.39) | collective-permute-done | bytes 663584 | tf_op jit(solution)/shard_map/ppermute | solution.py:319
  312.6 8.0 %collective-permute-done.45 = bf16[216,768]{1,0:T(8,128)(2,1)S(1)} collective-permute-done((bf16[216,768]{1,0:T(8,128)(2,1)S(1)}, bf16[216,768]{1,0:T(8,128)(2,1)S(1)}, u32[]{:S(2)}, u32[]{:S(2)}) %collective-permute-start.45) | collective-permute-done | bytes 331808 | tf_op jit(solution)/shard_map/ppermute | solution.py:319
  327.2 3.4 collective-permute-start.53
  331.2 3.8 %collective-permute-start.50 = (f32[24,768]{1,0:T(8,128)S(1)}, f32[24,768]{1,0:T(8,128)S(1)}, u32[]{:S(2)}, u32[]{:S(2)}) collective-permute-start(f32[24,768]{1,0:T(8,128)S(1)} %add_add_fusion.1), channel_id=1, source_target_pairs={{0,2},{1,3},{2,0},{3,1},{4,6},{5,7},{6,4},{7,5},{8,10},{9,11},{10,... | collective-permute-start | bytes 221192 | tf_op jit(solution)/shard_map/ppermute | solution.py:319
  335.0 3.7 %collective-permute-start.51 = (f32[24,768]{1,0:T(8,128)S(1)}, f32[24,768]{1,0:T(8,128)S(1)}, u32[]{:S(2)}, u32[]{:S(2)}) collective-permute-start(f32[24,768]{1,0:T(8,128)S(1)} %add_add_fusion.1), channel_id=1, source_target_pairs={{0,3},{1,2},{2,1},{3,0},{4,7},{5,6},{6,5},{7,4},{8,11},{9,10},{10,... | collective-permute-start | bytes 221192 | tf_op jit(solution)/shard_map/ppermute | solution.py:319
  338.7 5.8 %collective-permute-done.53 = bf16[3,96,192]{2,1,0:T(8,128)(2,1)S(1)} collective-permute-done((bf16[3,96,192]{2,1,0:T(8,128)(2,1)S(1)}, bf16[3,96,192]{2,1,0:T(8,128)(2,1)S(1)}, u32[]{:S(2)}, u32[]{:S(2)}) %collective-permute-start.53) | collective-permute-done | bytes 110624 | tf_op jit(solution)/shard_map/ppermute | solution.py:319
  (253 shorter events, 113.0 us)
Async XLA Ops:
  30.7 17.8 %collective-permute-start.3 = (bf16[512,768]{1,0:T(8,128)(2,1)S(1)}, bf16[512,768]{1,0:T(8,128)(2,1)S(1)}, u32[]{:S(2)}, u32[]{:S(2)}) collective-permute-start(bf16[512,768]{1,0:T(8,128)(2,1)S(1)} %add_convert_fusion.2.refs_0_), channel_id=1, source_target_pairs={{0,1},{1,2},{2,3},{4,5},{5,6},{6,7},{8,9},{9,10},{10,11},{12,13},{... | collective-permute-start | bytes 2359304 | tf_op jit(solution)/shard_map/ppermute | solution.py:1080
  34.0 22.4 %collective-permute-start.4 = (bf16[512,768]{1,0:T(8,128)(2,1)S(1)}, bf16[512,768]{1,0:T(8,128)(2,1)S(1)}, u32[]{:S(2)}, u32[]{:S(2)}) collective-permute-start(bf16[512,768]{1,0:T(8,128)(2,1)S(1)} %add_convert_fusion.2.refs_0_), channel_id=1, source_target_pairs={{1,0},{2,1},{3,2},{5,4},{6,5},{7,6},{9,8},{10,9},{11,10},{13,12},{... | collective-permute-start | bytes 2359304 | tf_op jit(solution)/shard_map/ppermute | solution.py:1080
  37.3 28.5 %collective-permute-start.12 = (bf16[384,768]{1,0:T(8,128)(2,1)}, bf16[384,768]{1,0:T(8,128)(2,1)}, u32[]{:S(2)}, u32[]{:S(2)}) collective-permute-start(bf16[384,768]{1,0:T(8,128)(2,1)} %collective-permute-done.7), channel_id=1, source_target_pairs={{1,0},{2,3},{5,4},{6,7},{9,8},{10,11},{13,12},{14,15},{17,16},{18,... | collective-permute-start | bytes 1769480 | tf_op jit(solution)/shard_map/ppermute | solution.py:1080
  56.4 25.4 %collective-permute-start.10 = (bf16[512,768]{1,0:T(8,128)(2,1)S(1)}, bf16[512,768]{1,0:T(8,128)(2,1)}, u32[]{:S(2)}, u32[]{:S(2)}) collective-permute-start(bf16[512,768]{1,0:T(8,128)(2,1)S(1)} %collective-permute-done.3), channel_id=1, source_target_pairs={{1,2},{2,3},{5,6},{6,7},{9,10},{10,11},{13,14},{14,15},{17,18},{18... | collective-permute-start | bytes 2359304 | tf_op jit(solution)/shard_map/ppermute | solution.py:1080
  58.7 24.4 %collective-permute-start.11 = (bf16[512,768]{1,0:T(8,128)(2,1)S(1)}, bf16[512,768]{1,0:T(8,128)(2,1)}, u32[]{:S(2)}, u32[]{:S(2)}) collective-permute-start(bf16[512,768]{1,0:T(8,128)(2,1)S(1)} %collective-permute-done.4), channel_id=1, source_target_pairs={{1,0},{2,1},{5,4},{6,5},{9,8},{10,9},{13,12},{14,13},{17,16},{18,1... | collective-permute-start | bytes 2359304 | tf_op jit(solution)/shard_map/ppermute | solution.py:1080
  67.0 17.4 %collective-permute-start.19 = (bf16[432,768]{1,0:T(8,128)(2,1)S(1)}, bf16[432,768]{1,0:T(8,128)(2,1)S(1)}, u32[]{:S(2)}, u32[]{:S(2)}) collective-permute-start(bf16[432,768]{1,0:T(8,128)(2,1)S(1)} %fusion.6), channel_id=1, source_target_pairs={{0,16},{4,20},{8,24},{12,28},{16,0},{20,4},{24,8},{28,12},{1,17},{... | collective-permute-start | bytes 1990664 | tf_op jit(solution)/shard_map/ppermute | solution.py:319
  67.6 17.1 %collective-permute-start.18 = (bf16[432,768]{1,0:T(8,128)(2,1)S(1)}, bf16[432,768]{1,0:T(8,128)(2,1)}, u32[]{:S(2)}, u32[]{:S(2)}) collective-permute-start(bf16[432,768]{1,0:T(8,128)(2,1)S(1)} %pad_maximum_fusion.4), channel_id=1, source_target_pairs={{0,8},{4,12},{8,0},{12,4},{16,24},{20,28},{24,16},{28,20},{1,9},{5... | collective-permute-start | bytes 1990664 | tf_op jit(solution)/shard_map/ppermute | solution.py:319
  86.6 39.1 %collective-permute-start.20 = (bf16[864,768]{1,0:T(8,128)(2,1)S(1)}, bf16[864,768]{1,0:T(8,128)(2,1)}, u32[]{:S(2)}, u32[]{:S(2)}) collective-permute-start(bf16[864,768]{1,0:T(8,128)(2,1)S(1)} %pad_maximum_fusion.1.refs_7_), channel_id=1, source_target_pairs={{0,16},{4,20},{8,24},{12,28},{16,0},{20,4},{24,8},{28,12},{1,17},{... | collective-permute-start | bytes 3981320 | tf_op jit(solution)/shard_map/ppermute | solution.py:319
  88.2 37.5 %collective-permute-start.21 = (bf16[864,768]{1,0:T(8,128)(2,1)S(1)}, bf16[864,768]{1,0:T(8,128)(2,1)}, u32[]{:S(2)}, u32[]{:S(2)}) collective-permute-start(bf16[864,768]{1,0:T(8,128)(2,1)S(1)} %pad_maximum_fusion.2.refs_11_), channel_id=1, source_target_pairs={{0,8},{4,12},{8,0},{12,4},{16,24},{20,28},{24,16},{28,20},{1,9},{5... | collective-permute-start | bytes 3981320 | tf_op jit(solution)/shard_map/ppermute | solution.py:319
  89.4 22.1 %collective-permute-start.17 = (bf16[512,768]{1,0:T(8,128)(2,1)S(1)}, bf16[512,768]{1,0:T(8,128)(2,1)S(1)}, u32[]{:S(2)}, u32[]{:S(2)}) collective-permute-start(bf16[512,768]{1,0:T(8,128)(2,1)S(1)} %broadcast_select_fusion.1.refs_1_.refs_2_), channel_id=1, source_target_pairs={{1,0},{2,3},{5,4},{6,7},{9,8},{10,11},{13,12},{14,15},{17,16},{18,... | collective-permute-start | bytes 2359304 | tf_op jit(solution)/shard_map/ppermute | solution.py:1080
  91.9 34.4 %collective-permute-start.22 = (bf16[864,768]{1,0:T(8,128)(2,1)S(1)}, bf16[864,768]{1,0:T(8,128)(2,1)}, u32[]{:S(2)}, u32[]{:S(2)}) collective-permute-start(bf16[864,768]{1,0:T(8,128)(2,1)S(1)} %pad_maximum_fusion.1.refs_7_), channel_id=1, source_target_pairs={{0,4},{4,0},{8,12},{12,8},{16,20},{20,16},{24,28},{28,24},{1,5},{5... | collective-permute-start | bytes 3981320 | tf_op jit(solution)/shard_map/ppermute | solution.py:319
  91.9 34.4 %collective-permute-start.24 = (bf16[864,768]{1,0:T(8,128)(2,1)S(1)}, bf16[864,768]{1,0:T(8,128)(2,1)}, u32[]{:S(2)}, u32[]{:S(2)}) collective-permute-start(bf16[864,768]{1,0:T(8,128)(2,1)S(1)} %pad_maximum_fusion.2.refs_11_), channel_id=1, source_target_pairs={{0,4},{4,0},{8,12},{12,8},{16,20},{20,16},{24,28},{28,24},{1,5},{5... | collective-permute-start | bytes 3981320 | tf_op jit(solution)/shard_map/ppermute | solution.py:319
  167.7 21.6 %collective-permute-start.27 = (bf16[5,4,96,768]{3,2,1,0:T(8,128)(2,1)}, bf16[5,4,96,768]{3,2,1,0:T(8,128)(2,1)S(1)}, u32[]{:S(2)}, u32[]{:S(2)}) collective-permute-start(bf16[5,4,96,768]{3,2,1,0:T(8,128)(2,1)} %get-tuple-element.283), channel_id=1, source_target_pairs={{0,4},{4,0},{8,12},{12,8},{16,20},{20,16},{24,28},{28,24},{1,5},{5... | collective-permute-start | bytes 8847368 | tf_op jit(solution)/shard_map/ppermute | solution.py:319
  167.9 21.4 %collective-permute-start.26 = (bf16[4,4,96,768]{3,2,1,0:T(8,128)(2,1)}, bf16[4,4,96,768]{3,2,1,0:T(8,128)(2,1)S(1)}, u32[]{:S(2)}, u32[]{:S(2)}) collective-permute-start(bf16[4,4,96,768]{3,2,1,0:T(8,128)(2,1)} %get-tuple-element.282), channel_id=1, source_target_pairs={{0,4},{4,0},{8,12},{12,8},{16,20},{20,16},{24,28},{28,24},{1,5},{5... | collective-permute-start | bytes 7077896 | tf_op jit(solution)/shard_map/ppermute | solution.py:319
  182.6 27.8 %collective-permute-start.28 = (bf16[512,768]{1,0:T(8,128)(2,1)}, bf16[512,768]{1,0:T(8,128)(2,1)S(1)}, u32[]{:S(2)}, u32[]{:S(2)}) collective-permute-start(bf16[512,768]{1,0:T(8,128)(2,1)} %get-tuple-element.288), channel_id=1, source_target_pairs={{0,1},{3,2},{4,5},{7,6},{8,9},{11,10},{12,13},{15,14},{16,17},{19,... | collective-permute-start | bytes 2359304 | tf_op jit(solution)/shard_map/ppermute | solution.py:1080
  209.5 34.3 %collective-permute-start.32 = (bf16[5,2,96,768]{3,2,1,0:T(8,128)(2,1)}, bf16[5,2,96,768]{3,2,1,0:T(8,128)(2,1)S(1)}, u32[]{:S(2)}, u32[]{:S(2)}) collective-permute-start(bf16[5,2,96,768]{3,2,1,0:T(8,128)(2,1)} %get-tuple-element.298), channel_id=1, source_target_pairs={{0,8},{4,12},{8,0},{12,4},{16,24},{20,28},{24,16},{28,20},{1,9},{5... | collective-permute-start | bytes 4423688 | tf_op jit(solution)/shard_map/ppermute | solution.py:319
  211.9 19.1 %collective-permute-start.30 = (bf16[512,768]{1,0:T(8,128)(2,1)S(1)}, bf16[512,768]{1,0:T(8,128)(2,1)S(1)}, u32[]{:S(2)}, u32[]{:S(2)}) collective-permute-start(bf16[512,768]{1,0:T(8,128)(2,1)S(1)} %add_convert_fusion.1), channel_id=1, source_target_pairs={{3,2},{2,1},{7,6},{6,5},{11,10},{10,9},{15,14},{14,13},{19,18},{18... | collective-permute-start | bytes 2359304 | tf_op jit(solution)/shard_map/ppermute | solution.py:1080
  212.6 27.7 %collective-permute-start.31 = (bf16[4,2,96,768]{3,2,1,0:T(8,128)(2,1)}, bf16[4,2,96,768]{3,2,1,0:T(8,128)(2,1)S(1)}, u32[]{:S(2)}, u32[]{:S(2)}) collective-permute-start(bf16[4,2,96,768]{3,2,1,0:T(8,128)(2,1)} %get-tuple-element.297), channel_id=1, source_target_pairs={{0,16},{4,20},{8,24},{12,28},{16,0},{20,4},{24,8},{28,12},{1,17},{... | collective-permute-start | bytes 3538952 | tf_op jit(solution)/shard_map/ppermute | solution.py:319
  214.2 18.5 %collective-permute-start.29 = (bf16[512,768]{1,0:T(8,128)(2,1)S(1)}, bf16[512,768]{1,0:T(8,128)(2,1)S(1)}, u32[]{:S(2)}, u32[]{:S(2)}) collective-permute-start(bf16[512,768]{1,0:T(8,128)(2,1)S(1)} %add_convert_fusion.1), channel_id=1, source_target_pairs={{0,1},{1,2},{4,5},{5,6},{8,9},{9,10},{12,13},{13,14},{16,17},{17,1... | collective-permute-start | bytes 2359304 | tf_op jit(solution)/shard_map/ppermute | solution.py:1080
  233.4 33.6 %collective-permute-start.33 = (bf16[512,768]{1,0:T(8,128)(2,1)S(1)}, bf16[512,768]{1,0:T(8,128)(2,1)S(1)}, u32[]{:S(2)}, u32[]{:S(2)}) collective-permute-start(bf16[512,768]{1,0:T(8,128)(2,1)S(1)} %select_convert_fusion), channel_id=1, source_target_pairs={{0,1},{1,2},{2,3},{4,5},{5,6},{6,7},{8,9},{9,10},{10,11},{12,13},{... | collective-permute-start | bytes 2359304 | tf_op jit(solution)/shard_map/ppermute | solution.py:1080
  238.8 28.2 %collective-permute-start.34 = (bf16[512,768]{1,0:T(8,128)(2,1)S(1)}, bf16[512,768]{1,0:T(8,128)(2,1)S(1)}, u32[]{:S(2)}, u32[]{:S(2)}) collective-permute-start(bf16[512,768]{1,0:T(8,128)(2,1)S(1)} %add_convert_fusion), channel_id=1, source_target_pairs={{3,2},{2,1},{1,0},{7,6},{6,5},{5,4},{11,10},{10,9},{9,8},{15,14},{... | collective-permute-start | bytes 2359304 | tf_op jit(solution)/shard_map/ppermute | solution.py:1080
  264.6 17.8 %collective-permute-start.38 = (bf16[5,1,96,768]{3,2,1,0:T(8,128)(2,1)}, bf16[5,1,96,768]{3,2,1,0:T(8,128)(2,1)}, u32[]{:S(2)}, u32[]{:S(2)}) collective-permute-start(bf16[5,1,96,768]{3,2,1,0:T(8,128)(2,1)} %get-tuple-element.316), channel_id=1, source_target_pairs={{0,16},{4,20},{8,24},{12,28},{16,0},{20,4},{24,8},{28,12},{1,17},{... | collective-permute-start | bytes 2211848 | tf_op jit(solution)/shard_map/ppermute | solution.py:319
  327.2 17.4 %collective-permute-start.53 = (bf16[3,96,192]{2,1,0:T(8,128)(2,1)S(1)}, bf16[3,96,192]{2,1,0:T(8,128)(2,1)S(1)}, u32[]{:S(2)}, u32[]{:S(2)}) collective-permute-start(bf16[3,96,192]{2,1,0:T(8,128)(2,1)S(1)} %get-tuple-element.368), channel_id=1, source_target_pairs={{0,2},{1,3},{2,0},{3,1},{4,6},{5,7},{6,4},{7,5},{8,10},{9,11},{10,... | collective-permute-start | bytes 331784 | tf_op jit(solution)/shard_map/ppermute | solution.py:319
  331.2 17.3 %collective-permute-start.50 = (f32[24,768]{1,0:T(8,128)S(1)}, f32[24,768]{1,0:T(8,128)S(1)}, u32[]{:S(2)}, u32[]{:S(2)}) collective-permute-start(f32[24,768]{1,0:T(8,128)S(1)} %add_add_fusion.1), channel_id=1, source_target_pairs={{0,2},{1,3},{2,0},{3,1},{4,6},{5,7},{6,4},{7,5},{8,10},{9,11},{10,... | collective-permute-start | bytes 221192 | tf_op jit(solution)/shard_map/ppermute | solution.py:319
  (73 other events, 694.0 us)

commit v11 on v9

--- a/solution.py
+++ b/solution.py
@@ -561,11 +561,20 @@
 
     def forward(m, _):
         place = pl.ds(pl.multiple_of(m * D, D), D)
-        value = dot_of(second[...], up[place, :], 1, 0) + vector_ref[pl.ds(8 + m, 1), :]
-        cumulative = 0.5 + 0.5 * lax.erf(value * (0.5**0.5))
-        right[m] = (value * cumulative).astype(low)
-        slope[m] = cumulative + value * jnp.exp(-0.5 * value * value) * 0.3989422804014327
-        accum[...] += dot_of(right[m], down[place, :], 1, 1)
+        half = rows // 2
+        spans = [pl.ds(part * half, half) for part in range(2)]
+        values = [
+            dot_of(second[span, :], up[place, :], 1, 0) + vector_ref[pl.ds(8 + m, 1), :]
+            for span in spans
+        ]
+        for span, value in zip(spans, values):
+            cumulative = 0.5 + 0.5 * lax.erf(value * (0.5**0.5))
+            active = (value * cumulative).astype(low)
+            right[m, span, :] = active
+            slope[m, span, :] = (
+                cumulative + value * jnp.exp(-0.5 * value * value) * 0.3989422804014327
+            )
+            accum[span, :] += dot_of(active, down[place, :], 1, 1)
         return 0
 
     lax.fori_loop(0, FF // D, forward, 0)

time: 355 us -> 354 us (level)
  transfers between devices with their start and end apart: 55 -> 55, of which waited for: 22 -> 22; matrix products, arithmetic and copies ran while one was open for 8% -> 8% of each run, Pallas kernels for 40% -> 41%
where the time goes in v11:
time: 354 us; the launch traced here: 347 us
  Pallas kernels  175 us (49%)
  starting transfers between devices  69.6 us (20%)
  waiting for transfers between devices  53 us (15%)
  local copies, waits for them, and re-layouts  21.5 us (6%)
  other arithmetic  19.6 us (6%)
  between operations  5.39 us (2%)
    pallas_call x4, Pallas kernels, attend_backward(): pl.pallas_call(functools.partial(backward_kernel, number, first, last, fo...  66.7 us
    pallas_call x3, Pallas kernels, attend_forward(): pl.pallas_call(functools.partial(forward_kernel, numbers, first, final),...  45.1 us
    ppermute x43, starting transfers between devices, swap(): return lax.ppermute(value, axis, [(i, i ^ bit) for i in range(count)])  42 us
    ppermute x43, waiting for transfers between devices, swap(): return lax.ppermute(value, axis, [(i, i ^ bit) for i in range(count)])  40.7 us
    pallas_call x1, Pallas kernels, middle_call(): pl.pallas_call(functools.partial(middle_kernel, plan, block, len(arrays))...  34.2 us
    ppermute x12, starting transfers between devices, shards(): along = lambda value, pairs: lax.ppermute(value, 'mp', pairs)  27.5 us
    pallas_call x1, Pallas kernels, qkv_grads(): pl.pallas_call(functools.partial(qkv_grad_kernel, count), out_shape=[jax....  13.1 us
    ppermute x12, waiting for transfers between devices, shards(): along = lambda value, pairs: lax.ppermute(value, 'mp', pairs)  12.3 us
  transfers between devices with their start and end apart: 55, of which 22 were waited for; matrix products, arithmetic and copies ran while one was open for 8% of the time, Pallas kernels for 41%

profile of v11, /device:TPU:0, one launch (start us, length us, event | category | flops | bytes accessed | tf_op | source)
XLA Modules:
  0.0 347.5 jit_solution(4628230179496429681)
XLA Ops:
  30.7 3.2 collective-permute-start.3
  38.6 6.4 %collective-permute-done.8.refs_1_ = bf16[288,768]{1,0:T(8,128)(2,1)S(1)} collective-permute-done((bf16[288,768]{1,0:T(8,128)(2,1)S(1)}, bf16[288,768]{1,0:T(8,128)(2,1)S(1)}, u32[]{:S(2)}, u32[]{:S(2)}) %collective-permute-start.8) | collective-permute-done | bytes 442400 | tf_op jit(solution)/shard_map/ppermute | solution.py:319
  48.5 7.8 %collective-permute-done.4 = bf16[512,768]{1,0:T(8,128)(2,1)S(1)} collective-permute-done((bf16[512,768]{1,0:T(8,128)(2,1)S(1)}, bf16[512,768]{1,0:T(8,128)(2,1)S(1)}, u32[]{:S(2)}, u32[]{:S(2)}) %collective-permute-start.4) | collective-permute-done | bytes 786464 | tf_op jit(solution)/shard_map/ppermute | solution.py:1089
  61.6 4.1 %place.1 = (bf16[768,768]{1,0:T(8,128)(2,1)}, bf16[768,1536]{1,0:T(8,128)(2,1)}) custom-call(bf16[288,768]{1,0:T(8,128)(2,1)} %copy-done.12, bf16[288,768]{1,0:T(8,128)(2,1)} %copy-done.26, bf16[288,768]{1,0:T(8,128)(2,1)} %copy-done.28, bf16[288,768]{1,0:T(8,128)(2,1)} %copy-done.29, bf16[288,768]{1,0:T(8,128)(2,1)} %copy-done.11, ...), custom_call_target="tpu_custom_call" | custom-call | flops 1048576 | bytes 65536 | tf_op jit(solution)/shard_map/place/pallas_call | solution.py:434
  68.7 13.1 %attend_forward.3 = (bf16[512,768]{1,0:T(8,128)(2,1)}, bf16[512,768]{1,0:T(8,128)(2,1)}, bf16[512,768]{1,0:T(8,128)(2,1)}, f32[512,768]{1,0:T(8,128)}, f32[512,768]{1,0:T(8,128)}, /*index=5*/f32[512,768]{1,0:T(8,128)}) custom-call(s32[6]{0:T(128)} %stack.42.scalars.refs_0_, bf16[512,768]{1,0:T(8,128)(2,1)} %copy-done.1, ...), custom_call_target="tpu_custom_call" | custom-call | flops 1048576 | bytes 65536 | tf_op jit(solution)/shard_map/attend_forward/pallas_call | solution.py:129
  92.4 18.8 %attend_forward.4 = (bf16[512,768]{1,0:T(8,128)(2,1)}, bf16[512,768]{1,0:T(8,128)(2,1)}, bf16[512,768]{1,0:T(8,128)(2,1)}, bf16[512,768]{1,0:T(8,128)(2,1)}, f32...) custom-call(s32[6]{0:T(128)} %stack.42.scalars.refs_0_, ...), custom_call_target="tpu_custom_call" | custom-call | flops 1048576 | bytes 65536 | tf_op jit(solution)/shard_map/attend_forward/pallas_call | solution.py:129
  112.5 13.1 %attend_forward.5 = (bf16[512,768]{1,0:T(8,128)(2,1)}, bf16[512,768]{1,0:T(8,128)(2,1)}, f32[512,768]{1,0:T(8,128)}, f32[512,768]{1,0:T(8,128)}) custom-call(s32[6]{0:T(128)} %stack.42.scalars.refs_0_, bf16[512,768]{1,0:T(8,128)(2,1)} %broadcast_select_fusion.2.refs_0_.refs_3_, bf16[768,1536]{1,0:T(8,128)(2,1)} %get-tuple-element.225.refs_1_.refs_2_.refs_3_.wk_ref.wv_ref, ...), custom_call_target="tpu_custom_call" | custom-call | flops 1048576 | bytes 65536 | tf_op jit(solution)/shard_map/attend_forward/pallas_call | solution.py:129
  132.0 34.2 %middle.1 = (bf16[512,768]{1,0:T(8,128)(2,1)}, f32[512,768]{1,0:T(8,128)}, bf16[512,768]{1,0:T(8,128)(2,1)}, bf16[4,4,96,768]{3,2,1,0:T(8,128)(2,1)}, bf16[4,4,9...) custom-call(s32[6]{0:T(128)} %stack.42.scalars.refs_0_, ...), custom_call_target="tpu_custom_call" | custom-call | flops 1048576 | bytes 65536 | tf_op jit(solution)/shard_map/middle/pallas_call | solution.py:678
  166.8 14.2 %attend_backward.4 = (f32[512,768]{1,0:T(8,128)}, bf16[512,768]{1,0:T(8,128)(2,1)}, bf16[512,768]{1,0:T(8,128)(2,1)}, bf16[512,768]{1,0:T(8,128)(2,1)}) custom-call(s32[6]{0:T(128)} %stack.42.scalars.refs_0_, bf16[512,768]{1,0:T(8,128)(2,1)} %get-tuple-element.238.refs_5_.refs_4_.q_ref, bf16[512,768]{1,0:T(8,128)(2,1)} %get-tuple-element.274.k_ref, ...), custom_call_target="tpu_custom_call" | custom-call | flops 1048576 | bytes 65536 | tf_op jit(solution)/shard_map/attend_backward/pallas_call | solution.py:266
  181.0 6.6 %collective-permute-start.28 = (bf16[512,768]{1,0:T(8,128)(2,1)}, bf16[512,768]{1,0:T(8,128)(2,1)S(1)}, u32[]{:S(2)}, u32[]{:S(2)}) collective-permute-start(bf16[512,768]{1,0:T(8,128)(2,1)} %get-tuple-element.288), channel_id=1, source_target_pairs={{0,1},{3,2},{4,5},{7,6},{8,9},{11,10},{12,13},{15,14},{16,17},{19,... | collective-permute-start | bytes 2359304 | tf_op jit(solution)/shard_map/ppermute | solution.py:1089
  190.0 17.9 %attend_backward.5 = (f32[512,768]{1,0:T(8,128)}, bf16[512,768]{1,0:T(8,128)(2,1)}, bf16[512,768]{1,0:T(8,128)(2,1)}, f32[512,768]{1,0:T(8,128)}, bf16[4,2,96,76...) custom-call(s32[6]{0:T(128)} %stack.42.scalars.refs_0_, ...), custom_call_target="tpu_custom_call" | custom-call | flops 1048576 | bytes 65536 | tf_op jit(solution)/shard_map/attend_backward/pallas_call | solution.py:266
  214.5 14.9 %attend_backward.6 = (f32[512,768]{1,0:T(8,128)}, bf16[512,768]{1,0:T(8,128)(2,1)}, bf16[512,768]{1,0:T(8,128)(2,1)}, f32[512,768]{1,0:T(8,128)}) custom-call(s32[6]{0:T(128)} %stack.42.scalars.refs_0_, bf16[512,768]{1,0:T(8,128)(2,1)} %get-tuple-element.238.refs_5_.refs_4_.q_ref, bf16[512,768]{1,0:T(8,128)(2,1)} %get-tuple-element.258.k_ref, ...), custom_call_target="tpu_custom_call" | custom-call | flops 1048576 | bytes 65536 | tf_op jit(solution)/shard_map/attend_backward/pallas_call | solution.py:266
  231.8 5.4 %collective-permute-start.33 = (bf16[512,768]{1,0:T(8,128)(2,1)S(1)}, bf16[512,768]{1,0:T(8,128)(2,1)S(1)}, u32[]{:S(2)}, u32[]{:S(2)}) collective-permute-start(bf16[512,768]{1,0:T(8,128)(2,1)S(1)} %select_convert_fusion), channel_id=1, source_target_pairs={{0,1},{1,2},{2,3},{4,5},{5,6},{6,7},{8,9},{9,10},{10,11},{12,13},{... | collective-permute-start | bytes 2359304 | tf_op jit(solution)/shard_map/ppermute | solution.py:1089
  238.8 3.4 collective-permute-done.32.refs_5_
  243.3 19.7 %attend_backward.7 = (bf16[512,768]{1,0:T(8,128)(2,1)}, bf16[512,768]{1,0:T(8,128)(2,1)}, bf16[512,768]{1,0:T(8,128)(2,1)}, f32[512,768]{1,0:T(8,128)}, bf16[4,1...) custom-call(s32[6]{0:T(128)} %stack.42.scalars.refs_0_, ...), custom_call_target="tpu_custom_call" | custom-call | flops 1048576 | bytes 65536 | tf_op jit(solution)/shard_map/attend_backward/pallas_call | solution.py:266
  265.4 13.1 %qkv_grads.1 = (bf16[3,4,96,384]{3,2,1,0:T(8,128)(2,1)}, bf16[3,4,96,384]{3,2,1,0:T(8,128)(2,1)}, bf16[3,4,96,384]{3,2,1,0:T(8,128)(2,1)}, bf16[3,4,96,384]{3,2,1,0:T(8,128)(2,1)}, f32[16,768]{1,0:T(8,128)}) custom-call(bf16[512,768]{1,0:T(8,128)(2,1)} %copy-done.1, bf16[512,768]{1,0:T(8,128)(2,1)} %broadcast_select_fusion.refs_0_.refs_1_, ...), custom_call_target="tpu_custom_call" | custom-call | flops 1048576 | bytes 65536 | tf_op jit(solution)/shard_map/qkv_grads/pallas_call | solution.py:828
  285.3 4.0 %fold.2 = (bf16[3,2,96,384]{3,2,1,0:T(8,128)(2,1)}, bf16[3,2,96,384]{3,2,1,0:T(8,128)(2,1)}, bf16[3,2,96,384]{3,2,1,0:T(8,128)(2,1)}, bf16[3,2,96,384]{3,2,1,0:T(8,128)(2,1)}) custom-call(bf16[3,4,96,384]{3,2,1,0:T(8,128)(2,1)} %get-tuple-element.326.refs_0_, bf16[3,4,96,384]{3,2,1,0:T(8,128)(2,1)} %collective-permute-done.35.refs_1_, ...), custom_call_target="tpu_custom_call" | custom-call | bytes 16777216 | tf_op jit(solution)/shard_map/fold/pallas_call | solution.py:756
  291.6 5.2 %last_norm.1 = (f32[512,768]{1,0:T(8,128)}, f32[24,768]{1,0:T(8,128)}) custom-call(bf16[512,768]{1,0:T(8,128)(2,1)} %token_ref, f32[512,768]{1,0:T(8,128)} %get-tuple-element.344.first_ref, bf16[512,768]{1,0:T(8,128)(2,1)} %copy-done.20, bf16[512,768]{1,0:T(8,128)(2,1)} %copy-done.21, f32[512,768]{1,0:T(8,128)} %get-tuple-element.345.middle_ref, ...), custom_call_target="tpu_custom_call" | custom-call | flops 1048576 | bytes 65536 | tf_op jit(solution)/shard_map/last_norm/pallas_call | solution.py:888
  296.8 3.9 %collective-permute-done.39 = bf16[2,216,768]{2,1,0:T(8,128)(2,1)} collective-permute-done((bf16[2,216,768]{2,1,0:T(8,128)(2,1)S(1)}, bf16[2,216,768]{2,1,0:T(8,128)(2,1)}, u32[]{:S(2)}, u32[]{:S(2)}) %collective-permute-start.39) | collective-permute-done | bytes 663584 | tf_op jit(solution)/shard_map/ppermute | solution.py:319
  306.6 3.2 fold.3
  313.1 5.7 %collective-permute-done.45 = bf16[216,768]{1,0:T(8,128)(2,1)S(1)} collective-permute-done((bf16[216,768]{1,0:T(8,128)(2,1)S(1)}, bf16[216,768]{1,0:T(8,128)(2,1)S(1)}, u32[]{:S(2)}, u32[]{:S(2)}) %collective-permute-start.45) | collective-permute-done | bytes 331808 | tf_op jit(solution)/shard_map/ppermute | solution.py:319
  326.2 3.4 collective-permute-start.50
  331.0 3.8 %collective-permute-start.53 = (bf16[3,96,192]{2,1,0:T(8,128)(2,1)S(1)}, bf16[3,96,192]{2,1,0:T(8,128)(2,1)S(1)}, u32[]{:S(2)}, u32[]{:S(2)}) collective-permute-start(bf16[3,96,192]{2,1,0:T(8,128)(2,1)S(1)} %get-tuple-element.368), channel_id=1, source_target_pairs={{0,2},{1,3},{2,0},{3,1},{4,6},{5,7},{6,4},{7,5},{8,10},{9,11},{10,... | collective-permute-start | bytes 331784 | tf_op jit(solution)/shard_map/ppermute | solution.py:319
  340.9 4.8 %collective-permute-done.53 = bf16[3,96,192]{2,1,0:T(8,128)(2,1)S(1)} collective-permute-done((bf16[3,96,192]{2,1,0:T(8,128)(2,1)S(1)}, bf16[3,96,192]{2,1,0:T(8,128)(2,1)S(1)}, u32[]{:S(2)}, u32[]{:S(2)}) %collective-permute-start.53) | collective-permute-done | bytes 110624 | tf_op jit(solution)/shard_map/ppermute | solution.py:319
  (257 shorter events, 112.1 us)
Async XLA Ops:
  6.7 16.4 %collective-permute-start.1 = (bf16[192,768]{1,0:T(8,128)(2,1)S(1)}, bf16[192,768]{1,0:T(8,128)(2,1)S(1)}, u32[]{:S(2)}, u32[]{:S(2)}) collective-permute-start(bf16[192,768]{1,0:T(8,128)(2,1)S(1)} %pad_maximum_fusion.9), channel_id=1, source_target_pairs={{0,1},{1,0},{2,3},{3,2},{4,5},{5,4},{6,7},{7,6},{8,9},{9,8},{10,11... | collective-permute-start | bytes 884744 | tf_op jit(solution)/shard_map/ppermute | solution.py:319
  30.7 17.8 %collective-permute-start.3 = (bf16[512,768]{1,0:T(8,128)(2,1)S(1)}, bf16[512,768]{1,0:T(8,128)(2,1)S(1)}, u32[]{:S(2)}, u32[]{:S(2)}) collective-permute-start(bf16[512,768]{1,0:T(8,128)(2,1)S(1)} %add_convert_fusion.2.refs_0_), channel_id=1, source_target_pairs={{0,1},{1,2},{2,3},{4,5},{5,6},{6,7},{8,9},{9,10},{10,11},{12,13},{... | collective-permute-start | bytes 2359304 | tf_op jit(solution)/shard_map/ppermute | solution.py:1089
  34.0 22.4 %collective-permute-start.4 = (bf16[512,768]{1,0:T(8,128)(2,1)S(1)}, bf16[512,768]{1,0:T(8,128)(2,1)S(1)}, u32[]{:S(2)}, u32[]{:S(2)}) collective-permute-start(bf16[512,768]{1,0:T(8,128)(2,1)S(1)} %add_convert_fusion.2.refs_0_), channel_id=1, source_target_pairs={{1,0},{2,1},{3,2},{5,4},{6,5},{7,6},{9,8},{10,9},{11,10},{13,12},{... | collective-permute-start | bytes 2359304 | tf_op jit(solution)/shard_map/ppermute | solution.py:1089
  37.3 28.5 %collective-permute-start.12 = (bf16[384,768]{1,0:T(8,128)(2,1)}, bf16[384,768]{1,0:T(8,128)(2,1)}, u32[]{:S(2)}, u32[]{:S(2)}) collective-permute-start(bf16[384,768]{1,0:T(8,128)(2,1)} %collective-permute-done.7), channel_id=1, source_target_pairs={{1,0},{2,3},{5,4},{6,7},{9,8},{10,11},{13,12},{14,15},{17,16},{18,... | collective-permute-start | bytes 1769480 | tf_op jit(solution)/shard_map/ppermute | solution.py:1089
  56.4 25.4 %collective-permute-start.10 = (bf16[512,768]{1,0:T(8,128)(2,1)S(1)}, bf16[512,768]{1,0:T(8,128)(2,1)}, u32[]{:S(2)}, u32[]{:S(2)}) collective-permute-start(bf16[512,768]{1,0:T(8,128)(2,1)S(1)} %collective-permute-done.3), channel_id=1, source_target_pairs={{1,2},{2,3},{5,6},{6,7},{9,10},{10,11},{13,14},{14,15},{17,18},{18... | collective-permute-start | bytes 2359304 | tf_op jit(solution)/shard_map/ppermute | solution.py:1089
  58.7 24.4 %collective-permute-start.11 = (bf16[512,768]{1,0:T(8,128)(2,1)S(1)}, bf16[512,768]{1,0:T(8,128)(2,1)}, u32[]{:S(2)}, u32[]{:S(2)}) collective-permute-start(bf16[512,768]{1,0:T(8,128)(2,1)S(1)} %collective-permute-done.4), channel_id=1, source_target_pairs={{1,0},{2,1},{5,4},{6,5},{9,8},{10,9},{13,12},{14,13},{17,16},{18,1... | collective-permute-start | bytes 2359304 | tf_op jit(solution)/shard_map/ppermute | solution.py:1089
  67.0 17.4 %collective-permute-start.19 = (bf16[432,768]{1,0:T(8,128)(2,1)S(1)}, bf16[432,768]{1,0:T(8,128)(2,1)S(1)}, u32[]{:S(2)}, u32[]{:S(2)}) collective-permute-start(bf16[432,768]{1,0:T(8,128)(2,1)S(1)} %fusion.6), channel_id=1, source_target_pairs={{0,16},{4,20},{8,24},{12,28},{16,0},{20,4},{24,8},{28,12},{1,17},{... | collective-permute-start | bytes 1990664 | tf_op jit(solution)/shard_map/ppermute | solution.py:319
  67.6 17.1 %collective-permute-start.18 = (bf16[432,768]{1,0:T(8,128)(2,1)S(1)}, bf16[432,768]{1,0:T(8,128)(2,1)}, u32[]{:S(2)}, u32[]{:S(2)}) collective-permute-start(bf16[432,768]{1,0:T(8,128)(2,1)S(1)} %pad_maximum_fusion.4), channel_id=1, source_target_pairs={{0,8},{4,12},{8,0},{12,4},{16,24},{20,28},{24,16},{28,20},{1,9},{5... | collective-permute-start | bytes 1990664 | tf_op jit(solution)/shard_map/ppermute | solution.py:319
  86.6 39.1 %collective-permute-start.20 = (bf16[864,768]{1,0:T(8,128)(2,1)S(1)}, bf16[864,768]{1,0:T(8,128)(2,1)}, u32[]{:S(2)}, u32[]{:S(2)}) collective-permute-start(bf16[864,768]{1,0:T(8,128)(2,1)S(1)} %pad_maximum_fusion.1.refs_7_), channel_id=1, source_target_pairs={{0,16},{4,20},{8,24},{12,28},{16,0},{20,4},{24,8},{28,12},{1,17},{... | collective-permute-start | bytes 3981320 | tf_op jit(solution)/shard_map/ppermute | solution.py:319
  88.2 37.5 %collective-permute-start.21 = (bf16[864,768]{1,0:T(8,128)(2,1)S(1)}, bf16[864,768]{1,0:T(8,128)(2,1)}, u32[]{:S(2)}, u32[]{:S(2)}) collective-permute-start(bf16[864,768]{1,0:T(8,128)(2,1)S(1)} %pad_maximum_fusion.2.refs_11_), channel_id=1, source_target_pairs={{0,8},{4,12},{8,0},{12,4},{16,24},{20,28},{24,16},{28,20},{1,9},{5... | collective-permute-start | bytes 3981320 | tf_op jit(solution)/shard_map/ppermute | solution.py:319
  89.4 22.1 %collective-permute-start.17 = (bf16[512,768]{1,0:T(8,128)(2,1)S(1)}, bf16[512,768]{1,0:T(8,128)(2,1)S(1)}, u32[]{:S(2)}, u32[]{:S(2)}) collective-permute-start(bf16[512,768]{1,0:T(8,128)(2,1)S(1)} %broadcast_select_fusion.1.refs_1_.refs_2_), channel_id=1, source_target_pairs={{1,0},{2,3},{5,4},{6,7},{9,8},{10,11},{13,12},{14,15},{17,16},{18,... | collective-permute-start | bytes 2359304 | tf_op jit(solution)/shard_map/ppermute | solution.py:1089
  91.9 34.4 %collective-permute-start.22 = (bf16[864,768]{1,0:T(8,128)(2,1)S(1)}, bf16[864,768]{1,0:T(8,128)(2,1)}, u32[]{:S(2)}, u32[]{:S(2)}) collective-permute-start(bf16[864,768]{1,0:T(8,128)(2,1)S(1)} %pad_maximum_fusion.1.refs_7_), channel_id=1, source_target_pairs={{0,4},{4,0},{8,12},{12,8},{16,20},{20,16},{24,28},{28,24},{1,5},{5... | collective-permute-start | bytes 3981320 | tf_op jit(solution)/shard_map/ppermute | solution.py:319
  91.9 34.4 %collective-permute-start.24 = (bf16[864,768]{1,0:T(8,128)(2,1)S(1)}, bf16[864,768]{1,0:T(8,128)(2,1)}, u32[]{:S(2)}, u32[]{:S(2)}) collective-permute-start(bf16[864,768]{1,0:T(8,128)(2,1)S(1)} %pad_maximum_fusion.2.refs_11_), channel_id=1, source_target_pairs={{0,4},{4,0},{8,12},{12,8},{16,20},{20,16},{24,28},{28,24},{1,5},{5... | collective-permute-start | bytes 3981320 | tf_op jit(solution)/shard_map/ppermute | solution.py:319
  166.2 21.5 %collective-permute-start.27 = (bf16[5,4,96,768]{3,2,1,0:T(8,128)(2,1)}, bf16[5,4,96,768]{3,2,1,0:T(8,128)(2,1)S(1)}, u32[]{:S(2)}, u32[]{:S(2)}) collective-permute-start(bf16[5,4,96,768]{3,2,1,0:T(8,128)(2,1)} %get-tuple-element.283), channel_id=1, source_target_pairs={{0,4},{4,0},{8,12},{12,8},{16,20},{20,16},{24,28},{28,24},{1,5},{5... | collective-permute-start | bytes 8847368 | tf_op jit(solution)/shard_map/ppermute | solution.py:319
  166.4 21.3 %collective-permute-start.26 = (bf16[4,4,96,768]{3,2,1,0:T(8,128)(2,1)}, bf16[4,4,96,768]{3,2,1,0:T(8,128)(2,1)S(1)}, u32[]{:S(2)}, u32[]{:S(2)}) collective-permute-start(bf16[4,4,96,768]{3,2,1,0:T(8,128)(2,1)} %get-tuple-element.282), channel_id=1, source_target_pairs={{0,4},{4,0},{8,12},{12,8},{16,20},{20,16},{24,28},{28,24},{1,5},{5... | collective-permute-start | bytes 7077896 | tf_op jit(solution)/shard_map/ppermute | solution.py:319
  181.0 27.7 %collective-permute-start.28 = (bf16[512,768]{1,0:T(8,128)(2,1)}, bf16[512,768]{1,0:T(8,128)(2,1)S(1)}, u32[]{:S(2)}, u32[]{:S(2)}) collective-permute-start(bf16[512,768]{1,0:T(8,128)(2,1)} %get-tuple-element.288), channel_id=1, source_target_pairs={{0,1},{3,2},{4,5},{7,6},{8,9},{11,10},{12,13},{15,14},{16,17},{19,... | collective-permute-start | bytes 2359304 | tf_op jit(solution)/shard_map/ppermute | solution.py:1089
  207.9 34.3 %collective-permute-start.32 = (bf16[5,2,96,768]{3,2,1,0:T(8,128)(2,1)}, bf16[5,2,96,768]{3,2,1,0:T(8,128)(2,1)S(1)}, u32[]{:S(2)}, u32[]{:S(2)}) collective-permute-start(bf16[5,2,96,768]{3,2,1,0:T(8,128)(2,1)} %get-tuple-element.298), channel_id=1, source_target_pairs={{0,8},{4,12},{8,0},{12,4},{16,24},{20,28},{24,16},{28,20},{1,9},{5... | collective-permute-start | bytes 4423688 | tf_op jit(solution)/shard_map/ppermute | solution.py:319
  210.3 19.1 %collective-permute-start.30 = (bf16[512,768]{1,0:T(8,128)(2,1)S(1)}, bf16[512,768]{1,0:T(8,128)(2,1)S(1)}, u32[]{:S(2)}, u32[]{:S(2)}) collective-permute-start(bf16[512,768]{1,0:T(8,128)(2,1)S(1)} %add_convert_fusion.1), channel_id=1, source_target_pairs={{3,2},{2,1},{7,6},{6,5},{11,10},{10,9},{15,14},{14,13},{19,18},{18... | collective-permute-start | bytes 2359304 | tf_op jit(solution)/shard_map/ppermute | solution.py:1089
  211.1 27.7 %collective-permute-start.31 = (bf16[4,2,96,768]{3,2,1,0:T(8,128)(2,1)}, bf16[4,2,96,768]{3,2,1,0:T(8,128)(2,1)S(1)}, u32[]{:S(2)}, u32[]{:S(2)}) collective-permute-start(bf16[4,2,96,768]{3,2,1,0:T(8,128)(2,1)} %get-tuple-element.297), channel_id=1, source_target_pairs={{0,16},{4,20},{8,24},{12,28},{16,0},{20,4},{24,8},{28,12},{1,17},{... | collective-permute-start | bytes 3538952 | tf_op jit(solution)/shard_map/ppermute | solution.py:319
  212.6 18.5 %collective-permute-start.29 = (bf16[512,768]{1,0:T(8,128)(2,1)S(1)}, bf16[512,768]{1,0:T(8,128)(2,1)S(1)}, u32[]{:S(2)}, u32[]{:S(2)}) collective-permute-start(bf16[512,768]{1,0:T(8,128)(2,1)S(1)} %add_convert_fusion.1), channel_id=1, source_target_pairs={{0,1},{1,2},{4,5},{5,6},{8,9},{9,10},{12,13},{13,14},{16,17},{17,1... | collective-permute-start | bytes 2359304 | tf_op jit(solution)/shard_map/ppermute | solution.py:1089
  231.8 33.6 %collective-permute-start.33 = (bf16[512,768]{1,0:T(8,128)(2,1)S(1)}, bf16[512,768]{1,0:T(8,128)(2,1)S(1)}, u32[]{:S(2)}, u32[]{:S(2)}) collective-permute-start(bf16[512,768]{1,0:T(8,128)(2,1)S(1)} %select_convert_fusion), channel_id=1, source_target_pairs={{0,1},{1,2},{2,3},{4,5},{5,6},{6,7},{8,9},{9,10},{10,11},{12,13},{... | collective-permute-start | bytes 2359304 | tf_op jit(solution)/shard_map/ppermute | solution.py:1089
  237.2 28.2 %collective-permute-start.34 = (bf16[512,768]{1,0:T(8,128)(2,1)S(1)}, bf16[512,768]{1,0:T(8,128)(2,1)S(1)}, u32[]{:S(2)}, u32[]{:S(2)}) collective-permute-start(bf16[512,768]{1,0:T(8,128)(2,1)S(1)} %add_convert_fusion), channel_id=1, source_target_pairs={{3,2},{2,1},{1,0},{7,6},{6,5},{5,4},{11,10},{10,9},{9,8},{15,14},{... | collective-permute-start | bytes 2359304 | tf_op jit(solution)/shard_map/ppermute | solution.py:1089
  263.0 17.7 %collective-permute-start.38 = (bf16[5,1,96,768]{3,2,1,0:T(8,128)(2,1)}, bf16[5,1,96,768]{3,2,1,0:T(8,128)(2,1)}, u32[]{:S(2)}, u32[]{:S(2)}) collective-permute-start(bf16[5,1,96,768]{3,2,1,0:T(8,128)(2,1)} %get-tuple-element.316), channel_id=1, source_target_pairs={{0,16},{4,20},{8,24},{12,28},{16,0},{20,4},{24,8},{28,12},{1,17},{... | collective-permute-start | bytes 2211848 | tf_op jit(solution)/shard_map/ppermute | solution.py:319
  289.3 16.4 %collective-permute-start.41 = (bf16[3,2,96,384]{3,2,1,0:T(8,128)(2,1)}, bf16[3,2,96,384]{3,2,1,0:T(8,128)(2,1)S(1)}, u32[]{:S(2)}, u32[]{:S(2)}) collective-permute-start(bf16[3,2,96,384]{3,2,1,0:T(8,128)(2,1)} %get-tuple-element.341), channel_id=1, source_target_pairs={{0,8},{4,12},{8,0},{12,4},{16,24},{20,28},{24,16},{28,20},{1,9},{5... | collective-permute-start | bytes 1327112 | tf_op jit(solution)/shard_map/ppermute | solution.py:319
  (75 other events, 652.9 us)

commit v12 on v11

--- a/solution.py
+++ b/solution.py
@@ -769,55 +769,60 @@
 def qkv_grad_kernel(count, *refs):
     sources = refs[: 3 * count + 1]
     outs = refs[3 * count + 1 : 3 * count + 5]
-    sum_ref, held, turned, total, stage, in_sems, out_sems = refs[3 * count + 5 :]
-    first_use = [0, count] + list(range(1, count)) + list(range(count + 1, 3 * count + 1))
+    sum_ref, held, *turned, totals, stage, in_sems, out_sems = refs[3 * count + 5 :]
+    first_use = [0, count, count + 1, 2 * count + 1]
+    for n in range(1, count):
+        first_use += [n, count + 1 + n, 2 * count + 1 + n]
+    copies = {}
     for n in first_use:
-        pltpu.make_async_copy(sources[n], held.at[n], in_sems.at[n]).start()
-
-    def wait(n):
-        pltpu.make_async_copy(sources[0], held.at[n], in_sems.at[n]).wait()
-
-    def turn(n, _):
-        wait(n)
-        turned[n] = held[n].T
-        return 0
-
-    lax.fori_loop(0, count, turn, 0)
+        copies[n] = pltpu.make_async_copy(sources[n], held.at[n], in_sems.at[n])
+        copies[n].start()
+
+    def column_sum(n):
+        return jnp.sum(held[n].astype(full), axis=0, keepdims=True)
+
+    puts = []
+
+    def store(value, c):
+        for part in range(2):
+            store_split(
+                value[:, part * D // 2 : (part + 1) * D // 2],
+                stage.at[part],
+                stage.at[2 + part],
+                c,
+            )
+        for k in range(4):
+            put = pltpu.make_async_copy(stage.at[k, c], outs[k].at[c], out_sems.at[k * 3 + c])
+            put.start()
+            puts.append(put)
+
     sum_ref[...] = jnp.zeros_like(sum_ref)
-
-    def step(i, _):
-        c = (i + count - 1) // count
-        n = jnp.where(i == 0, 0, (i + count - 1) % count)
-        wait(count + i)
-        right = held[count + i]
-        value = dot_of(turned[n], right, 1, 0)
-        total[...] = value + jnp.where(n == 0, jnp.zeros_like(value), total[...])
-
-        @pl.when(c != 1)
-        def _():
-            row = pl.ds(pl.multiple_of(c * 4, 8), 1)
-            sum_ref[row, :] += jnp.sum(right.astype(full), axis=0, keepdims=True)
-
-        @pl.when(i % count == 0)
-        def _():
-            for part in range(2):
-                store_split(
-                    total[:, part * D // 2 : (part + 1) * D // 2],
-                    stage.at[part],
-                    stage.at[2 + part],
-                    c,
-                )
-            for k in range(4):
-                pltpu.make_async_copy(
-                    stage.at[k, c], outs[k].at[c], out_sems.at[k * 3 + c]
-                ).start()
-
-        return 0
-
-    lax.fori_loop(0, 2 * count + 1, step, 0)
-    for k in range(4):
-        for c in range(3):
-            pltpu.make_async_copy(stage.at[k, c], outs[k].at[c], out_sems.at[k * 3 + c]).wait()
+    copies[0].wait()
+    turned[0][...] = held[0].T
+    copies[count].wait()
+    store(dot_of(turned[0][...], held[count], 1, 0), 0)
+    sum_ref[0:1, :] = column_sum(count)
+    value_sum = jnp.zeros((1, D), full)
+    for n in range(count):
+        if n + 1 < count:
+            copies[n + 1].wait()
+        copies[count + 1 + n].wait()
+        copies[2 * count + 1 + n].wait()
+        left = turned[n % 2][...]
+        if n + 1 < count:
+            turned[(n + 1) % 2][...] = held[n + 1].T
+        for c in (1, 2):
+            value = dot_of(left, held[c * count + 1 + n], 1, 0)
+            if n > 0:
+                value = value + totals[c - 1]
+            if n + 1 < count:
+                totals[c - 1] = value
+            else:
+                store(value, c)
+        value_sum = value_sum + column_sum(2 * count + 1 + n)
+    sum_ref[8:9, :] = value_sum
+    for put in puts:
+        put.wait()
 
 
 def qkv_grads(chunks, query_grad, key_grads, value_grads, dp):
@@ -833,8 +838,9 @@
         out_specs=[anywhere] * 4 + [pl.BlockSpec(memory_space=pltpu.VMEM)],
         scratch_shapes=[
             pltpu.VMEM((3 * count + 1, rows, D), low),
-            pltpu.VMEM((count, D, rows), low),
-            pltpu.VMEM((D, D), full),
+            pltpu.VMEM((D, rows), low),
+            pltpu.VMEM((D, rows), low),
+            pltpu.VMEM((2, D, D), full),
             pltpu.VMEM((4,) + shape, low),
             pltpu.SemaphoreType.DMA((3 * count + 1,)),
             pltpu.SemaphoreType.DMA((12,)),

time: 354 us -> 354 us (level)
  transfers between devices with their start and end apart: 55 -> 55, of which waited for: 22 -> 24; matrix products, arithmetic and copies ran while one was open for 8% -> 8% of each run, Pallas kernels for 41% -> 40%
where the time goes in v12:
time: 354 us; the launch traced here: 348 us
  Pallas kernels  173 us (49%)
  starting transfers between devices  70.1 us (20%)
  waiting for transfers between devices  55.1 us (16%)
  local copies, waits for them, and re-layouts  21.4 us (6%)
  other arithmetic  19.6 us (6%)
  between operations  5.15 us (1%)
    pallas_call x4, Pallas kernels, attend_backward(): pl.pallas_call(functools.partial(backward_kernel, number, first, last, fo...  66.8 us
    pallas_call x3, Pallas kernels, attend_forward(): pl.pallas_call(functools.partial(forward_kernel, numbers, first, final),...  45.1 us
    ppermute x43, waiting for transfers between devices, swap(): return lax.ppermute(value, axis, [(i, i ^ bit) for i in range(count)])  42.7 us
    ppermute x43, starting transfers between devices, swap(): return lax.ppermute(value, axis, [(i, i ^ bit) for i in range(count)])  42.5 us
    pallas_call x1, Pallas kernels, middle_call(): pl.pallas_call(functools.partial(middle_kernel, plan, block, len(arrays))...  34.2 us
    ppermute x12, starting transfers between devices, shards(): along = lambda value, pairs: lax.ppermute(value, 'mp', pairs)  27.6 us
    ppermute x12, waiting for transfers between devices, shards(): along = lambda value, pairs: lax.ppermute(value, 'mp', pairs)  12.4 us
    unnamed x87, local copies, waits for them, and re-layouts  11.1 us
  transfers between devices with their start and end apart: 55, of which 24 were waited for; matrix products, arithmetic and copies ran while one was open for 8% of the time, Pallas kernels for 40%

profile of v12, /device:TPU:0, one launch (start us, length us, event | category | flops | bytes accessed | tf_op | source)
XLA Modules:
  0.0 347.7 jit_solution(14836292904709744542)
XLA Ops:
  30.7 3.2 collective-permute-start.3
  38.6 6.4 %collective-permute-done.8.refs_1_ = bf16[288,768]{1,0:T(8,128)(2,1)S(1)} collective-permute-done((bf16[288,768]{1,0:T(8,128)(2,1)S(1)}, bf16[288,768]{1,0:T(8,128)(2,1)S(1)}, u32[]{:S(2)}, u32[]{:S(2)}) %collective-permute-start.8) | collective-permute-done | bytes 442400 | tf_op jit(solution)/shard_map/ppermute | solution.py:319
  48.5 7.8 %collective-permute-done.4 = bf16[512,768]{1,0:T(8,128)(2,1)S(1)} collective-permute-done((bf16[512,768]{1,0:T(8,128)(2,1)S(1)}, bf16[512,768]{1,0:T(8,128)(2,1)S(1)}, u32[]{:S(2)}, u32[]{:S(2)}) %collective-permute-start.4) | collective-permute-done | bytes 786464 | tf_op jit(solution)/shard_map/ppermute | solution.py:1095
  61.6 4.1 %place.1 = (bf16[768,768]{1,0:T(8,128)(2,1)}, bf16[768,1536]{1,0:T(8,128)(2,1)}) custom-call(bf16[288,768]{1,0:T(8,128)(2,1)} %copy-done.12, bf16[288,768]{1,0:T(8,128)(2,1)} %copy-done.26, bf16[288,768]{1,0:T(8,128)(2,1)} %copy-done.28, bf16[288,768]{1,0:T(8,128)(2,1)} %copy-done.29, bf16[288,768]{1,0:T(8,128)(2,1)} %copy-done.11, ...), custom_call_target="tpu_custom_call" | custom-call | flops 1048576 | bytes 65536 | tf_op jit(solution)/shard_map/place/pallas_call | solution.py:434
  68.7 13.1 %attend_forward.3 = (bf16[512,768]{1,0:T(8,128)(2,1)}, bf16[512,768]{1,0:T(8,128)(2,1)}, bf16[512,768]{1,0:T(8,128)(2,1)}, f32[512,768]{1,0:T(8,128)}, f32[512,768]{1,0:T(8,128)}, /*index=5*/f32[512,768]{1,0:T(8,128)}) custom-call(s32[6]{0:T(128)} %stack.42.scalars.refs_0_, bf16[512,768]{1,0:T(8,128)(2,1)} %copy-done.1, ...), custom_call_target="tpu_custom_call" | custom-call | flops 1048576 | bytes 65536 | tf_op jit(solution)/shard_map/attend_forward/pallas_call | solution.py:129
  92.4 18.8 %attend_forward.4 = (bf16[512,768]{1,0:T(8,128)(2,1)}, bf16[512,768]{1,0:T(8,128)(2,1)}, bf16[512,768]{1,0:T(8,128)(2,1)}, bf16[512,768]{1,0:T(8,128)(2,1)}, f32...) custom-call(s32[6]{0:T(128)} %stack.42.scalars.refs_0_, ...), custom_call_target="tpu_custom_call" | custom-call | flops 1048576 | bytes 65536 | tf_op jit(solution)/shard_map/attend_forward/pallas_call | solution.py:129
  112.5 13.1 %attend_forward.5 = (bf16[512,768]{1,0:T(8,128)(2,1)}, bf16[512,768]{1,0:T(8,128)(2,1)}, f32[512,768]{1,0:T(8,128)}, f32[512,768]{1,0:T(8,128)}) custom-call(s32[6]{0:T(128)} %stack.42.scalars.refs_0_, bf16[512,768]{1,0:T(8,128)(2,1)} %broadcast_select_fusion.2.refs_0_.refs_3_, bf16[768,1536]{1,0:T(8,128)(2,1)} %get-tuple-element.225.refs_1_.refs_2_.refs_3_.wk_ref.wv_ref, ...), custom_call_target="tpu_custom_call" | custom-call | flops 1048576 | bytes 65536 | tf_op jit(solution)/shard_map/attend_forward/pallas_call | solution.py:129
  132.0 34.2 %middle.1 = (bf16[512,768]{1,0:T(8,128)(2,1)}, f32[512,768]{1,0:T(8,128)}, bf16[512,768]{1,0:T(8,128)(2,1)}, bf16[4,4,96,768]{3,2,1,0:T(8,128)(2,1)}, bf16[4,4,9...) custom-call(s32[6]{0:T(128)} %stack.42.scalars.refs_0_, ...), custom_call_target="tpu_custom_call" | custom-call | flops 1048576 | bytes 65536 | tf_op jit(solution)/shard_map/middle/pallas_call | solution.py:678
  166.8 14.2 %attend_backward.4 = (f32[512,768]{1,0:T(8,128)}, bf16[512,768]{1,0:T(8,128)(2,1)}, bf16[512,768]{1,0:T(8,128)(2,1)}, bf16[512,768]{1,0:T(8,128)(2,1)}) custom-call(s32[6]{0:T(128)} %stack.42.scalars.refs_0_, bf16[512,768]{1,0:T(8,128)(2,1)} %get-tuple-element.238.refs_5_.refs_4_.q_ref, bf16[512,768]{1,0:T(8,128)(2,1)} %get-tuple-element.274.k_ref, ...), custom_call_target="tpu_custom_call" | custom-call | flops 1048576 | bytes 65536 | tf_op jit(solution)/shard_map/attend_backward/pallas_call | solution.py:266
  181.0 6.6 %collective-permute-start.28 = (bf16[512,768]{1,0:T(8,128)(2,1)}, bf16[512,768]{1,0:T(8,128)(2,1)S(1)}, u32[]{:S(2)}, u32[]{:S(2)}) collective-permute-start(bf16[512,768]{1,0:T(8,128)(2,1)} %get-tuple-element.288), channel_id=1, source_target_pairs={{0,1},{3,2},{4,5},{7,6},{8,9},{11,10},{12,13},{15,14},{16,17},{19,... | collective-permute-start | bytes 2359304 | tf_op jit(solution)/shard_map/ppermute | solution.py:1095
  190.0 17.9 %attend_backward.5 = (f32[512,768]{1,0:T(8,128)}, bf16[512,768]{1,0:T(8,128)(2,1)}, bf16[512,768]{1,0:T(8,128)(2,1)}, f32[512,768]{1,0:T(8,128)}, bf16[4,2,96,76...) custom-call(s32[6]{0:T(128)} %stack.42.scalars.refs_0_, ...), custom_call_target="tpu_custom_call" | custom-call | flops 1048576 | bytes 65536 | tf_op jit(solution)/shard_map/attend_backward/pallas_call | solution.py:266
  214.5 14.6 %attend_backward.6 = (f32[512,768]{1,0:T(8,128)}, bf16[512,768]{1,0:T(8,128)(2,1)}, bf16[512,768]{1,0:T(8,128)(2,1)}, f32[512,768]{1,0:T(8,128)}) custom-call(s32[6]{0:T(128)} %stack.42.scalars.refs_0_, bf16[512,768]{1,0:T(8,128)(2,1)} %get-tuple-element.238.refs_5_.refs_4_.q_ref, bf16[512,768]{1,0:T(8,128)(2,1)} %get-tuple-element.258.k_ref, ...), custom_call_target="tpu_custom_call" | custom-call | flops 1048576 | bytes 65536 | tf_op jit(solution)/shard_map/attend_backward/pallas_call | solution.py:266
  231.5 5.5 %collective-permute-start.33 = (bf16[512,768]{1,0:T(8,128)(2,1)S(1)}, bf16[512,768]{1,0:T(8,128)(2,1)S(1)}, u32[]{:S(2)}, u32[]{:S(2)}) collective-permute-start(bf16[512,768]{1,0:T(8,128)(2,1)S(1)} %select_convert_fusion), channel_id=1, source_target_pairs={{0,1},{1,2},{2,3},{4,5},{5,6},{6,7},{8,9},{9,10},{10,11},{12,13},{... | collective-permute-start | bytes 2359304 | tf_op jit(solution)/shard_map/ppermute | solution.py:1095
  238.8 3.4 collective-permute-done.32.refs_5_
  243.3 20.1 %attend_backward.7 = (bf16[512,768]{1,0:T(8,128)(2,1)}, bf16[512,768]{1,0:T(8,128)(2,1)}, bf16[512,768]{1,0:T(8,128)(2,1)}, f32[512,768]{1,0:T(8,128)}, bf16[4,1...) custom-call(s32[6]{0:T(128)} %stack.42.scalars.refs_0_, ...), custom_call_target="tpu_custom_call" | custom-call | flops 1048576 | bytes 65536 | tf_op jit(solution)/shard_map/attend_backward/pallas_call | solution.py:266
  265.8 10.7 %qkv_grads.1 = (bf16[3,4,96,384]{3,2,1,0:T(8,128)(2,1)}, bf16[3,4,96,384]{3,2,1,0:T(8,128)(2,1)}, bf16[3,4,96,384]{3,2,1,0:T(8,128)(2,1)}, bf16[3,4,96,384]{3,2,1,0:T(8,128)(2,1)}, f32[16,768]{1,0:T(8,128)}) custom-call(bf16[512,768]{1,0:T(8,128)(2,1)} %copy-done.1, bf16[512,768]{1,0:T(8,128)(2,1)} %broadcast_select_fusion.refs_0_.refs_1_, ...), custom_call_target="tpu_custom_call" | custom-call | flops 1048576 | bytes 65536 | tf_op jit(solution)/shard_map/qkv_grads/pallas_call | solution.py:833
  285.7 4.0 %fold.2 = (bf16[3,2,96,384]{3,2,1,0:T(8,128)(2,1)}, bf16[3,2,96,384]{3,2,1,0:T(8,128)(2,1)}, bf16[3,2,96,384]{3,2,1,0:T(8,128)(2,1)}, bf16[3,2,96,384]{3,2,1,0:T(8,128)(2,1)}) custom-call(bf16[3,4,96,384]{3,2,1,0:T(8,128)(2,1)} %get-tuple-element.326.refs_0_, bf16[3,4,96,384]{3,2,1,0:T(8,128)(2,1)} %collective-permute-done.35.refs_1_, ...), custom_call_target="tpu_custom_call" | custom-call | bytes 16777216 | tf_op jit(solution)/shard_map/fold/pallas_call | solution.py:756
  292.0 5.2 %last_norm.1 = (f32[512,768]{1,0:T(8,128)}, f32[24,768]{1,0:T(8,128)}) custom-call(bf16[512,768]{1,0:T(8,128)(2,1)} %token_ref, f32[512,768]{1,0:T(8,128)} %get-tuple-element.344.first_ref, bf16[512,768]{1,0:T(8,128)(2,1)} %copy-done.20, bf16[512,768]{1,0:T(8,128)(2,1)} %copy-done.21, f32[512,768]{1,0:T(8,128)} %get-tuple-element.345.middle_ref, ...), custom_call_target="tpu_custom_call" | custom-call | flops 1048576 | bytes 65536 | tf_op jit(solution)/shard_map/last_norm/pallas_call | solution.py:894
  297.2 3.4 collective-permute-done.39
  306.4 3.3 fold.3
  313.7 4.2 %collective-permute-done.45 = bf16[216,768]{1,0:T(8,128)(2,1)S(1)} collective-permute-done((bf16[216,768]{1,0:T(8,128)(2,1)S(1)}, bf16[216,768]{1,0:T(8,128)(2,1)S(1)}, u32[]{:S(2)}, u32[]{:S(2)}) %collective-permute-start.45) | collective-permute-done | bytes 331808 | tf_op jit(solution)/shard_map/ppermute | solution.py:319
  326.7 3.4 collective-permute-start.50
  331.5 3.8 %collective-permute-start.53 = (bf16[3,96,192]{2,1,0:T(8,128)(2,1)S(1)}, bf16[3,96,192]{2,1,0:T(8,128)(2,1)S(1)}, u32[]{:S(2)}, u32[]{:S(2)}) collective-permute-start(bf16[3,96,192]{2,1,0:T(8,128)(2,1)S(1)} %get-tuple-element.368), channel_id=1, source_target_pairs={{0,2},{1,3},{2,0},{3,1},{4,6},{5,7},{6,4},{7,5},{8,10},{9,11},{10,... | collective-permute-start | bytes 331784 | tf_op jit(solution)/shard_map/ppermute | solution.py:319
  341.4 4.8 %collective-permute-done.53 = bf16[3,96,192]{2,1,0:T(8,128)(2,1)S(1)} collective-permute-done((bf16[3,96,192]{2,1,0:T(8,128)(2,1)S(1)}, bf16[3,96,192]{2,1,0:T(8,128)(2,1)S(1)}, u32[]{:S(2)}, u32[]{:S(2)}) %collective-permute-start.53) | collective-permute-done | bytes 110624 | tf_op jit(solution)/shard_map/ppermute | solution.py:319
  (257 shorter events, 116.6 us)
Async XLA Ops:
  6.7 16.4 %collective-permute-start.1 = (bf16[192,768]{1,0:T(8,128)(2,1)S(1)}, bf16[192,768]{1,0:T(8,128)(2,1)S(1)}, u32[]{:S(2)}, u32[]{:S(2)}) collective-permute-start(bf16[192,768]{1,0:T(8,128)(2,1)S(1)} %pad_maximum_fusion.9), channel_id=1, source_target_pairs={{0,1},{1,0},{2,3},{3,2},{4,5},{5,4},{6,7},{7,6},{8,9},{9,8},{10,11... | collective-permute-start | bytes 884744 | tf_op jit(solution)/shard_map/ppermute | solution.py:319
  30.7 17.8 %collective-permute-start.3 = (bf16[512,768]{1,0:T(8,128)(2,1)S(1)}, bf16[512,768]{1,0:T(8,128)(2,1)S(1)}, u32[]{:S(2)}, u32[]{:S(2)}) collective-permute-start(bf16[512,768]{1,0:T(8,128)(2,1)S(1)} %add_convert_fusion.2.refs_0_), channel_id=1, source_target_pairs={{0,1},{1,2},{2,3},{4,5},{5,6},{6,7},{8,9},{9,10},{10,11},{12,13},{... | collective-permute-start | bytes 2359304 | tf_op jit(solution)/shard_map/ppermute | solution.py:1095
  34.0 22.4 %collective-permute-start.4 = (bf16[512,768]{1,0:T(8,128)(2,1)S(1)}, bf16[512,768]{1,0:T(8,128)(2,1)S(1)}, u32[]{:S(2)}, u32[]{:S(2)}) collective-permute-start(bf16[512,768]{1,0:T(8,128)(2,1)S(1)} %add_convert_fusion.2.refs_0_), channel_id=1, source_target_pairs={{1,0},{2,1},{3,2},{5,4},{6,5},{7,6},{9,8},{10,9},{11,10},{13,12},{... | collective-permute-start | bytes 2359304 | tf_op jit(solution)/shard_map/ppermute | solution.py:1095
  37.3 28.5 %collective-permute-start.12 = (bf16[384,768]{1,0:T(8,128)(2,1)}, bf16[384,768]{1,0:T(8,128)(2,1)}, u32[]{:S(2)}, u32[]{:S(2)}) collective-permute-start(bf16[384,768]{1,0:T(8,128)(2,1)} %collective-permute-done.7), channel_id=1, source_target_pairs={{1,0},{2,3},{5,4},{6,7},{9,8},{10,11},{13,12},{14,15},{17,16},{18,... | collective-permute-start | bytes 1769480 | tf_op jit(solution)/shard_map/ppermute | solution.py:1095
  56.4 25.4 %collective-permute-start.10 = (bf16[512,768]{1,0:T(8,128)(2,1)S(1)}, bf16[512,768]{1,0:T(8,128)(2,1)}, u32[]{:S(2)}, u32[]{:S(2)}) collective-permute-start(bf16[512,768]{1,0:T(8,128)(2,1)S(1)} %collective-permute-done.3), channel_id=1, source_target_pairs={{1,2},{2,3},{5,6},{6,7},{9,10},{10,11},{13,14},{14,15},{17,18},{18... | collective-permute-start | bytes 2359304 | tf_op jit(solution)/shard_map/ppermute | solution.py:1095
  58.7 24.4 %collective-permute-start.11 = (bf16[512,768]{1,0:T(8,128)(2,1)S(1)}, bf16[512,768]{1,0:T(8,128)(2,1)}, u32[]{:S(2)}, u32[]{:S(2)}) collective-permute-start(bf16[512,768]{1,0:T(8,128)(2,1)S(1)} %collective-permute-done.4), channel_id=1, source_target_pairs={{1,0},{2,1},{5,4},{6,5},{9,8},{10,9},{13,12},{14,13},{17,16},{18,1... | collective-permute-start | bytes 2359304 | tf_op jit(solution)/shard_map/ppermute | solution.py:1095
  67.0 17.4 %collective-permute-start.19 = (bf16[432,768]{1,0:T(8,128)(2,1)S(1)}, bf16[432,768]{1,0:T(8,128)(2,1)S(1)}, u32[]{:S(2)}, u32[]{:S(2)}) collective-permute-start(bf16[432,768]{1,0:T(8,128)(2,1)S(1)} %fusion.6), channel_id=1, source_target_pairs={{0,16},{4,20},{8,24},{12,28},{16,0},{20,4},{24,8},{28,12},{1,17},{... | collective-permute-start | bytes 1990664 | tf_op jit(solution)/shard_map/ppermute | solution.py:319
  67.6 17.1 %collective-permute-start.18 = (bf16[432,768]{1,0:T(8,128)(2,1)S(1)}, bf16[432,768]{1,0:T(8,128)(2,1)}, u32[]{:S(2)}, u32[]{:S(2)}) collective-permute-start(bf16[432,768]{1,0:T(8,128)(2,1)S(1)} %pad_maximum_fusion.4), channel_id=1, source_target_pairs={{0,8},{4,12},{8,0},{12,4},{16,24},{20,28},{24,16},{28,20},{1,9},{5... | collective-permute-start | bytes 1990664 | tf_op jit(solution)/shard_map/ppermute | solution.py:319
  86.6 39.1 %collective-permute-start.20 = (bf16[864,768]{1,0:T(8,128)(2,1)S(1)}, bf16[864,768]{1,0:T(8,128)(2,1)}, u32[]{:S(2)}, u32[]{:S(2)}) collective-permute-start(bf16[864,768]{1,0:T(8,128)(2,1)S(1)} %pad_maximum_fusion.1.refs_7_), channel_id=1, source_target_pairs={{0,16},{4,20},{8,24},{12,28},{16,0},{20,4},{24,8},{28,12},{1,17},{... | collective-permute-start | bytes 3981320 | tf_op jit(solution)/shard_map/ppermute | solution.py:319
  88.2 37.5 %collective-permute-start.21 = (bf16[864,768]{1,0:T(8,128)(2,1)S(1)}, bf16[864,768]{1,0:T(8,128)(2,1)}, u32[]{:S(2)}, u32[]{:S(2)}) collective-permute-start(bf16[864,768]{1,0:T(8,128)(2,1)S(1)} %pad_maximum_fusion.2.refs_11_), channel_id=1, source_target_pairs={{0,8},{4,12},{8,0},{12,4},{16,24},{20,28},{24,16},{28,20},{1,9},{5... | collective-permute-start | bytes 3981320 | tf_op jit(solution)/shard_map/ppermute | solution.py:319
  89.4 22.1 %collective-permute-start.17 = (bf16[512,768]{1,0:T(8,128)(2,1)S(1)}, bf16[512,768]{1,0:T(8,128)(2,1)S(1)}, u32[]{:S(2)}, u32[]{:S(2)}) collective-permute-start(bf16[512,768]{1,0:T(8,128)(2,1)S(1)} %broadcast_select_fusion.1.refs_1_.refs_2_), channel_id=1, source_target_pairs={{1,0},{2,3},{5,4},{6,7},{9,8},{10,11},{13,12},{14,15},{17,16},{18,... | collective-permute-start | bytes 2359304 | tf_op jit(solution)/shard_map/ppermute | solution.py:1095
  91.9 34.4 %collective-permute-start.22 = (bf16[864,768]{1,0:T(8,128)(2,1)S(1)}, bf16[864,768]{1,0:T(8,128)(2,1)}, u32[]{:S(2)}, u32[]{:S(2)}) collective-permute-start(bf16[864,768]{1,0:T(8,128)(2,1)S(1)} %pad_maximum_fusion.1.refs_7_), channel_id=1, source_target_pairs={{0,4},{4,0},{8,12},{12,8},{16,20},{20,16},{24,28},{28,24},{1,5},{5... | collective-permute-start | bytes 3981320 | tf_op jit(solution)/shard_map/ppermute | solution.py:319
  91.9 34.4 %collective-permute-start.24 = (bf16[864,768]{1,0:T(8,128)(2,1)S(1)}, bf16[864,768]{1,0:T(8,128)(2,1)}, u32[]{:S(2)}, u32[]{:S(2)}) collective-permute-start(bf16[864,768]{1,0:T(8,128)(2,1)S(1)} %pad_maximum_fusion.2.refs_11_), channel_id=1, source_target_pairs={{0,4},{4,0},{8,12},{12,8},{16,20},{20,16},{24,28},{28,24},{1,5},{5... | collective-permute-start | bytes 3981320 | tf_op jit(solution)/shard_map/ppermute | solution.py:319
  166.2 21.5 %collective-permute-start.27 = (bf16[5,4,96,768]{3,2,1,0:T(8,128)(2,1)}, bf16[5,4,96,768]{3,2,1,0:T(8,128)(2,1)S(1)}, u32[]{:S(2)}, u32[]{:S(2)}) collective-permute-start(bf16[5,4,96,768]{3,2,1,0:T(8,128)(2,1)} %get-tuple-element.283), channel_id=1, source_target_pairs={{0,4},{4,0},{8,12},{12,8},{16,20},{20,16},{24,28},{28,24},{1,5},{5... | collective-permute-start | bytes 8847368 | tf_op jit(solution)/shard_map/ppermute | solution.py:319
  166.4 21.3 %collective-permute-start.26 = (bf16[4,4,96,768]{3,2,1,0:T(8,128)(2,1)}, bf16[4,4,96,768]{3,2,1,0:T(8,128)(2,1)S(1)}, u32[]{:S(2)}, u32[]{:S(2)}) collective-permute-start(bf16[4,4,96,768]{3,2,1,0:T(8,128)(2,1)} %get-tuple-element.282), channel_id=1, source_target_pairs={{0,4},{4,0},{8,12},{12,8},{16,20},{20,16},{24,28},{28,24},{1,5},{5... | collective-permute-start | bytes 7077896 | tf_op jit(solution)/shard_map/ppermute | solution.py:319
  181.0 27.7 %collective-permute-start.28 = (bf16[512,768]{1,0:T(8,128)(2,1)}, bf16[512,768]{1,0:T(8,128)(2,1)S(1)}, u32[]{:S(2)}, u32[]{:S(2)}) collective-permute-start(bf16[512,768]{1,0:T(8,128)(2,1)} %get-tuple-element.288), channel_id=1, source_target_pairs={{0,1},{3,2},{4,5},{7,6},{8,9},{11,10},{12,13},{15,14},{16,17},{19,... | collective-permute-start | bytes 2359304 | tf_op jit(solution)/shard_map/ppermute | solution.py:1095
  207.9 34.3 %collective-permute-start.32 = (bf16[5,2,96,768]{3,2,1,0:T(8,128)(2,1)}, bf16[5,2,96,768]{3,2,1,0:T(8,128)(2,1)S(1)}, u32[]{:S(2)}, u32[]{:S(2)}) collective-permute-start(bf16[5,2,96,768]{3,2,1,0:T(8,128)(2,1)} %get-tuple-element.298), channel_id=1, source_target_pairs={{0,8},{4,12},{8,0},{12,4},{16,24},{20,28},{24,16},{28,20},{1,9},{5... | collective-permute-start | bytes 4423688 | tf_op jit(solution)/shard_map/ppermute | solution.py:319
  210.3 18.8 %collective-permute-start.30 = (bf16[512,768]{1,0:T(8,128)(2,1)S(1)}, bf16[512,768]{1,0:T(8,128)(2,1)S(1)}, u32[]{:S(2)}, u32[]{:S(2)}) collective-permute-start(bf16[512,768]{1,0:T(8,128)(2,1)S(1)} %add_convert_fusion.1), channel_id=1, source_target_pairs={{3,2},{2,1},{7,6},{6,5},{11,10},{10,9},{15,14},{14,13},{19,18},{18... | collective-permute-start | bytes 2359304 | tf_op jit(solution)/shard_map/ppermute | solution.py:1095
  211.1 27.7 %collective-permute-start.31 = (bf16[4,2,96,768]{3,2,1,0:T(8,128)(2,1)}, bf16[4,2,96,768]{3,2,1,0:T(8,128)(2,1)S(1)}, u32[]{:S(2)}, u32[]{:S(2)}) collective-permute-start(bf16[4,2,96,768]{3,2,1,0:T(8,128)(2,1)} %get-tuple-element.297), channel_id=1, source_target_pairs={{0,16},{4,20},{8,24},{12,28},{16,0},{20,4},{24,8},{28,12},{1,17},{... | collective-permute-start | bytes 3538952 | tf_op jit(solution)/shard_map/ppermute | solution.py:319
  212.6 18.3 %collective-permute-start.29 = (bf16[512,768]{1,0:T(8,128)(2,1)S(1)}, bf16[512,768]{1,0:T(8,128)(2,1)S(1)}, u32[]{:S(2)}, u32[]{:S(2)}) collective-permute-start(bf16[512,768]{1,0:T(8,128)(2,1)S(1)} %add_convert_fusion.1), channel_id=1, source_target_pairs={{0,1},{1,2},{4,5},{5,6},{8,9},{9,10},{12,13},{13,14},{16,17},{17,1... | collective-permute-start | bytes 2359304 | tf_op jit(solution)/shard_map/ppermute | solution.py:1095
  231.5 34.3 %collective-permute-start.33 = (bf16[512,768]{1,0:T(8,128)(2,1)S(1)}, bf16[512,768]{1,0:T(8,128)(2,1)S(1)}, u32[]{:S(2)}, u32[]{:S(2)}) collective-permute-start(bf16[512,768]{1,0:T(8,128)(2,1)S(1)} %select_convert_fusion), channel_id=1, source_target_pairs={{0,1},{1,2},{2,3},{4,5},{5,6},{6,7},{8,9},{9,10},{10,11},{12,13},{... | collective-permute-start | bytes 2359304 | tf_op jit(solution)/shard_map/ppermute | solution.py:1095
  237.0 28.8 %collective-permute-start.34 = (bf16[512,768]{1,0:T(8,128)(2,1)S(1)}, bf16[512,768]{1,0:T(8,128)(2,1)S(1)}, u32[]{:S(2)}, u32[]{:S(2)}) collective-permute-start(bf16[512,768]{1,0:T(8,128)(2,1)S(1)} %add_convert_fusion), channel_id=1, source_target_pairs={{3,2},{2,1},{1,0},{7,6},{6,5},{5,4},{11,10},{10,9},{9,8},{15,14},{... | collective-permute-start | bytes 2359304 | tf_op jit(solution)/shard_map/ppermute | solution.py:1095
  263.4 17.7 %collective-permute-start.38 = (bf16[5,1,96,768]{3,2,1,0:T(8,128)(2,1)}, bf16[5,1,96,768]{3,2,1,0:T(8,128)(2,1)}, u32[]{:S(2)}, u32[]{:S(2)}) collective-permute-start(bf16[5,1,96,768]{3,2,1,0:T(8,128)(2,1)} %get-tuple-element.316), channel_id=1, source_target_pairs={{0,16},{4,20},{8,24},{12,28},{16,0},{20,4},{24,8},{28,12},{1,17},{... | collective-permute-start | bytes 2211848 | tf_op jit(solution)/shard_map/ppermute | solution.py:319
  289.7 15.8 %collective-permute-start.41 = (bf16[3,2,96,384]{3,2,1,0:T(8,128)(2,1)}, bf16[3,2,96,384]{3,2,1,0:T(8,128)(2,1)S(1)}, u32[]{:S(2)}, u32[]{:S(2)}) collective-permute-start(bf16[3,2,96,384]{3,2,1,0:T(8,128)(2,1)} %get-tuple-element.341), channel_id=1, source_target_pairs={{0,8},{4,12},{8,0},{12,4},{16,24},{20,28},{24,16},{28,20},{1,9},{5... | collective-permute-start | bytes 1327112 | tf_op jit(solution)/shard_map/ppermute | solution.py:319
  (75 other events, 647.8 us)

commit v13 on v11

--- a/solution.py
+++ b/solution.py
@@ -73,6 +73,7 @@
         value_outs[n][...] = values[n]
     rows = q_pair.shape[0]
     size = keys[0].shape[0]
+    values = [jnp.concatenate([value, jnp.ones((size, PAIR), low)], axis=1) for value in values]
     place = lax.broadcasted_iota(jnp.int32, (1, size), 1)
     lower = first_half((rows, PAIR))
     parts = []
@@ -86,13 +87,12 @@
         highest = functools.reduce(
             jnp.maximum, [jnp.max(score, axis=-1, keepdims=True) for score in scores]
         )
-        totals = jnp.zeros_like(highest)
-        mixed = jnp.zeros((rows, PAIR), full)
+        weighed = None
         for n in range(count):
-            exp_scores = jnp.exp(scores[n] - highest)
-            totals = totals + jnp.sum(exp_scores, axis=-1, keepdims=True)
-            mixed = mixed + dot_of(exp_scores.astype(low), values[n], 1, 0)
-        parts.append((highest, totals, mixed))
+            exp_scores = jnp.exp(scores[n] - highest).astype(low)
+            part = dot_of(exp_scores, values[n], 1, 0)
+            weighed = part if weighed is None else weighed + part
+        parts.append((highest, weighed[:, PAIR:], weighed[:, :PAIR]))
     top = jnp.where(lower, parts[0][0], parts[1][0])
     total = jnp.where(lower, parts[0][1], parts[1][1])
     mixed = jnp.where(lower, parts[0][2], parts[1][2])

time: 354 us -> 353 us (level)
  transfers between devices with their start and end apart: 55 -> 55, of which waited for: 22 -> 22; matrix products, arithmetic and copies ran while one was open for 8% -> 8% of each run, Pallas kernels for 41% -> 40%
where the time goes in v13:
time: 353 us; the launch traced here: 347 us
  Pallas kernels  174 us (49%)
  starting transfers between devices  68.8 us (19%)
  waiting for transfers between devices  53.9 us (15%)
  local copies, waits for them, and re-layouts  21.5 us (6%)
  other arithmetic  19.6 us (6%)
  between operations  5.39 us (2%)
    pallas_call x4, Pallas kernels, attend_backward(): pl.pallas_call(functools.partial(backward_kernel, number, first, last, fo...  66.7 us
    pallas_call x3, Pallas kernels, attend_forward(): pl.pallas_call(functools.partial(forward_kernel, numbers, first, final),...  44.1 us
    ppermute x43, starting transfers between devices, swap(): return lax.ppermute(value, axis, [(i, i ^ bit) for i in range(count)])  41.8 us
    ppermute x43, waiting for transfers between devices, swap(): return lax.ppermute(value, axis, [(i, i ^ bit) for i in range(count)])  40.8 us
    pallas_call x1, Pallas kernels, middle_call(): pl.pallas_call(functools.partial(middle_kernel, plan, block, len(arrays))...  34.2 us
    ppermute x12, starting transfers between devices, shards(): along = lambda value, pairs: lax.ppermute(value, 'mp', pairs)  26.9 us
    pallas_call x1, Pallas kernels, qkv_grads(): pl.pallas_call(functools.partial(qkv_grad_kernel, count), out_shape=[jax....  13.1 us
    ppermute x12, waiting for transfers between devices, shards(): along = lambda value, pairs: lax.ppermute(value, 'mp', pairs)  13 us
  transfers between devices with their start and end apart: 55, of which 22 were waited for; matrix products, arithmetic and copies ran while one was open for 8% of the time, Pallas kernels for 40%

profile of v13, /device:TPU:0, one launch (start us, length us, event | category | flops | bytes accessed | tf_op | source)
XLA Modules:
  0.0 346.5 jit_solution(11554516878557752494)
XLA Ops:
  30.7 3.2 collective-permute-start.3
  38.6 6.4 %collective-permute-done.8.refs_1_ = bf16[288,768]{1,0:T(8,128)(2,1)S(1)} collective-permute-done((bf16[288,768]{1,0:T(8,128)(2,1)S(1)}, bf16[288,768]{1,0:T(8,128)(2,1)S(1)}, u32[]{:S(2)}, u32[]{:S(2)}) %collective-permute-start.8) | collective-permute-done | bytes 442400 | tf_op jit(solution)/shard_map/ppermute | solution.py:319
  48.5 7.8 %collective-permute-done.4 = bf16[512,768]{1,0:T(8,128)(2,1)S(1)} collective-permute-done((bf16[512,768]{1,0:T(8,128)(2,1)S(1)}, bf16[512,768]{1,0:T(8,128)(2,1)S(1)}, u32[]{:S(2)}, u32[]{:S(2)}) %collective-permute-start.4) | collective-permute-done | bytes 786464 | tf_op jit(solution)/shard_map/ppermute | solution.py:1089
  61.6 4.1 %place.1 = (bf16[768,768]{1,0:T(8,128)(2,1)}, bf16[768,1536]{1,0:T(8,128)(2,1)}) custom-call(bf16[288,768]{1,0:T(8,128)(2,1)} %copy-done.12, bf16[288,768]{1,0:T(8,128)(2,1)} %copy-done.26, bf16[288,768]{1,0:T(8,128)(2,1)} %copy-done.28, bf16[288,768]{1,0:T(8,128)(2,1)} %copy-done.29, bf16[288,768]{1,0:T(8,128)(2,1)} %copy-done.11, ...), custom_call_target="tpu_custom_call" | custom-call | flops 1048576 | bytes 65536 | tf_op jit(solution)/shard_map/place/pallas_call | solution.py:434
  68.7 13.0 %attend_forward.3 = (bf16[512,768]{1,0:T(8,128)(2,1)}, bf16[512,768]{1,0:T(8,128)(2,1)}, bf16[512,768]{1,0:T(8,128)(2,1)}, f32[512,768]{1,0:T(8,128)}, f32[512,768]{1,0:T(8,128)}, /*index=5*/f32[512,768]{1,0:T(8,128)}) custom-call(s32[6]{0:T(128)} %stack.42.scalars.refs_0_, bf16[512,768]{1,0:T(8,128)(2,1)} %copy-done.1, ...), custom_call_target="tpu_custom_call" | custom-call | flops 1048576 | bytes 65536 | tf_op jit(solution)/shard_map/attend_forward/pallas_call | solution.py:129
  92.4 18.2 %attend_forward.4 = (bf16[512,768]{1,0:T(8,128)(2,1)}, bf16[512,768]{1,0:T(8,128)(2,1)}, bf16[512,768]{1,0:T(8,128)(2,1)}, bf16[512,768]{1,0:T(8,128)(2,1)}, f32...) custom-call(s32[6]{0:T(128)} %stack.42.scalars.refs_0_, ...), custom_call_target="tpu_custom_call" | custom-call | flops 1048576 | bytes 65536 | tf_op jit(solution)/shard_map/attend_forward/pallas_call | solution.py:129
  112.5 12.9 %attend_forward.5 = (bf16[512,768]{1,0:T(8,128)(2,1)}, bf16[512,768]{1,0:T(8,128)(2,1)}, f32[512,768]{1,0:T(8,128)}, f32[512,768]{1,0:T(8,128)}) custom-call(s32[6]{0:T(128)} %stack.42.scalars.refs_0_, bf16[512,768]{1,0:T(8,128)(2,1)} %broadcast_select_fusion.2.refs_0_.refs_3_, bf16[768,1536]{1,0:T(8,128)(2,1)} %get-tuple-element.225.refs_1_.refs_2_.refs_3_.wk_ref.wv_ref, ...), custom_call_target="tpu_custom_call" | custom-call | flops 1048576 | bytes 65536 | tf_op jit(solution)/shard_map/attend_forward/pallas_call | solution.py:129
  131.8 34.2 %middle.1 = (bf16[512,768]{1,0:T(8,128)(2,1)}, f32[512,768]{1,0:T(8,128)}, bf16[512,768]{1,0:T(8,128)(2,1)}, bf16[4,4,96,768]{3,2,1,0:T(8,128)(2,1)}, bf16[4,4,9...) custom-call(s32[6]{0:T(128)} %stack.42.scalars.refs_0_, ...), custom_call_target="tpu_custom_call" | custom-call | flops 1048576 | bytes 65536 | tf_op jit(solution)/shard_map/middle/pallas_call | solution.py:678
  166.5 14.2 %attend_backward.4 = (f32[512,768]{1,0:T(8,128)}, bf16[512,768]{1,0:T(8,128)(2,1)}, bf16[512,768]{1,0:T(8,128)(2,1)}, bf16[512,768]{1,0:T(8,128)(2,1)}) custom-call(s32[6]{0:T(128)} %stack.42.scalars.refs_0_, bf16[512,768]{1,0:T(8,128)(2,1)} %get-tuple-element.238.refs_5_.refs_4_.q_ref, bf16[512,768]{1,0:T(8,128)(2,1)} %get-tuple-element.274.k_ref, ...), custom_call_target="tpu_custom_call" | custom-call | flops 1048576 | bytes 65536 | tf_op jit(solution)/shard_map/attend_backward/pallas_call | solution.py:266
  180.8 6.0 %collective-permute-start.28 = (bf16[512,768]{1,0:T(8,128)(2,1)}, bf16[512,768]{1,0:T(8,128)(2,1)S(1)}, u32[]{:S(2)}, u32[]{:S(2)}) collective-permute-start(bf16[512,768]{1,0:T(8,128)(2,1)} %get-tuple-element.288), channel_id=1, source_target_pairs={{0,1},{3,2},{4,5},{7,6},{8,9},{11,10},{12,13},{15,14},{16,17},{19,... | collective-permute-start | bytes 2359304 | tf_op jit(solution)/shard_map/ppermute | solution.py:1089
  189.1 17.9 %attend_backward.5 = (f32[512,768]{1,0:T(8,128)}, bf16[512,768]{1,0:T(8,128)(2,1)}, bf16[512,768]{1,0:T(8,128)(2,1)}, f32[512,768]{1,0:T(8,128)}, bf16[4,2,96,76...) custom-call(s32[6]{0:T(128)} %stack.42.scalars.refs_0_, ...), custom_call_target="tpu_custom_call" | custom-call | flops 1048576 | bytes 65536 | tf_op jit(solution)/shard_map/attend_backward/pallas_call | solution.py:266
  213.5 14.9 %attend_backward.6 = (f32[512,768]{1,0:T(8,128)}, bf16[512,768]{1,0:T(8,128)(2,1)}, bf16[512,768]{1,0:T(8,128)(2,1)}, f32[512,768]{1,0:T(8,128)}) custom-call(s32[6]{0:T(128)} %stack.42.scalars.refs_0_, bf16[512,768]{1,0:T(8,128)(2,1)} %get-tuple-element.238.refs_5_.refs_4_.q_ref, bf16[512,768]{1,0:T(8,128)(2,1)} %get-tuple-element.258.k_ref, ...), custom_call_target="tpu_custom_call" | custom-call | flops 1048576 | bytes 65536 | tf_op jit(solution)/shard_map/attend_backward/pallas_call | solution.py:266
  230.8 5.5 %collective-permute-start.33 = (bf16[512,768]{1,0:T(8,128)(2,1)S(1)}, bf16[512,768]{1,0:T(8,128)(2,1)S(1)}, u32[]{:S(2)}, u32[]{:S(2)}) collective-permute-start(bf16[512,768]{1,0:T(8,128)(2,1)S(1)} %select_convert_fusion), channel_id=1, source_target_pairs={{0,1},{1,2},{2,3},{4,5},{5,6},{6,7},{8,9},{9,10},{10,11},{12,13},{... | collective-permute-start | bytes 2359304 | tf_op jit(solution)/shard_map/ppermute | solution.py:1089
  237.8 3.5 %collective-permute-done.32.refs_5_ = bf16[5,2,96,768]{3,2,1,0:T(8,128)(2,1)S(1)} collective-permute-done((bf16[5,2,96,768]{3,2,1,0:T(8,128)(2,1)}, bf16[5,2,96,768]{3,2,1,0:T(8,128)(2,1)S(1)}, u32[]{:S(2)}, u32[]{:S(2)}) %collective-permute-start.32) | collective-permute-done | bytes 1474592 | tf_op jit(solution)/shard_map/ppermute | solution.py:319
  242.4 19.7 %attend_backward.7 = (bf16[512,768]{1,0:T(8,128)(2,1)}, bf16[512,768]{1,0:T(8,128)(2,1)}, bf16[512,768]{1,0:T(8,128)(2,1)}, f32[512,768]{1,0:T(8,128)}, bf16[4,1...) custom-call(s32[6]{0:T(128)} %stack.42.scalars.refs_0_, ...), custom_call_target="tpu_custom_call" | custom-call | flops 1048576 | bytes 65536 | tf_op jit(solution)/shard_map/attend_backward/pallas_call | solution.py:266
  264.4 13.1 %qkv_grads.1 = (bf16[3,4,96,384]{3,2,1,0:T(8,128)(2,1)}, bf16[3,4,96,384]{3,2,1,0:T(8,128)(2,1)}, bf16[3,4,96,384]{3,2,1,0:T(8,128)(2,1)}, bf16[3,4,96,384]{3,2,1,0:T(8,128)(2,1)}, f32[16,768]{1,0:T(8,128)}) custom-call(bf16[512,768]{1,0:T(8,128)(2,1)} %copy-done.1, bf16[512,768]{1,0:T(8,128)(2,1)} %broadcast_select_fusion.refs_0_.refs_1_, ...), custom_call_target="tpu_custom_call" | custom-call | flops 1048576 | bytes 65536 | tf_op jit(solution)/shard_map/qkv_grads/pallas_call | solution.py:828
  284.4 4.0 %fold.2 = (bf16[3,2,96,384]{3,2,1,0:T(8,128)(2,1)}, bf16[3,2,96,384]{3,2,1,0:T(8,128)(2,1)}, bf16[3,2,96,384]{3,2,1,0:T(8,128)(2,1)}, bf16[3,2,96,384]{3,2,1,0:T(8,128)(2,1)}) custom-call(bf16[3,4,96,384]{3,2,1,0:T(8,128)(2,1)} %get-tuple-element.326.refs_0_, bf16[3,4,96,384]{3,2,1,0:T(8,128)(2,1)} %collective-permute-done.35.refs_1_, ...), custom_call_target="tpu_custom_call" | custom-call | bytes 16777216 | tf_op jit(solution)/shard_map/fold/pallas_call | solution.py:756
  290.6 5.2 %last_norm.1 = (f32[512,768]{1,0:T(8,128)}, f32[24,768]{1,0:T(8,128)}) custom-call(bf16[512,768]{1,0:T(8,128)(2,1)} %token_ref, f32[512,768]{1,0:T(8,128)} %get-tuple-element.344.first_ref, bf16[512,768]{1,0:T(8,128)(2,1)} %copy-done.20, bf16[512,768]{1,0:T(8,128)(2,1)} %copy-done.21, f32[512,768]{1,0:T(8,128)} %get-tuple-element.345.middle_ref, ...), custom_call_target="tpu_custom_call" | custom-call | flops 1048576 | bytes 65536 | tf_op jit(solution)/shard_map/last_norm/pallas_call | solution.py:888
  295.8 3.9 %collective-permute-done.39 = bf16[2,216,768]{2,1,0:T(8,128)(2,1)} collective-permute-done((bf16[2,216,768]{2,1,0:T(8,128)(2,1)S(1)}, bf16[2,216,768]{2,1,0:T(8,128)(2,1)}, u32[]{:S(2)}, u32[]{:S(2)}) %collective-permute-start.39) | collective-permute-done | bytes 663584 | tf_op jit(solution)/shard_map/ppermute | solution.py:319
  305.6 3.2 fold.3
  312.2 5.6 %collective-permute-done.45 = bf16[216,768]{1,0:T(8,128)(2,1)S(1)} collective-permute-done((bf16[216,768]{1,0:T(8,128)(2,1)S(1)}, bf16[216,768]{1,0:T(8,128)(2,1)S(1)}, u32[]{:S(2)}, u32[]{:S(2)}) %collective-permute-start.45) | collective-permute-done | bytes 331808 | tf_op jit(solution)/shard_map/ppermute | solution.py:319
  325.2 3.4 collective-permute-start.50
  330.1 3.8 %collective-permute-start.53 = (bf16[3,96,192]{2,1,0:T(8,128)(2,1)S(1)}, bf16[3,96,192]{2,1,0:T(8,128)(2,1)S(1)}, u32[]{:S(2)}, u32[]{:S(2)}) collective-permute-start(bf16[3,96,192]{2,1,0:T(8,128)(2,1)S(1)} %get-tuple-element.368), channel_id=1, source_target_pairs={{0,2},{1,3},{2,0},{3,1},{4,6},{5,7},{6,4},{7,5},{8,10},{9,11},{10,... | collective-permute-start | bytes 331784 | tf_op jit(solution)/shard_map/ppermute | solution.py:319
  340.0 4.8 %collective-permute-done.53 = bf16[3,96,192]{2,1,0:T(8,128)(2,1)S(1)} collective-permute-done((bf16[3,96,192]{2,1,0:T(8,128)(2,1)S(1)}, bf16[3,96,192]{2,1,0:T(8,128)(2,1)S(1)}, u32[]{:S(2)}, u32[]{:S(2)}) %collective-permute-start.53) | collective-permute-done | bytes 110624 | tf_op jit(solution)/shard_map/ppermute | solution.py:319
  (257 shorter events, 112.9 us)
Async XLA Ops:
  6.7 16.4 %collective-permute-start.1 = (bf16[192,768]{1,0:T(8,128)(2,1)S(1)}, bf16[192,768]{1,0:T(8,128)(2,1)S(1)}, u32[]{:S(2)}, u32[]{:S(2)}) collective-permute-start(bf16[192,768]{1,0:T(8,128)(2,1)S(1)} %pad_maximum_fusion.9), channel_id=1, source_target_pairs={{0,1},{1,0},{2,3},{3,2},{4,5},{5,4},{6,7},{7,6},{8,9},{9,8},{10,11... | collective-permute-start | bytes 884744 | tf_op jit(solution)/shard_map/ppermute | solution.py:319
  30.7 17.8 %collective-permute-start.3 = (bf16[512,768]{1,0:T(8,128)(2,1)S(1)}, bf16[512,768]{1,0:T(8,128)(2,1)S(1)}, u32[]{:S(2)}, u32[]{:S(2)}) collective-permute-start(bf16[512,768]{1,0:T(8,128)(2,1)S(1)} %add_convert_fusion.2.refs_0_), channel_id=1, source_target_pairs={{0,1},{1,2},{2,3},{4,5},{5,6},{6,7},{8,9},{9,10},{10,11},{12,13},{... | collective-permute-start | bytes 2359304 | tf_op jit(solution)/shard_map/ppermute | solution.py:1089
  34.0 22.4 %collective-permute-start.4 = (bf16[512,768]{1,0:T(8,128)(2,1)S(1)}, bf16[512,768]{1,0:T(8,128)(2,1)S(1)}, u32[]{:S(2)}, u32[]{:S(2)}) collective-permute-start(bf16[512,768]{1,0:T(8,128)(2,1)S(1)} %add_convert_fusion.2.refs_0_), channel_id=1, source_target_pairs={{1,0},{2,1},{3,2},{5,4},{6,5},{7,6},{9,8},{10,9},{11,10},{13,12},{... | collective-permute-start | bytes 2359304 | tf_op jit(solution)/shard_map/ppermute | solution.py:1089
  37.3 28.5 %collective-permute-start.12 = (bf16[384,768]{1,0:T(8,128)(2,1)}, bf16[384,768]{1,0:T(8,128)(2,1)}, u32[]{:S(2)}, u32[]{:S(2)}) collective-permute-start(bf16[384,768]{1,0:T(8,128)(2,1)} %collective-permute-done.7), channel_id=1, source_target_pairs={{1,0},{2,3},{5,4},{6,7},{9,8},{10,11},{13,12},{14,15},{17,16},{18,... | collective-permute-start | bytes 1769480 | tf_op jit(solution)/shard_map/ppermute | solution.py:1089
  56.4 25.4 %collective-permute-start.10 = (bf16[512,768]{1,0:T(8,128)(2,1)S(1)}, bf16[512,768]{1,0:T(8,128)(2,1)}, u32[]{:S(2)}, u32[]{:S(2)}) collective-permute-start(bf16[512,768]{1,0:T(8,128)(2,1)S(1)} %collective-permute-done.3), channel_id=1, source_target_pairs={{1,2},{2,3},{5,6},{6,7},{9,10},{10,11},{13,14},{14,15},{17,18},{18... | collective-permute-start | bytes 2359304 | tf_op jit(solution)/shard_map/ppermute | solution.py:1089
  58.7 24.4 %collective-permute-start.11 = (bf16[512,768]{1,0:T(8,128)(2,1)S(1)}, bf16[512,768]{1,0:T(8,128)(2,1)}, u32[]{:S(2)}, u32[]{:S(2)}) collective-permute-start(bf16[512,768]{1,0:T(8,128)(2,1)S(1)} %collective-permute-done.4), channel_id=1, source_target_pairs={{1,0},{2,1},{5,4},{6,5},{9,8},{10,9},{13,12},{14,13},{17,16},{18,1... | collective-permute-start | bytes 2359304 | tf_op jit(solution)/shard_map/ppermute | solution.py:1089
  67.0 17.4 %collective-permute-start.19 = (bf16[432,768]{1,0:T(8,128)(2,1)S(1)}, bf16[432,768]{1,0:T(8,128)(2,1)S(1)}, u32[]{:S(2)}, u32[]{:S(2)}) collective-permute-start(bf16[432,768]{1,0:T(8,128)(2,1)S(1)} %fusion.6), channel_id=1, source_target_pairs={{0,16},{4,20},{8,24},{12,28},{16,0},{20,4},{24,8},{28,12},{1,17},{... | collective-permute-start | bytes 1990664 | tf_op jit(solution)/shard_map/ppermute | solution.py:319
  67.6 17.1 %collective-permute-start.18 = (bf16[432,768]{1,0:T(8,128)(2,1)S(1)}, bf16[432,768]{1,0:T(8,128)(2,1)}, u32[]{:S(2)}, u32[]{:S(2)}) collective-permute-start(bf16[432,768]{1,0:T(8,128)(2,1)S(1)} %pad_maximum_fusion.4), channel_id=1, source_target_pairs={{0,8},{4,12},{8,0},{12,4},{16,24},{20,28},{24,16},{28,20},{1,9},{5... | collective-permute-start | bytes 1990664 | tf_op jit(solution)/shard_map/ppermute | solution.py:319
  86.6 38.8 %collective-permute-start.20 = (bf16[864,768]{1,0:T(8,128)(2,1)S(1)}, bf16[864,768]{1,0:T(8,128)(2,1)}, u32[]{:S(2)}, u32[]{:S(2)}) collective-permute-start(bf16[864,768]{1,0:T(8,128)(2,1)S(1)} %pad_maximum_fusion.1.refs_7_), channel_id=1, source_target_pairs={{0,16},{4,20},{8,24},{12,28},{16,0},{20,4},{24,8},{28,12},{1,17},{... | collective-permute-start | bytes 3981320 | tf_op jit(solution)/shard_map/ppermute | solution.py:319
  88.2 37.2 %collective-permute-start.21 = (bf16[864,768]{1,0:T(8,128)(2,1)S(1)}, bf16[864,768]{1,0:T(8,128)(2,1)}, u32[]{:S(2)}, u32[]{:S(2)}) collective-permute-start(bf16[864,768]{1,0:T(8,128)(2,1)S(1)} %pad_maximum_fusion.2.refs_11_), channel_id=1, source_target_pairs={{0,8},{4,12},{8,0},{12,4},{16,24},{20,28},{24,16},{28,20},{1,9},{5... | collective-permute-start | bytes 3981320 | tf_op jit(solution)/shard_map/ppermute | solution.py:319
  89.4 22.1 %collective-permute-start.17 = (bf16[512,768]{1,0:T(8,128)(2,1)S(1)}, bf16[512,768]{1,0:T(8,128)(2,1)S(1)}, u32[]{:S(2)}, u32[]{:S(2)}) collective-permute-start(bf16[512,768]{1,0:T(8,128)(2,1)S(1)} %broadcast_select_fusion.1.refs_1_.refs_2_), channel_id=1, source_target_pairs={{1,0},{2,3},{5,4},{6,7},{9,8},{10,11},{13,12},{14,15},{17,16},{18,... | collective-permute-start | bytes 2359304 | tf_op jit(solution)/shard_map/ppermute | solution.py:1089
  91.9 34.1 %collective-permute-start.22 = (bf16[864,768]{1,0:T(8,128)(2,1)S(1)}, bf16[864,768]{1,0:T(8,128)(2,1)}, u32[]{:S(2)}, u32[]{:S(2)}) collective-permute-start(bf16[864,768]{1,0:T(8,128)(2,1)S(1)} %pad_maximum_fusion.1.refs_7_), channel_id=1, source_target_pairs={{0,4},{4,0},{8,12},{12,8},{16,20},{20,16},{24,28},{28,24},{1,5},{5... | collective-permute-start | bytes 3981320 | tf_op jit(solution)/shard_map/ppermute | solution.py:319
  91.9 34.1 %collective-permute-start.24 = (bf16[864,768]{1,0:T(8,128)(2,1)S(1)}, bf16[864,768]{1,0:T(8,128)(2,1)}, u32[]{:S(2)}, u32[]{:S(2)}) collective-permute-start(bf16[864,768]{1,0:T(8,128)(2,1)S(1)} %pad_maximum_fusion.2.refs_11_), channel_id=1, source_target_pairs={{0,4},{4,0},{8,12},{12,8},{16,20},{20,16},{24,28},{28,24},{1,5},{5... | collective-permute-start | bytes 3981320 | tf_op jit(solution)/shard_map/ppermute | solution.py:319
  165.9 20.9 %collective-permute-start.27 = (bf16[5,4,96,768]{3,2,1,0:T(8,128)(2,1)}, bf16[5,4,96,768]{3,2,1,0:T(8,128)(2,1)S(1)}, u32[]{:S(2)}, u32[]{:S(2)}) collective-permute-start(bf16[5,4,96,768]{3,2,1,0:T(8,128)(2,1)} %get-tuple-element.283), channel_id=1, source_target_pairs={{0,4},{4,0},{8,12},{12,8},{16,20},{20,16},{24,28},{28,24},{1,5},{5... | collective-permute-start | bytes 8847368 | tf_op jit(solution)/shard_map/ppermute | solution.py:319
  166.1 20.6 %collective-permute-start.26 = (bf16[4,4,96,768]{3,2,1,0:T(8,128)(2,1)}, bf16[4,4,96,768]{3,2,1,0:T(8,128)(2,1)S(1)}, u32[]{:S(2)}, u32[]{:S(2)}) collective-permute-start(bf16[4,4,96,768]{3,2,1,0:T(8,128)(2,1)} %get-tuple-element.282), channel_id=1, source_target_pairs={{0,4},{4,0},{8,12},{12,8},{16,20},{20,16},{24,28},{28,24},{1,5},{5... | collective-permute-start | bytes 7077896 | tf_op jit(solution)/shard_map/ppermute | solution.py:319
  180.8 27.0 %collective-permute-start.28 = (bf16[512,768]{1,0:T(8,128)(2,1)}, bf16[512,768]{1,0:T(8,128)(2,1)S(1)}, u32[]{:S(2)}, u32[]{:S(2)}) collective-permute-start(bf16[512,768]{1,0:T(8,128)(2,1)} %get-tuple-element.288), channel_id=1, source_target_pairs={{0,1},{3,2},{4,5},{7,6},{8,9},{11,10},{12,13},{15,14},{16,17},{19,... | collective-permute-start | bytes 2359304 | tf_op jit(solution)/shard_map/ppermute | solution.py:1089
  206.9 34.3 %collective-permute-start.32 = (bf16[5,2,96,768]{3,2,1,0:T(8,128)(2,1)}, bf16[5,2,96,768]{3,2,1,0:T(8,128)(2,1)S(1)}, u32[]{:S(2)}, u32[]{:S(2)}) collective-permute-start(bf16[5,2,96,768]{3,2,1,0:T(8,128)(2,1)} %get-tuple-element.298), channel_id=1, source_target_pairs={{0,8},{4,12},{8,0},{12,4},{16,24},{20,28},{24,16},{28,20},{1,9},{5... | collective-permute-start | bytes 4423688 | tf_op jit(solution)/shard_map/ppermute | solution.py:319
  209.3 19.1 %collective-permute-start.30 = (bf16[512,768]{1,0:T(8,128)(2,1)S(1)}, bf16[512,768]{1,0:T(8,128)(2,1)S(1)}, u32[]{:S(2)}, u32[]{:S(2)}) collective-permute-start(bf16[512,768]{1,0:T(8,128)(2,1)S(1)} %add_convert_fusion.1), channel_id=1, source_target_pairs={{3,2},{2,1},{7,6},{6,5},{11,10},{10,9},{15,14},{14,13},{19,18},{18... | collective-permute-start | bytes 2359304 | tf_op jit(solution)/shard_map/ppermute | solution.py:1089
  210.0 27.7 %collective-permute-start.31 = (bf16[4,2,96,768]{3,2,1,0:T(8,128)(2,1)}, bf16[4,2,96,768]{3,2,1,0:T(8,128)(2,1)S(1)}, u32[]{:S(2)}, u32[]{:S(2)}) collective-permute-start(bf16[4,2,96,768]{3,2,1,0:T(8,128)(2,1)} %get-tuple-element.297), channel_id=1, source_target_pairs={{0,16},{4,20},{8,24},{12,28},{16,0},{20,4},{24,8},{28,12},{1,17},{... | collective-permute-start | bytes 3538952 | tf_op jit(solution)/shard_map/ppermute | solution.py:319
  211.6 18.5 %collective-permute-start.29 = (bf16[512,768]{1,0:T(8,128)(2,1)S(1)}, bf16[512,768]{1,0:T(8,128)(2,1)S(1)}, u32[]{:S(2)}, u32[]{:S(2)}) collective-permute-start(bf16[512,768]{1,0:T(8,128)(2,1)S(1)} %add_convert_fusion.1), channel_id=1, source_target_pairs={{0,1},{1,2},{4,5},{5,6},{8,9},{9,10},{12,13},{13,14},{16,17},{17,1... | collective-permute-start | bytes 2359304 | tf_op jit(solution)/shard_map/ppermute | solution.py:1089
  230.8 33.6 %collective-permute-start.33 = (bf16[512,768]{1,0:T(8,128)(2,1)S(1)}, bf16[512,768]{1,0:T(8,128)(2,1)S(1)}, u32[]{:S(2)}, u32[]{:S(2)}) collective-permute-start(bf16[512,768]{1,0:T(8,128)(2,1)S(1)} %select_convert_fusion), channel_id=1, source_target_pairs={{0,1},{1,2},{2,3},{4,5},{5,6},{6,7},{8,9},{9,10},{10,11},{12,13},{... | collective-permute-start | bytes 2359304 | tf_op jit(solution)/shard_map/ppermute | solution.py:1089
  236.2 28.2 %collective-permute-start.34 = (bf16[512,768]{1,0:T(8,128)(2,1)S(1)}, bf16[512,768]{1,0:T(8,128)(2,1)S(1)}, u32[]{:S(2)}, u32[]{:S(2)}) collective-permute-start(bf16[512,768]{1,0:T(8,128)(2,1)S(1)} %add_convert_fusion), channel_id=1, source_target_pairs={{3,2},{2,1},{1,0},{7,6},{6,5},{5,4},{11,10},{10,9},{9,8},{15,14},{... | collective-permute-start | bytes 2359304 | tf_op jit(solution)/shard_map/ppermute | solution.py:1089
  262.1 17.7 %collective-permute-start.38 = (bf16[5,1,96,768]{3,2,1,0:T(8,128)(2,1)}, bf16[5,1,96,768]{3,2,1,0:T(8,128)(2,1)}, u32[]{:S(2)}, u32[]{:S(2)}) collective-permute-start(bf16[5,1,96,768]{3,2,1,0:T(8,128)(2,1)} %get-tuple-element.316), channel_id=1, source_target_pairs={{0,16},{4,20},{8,24},{12,28},{16,0},{20,4},{24,8},{28,12},{1,17},{... | collective-permute-start | bytes 2211848 | tf_op jit(solution)/shard_map/ppermute | solution.py:319
  288.4 16.4 %collective-permute-start.41 = (bf16[3,2,96,384]{3,2,1,0:T(8,128)(2,1)}, bf16[3,2,96,384]{3,2,1,0:T(8,128)(2,1)S(1)}, u32[]{:S(2)}, u32[]{:S(2)}) collective-permute-start(bf16[3,2,96,384]{3,2,1,0:T(8,128)(2,1)} %get-tuple-element.341), channel_id=1, source_target_pairs={{0,8},{4,12},{8,0},{12,4},{16,24},{20,28},{24,16},{28,20},{1,9},{5... | collective-permute-start | bytes 1327112 | tf_op jit(solution)/shard_map/ppermute | solution.py:319
  (75 other events, 652.3 us)

commit v14 on v11

--- a/solution.py
+++ b/solution.py
@@ -443,14 +443,14 @@
     )(*arrays)
 
 
-def store_split(value, keep, send, index):
+def store_split(value, keep, send, index, start=0):
     block = keep.shape[2]
     even = lax.axis_index("dp") % 2 == 0
-    for outer in range(keep.shape[1]):
+    for outer in range(value.shape[0] // (2 * block)):
         first = value[2 * outer * block : (2 * outer + 1) * block]
         other = value[(2 * outer + 1) * block : (2 * outer + 2) * block]
-        keep[index, outer] = jnp.where(even, first, other).astype(low)
-        send[index, outer] = jnp.where(even, other, first).astype(low)
+        keep[index, start + outer] = jnp.where(even, first, other).astype(low)
+        send[index, start + outer] = jnp.where(even, other, first).astype(low)
 
 
 def middle_kernel(plan, block, total, *refs):
@@ -593,11 +593,16 @@
 
     def backward(m, _):
         place = pl.ds(pl.multiple_of(m * D, D), D)
-        value = slope[m] * dot_of(final_low[...], down[place, :], 1, 0)
-        value = value.astype(low)
-        right[hidden + m] = value
-        sum_ref[pl.ds(8 + m, 1), :] = jnp.sum(value.astype(full), axis=0, keepdims=True)
-        accum[...] += dot_of(value, up[place, :], 1, 1)
+        half = rows // 2
+        spans = [pl.ds(part * half, half) for part in range(2)]
+        values = [dot_of(final_low[span, :], down[place, :], 1, 0) for span in spans]
+        sums = []
+        for span, value in zip(spans, values):
+            value = (slope[m, span, :] * value).astype(low)
+            right[hidden + m, span, :] = value
+            sums.append(jnp.sum(value.astype(full), axis=0, keepdims=True))
+            accum[span, :] += dot_of(value, up[place, :], 1, 1)
+        sum_ref[pl.ds(8 + m, 1), :] = sums[0] + sums[1]
         return 0
 
     lax.fori_loop(0, FF // D, backward, 0)
@@ -637,7 +642,13 @@
     turned[2] = middle_low[...].T
 
     def weights(i, _):
-        store_split(dot_of(turned[i // hidden], right[i], 1, 0), stage_keep, stage_send, i)
+        half = D // 2
+        values = [
+            dot_of(turned[i // hidden, part * half : (part + 1) * half, :], right[i], 1, 0)
+            for part in range(2)
+        ]
+        for part, value in enumerate(values):
+            store_split(value, stage_keep, stage_send, i, part * stage_keep.shape[1] // 2)
 
         @pl.when(i < hidden)
         def _():

time: 354 us -> 353 us (level)
  no operation moved by 1% of the time
where the time goes in v14:
time: 353 us; the launch traced here: 347 us
  Pallas kernels  175 us (50%)
  starting transfers between devices  69.6 us (20%)
  waiting for transfers between devices  53 us (15%)
  local copies, waits for them, and re-layouts  21.5 us (6%)
  other arithmetic  19.6 us (6%)
  between operations  5.39 us (2%)
    pallas_call x4, Pallas kernels, attend_backward(): pl.pallas_call(functools.partial(backward_kernel, number, first, last, fo...  66.7 us
    pallas_call x3, Pallas kernels, attend_forward(): pl.pallas_call(functools.partial(forward_kernel, numbers, first, final),...  45.1 us
    ppermute x43, starting transfers between devices, swap(): return lax.ppermute(value, axis, [(i, i ^ bit) for i in range(count)])  42 us
    ppermute x43, waiting for transfers between devices, swap(): return lax.ppermute(value, axis, [(i, i ^ bit) for i in range(count)])  40.7 us
    pallas_call x1, Pallas kernels, middle_call(): pl.pallas_call(functools.partial(middle_kernel, plan, block, len(arrays))...  33.7 us
    ppermute x12, starting transfers between devices, shards(): along = lambda value, pairs: lax.ppermute(value, 'mp', pairs)  27.5 us
    pallas_call x1, Pallas kernels, qkv_grads(): pl.pallas_call(functools.partial(qkv_grad_kernel, count), out_shape=[jax....  13.1 us
    ppermute x12, waiting for transfers between devices, shards(): along = lambda value, pairs: lax.ppermute(value, 'mp', pairs)  12.3 us
  transfers between devices with their start and end apart: 55, of which 22 were waited for; matrix products, arithmetic and copies ran while one was open for 8% of the time, Pallas kernels for 41%

profile of v14, /device:TPU:0, one launch (start us, length us, event | category | flops | bytes accessed | tf_op | source)
XLA Modules:
  0.0 347.0 jit_solution(7286693386585834528)
XLA Ops:
  30.7 3.2 collective-permute-start.3
  38.6 6.4 %collective-permute-done.8.refs_1_ = bf16[288,768]{1,0:T(8,128)(2,1)S(1)} collective-permute-done((bf16[288,768]{1,0:T(8,128)(2,1)S(1)}, bf16[288,768]{1,0:T(8,128)(2,1)S(1)}, u32[]{:S(2)}, u32[]{:S(2)}) %collective-permute-start.8) | collective-permute-done | bytes 442400 | tf_op jit(solution)/shard_map/ppermute | solution.py:319
  48.5 7.8 %collective-permute-done.4 = bf16[512,768]{1,0:T(8,128)(2,1)S(1)} collective-permute-done((bf16[512,768]{1,0:T(8,128)(2,1)S(1)}, bf16[512,768]{1,0:T(8,128)(2,1)S(1)}, u32[]{:S(2)}, u32[]{:S(2)}) %collective-permute-start.4) | collective-permute-done | bytes 786464 | tf_op jit(solution)/shard_map/ppermute | solution.py:1100
  61.6 4.1 %place.1 = (bf16[768,768]{1,0:T(8,128)(2,1)}, bf16[768,1536]{1,0:T(8,128)(2,1)}) custom-call(bf16[288,768]{1,0:T(8,128)(2,1)} %copy-done.12, bf16[288,768]{1,0:T(8,128)(2,1)} %copy-done.26, bf16[288,768]{1,0:T(8,128)(2,1)} %copy-done.28, bf16[288,768]{1,0:T(8,128)(2,1)} %copy-done.29, bf16[288,768]{1,0:T(8,128)(2,1)} %copy-done.11, ...), custom_call_target="tpu_custom_call" | custom-call | flops 1048576 | bytes 65536 | tf_op jit(solution)/shard_map/place/pallas_call | solution.py:434
  68.7 13.1 %attend_forward.3 = (bf16[512,768]{1,0:T(8,128)(2,1)}, bf16[512,768]{1,0:T(8,128)(2,1)}, bf16[512,768]{1,0:T(8,128)(2,1)}, f32[512,768]{1,0:T(8,128)}, f32[512,768]{1,0:T(8,128)}, /*index=5*/f32[512,768]{1,0:T(8,128)}) custom-call(s32[6]{0:T(128)} %stack.42.scalars.refs_0_, bf16[512,768]{1,0:T(8,128)(2,1)} %copy-done.1, ...), custom_call_target="tpu_custom_call" | custom-call | flops 1048576 | bytes 65536 | tf_op jit(solution)/shard_map/attend_forward/pallas_call | solution.py:129
  92.4 18.8 %attend_forward.4 = (bf16[512,768]{1,0:T(8,128)(2,1)}, bf16[512,768]{1,0:T(8,128)(2,1)}, bf16[512,768]{1,0:T(8,128)(2,1)}, bf16[512,768]{1,0:T(8,128)(2,1)}, f32...) custom-call(s32[6]{0:T(128)} %stack.42.scalars.refs_0_, ...), custom_call_target="tpu_custom_call" | custom-call | flops 1048576 | bytes 65536 | tf_op jit(solution)/shard_map/attend_forward/pallas_call | solution.py:129
  112.5 13.1 %attend_forward.5 = (bf16[512,768]{1,0:T(8,128)(2,1)}, bf16[512,768]{1,0:T(8,128)(2,1)}, f32[512,768]{1,0:T(8,128)}, f32[512,768]{1,0:T(8,128)}) custom-call(s32[6]{0:T(128)} %stack.42.scalars.refs_0_, bf16[512,768]{1,0:T(8,128)(2,1)} %broadcast_select_fusion.2.refs_0_.refs_3_, bf16[768,1536]{1,0:T(8,128)(2,1)} %get-tuple-element.225.refs_1_.refs_2_.refs_3_.wk_ref.wv_ref, ...), custom_call_target="tpu_custom_call" | custom-call | flops 1048576 | bytes 65536 | tf_op jit(solution)/shard_map/attend_forward/pallas_call | solution.py:129
  132.0 33.7 %middle.1 = (bf16[512,768]{1,0:T(8,128)(2,1)}, f32[512,768]{1,0:T(8,128)}, bf16[512,768]{1,0:T(8,128)(2,1)}, bf16[4,4,96,768]{3,2,1,0:T(8,128)(2,1)}, bf16[4,4,9...) custom-call(s32[6]{0:T(128)} %stack.42.scalars.refs_0_, ...), custom_call_target="tpu_custom_call" | custom-call | flops 1048576 | bytes 65536 | tf_op jit(solution)/shard_map/middle/pallas_call | solution.py:689
  166.3 14.3 %attend_backward.4 = (f32[512,768]{1,0:T(8,128)}, bf16[512,768]{1,0:T(8,128)(2,1)}, bf16[512,768]{1,0:T(8,128)(2,1)}, bf16[512,768]{1,0:T(8,128)(2,1)}) custom-call(s32[6]{0:T(128)} %stack.42.scalars.refs_0_, bf16[512,768]{1,0:T(8,128)(2,1)} %get-tuple-element.238.refs_5_.refs_4_.q_ref, bf16[512,768]{1,0:T(8,128)(2,1)} %get-tuple-element.274.k_ref, ...), custom_call_target="tpu_custom_call" | custom-call | flops 1048576 | bytes 65536 | tf_op jit(solution)/shard_map/attend_backward/pallas_call | solution.py:266
  180.6 6.6 %collective-permute-start.28 = (bf16[512,768]{1,0:T(8,128)(2,1)}, bf16[512,768]{1,0:T(8,128)(2,1)S(1)}, u32[]{:S(2)}, u32[]{:S(2)}) collective-permute-start(bf16[512,768]{1,0:T(8,128)(2,1)} %get-tuple-element.288), channel_id=1, source_target_pairs={{0,1},{3,2},{4,5},{7,6},{8,9},{11,10},{12,13},{15,14},{16,17},{19,... | collective-permute-start | bytes 2359304 | tf_op jit(solution)/shard_map/ppermute | solution.py:1100
  189.5 17.9 %attend_backward.5 = (f32[512,768]{1,0:T(8,128)}, bf16[512,768]{1,0:T(8,128)(2,1)}, bf16[512,768]{1,0:T(8,128)(2,1)}, f32[512,768]{1,0:T(8,128)}, bf16[4,2,96,76...) custom-call(s32[6]{0:T(128)} %stack.42.scalars.refs_0_, ...), custom_call_target="tpu_custom_call" | custom-call | flops 1048576 | bytes 65536 | tf_op jit(solution)/shard_map/attend_backward/pallas_call | solution.py:266
  214.0 14.9 %attend_backward.6 = (f32[512,768]{1,0:T(8,128)}, bf16[512,768]{1,0:T(8,128)(2,1)}, bf16[512,768]{1,0:T(8,128)(2,1)}, f32[512,768]{1,0:T(8,128)}) custom-call(s32[6]{0:T(128)} %stack.42.scalars.refs_0_, bf16[512,768]{1,0:T(8,128)(2,1)} %get-tuple-element.238.refs_5_.refs_4_.q_ref, bf16[512,768]{1,0:T(8,128)(2,1)} %get-tuple-element.258.k_ref, ...), custom_call_target="tpu_custom_call" | custom-call | flops 1048576 | bytes 65536 | tf_op jit(solution)/shard_map/attend_backward/pallas_call | solution.py:266
  231.3 5.4 %collective-permute-start.33 = (bf16[512,768]{1,0:T(8,128)(2,1)S(1)}, bf16[512,768]{1,0:T(8,128)(2,1)S(1)}, u32[]{:S(2)}, u32[]{:S(2)}) collective-permute-start(bf16[512,768]{1,0:T(8,128)(2,1)S(1)} %select_convert_fusion), channel_id=1, source_target_pairs={{0,1},{1,2},{2,3},{4,5},{5,6},{6,7},{8,9},{9,10},{10,11},{12,13},{... | collective-permute-start | bytes 2359304 | tf_op jit(solution)/shard_map/ppermute | solution.py:1100
  238.3 3.4 collective-permute-done.32.refs_5_
  242.9 19.7 %attend_backward.7 = (bf16[512,768]{1,0:T(8,128)(2,1)}, bf16[512,768]{1,0:T(8,128)(2,1)}, bf16[512,768]{1,0:T(8,128)(2,1)}, f32[512,768]{1,0:T(8,128)}, bf16[4,1...) custom-call(s32[6]{0:T(128)} %stack.42.scalars.refs_0_, ...), custom_call_target="tpu_custom_call" | custom-call | flops 1048576 | bytes 65536 | tf_op jit(solution)/shard_map/attend_backward/pallas_call | solution.py:266
  265.0 13.1 %qkv_grads.1 = (bf16[3,4,96,384]{3,2,1,0:T(8,128)(2,1)}, bf16[3,4,96,384]{3,2,1,0:T(8,128)(2,1)}, bf16[3,4,96,384]{3,2,1,0:T(8,128)(2,1)}, bf16[3,4,96,384]{3,2,1,0:T(8,128)(2,1)}, f32[16,768]{1,0:T(8,128)}) custom-call(bf16[512,768]{1,0:T(8,128)(2,1)} %copy-done.1, bf16[512,768]{1,0:T(8,128)(2,1)} %broadcast_select_fusion.refs_0_.refs_1_, ...), custom_call_target="tpu_custom_call" | custom-call | flops 1048576 | bytes 65536 | tf_op jit(solution)/shard_map/qkv_grads/pallas_call | solution.py:839
  284.9 4.0 %fold.2 = (bf16[3,2,96,384]{3,2,1,0:T(8,128)(2,1)}, bf16[3,2,96,384]{3,2,1,0:T(8,128)(2,1)}, bf16[3,2,96,384]{3,2,1,0:T(8,128)(2,1)}, bf16[3,2,96,384]{3,2,1,0:T(8,128)(2,1)}) custom-call(bf16[3,4,96,384]{3,2,1,0:T(8,128)(2,1)} %get-tuple-element.326.refs_0_, bf16[3,4,96,384]{3,2,1,0:T(8,128)(2,1)} %collective-permute-done.35.refs_1_, ...), custom_call_target="tpu_custom_call" | custom-call | bytes 16777216 | tf_op jit(solution)/shard_map/fold/pallas_call | solution.py:767
  291.2 5.2 %last_norm.1 = (f32[512,768]{1,0:T(8,128)}, f32[24,768]{1,0:T(8,128)}) custom-call(bf16[512,768]{1,0:T(8,128)(2,1)} %token_ref, f32[512,768]{1,0:T(8,128)} %get-tuple-element.344.first_ref, bf16[512,768]{1,0:T(8,128)(2,1)} %copy-done.20, bf16[512,768]{1,0:T(8,128)(2,1)} %copy-done.21, f32[512,768]{1,0:T(8,128)} %get-tuple-element.345.middle_ref, ...), custom_call_target="tpu_custom_call" | custom-call | flops 1048576 | bytes 65536 | tf_op jit(solution)/shard_map/last_norm/pallas_call | solution.py:899
  296.3 3.9 %collective-permute-done.39 = bf16[2,216,768]{2,1,0:T(8,128)(2,1)} collective-permute-done((bf16[2,216,768]{2,1,0:T(8,128)(2,1)S(1)}, bf16[2,216,768]{2,1,0:T(8,128)(2,1)}, u32[]{:S(2)}, u32[]{:S(2)}) %collective-permute-start.39) | collective-permute-done | bytes 663584 | tf_op jit(solution)/shard_map/ppermute | solution.py:319
  306.2 3.2 fold.3
  312.6 5.7 %collective-permute-done.45 = bf16[216,768]{1,0:T(8,128)(2,1)S(1)} collective-permute-done((bf16[216,768]{1,0:T(8,128)(2,1)S(1)}, bf16[216,768]{1,0:T(8,128)(2,1)S(1)}, u32[]{:S(2)}, u32[]{:S(2)}) %collective-permute-start.45) | collective-permute-done | bytes 331808 | tf_op jit(solution)/shard_map/ppermute | solution.py:319
  325.7 3.4 collective-permute-start.50
  330.5 3.8 %collective-permute-start.53 = (bf16[3,96,192]{2,1,0:T(8,128)(2,1)S(1)}, bf16[3,96,192]{2,1,0:T(8,128)(2,1)S(1)}, u32[]{:S(2)}, u32[]{:S(2)}) collective-permute-start(bf16[3,96,192]{2,1,0:T(8,128)(2,1)S(1)} %get-tuple-element.368), channel_id=1, source_target_pairs={{0,2},{1,3},{2,0},{3,1},{4,6},{5,7},{6,4},{7,5},{8,10},{9,11},{10,... | collective-permute-start | bytes 331784 | tf_op jit(solution)/shard_map/ppermute | solution.py:319
  340.4 4.8 %collective-permute-done.53 = bf16[3,96,192]{2,1,0:T(8,128)(2,1)S(1)} collective-permute-done((bf16[3,96,192]{2,1,0:T(8,128)(2,1)S(1)}, bf16[3,96,192]{2,1,0:T(8,128)(2,1)S(1)}, u32[]{:S(2)}, u32[]{:S(2)}) %collective-permute-start.53) | collective-permute-done | bytes 110624 | tf_op jit(solution)/shard_map/ppermute | solution.py:319
  (257 shorter events, 112.1 us)
Async XLA Ops:
  6.7 16.4 %collective-permute-start.1 = (bf16[192,768]{1,0:T(8,128)(2,1)S(1)}, bf16[192,768]{1,0:T(8,128)(2,1)S(1)}, u32[]{:S(2)}, u32[]{:S(2)}) collective-permute-start(bf16[192,768]{1,0:T(8,128)(2,1)S(1)} %pad_maximum_fusion.9), channel_id=1, source_target_pairs={{0,1},{1,0},{2,3},{3,2},{4,5},{5,4},{6,7},{7,6},{8,9},{9,8},{10,11... | collective-permute-start | bytes 884744 | tf_op jit(solution)/shard_map/ppermute | solution.py:319
  30.7 17.8 %collective-permute-start.3 = (bf16[512,768]{1,0:T(8,128)(2,1)S(1)}, bf16[512,768]{1,0:T(8,128)(2,1)S(1)}, u32[]{:S(2)}, u32[]{:S(2)}) collective-permute-start(bf16[512,768]{1,0:T(8,128)(2,1)S(1)} %add_convert_fusion.2.refs_0_), channel_id=1, source_target_pairs={{0,1},{1,2},{2,3},{4,5},{5,6},{6,7},{8,9},{9,10},{10,11},{12,13},{... | collective-permute-start | bytes 2359304 | tf_op jit(solution)/shard_map/ppermute | solution.py:1100
  34.0 22.4 %collective-permute-start.4 = (bf16[512,768]{1,0:T(8,128)(2,1)S(1)}, bf16[512,768]{1,0:T(8,128)(2,1)S(1)}, u32[]{:S(2)}, u32[]{:S(2)}) collective-permute-start(bf16[512,768]{1,0:T(8,128)(2,1)S(1)} %add_convert_fusion.2.refs_0_), channel_id=1, source_target_pairs={{1,0},{2,1},{3,2},{5,4},{6,5},{7,6},{9,8},{10,9},{11,10},{13,12},{... | collective-permute-start | bytes 2359304 | tf_op jit(solution)/shard_map/ppermute | solution.py:1100
  37.3 28.5 %collective-permute-start.12 = (bf16[384,768]{1,0:T(8,128)(2,1)}, bf16[384,768]{1,0:T(8,128)(2,1)}, u32[]{:S(2)}, u32[]{:S(2)}) collective-permute-start(bf16[384,768]{1,0:T(8,128)(2,1)} %collective-permute-done.7), channel_id=1, source_target_pairs={{1,0},{2,3},{5,4},{6,7},{9,8},{10,11},{13,12},{14,15},{17,16},{18,... | collective-permute-start | bytes 1769480 | tf_op jit(solution)/shard_map/ppermute | solution.py:1100
  56.4 25.4 %collective-permute-start.10 = (bf16[512,768]{1,0:T(8,128)(2,1)S(1)}, bf16[512,768]{1,0:T(8,128)(2,1)}, u32[]{:S(2)}, u32[]{:S(2)}) collective-permute-start(bf16[512,768]{1,0:T(8,128)(2,1)S(1)} %collective-permute-done.3), channel_id=1, source_target_pairs={{1,2},{2,3},{5,6},{6,7},{9,10},{10,11},{13,14},{14,15},{17,18},{18... | collective-permute-start | bytes 2359304 | tf_op jit(solution)/shard_map/ppermute | solution.py:1100
  58.7 24.4 %collective-permute-start.11 = (bf16[512,768]{1,0:T(8,128)(2,1)S(1)}, bf16[512,768]{1,0:T(8,128)(2,1)}, u32[]{:S(2)}, u32[]{:S(2)}) collective-permute-start(bf16[512,768]{1,0:T(8,128)(2,1)S(1)} %collective-permute-done.4), channel_id=1, source_target_pairs={{1,0},{2,1},{5,4},{6,5},{9,8},{10,9},{13,12},{14,13},{17,16},{18,1... | collective-permute-start | bytes 2359304 | tf_op jit(solution)/shard_map/ppermute | solution.py:1100
  67.0 17.4 %collective-permute-start.19 = (bf16[432,768]{1,0:T(8,128)(2,1)S(1)}, bf16[432,768]{1,0:T(8,128)(2,1)S(1)}, u32[]{:S(2)}, u32[]{:S(2)}) collective-permute-start(bf16[432,768]{1,0:T(8,128)(2,1)S(1)} %fusion.6), channel_id=1, source_target_pairs={{0,16},{4,20},{8,24},{12,28},{16,0},{20,4},{24,8},{28,12},{1,17},{... | collective-permute-start | bytes 1990664 | tf_op jit(solution)/shard_map/ppermute | solution.py:319
  67.6 17.1 %collective-permute-start.18 = (bf16[432,768]{1,0:T(8,128)(2,1)S(1)}, bf16[432,768]{1,0:T(8,128)(2,1)}, u32[]{:S(2)}, u32[]{:S(2)}) collective-permute-start(bf16[432,768]{1,0:T(8,128)(2,1)S(1)} %pad_maximum_fusion.4), channel_id=1, source_target_pairs={{0,8},{4,12},{8,0},{12,4},{16,24},{20,28},{24,16},{28,20},{1,9},{5... | collective-permute-start | bytes 1990664 | tf_op jit(solution)/shard_map/ppermute | solution.py:319
  86.6 39.1 %collective-permute-start.20 = (bf16[864,768]{1,0:T(8,128)(2,1)S(1)}, bf16[864,768]{1,0:T(8,128)(2,1)}, u32[]{:S(2)}, u32[]{:S(2)}) collective-permute-start(bf16[864,768]{1,0:T(8,128)(2,1)S(1)} %pad_maximum_fusion.1.refs_7_), channel_id=1, source_target_pairs={{0,16},{4,20},{8,24},{12,28},{16,0},{20,4},{24,8},{28,12},{1,17},{... | collective-permute-start | bytes 3981320 | tf_op jit(solution)/shard_map/ppermute | solution.py:319
  88.2 37.5 %collective-permute-start.21 = (bf16[864,768]{1,0:T(8,128)(2,1)S(1)}, bf16[864,768]{1,0:T(8,128)(2,1)}, u32[]{:S(2)}, u32[]{:S(2)}) collective-permute-start(bf16[864,768]{1,0:T(8,128)(2,1)S(1)} %pad_maximum_fusion.2.refs_11_), channel_id=1, source_target_pairs={{0,8},{4,12},{8,0},{12,4},{16,24},{20,28},{24,16},{28,20},{1,9},{5... | collective-permute-start | bytes 3981320 | tf_op jit(solution)/shard_map/ppermute | solution.py:319
  89.4 22.1 %collective-permute-start.17 = (bf16[512,768]{1,0:T(8,128)(2,1)S(1)}, bf16[512,768]{1,0:T(8,128)(2,1)S(1)}, u32[]{:S(2)}, u32[]{:S(2)}) collective-permute-start(bf16[512,768]{1,0:T(8,128)(2,1)S(1)} %broadcast_select_fusion.1.refs_1_.refs_2_), channel_id=1, source_target_pairs={{1,0},{2,3},{5,4},{6,7},{9,8},{10,11},{13,12},{14,15},{17,16},{18,... | collective-permute-start | bytes 2359304 | tf_op jit(solution)/shard_map/ppermute | solution.py:1100
  91.9 34.4 %collective-permute-start.22 = (bf16[864,768]{1,0:T(8,128)(2,1)S(1)}, bf16[864,768]{1,0:T(8,128)(2,1)}, u32[]{:S(2)}, u32[]{:S(2)}) collective-permute-start(bf16[864,768]{1,0:T(8,128)(2,1)S(1)} %pad_maximum_fusion.1.refs_7_), channel_id=1, source_target_pairs={{0,4},{4,0},{8,12},{12,8},{16,20},{20,16},{24,28},{28,24},{1,5},{5... | collective-permute-start | bytes 3981320 | tf_op jit(solution)/shard_map/ppermute | solution.py:319
  91.9 34.4 %collective-permute-start.24 = (bf16[864,768]{1,0:T(8,128)(2,1)S(1)}, bf16[864,768]{1,0:T(8,128)(2,1)}, u32[]{:S(2)}, u32[]{:S(2)}) collective-permute-start(bf16[864,768]{1,0:T(8,128)(2,1)S(1)} %pad_maximum_fusion.2.refs_11_), channel_id=1, source_target_pairs={{0,4},{4,0},{8,12},{12,8},{16,20},{20,16},{24,28},{28,24},{1,5},{5... | collective-permute-start | bytes 3981320 | tf_op jit(solution)/shard_map/ppermute | solution.py:319
  165.7 21.5 %collective-permute-start.27 = (bf16[5,4,96,768]{3,2,1,0:T(8,128)(2,1)}, bf16[5,4,96,768]{3,2,1,0:T(8,128)(2,1)S(1)}, u32[]{:S(2)}, u32[]{:S(2)}) collective-permute-start(bf16[5,4,96,768]{3,2,1,0:T(8,128)(2,1)} %get-tuple-element.283), channel_id=1, source_target_pairs={{0,4},{4,0},{8,12},{12,8},{16,20},{20,16},{24,28},{28,24},{1,5},{5... | collective-permute-start | bytes 8847368 | tf_op jit(solution)/shard_map/ppermute | solution.py:319
  165.9 21.3 %collective-permute-start.26 = (bf16[4,4,96,768]{3,2,1,0:T(8,128)(2,1)}, bf16[4,4,96,768]{3,2,1,0:T(8,128)(2,1)S(1)}, u32[]{:S(2)}, u32[]{:S(2)}) collective-permute-start(bf16[4,4,96,768]{3,2,1,0:T(8,128)(2,1)} %get-tuple-element.282), channel_id=1, source_target_pairs={{0,4},{4,0},{8,12},{12,8},{16,20},{20,16},{24,28},{28,24},{1,5},{5... | collective-permute-start | bytes 7077896 | tf_op jit(solution)/shard_map/ppermute | solution.py:319
  180.6 27.7 %collective-permute-start.28 = (bf16[512,768]{1,0:T(8,128)(2,1)}, bf16[512,768]{1,0:T(8,128)(2,1)S(1)}, u32[]{:S(2)}, u32[]{:S(2)}) collective-permute-start(bf16[512,768]{1,0:T(8,128)(2,1)} %get-tuple-element.288), channel_id=1, source_target_pairs={{0,1},{3,2},{4,5},{7,6},{8,9},{11,10},{12,13},{15,14},{16,17},{19,... | collective-permute-start | bytes 2359304 | tf_op jit(solution)/shard_map/ppermute | solution.py:1100
  207.4 34.3 %collective-permute-start.32 = (bf16[5,2,96,768]{3,2,1,0:T(8,128)(2,1)}, bf16[5,2,96,768]{3,2,1,0:T(8,128)(2,1)S(1)}, u32[]{:S(2)}, u32[]{:S(2)}) collective-permute-start(bf16[5,2,96,768]{3,2,1,0:T(8,128)(2,1)} %get-tuple-element.298), channel_id=1, source_target_pairs={{0,8},{4,12},{8,0},{12,4},{16,24},{20,28},{24,16},{28,20},{1,9},{5... | collective-permute-start | bytes 4423688 | tf_op jit(solution)/shard_map/ppermute | solution.py:319
  209.9 19.1 %collective-permute-start.30 = (bf16[512,768]{1,0:T(8,128)(2,1)S(1)}, bf16[512,768]{1,0:T(8,128)(2,1)S(1)}, u32[]{:S(2)}, u32[]{:S(2)}) collective-permute-start(bf16[512,768]{1,0:T(8,128)(2,1)S(1)} %add_convert_fusion.1), channel_id=1, source_target_pairs={{3,2},{2,1},{7,6},{6,5},{11,10},{10,9},{15,14},{14,13},{19,18},{18... | collective-permute-start | bytes 2359304 | tf_op jit(solution)/shard_map/ppermute | solution.py:1100
  210.6 27.7 %collective-permute-start.31 = (bf16[4,2,96,768]{3,2,1,0:T(8,128)(2,1)}, bf16[4,2,96,768]{3,2,1,0:T(8,128)(2,1)S(1)}, u32[]{:S(2)}, u32[]{:S(2)}) collective-permute-start(bf16[4,2,96,768]{3,2,1,0:T(8,128)(2,1)} %get-tuple-element.297), channel_id=1, source_target_pairs={{0,16},{4,20},{8,24},{12,28},{16,0},{20,4},{24,8},{28,12},{1,17},{... | collective-permute-start | bytes 3538952 | tf_op jit(solution)/shard_map/ppermute | solution.py:319
  212.2 18.5 %collective-permute-start.29 = (bf16[512,768]{1,0:T(8,128)(2,1)S(1)}, bf16[512,768]{1,0:T(8,128)(2,1)S(1)}, u32[]{:S(2)}, u32[]{:S(2)}) collective-permute-start(bf16[512,768]{1,0:T(8,128)(2,1)S(1)} %add_convert_fusion.1), channel_id=1, source_target_pairs={{0,1},{1,2},{4,5},{5,6},{8,9},{9,10},{12,13},{13,14},{16,17},{17,1... | collective-permute-start | bytes 2359304 | tf_op jit(solution)/shard_map/ppermute | solution.py:1100
  231.3 33.6 %collective-permute-start.33 = (bf16[512,768]{1,0:T(8,128)(2,1)S(1)}, bf16[512,768]{1,0:T(8,128)(2,1)S(1)}, u32[]{:S(2)}, u32[]{:S(2)}) collective-permute-start(bf16[512,768]{1,0:T(8,128)(2,1)S(1)} %select_convert_fusion), channel_id=1, source_target_pairs={{0,1},{1,2},{2,3},{4,5},{5,6},{6,7},{8,9},{9,10},{10,11},{12,13},{... | collective-permute-start | bytes 2359304 | tf_op jit(solution)/shard_map/ppermute | solution.py:1100
  236.8 28.2 %collective-permute-start.34 = (bf16[512,768]{1,0:T(8,128)(2,1)S(1)}, bf16[512,768]{1,0:T(8,128)(2,1)S(1)}, u32[]{:S(2)}, u32[]{:S(2)}) collective-permute-start(bf16[512,768]{1,0:T(8,128)(2,1)S(1)} %add_convert_fusion), channel_id=1, source_target_pairs={{3,2},{2,1},{1,0},{7,6},{6,5},{5,4},{11,10},{10,9},{9,8},{15,14},{... | collective-permute-start | bytes 2359304 | tf_op jit(solution)/shard_map/ppermute | solution.py:1100
  262.5 17.7 %collective-permute-start.38 = (bf16[5,1,96,768]{3,2,1,0:T(8,128)(2,1)}, bf16[5,1,96,768]{3,2,1,0:T(8,128)(2,1)}, u32[]{:S(2)}, u32[]{:S(2)}) collective-permute-start(bf16[5,1,96,768]{3,2,1,0:T(8,128)(2,1)} %get-tuple-element.316), channel_id=1, source_target_pairs={{0,16},{4,20},{8,24},{12,28},{16,0},{20,4},{24,8},{28,12},{1,17},{... | collective-permute-start | bytes 2211848 | tf_op jit(solution)/shard_map/ppermute | solution.py:319
  288.8 16.4 %collective-permute-start.41 = (bf16[3,2,96,384]{3,2,1,0:T(8,128)(2,1)}, bf16[3,2,96,384]{3,2,1,0:T(8,128)(2,1)S(1)}, u32[]{:S(2)}, u32[]{:S(2)}) collective-permute-start(bf16[3,2,96,384]{3,2,1,0:T(8,128)(2,1)} %get-tuple-element.341), channel_id=1, source_target_pairs={{0,8},{4,12},{8,0},{12,4},{16,24},{20,28},{24,16},{28,20},{1,9},{5... | collective-permute-start | bytes 1327112 | tf_op jit(solution)/shard_map/ppermute | solution.py:319
  (75 other events, 652.9 us)

commit v15 on v12

--- a/solution.py
+++ b/solution.py
@@ -443,14 +443,14 @@
     )(*arrays)
 
 
-def store_split(value, keep, send, index):
+def store_split(value, keep, send, index, start=0):
     block = keep.shape[2]
     even = lax.axis_index("dp") % 2 == 0
-    for outer in range(keep.shape[1]):
+    for outer in range(value.shape[0] // (2 * block)):
         first = value[2 * outer * block : (2 * outer + 1) * block]
         other = value[(2 * outer + 1) * block : (2 * outer + 2) * block]
-        keep[index, outer] = jnp.where(even, first, other).astype(low)
-        send[index, outer] = jnp.where(even, other, first).astype(low)
+        keep[index, start + outer] = jnp.where(even, first, other).astype(low)
+        send[index, start + outer] = jnp.where(even, other, first).astype(low)
 
 
 def middle_kernel(plan, block, total, *refs):
@@ -593,11 +593,16 @@
 
     def backward(m, _):
         place = pl.ds(pl.multiple_of(m * D, D), D)
-        value = slope[m] * dot_of(final_low[...], down[place, :], 1, 0)
-        value = value.astype(low)
-        right[hidden + m] = value
-        sum_ref[pl.ds(8 + m, 1), :] = jnp.sum(value.astype(full), axis=0, keepdims=True)
-        accum[...] += dot_of(value, up[place, :], 1, 1)
+        half = rows // 2
+        spans = [pl.ds(part * half, half) for part in range(2)]
+        values = [dot_of(final_low[span, :], down[place, :], 1, 0) for span in spans]
+        sums = []
+        for span, value in zip(spans, values):
+            value = (slope[m, span, :] * value).astype(low)
+            right[hidden + m, span, :] = value
+            sums.append(jnp.sum(value.astype(full), axis=0, keepdims=True))
+            accum[span, :] += dot_of(value, up[place, :], 1, 1)
+        sum_ref[pl.ds(8 + m, 1), :] = sums[0] + sums[1]
         return 0
 
     lax.fori_loop(0, FF // D, backward, 0)
@@ -637,7 +642,13 @@
     turned[2] = middle_low[...].T
 
     def weights(i, _):
-        store_split(dot_of(turned[i // hidden], right[i], 1, 0), stage_keep, stage_send, i)
+        half = D // 2
+        values = [
+            dot_of(turned[i // hidden, part * half : (part + 1) * half, :], right[i], 1, 0)
+            for part in range(2)
+        ]
+        for part, value in enumerate(values):
+            store_split(value, stage_keep, stage_send, i, part * stage_keep.shape[1] // 2)
 
         @pl.when(i < hidden)
         def _():

time: 354 us -> 354 us (level)
  no operation moved by 1% of the time
where the time goes in v15:
time: 354 us; the launch traced here: 347 us
  Pallas kernels  173 us (49%)
  starting transfers between devices  70.1 us (20%)
  waiting for transfers between devices  55.1 us (16%)
  local copies, waits for them, and re-layouts  21.4 us (6%)
  other arithmetic  19.6 us (6%)
  between operations  5.15 us (1%)
    pallas_call x4, Pallas kernels, attend_backward(): pl.pallas_call(functools.partial(backward_kernel, number, first, last, fo...  66.8 us
    pallas_call x3, Pallas kernels, attend_forward(): pl.pallas_call(functools.partial(forward_kernel, numbers, first, final),...  45.1 us
    ppermute x43, waiting for transfers between devices, swap(): return lax.ppermute(value, axis, [(i, i ^ bit) for i in range(count)])  42.7 us
    ppermute x43, starting transfers between devices, swap(): return lax.ppermute(value, axis, [(i, i ^ bit) for i in range(count)])  42.5 us
    pallas_call x1, Pallas kernels, middle_call(): pl.pallas_call(functools.partial(middle_kernel, plan, block, len(arrays))...  33.7 us
    ppermute x12, starting transfers between devices, shards(): along = lambda value, pairs: lax.ppermute(value, 'mp', pairs)  27.6 us
    ppermute x12, waiting for transfers between devices, shards(): along = lambda value, pairs: lax.ppermute(value, 'mp', pairs)  12.4 us
    unnamed x87, local copies, waits for them, and re-layouts  11.1 us
  transfers between devices with their start and end apart: 55, of which 24 were waited for; matrix products, arithmetic and copies ran while one was open for 8% of the time, Pallas kernels for 40%

profile of v15, /device:TPU:0, one launch (start us, length us, event | category | flops | bytes accessed | tf_op | source)
XLA Modules:
  0.0 347.2 jit_solution(14756785649865027893)
XLA Ops:
  30.7 3.2 collective-permute-start.3
  38.6 6.4 %collective-permute-done.8.refs_1_ = bf16[288,768]{1,0:T(8,128)(2,1)S(1)} collective-permute-done((bf16[288,768]{1,0:T(8,128)(2,1)S(1)}, bf16[288,768]{1,0:T(8,128)(2,1)S(1)}, u32[]{:S(2)}, u32[]{:S(2)}) %collective-permute-start.8) | collective-permute-done | bytes 442400 | tf_op jit(solution)/shard_map/ppermute | solution.py:319
  48.5 7.8 %collective-permute-done.4 = bf16[512,768]{1,0:T(8,128)(2,1)S(1)} collective-permute-done((bf16[512,768]{1,0:T(8,128)(2,1)S(1)}, bf16[512,768]{1,0:T(8,128)(2,1)S(1)}, u32[]{:S(2)}, u32[]{:S(2)}) %collective-permute-start.4) | collective-permute-done | bytes 786464 | tf_op jit(solution)/shard_map/ppermute | solution.py:1106
  61.6 4.1 %place.1 = (bf16[768,768]{1,0:T(8,128)(2,1)}, bf16[768,1536]{1,0:T(8,128)(2,1)}) custom-call(bf16[288,768]{1,0:T(8,128)(2,1)} %copy-done.12, bf16[288,768]{1,0:T(8,128)(2,1)} %copy-done.26, bf16[288,768]{1,0:T(8,128)(2,1)} %copy-done.28, bf16[288,768]{1,0:T(8,128)(2,1)} %copy-done.29, bf16[288,768]{1,0:T(8,128)(2,1)} %copy-done.11, ...), custom_call_target="tpu_custom_call" | custom-call | flops 1048576 | bytes 65536 | tf_op jit(solution)/shard_map/place/pallas_call | solution.py:434
  68.7 13.1 %attend_forward.3 = (bf16[512,768]{1,0:T(8,128)(2,1)}, bf16[512,768]{1,0:T(8,128)(2,1)}, bf16[512,768]{1,0:T(8,128)(2,1)}, f32[512,768]{1,0:T(8,128)}, f32[512,768]{1,0:T(8,128)}, /*index=5*/f32[512,768]{1,0:T(8,128)}) custom-call(s32[6]{0:T(128)} %stack.42.scalars.refs_0_, bf16[512,768]{1,0:T(8,128)(2,1)} %copy-done.1, ...), custom_call_target="tpu_custom_call" | custom-call | flops 1048576 | bytes 65536 | tf_op jit(solution)/shard_map/attend_forward/pallas_call | solution.py:129
  92.4 18.8 %attend_forward.4 = (bf16[512,768]{1,0:T(8,128)(2,1)}, bf16[512,768]{1,0:T(8,128)(2,1)}, bf16[512,768]{1,0:T(8,128)(2,1)}, bf16[512,768]{1,0:T(8,128)(2,1)}, f32...) custom-call(s32[6]{0:T(128)} %stack.42.scalars.refs_0_, ...), custom_call_target="tpu_custom_call" | custom-call | flops 1048576 | bytes 65536 | tf_op jit(solution)/shard_map/attend_forward/pallas_call | solution.py:129
  112.5 13.1 %attend_forward.5 = (bf16[512,768]{1,0:T(8,128)(2,1)}, bf16[512,768]{1,0:T(8,128)(2,1)}, f32[512,768]{1,0:T(8,128)}, f32[512,768]{1,0:T(8,128)}) custom-call(s32[6]{0:T(128)} %stack.42.scalars.refs_0_, bf16[512,768]{1,0:T(8,128)(2,1)} %broadcast_select_fusion.2.refs_0_.refs_3_, bf16[768,1536]{1,0:T(8,128)(2,1)} %get-tuple-element.225.refs_1_.refs_2_.refs_3_.wk_ref.wv_ref, ...), custom_call_target="tpu_custom_call" | custom-call | flops 1048576 | bytes 65536 | tf_op jit(solution)/shard_map/attend_forward/pallas_call | solution.py:129
  132.0 33.7 %middle.1 = (bf16[512,768]{1,0:T(8,128)(2,1)}, f32[512,768]{1,0:T(8,128)}, bf16[512,768]{1,0:T(8,128)(2,1)}, bf16[4,4,96,768]{3,2,1,0:T(8,128)(2,1)}, bf16[4,4,9...) custom-call(s32[6]{0:T(128)} %stack.42.scalars.refs_0_, ...), custom_call_target="tpu_custom_call" | custom-call | flops 1048576 | bytes 65536 | tf_op jit(solution)/shard_map/middle/pallas_call | solution.py:689
  166.3 14.3 %attend_backward.4 = (f32[512,768]{1,0:T(8,128)}, bf16[512,768]{1,0:T(8,128)(2,1)}, bf16[512,768]{1,0:T(8,128)(2,1)}, bf16[512,768]{1,0:T(8,128)(2,1)}) custom-call(s32[6]{0:T(128)} %stack.42.scalars.refs_0_, bf16[512,768]{1,0:T(8,128)(2,1)} %get-tuple-element.238.refs_5_.refs_4_.q_ref, bf16[512,768]{1,0:T(8,128)(2,1)} %get-tuple-element.274.k_ref, ...), custom_call_target="tpu_custom_call" | custom-call | flops 1048576 | bytes 65536 | tf_op jit(solution)/shard_map/attend_backward/pallas_call | solution.py:266
  180.6 6.6 %collective-permute-start.28 = (bf16[512,768]{1,0:T(8,128)(2,1)}, bf16[512,768]{1,0:T(8,128)(2,1)S(1)}, u32[]{:S(2)}, u32[]{:S(2)}) collective-permute-start(bf16[512,768]{1,0:T(8,128)(2,1)} %get-tuple-element.288), channel_id=1, source_target_pairs={{0,1},{3,2},{4,5},{7,6},{8,9},{11,10},{12,13},{15,14},{16,17},{19,... | collective-permute-start | bytes 2359304 | tf_op jit(solution)/shard_map/ppermute | solution.py:1106
  189.5 17.9 %attend_backward.5 = (f32[512,768]{1,0:T(8,128)}, bf16[512,768]{1,0:T(8,128)(2,1)}, bf16[512,768]{1,0:T(8,128)(2,1)}, f32[512,768]{1,0:T(8,128)}, bf16[4,2,96,76...) custom-call(s32[6]{0:T(128)} %stack.42.scalars.refs_0_, ...), custom_call_target="tpu_custom_call" | custom-call | flops 1048576 | bytes 65536 | tf_op jit(solution)/shard_map/attend_backward/pallas_call | solution.py:266
  214.0 14.6 %attend_backward.6 = (f32[512,768]{1,0:T(8,128)}, bf16[512,768]{1,0:T(8,128)(2,1)}, bf16[512,768]{1,0:T(8,128)(2,1)}, f32[512,768]{1,0:T(8,128)}) custom-call(s32[6]{0:T(128)} %stack.42.scalars.refs_0_, bf16[512,768]{1,0:T(8,128)(2,1)} %get-tuple-element.238.refs_5_.refs_4_.q_ref, bf16[512,768]{1,0:T(8,128)(2,1)} %get-tuple-element.258.k_ref, ...), custom_call_target="tpu_custom_call" | custom-call | flops 1048576 | bytes 65536 | tf_op jit(solution)/shard_map/attend_backward/pallas_call | solution.py:266
  231.0 5.5 %collective-permute-start.33 = (bf16[512,768]{1,0:T(8,128)(2,1)S(1)}, bf16[512,768]{1,0:T(8,128)(2,1)S(1)}, u32[]{:S(2)}, u32[]{:S(2)}) collective-permute-start(bf16[512,768]{1,0:T(8,128)(2,1)S(1)} %select_convert_fusion), channel_id=1, source_target_pairs={{0,1},{1,2},{2,3},{4,5},{5,6},{6,7},{8,9},{9,10},{10,11},{12,13},{... | collective-permute-start | bytes 2359304 | tf_op jit(solution)/shard_map/ppermute | solution.py:1106
  238.3 3.4 collective-permute-done.32.refs_5_
  242.9 20.1 %attend_backward.7 = (bf16[512,768]{1,0:T(8,128)(2,1)}, bf16[512,768]{1,0:T(8,128)(2,1)}, bf16[512,768]{1,0:T(8,128)(2,1)}, f32[512,768]{1,0:T(8,128)}, bf16[4,1...) custom-call(s32[6]{0:T(128)} %stack.42.scalars.refs_0_, ...), custom_call_target="tpu_custom_call" | custom-call | flops 1048576 | bytes 65536 | tf_op jit(solution)/shard_map/attend_backward/pallas_call | solution.py:266
  265.4 10.7 %qkv_grads.1 = (bf16[3,4,96,384]{3,2,1,0:T(8,128)(2,1)}, bf16[3,4,96,384]{3,2,1,0:T(8,128)(2,1)}, bf16[3,4,96,384]{3,2,1,0:T(8,128)(2,1)}, bf16[3,4,96,384]{3,2,1,0:T(8,128)(2,1)}, f32[16,768]{1,0:T(8,128)}) custom-call(bf16[512,768]{1,0:T(8,128)(2,1)} %copy-done.1, bf16[512,768]{1,0:T(8,128)(2,1)} %broadcast_select_fusion.refs_0_.refs_1_, ...), custom_call_target="tpu_custom_call" | custom-call | flops 1048576 | bytes 65536 | tf_op jit(solution)/shard_map/qkv_grads/pallas_call | solution.py:844
  285.3 4.0 %fold.2 = (bf16[3,2,96,384]{3,2,1,0:T(8,128)(2,1)}, bf16[3,2,96,384]{3,2,1,0:T(8,128)(2,1)}, bf16[3,2,96,384]{3,2,1,0:T(8,128)(2,1)}, bf16[3,2,96,384]{3,2,1,0:T(8,128)(2,1)}) custom-call(bf16[3,4,96,384]{3,2,1,0:T(8,128)(2,1)} %get-tuple-element.326.refs_0_, bf16[3,4,96,384]{3,2,1,0:T(8,128)(2,1)} %collective-permute-done.35.refs_1_, ...), custom_call_target="tpu_custom_call" | custom-call | bytes 16777216 | tf_op jit(solution)/shard_map/fold/pallas_call | solution.py:767
  291.6 5.2 %last_norm.1 = (f32[512,768]{1,0:T(8,128)}, f32[24,768]{1,0:T(8,128)}) custom-call(bf16[512,768]{1,0:T(8,128)(2,1)} %token_ref, f32[512,768]{1,0:T(8,128)} %get-tuple-element.344.first_ref, bf16[512,768]{1,0:T(8,128)(2,1)} %copy-done.20, bf16[512,768]{1,0:T(8,128)(2,1)} %copy-done.21, f32[512,768]{1,0:T(8,128)} %get-tuple-element.345.middle_ref, ...), custom_call_target="tpu_custom_call" | custom-call | flops 1048576 | bytes 65536 | tf_op jit(solution)/shard_map/last_norm/pallas_call | solution.py:905
  296.7 3.4 collective-permute-done.39
  305.9 3.3 fold.3
  313.3 4.2 %collective-permute-done.45 = bf16[216,768]{1,0:T(8,128)(2,1)S(1)} collective-permute-done((bf16[216,768]{1,0:T(8,128)(2,1)S(1)}, bf16[216,768]{1,0:T(8,128)(2,1)S(1)}, u32[]{:S(2)}, u32[]{:S(2)}) %collective-permute-start.45) | collective-permute-done | bytes 331808 | tf_op jit(solution)/shard_map/ppermute | solution.py:319
  326.2 3.4 collective-permute-start.50
  331.0 3.8 %collective-permute-start.53 = (bf16[3,96,192]{2,1,0:T(8,128)(2,1)S(1)}, bf16[3,96,192]{2,1,0:T(8,128)(2,1)S(1)}, u32[]{:S(2)}, u32[]{:S(2)}) collective-permute-start(bf16[3,96,192]{2,1,0:T(8,128)(2,1)S(1)} %get-tuple-element.368), channel_id=1, source_target_pairs={{0,2},{1,3},{2,0},{3,1},{4,6},{5,7},{6,4},{7,5},{8,10},{9,11},{10,... | collective-permute-start | bytes 331784 | tf_op jit(solution)/shard_map/ppermute | solution.py:319
  340.9 4.8 %collective-permute-done.53 = bf16[3,96,192]{2,1,0:T(8,128)(2,1)S(1)} collective-permute-done((bf16[3,96,192]{2,1,0:T(8,128)(2,1)S(1)}, bf16[3,96,192]{2,1,0:T(8,128)(2,1)S(1)}, u32[]{:S(2)}, u32[]{:S(2)}) %collective-permute-start.53) | collective-permute-done | bytes 110624 | tf_op jit(solution)/shard_map/ppermute | solution.py:319
  (257 shorter events, 116.6 us)
Async XLA Ops:
  6.7 16.4 %collective-permute-start.1 = (bf16[192,768]{1,0:T(8,128)(2,1)S(1)}, bf16[192,768]{1,0:T(8,128)(2,1)S(1)}, u32[]{:S(2)}, u32[]{:S(2)}) collective-permute-start(bf16[192,768]{1,0:T(8,128)(2,1)S(1)} %pad_maximum_fusion.9), channel_id=1, source_target_pairs={{0,1},{1,0},{2,3},{3,2},{4,5},{5,4},{6,7},{7,6},{8,9},{9,8},{10,11... | collective-permute-start | bytes 884744 | tf_op jit(solution)/shard_map/ppermute | solution.py:319
  30.7 17.8 %collective-permute-start.3 = (bf16[512,768]{1,0:T(8,128)(2,1)S(1)}, bf16[512,768]{1,0:T(8,128)(2,1)S(1)}, u32[]{:S(2)}, u32[]{:S(2)}) collective-permute-start(bf16[512,768]{1,0:T(8,128)(2,1)S(1)} %add_convert_fusion.2.refs_0_), channel_id=1, source_target_pairs={{0,1},{1,2},{2,3},{4,5},{5,6},{6,7},{8,9},{9,10},{10,11},{12,13},{... | collective-permute-start | bytes 2359304 | tf_op jit(solution)/shard_map/ppermute | solution.py:1106
  34.0 22.4 %collective-permute-start.4 = (bf16[512,768]{1,0:T(8,128)(2,1)S(1)}, bf16[512,768]{1,0:T(8,128)(2,1)S(1)}, u32[]{:S(2)}, u32[]{:S(2)}) collective-permute-start(bf16[512,768]{1,0:T(8,128)(2,1)S(1)} %add_convert_fusion.2.refs_0_), channel_id=1, source_target_pairs={{1,0},{2,1},{3,2},{5,4},{6,5},{7,6},{9,8},{10,9},{11,10},{13,12},{... | collective-permute-start | bytes 2359304 | tf_op jit(solution)/shard_map/ppermute | solution.py:1106
  37.3 28.5 %collective-permute-start.12 = (bf16[384,768]{1,0:T(8,128)(2,1)}, bf16[384,768]{1,0:T(8,128)(2,1)}, u32[]{:S(2)}, u32[]{:S(2)}) collective-permute-start(bf16[384,768]{1,0:T(8,128)(2,1)} %collective-permute-done.7), channel_id=1, source_target_pairs={{1,0},{2,3},{5,4},{6,7},{9,8},{10,11},{13,12},{14,15},{17,16},{18,... | collective-permute-start | bytes 1769480 | tf_op jit(solution)/shard_map/ppermute | solution.py:1106
  56.4 25.4 %collective-permute-start.10 = (bf16[512,768]{1,0:T(8,128)(2,1)S(1)}, bf16[512,768]{1,0:T(8,128)(2,1)}, u32[]{:S(2)}, u32[]{:S(2)}) collective-permute-start(bf16[512,768]{1,0:T(8,128)(2,1)S(1)} %collective-permute-done.3), channel_id=1, source_target_pairs={{1,2},{2,3},{5,6},{6,7},{9,10},{10,11},{13,14},{14,15},{17,18},{18... | collective-permute-start | bytes 2359304 | tf_op jit(solution)/shard_map/ppermute | solution.py:1106
  58.7 24.4 %collective-permute-start.11 = (bf16[512,768]{1,0:T(8,128)(2,1)S(1)}, bf16[512,768]{1,0:T(8,128)(2,1)}, u32[]{:S(2)}, u32[]{:S(2)}) collective-permute-start(bf16[512,768]{1,0:T(8,128)(2,1)S(1)} %collective-permute-done.4), channel_id=1, source_target_pairs={{1,0},{2,1},{5,4},{6,5},{9,8},{10,9},{13,12},{14,13},{17,16},{18,1... | collective-permute-start | bytes 2359304 | tf_op jit(solution)/shard_map/ppermute | solution.py:1106
  67.0 17.4 %collective-permute-start.19 = (bf16[432,768]{1,0:T(8,128)(2,1)S(1)}, bf16[432,768]{1,0:T(8,128)(2,1)S(1)}, u32[]{:S(2)}, u32[]{:S(2)}) collective-permute-start(bf16[432,768]{1,0:T(8,128)(2,1)S(1)} %fusion.6), channel_id=1, source_target_pairs={{0,16},{4,20},{8,24},{12,28},{16,0},{20,4},{24,8},{28,12},{1,17},{... | collective-permute-start | bytes 1990664 | tf_op jit(solution)/shard_map/ppermute | solution.py:319
  67.6 17.1 %collective-permute-start.18 = (bf16[432,768]{1,0:T(8,128)(2,1)S(1)}, bf16[432,768]{1,0:T(8,128)(2,1)}, u32[]{:S(2)}, u32[]{:S(2)}) collective-permute-start(bf16[432,768]{1,0:T(8,128)(2,1)S(1)} %pad_maximum_fusion.4), channel_id=1, source_target_pairs={{0,8},{4,12},{8,0},{12,4},{16,24},{20,28},{24,16},{28,20},{1,9},{5... | collective-permute-start | bytes 1990664 | tf_op jit(solution)/shard_map/ppermute | solution.py:319
  86.6 39.1 %collective-permute-start.20 = (bf16[864,768]{1,0:T(8,128)(2,1)S(1)}, bf16[864,768]{1,0:T(8,128)(2,1)}, u32[]{:S(2)}, u32[]{:S(2)}) collective-permute-start(bf16[864,768]{1,0:T(8,128)(2,1)S(1)} %pad_maximum_fusion.1.refs_7_), channel_id=1, source_target_pairs={{0,16},{4,20},{8,24},{12,28},{16,0},{20,4},{24,8},{28,12},{1,17},{... | collective-permute-start | bytes 3981320 | tf_op jit(solution)/shard_map/ppermute | solution.py:319
  88.2 37.5 %collective-permute-start.21 = (bf16[864,768]{1,0:T(8,128)(2,1)S(1)}, bf16[864,768]{1,0:T(8,128)(2,1)}, u32[]{:S(2)}, u32[]{:S(2)}) collective-permute-start(bf16[864,768]{1,0:T(8,128)(2,1)S(1)} %pad_maximum_fusion.2.refs_11_), channel_id=1, source_target_pairs={{0,8},{4,12},{8,0},{12,4},{16,24},{20,28},{24,16},{28,20},{1,9},{5... | collective-permute-start | bytes 3981320 | tf_op jit(solution)/shard_map/ppermute | solution.py:319
  89.4 22.1 %collective-permute-start.17 = (bf16[512,768]{1,0:T(8,128)(2,1)S(1)}, bf16[512,768]{1,0:T(8,128)(2,1)S(1)}, u32[]{:S(2)}, u32[]{:S(2)}) collective-permute-start(bf16[512,768]{1,0:T(8,128)(2,1)S(1)} %broadcast_select_fusion.1.refs_1_.refs_2_), channel_id=1, source_target_pairs={{1,0},{2,3},{5,4},{6,7},{9,8},{10,11},{13,12},{14,15},{17,16},{18,... | collective-permute-start | bytes 2359304 | tf_op jit(solution)/shard_map/ppermute | solution.py:1106
  91.9 34.4 %collective-permute-start.22 = (bf16[864,768]{1,0:T(8,128)(2,1)S(1)}, bf16[864,768]{1,0:T(8,128)(2,1)}, u32[]{:S(2)}, u32[]{:S(2)}) collective-permute-start(bf16[864,768]{1,0:T(8,128)(2,1)S(1)} %pad_maximum_fusion.1.refs_7_), channel_id=1, source_target_pairs={{0,4},{4,0},{8,12},{12,8},{16,20},{20,16},{24,28},{28,24},{1,5},{5... | collective-permute-start | bytes 3981320 | tf_op jit(solution)/shard_map/ppermute | solution.py:319
  91.9 34.4 %collective-permute-start.24 = (bf16[864,768]{1,0:T(8,128)(2,1)S(1)}, bf16[864,768]{1,0:T(8,128)(2,1)}, u32[]{:S(2)}, u32[]{:S(2)}) collective-permute-start(bf16[864,768]{1,0:T(8,128)(2,1)S(1)} %pad_maximum_fusion.2.refs_11_), channel_id=1, source_target_pairs={{0,4},{4,0},{8,12},{12,8},{16,20},{20,16},{24,28},{28,24},{1,5},{5... | collective-permute-start | bytes 3981320 | tf_op jit(solution)/shard_map/ppermute | solution.py:319
  165.7 21.5 %collective-permute-start.27 = (bf16[5,4,96,768]{3,2,1,0:T(8,128)(2,1)}, bf16[5,4,96,768]{3,2,1,0:T(8,128)(2,1)S(1)}, u32[]{:S(2)}, u32[]{:S(2)}) collective-permute-start(bf16[5,4,96,768]{3,2,1,0:T(8,128)(2,1)} %get-tuple-element.283), channel_id=1, source_target_pairs={{0,4},{4,0},{8,12},{12,8},{16,20},{20,16},{24,28},{28,24},{1,5},{5... | collective-permute-start | bytes 8847368 | tf_op jit(solution)/shard_map/ppermute | solution.py:319
  165.9 21.3 %collective-permute-start.26 = (bf16[4,4,96,768]{3,2,1,0:T(8,128)(2,1)}, bf16[4,4,96,768]{3,2,1,0:T(8,128)(2,1)S(1)}, u32[]{:S(2)}, u32[]{:S(2)}) collective-permute-start(bf16[4,4,96,768]{3,2,1,0:T(8,128)(2,1)} %get-tuple-element.282), channel_id=1, source_target_pairs={{0,4},{4,0},{8,12},{12,8},{16,20},{20,16},{24,28},{28,24},{1,5},{5... | collective-permute-start | bytes 7077896 | tf_op jit(solution)/shard_map/ppermute | solution.py:319
  180.6 27.7 %collective-permute-start.28 = (bf16[512,768]{1,0:T(8,128)(2,1)}, bf16[512,768]{1,0:T(8,128)(2,1)S(1)}, u32[]{:S(2)}, u32[]{:S(2)}) collective-permute-start(bf16[512,768]{1,0:T(8,128)(2,1)} %get-tuple-element.288), channel_id=1, source_target_pairs={{0,1},{3,2},{4,5},{7,6},{8,9},{11,10},{12,13},{15,14},{16,17},{19,... | collective-permute-start | bytes 2359304 | tf_op jit(solution)/shard_map/ppermute | solution.py:1106
  207.4 34.3 %collective-permute-start.32 = (bf16[5,2,96,768]{3,2,1,0:T(8,128)(2,1)}, bf16[5,2,96,768]{3,2,1,0:T(8,128)(2,1)S(1)}, u32[]{:S(2)}, u32[]{:S(2)}) collective-permute-start(bf16[5,2,96,768]{3,2,1,0:T(8,128)(2,1)} %get-tuple-element.298), channel_id=1, source_target_pairs={{0,8},{4,12},{8,0},{12,4},{16,24},{20,28},{24,16},{28,20},{1,9},{5... | collective-permute-start | bytes 4423688 | tf_op jit(solution)/shard_map/ppermute | solution.py:319
  209.9 18.8 %collective-permute-start.30 = (bf16[512,768]{1,0:T(8,128)(2,1)S(1)}, bf16[512,768]{1,0:T(8,128)(2,1)S(1)}, u32[]{:S(2)}, u32[]{:S(2)}) collective-permute-start(bf16[512,768]{1,0:T(8,128)(2,1)S(1)} %add_convert_fusion.1), channel_id=1, source_target_pairs={{3,2},{2,1},{7,6},{6,5},{11,10},{10,9},{15,14},{14,13},{19,18},{18... | collective-permute-start | bytes 2359304 | tf_op jit(solution)/shard_map/ppermute | solution.py:1106
  210.6 27.7 %collective-permute-start.31 = (bf16[4,2,96,768]{3,2,1,0:T(8,128)(2,1)}, bf16[4,2,96,768]{3,2,1,0:T(8,128)(2,1)S(1)}, u32[]{:S(2)}, u32[]{:S(2)}) collective-permute-start(bf16[4,2,96,768]{3,2,1,0:T(8,128)(2,1)} %get-tuple-element.297), channel_id=1, source_target_pairs={{0,16},{4,20},{8,24},{12,28},{16,0},{20,4},{24,8},{28,12},{1,17},{... | collective-permute-start | bytes 3538952 | tf_op jit(solution)/shard_map/ppermute | solution.py:319
  212.2 18.3 %collective-permute-start.29 = (bf16[512,768]{1,0:T(8,128)(2,1)S(1)}, bf16[512,768]{1,0:T(8,128)(2,1)S(1)}, u32[]{:S(2)}, u32[]{:S(2)}) collective-permute-start(bf16[512,768]{1,0:T(8,128)(2,1)S(1)} %add_convert_fusion.1), channel_id=1, source_target_pairs={{0,1},{1,2},{4,5},{5,6},{8,9},{9,10},{12,13},{13,14},{16,17},{17,1... | collective-permute-start | bytes 2359304 | tf_op jit(solution)/shard_map/ppermute | solution.py:1106
  231.0 34.3 %collective-permute-start.33 = (bf16[512,768]{1,0:T(8,128)(2,1)S(1)}, bf16[512,768]{1,0:T(8,128)(2,1)S(1)}, u32[]{:S(2)}, u32[]{:S(2)}) collective-permute-start(bf16[512,768]{1,0:T(8,128)(2,1)S(1)} %select_convert_fusion), channel_id=1, source_target_pairs={{0,1},{1,2},{2,3},{4,5},{5,6},{6,7},{8,9},{9,10},{10,11},{12,13},{... | collective-permute-start | bytes 2359304 | tf_op jit(solution)/shard_map/ppermute | solution.py:1106
  236.5 28.8 %collective-permute-start.34 = (bf16[512,768]{1,0:T(8,128)(2,1)S(1)}, bf16[512,768]{1,0:T(8,128)(2,1)S(1)}, u32[]{:S(2)}, u32[]{:S(2)}) collective-permute-start(bf16[512,768]{1,0:T(8,128)(2,1)S(1)} %add_convert_fusion), channel_id=1, source_target_pairs={{3,2},{2,1},{1,0},{7,6},{6,5},{5,4},{11,10},{10,9},{9,8},{15,14},{... | collective-permute-start | bytes 2359304 | tf_op jit(solution)/shard_map/ppermute | solution.py:1106
  262.9 17.7 %collective-permute-start.38 = (bf16[5,1,96,768]{3,2,1,0:T(8,128)(2,1)}, bf16[5,1,96,768]{3,2,1,0:T(8,128)(2,1)}, u32[]{:S(2)}, u32[]{:S(2)}) collective-permute-start(bf16[5,1,96,768]{3,2,1,0:T(8,128)(2,1)} %get-tuple-element.316), channel_id=1, source_target_pairs={{0,16},{4,20},{8,24},{12,28},{16,0},{20,4},{24,8},{28,12},{1,17},{... | collective-permute-start | bytes 2211848 | tf_op jit(solution)/shard_map/ppermute | solution.py:319
  289.2 15.8 %collective-permute-start.41 = (bf16[3,2,96,384]{3,2,1,0:T(8,128)(2,1)}, bf16[3,2,96,384]{3,2,1,0:T(8,128)(2,1)S(1)}, u32[]{:S(2)}, u32[]{:S(2)}) collective-permute-start(bf16[3,2,96,384]{3,2,1,0:T(8,128)(2,1)} %get-tuple-element.341), channel_id=1, source_target_pairs={{0,8},{4,12},{8,0},{12,4},{16,24},{20,28},{24,16},{28,20},{1,9},{5... | collective-permute-start | bytes 1327112 | tf_op jit(solution)/shard_map/ppermute | solution.py:319
  (75 other events, 647.8 us)

commit v16 on v14

--- a/solution.py
+++ b/solution.py
@@ -73,6 +73,7 @@
         value_outs[n][...] = values[n]
     rows = q_pair.shape[0]
     size = keys[0].shape[0]
+    values = [jnp.concatenate([value, jnp.ones((size, PAIR), low)], axis=1) for value in values]
     place = lax.broadcasted_iota(jnp.int32, (1, size), 1)
     lower = first_half((rows, PAIR))
     parts = []
@@ -86,13 +87,12 @@
         highest = functools.reduce(
             jnp.maximum, [jnp.max(score, axis=-1, keepdims=True) for score in scores]
         )
-        totals = jnp.zeros_like(highest)
-        mixed = jnp.zeros((rows, PAIR), full)
+        weighed = None
         for n in range(count):
-            exp_scores = jnp.exp(scores[n] - highest)
-            totals = totals + jnp.sum(exp_scores, axis=-1, keepdims=True)
-            mixed = mixed + dot_of(exp_scores.astype(low), values[n], 1, 0)
-        parts.append((highest, totals, mixed))
+            exp_scores = jnp.exp(scores[n] - highest).astype(low)
+            part = dot_of(exp_scores, values[n], 1, 0)
+            weighed = part if weighed is None else weighed + part
+        parts.append((highest, weighed[:, PAIR:], weighed[:, :PAIR]))
     top = jnp.where(lower, parts[0][0], parts[1][0])
     total = jnp.where(lower, parts[0][1], parts[1][1])
     mixed = jnp.where(lower, parts[0][2], parts[1][2])

time: 353 us -> 352 us (level)
  no operation moved by 1% of the time
where the time goes in v16:
time: 352 us; the launch traced here: 346 us
  Pallas kernels  174 us (49%)
  starting transfers between devices  68.8 us (20%)
  waiting for transfers between devices  53.9 us (15%)
  local copies, waits for them, and re-layouts  21.5 us (6%)
  other arithmetic  19.6 us (6%)
  between operations  5.39 us (2%)
    pallas_call x4, Pallas kernels, attend_backward(): pl.pallas_call(functools.partial(backward_kernel, number, first, last, fo...  66.7 us
    pallas_call x3, Pallas kernels, attend_forward(): pl.pallas_call(functools.partial(forward_kernel, numbers, first, final),...  44.1 us
    ppermute x43, starting transfers between devices, swap(): return lax.ppermute(value, axis, [(i, i ^ bit) for i in range(count)])  41.8 us
    ppermute x43, waiting for transfers between devices, swap(): return lax.ppermute(value, axis, [(i, i ^ bit) for i in range(count)])  40.8 us
    pallas_call x1, Pallas kernels, middle_call(): pl.pallas_call(functools.partial(middle_kernel, plan, block, len(arrays))...  33.7 us
    ppermute x12, starting transfers between devices, shards(): along = lambda value, pairs: lax.ppermute(value, 'mp', pairs)  26.9 us
    pallas_call x1, Pallas kernels, qkv_grads(): pl.pallas_call(functools.partial(qkv_grad_kernel, count), out_shape=[jax....  13.1 us
    ppermute x12, waiting for transfers between devices, shards(): along = lambda value, pairs: lax.ppermute(value, 'mp', pairs)  13 us
  transfers between devices with their start and end apart: 55, of which 22 were waited for; matrix products, arithmetic and copies ran while one was open for 8% of the time, Pallas kernels for 41%

profile of v16, /device:TPU:0, one launch (start us, length us, event | category | flops | bytes accessed | tf_op | source)
XLA Modules:
  0.0 346.1 jit_solution(11530687642355255261)
XLA Ops:
  30.7 3.2 collective-permute-start.3
  38.6 6.4 %collective-permute-done.8.refs_1_ = bf16[288,768]{1,0:T(8,128)(2,1)S(1)} collective-permute-done((bf16[288,768]{1,0:T(8,128)(2,1)S(1)}, bf16[288,768]{1,0:T(8,128)(2,1)S(1)}, u32[]{:S(2)}, u32[]{:S(2)}) %collective-permute-start.8) | collective-permute-done | bytes 442400 | tf_op jit(solution)/shard_map/ppermute | solution.py:319
  48.5 7.8 %collective-permute-done.4 = bf16[512,768]{1,0:T(8,128)(2,1)S(1)} collective-permute-done((bf16[512,768]{1,0:T(8,128)(2,1)S(1)}, bf16[512,768]{1,0:T(8,128)(2,1)S(1)}, u32[]{:S(2)}, u32[]{:S(2)}) %collective-permute-start.4) | collective-permute-done | bytes 786464 | tf_op jit(solution)/shard_map/ppermute | solution.py:1100
  61.6 4.1 %place.1 = (bf16[768,768]{1,0:T(8,128)(2,1)}, bf16[768,1536]{1,0:T(8,128)(2,1)}) custom-call(bf16[288,768]{1,0:T(8,128)(2,1)} %copy-done.12, bf16[288,768]{1,0:T(8,128)(2,1)} %copy-done.26, bf16[288,768]{1,0:T(8,128)(2,1)} %copy-done.28, bf16[288,768]{1,0:T(8,128)(2,1)} %copy-done.29, bf16[288,768]{1,0:T(8,128)(2,1)} %copy-done.11, ...), custom_call_target="tpu_custom_call" | custom-call | flops 1048576 | bytes 65536 | tf_op jit(solution)/shard_map/place/pallas_call | solution.py:434
  68.7 13.0 %attend_forward.3 = (bf16[512,768]{1,0:T(8,128)(2,1)}, bf16[512,768]{1,0:T(8,128)(2,1)}, bf16[512,768]{1,0:T(8,128)(2,1)}, f32[512,768]{1,0:T(8,128)}, f32[512,768]{1,0:T(8,128)}, /*index=5*/f32[512,768]{1,0:T(8,128)}) custom-call(s32[6]{0:T(128)} %stack.42.scalars.refs_0_, bf16[512,768]{1,0:T(8,128)(2,1)} %copy-done.1, ...), custom_call_target="tpu_custom_call" | custom-call | flops 1048576 | bytes 65536 | tf_op jit(solution)/shard_map/attend_forward/pallas_call | solution.py:129
  92.4 18.2 %attend_forward.4 = (bf16[512,768]{1,0:T(8,128)(2,1)}, bf16[512,768]{1,0:T(8,128)(2,1)}, bf16[512,768]{1,0:T(8,128)(2,1)}, bf16[512,768]{1,0:T(8,128)(2,1)}, f32...) custom-call(s32[6]{0:T(128)} %stack.42.scalars.refs_0_, ...), custom_call_target="tpu_custom_call" | custom-call | flops 1048576 | bytes 65536 | tf_op jit(solution)/shard_map/attend_forward/pallas_call | solution.py:129
  112.5 12.9 %attend_forward.5 = (bf16[512,768]{1,0:T(8,128)(2,1)}, bf16[512,768]{1,0:T(8,128)(2,1)}, f32[512,768]{1,0:T(8,128)}, f32[512,768]{1,0:T(8,128)}) custom-call(s32[6]{0:T(128)} %stack.42.scalars.refs_0_, bf16[512,768]{1,0:T(8,128)(2,1)} %broadcast_select_fusion.2.refs_0_.refs_3_, bf16[768,1536]{1,0:T(8,128)(2,1)} %get-tuple-element.225.refs_1_.refs_2_.refs_3_.wk_ref.wv_ref, ...), custom_call_target="tpu_custom_call" | custom-call | flops 1048576 | bytes 65536 | tf_op jit(solution)/shard_map/attend_forward/pallas_call | solution.py:129
  131.8 33.7 %middle.1 = (bf16[512,768]{1,0:T(8,128)(2,1)}, f32[512,768]{1,0:T(8,128)}, bf16[512,768]{1,0:T(8,128)(2,1)}, bf16[4,4,96,768]{3,2,1,0:T(8,128)(2,1)}, bf16[4,4,9...) custom-call(s32[6]{0:T(128)} %stack.42.scalars.refs_0_, ...), custom_call_target="tpu_custom_call" | custom-call | flops 1048576 | bytes 65536 | tf_op jit(solution)/shard_map/middle/pallas_call | solution.py:689
  166.0 14.3 %attend_backward.4 = (f32[512,768]{1,0:T(8,128)}, bf16[512,768]{1,0:T(8,128)(2,1)}, bf16[512,768]{1,0:T(8,128)(2,1)}, bf16[512,768]{1,0:T(8,128)(2,1)}) custom-call(s32[6]{0:T(128)} %stack.42.scalars.refs_0_, bf16[512,768]{1,0:T(8,128)(2,1)} %get-tuple-element.238.refs_5_.refs_4_.q_ref, bf16[512,768]{1,0:T(8,128)(2,1)} %get-tuple-element.274.k_ref, ...), custom_call_target="tpu_custom_call" | custom-call | flops 1048576 | bytes 65536 | tf_op jit(solution)/shard_map/attend_backward/pallas_call | solution.py:266
  180.3 6.0 %collective-permute-start.28 = (bf16[512,768]{1,0:T(8,128)(2,1)}, bf16[512,768]{1,0:T(8,128)(2,1)S(1)}, u32[]{:S(2)}, u32[]{:S(2)}) collective-permute-start(bf16[512,768]{1,0:T(8,128)(2,1)} %get-tuple-element.288), channel_id=1, source_target_pairs={{0,1},{3,2},{4,5},{7,6},{8,9},{11,10},{12,13},{15,14},{16,17},{19,... | collective-permute-start | bytes 2359304 | tf_op jit(solution)/shard_map/ppermute | solution.py:1100
  188.6 17.9 %attend_backward.5 = (f32[512,768]{1,0:T(8,128)}, bf16[512,768]{1,0:T(8,128)(2,1)}, bf16[512,768]{1,0:T(8,128)(2,1)}, f32[512,768]{1,0:T(8,128)}, bf16[4,2,96,76...) custom-call(s32[6]{0:T(128)} %stack.42.scalars.refs_0_, ...), custom_call_target="tpu_custom_call" | custom-call | flops 1048576 | bytes 65536 | tf_op jit(solution)/shard_map/attend_backward/pallas_call | solution.py:266
  213.0 14.9 %attend_backward.6 = (f32[512,768]{1,0:T(8,128)}, bf16[512,768]{1,0:T(8,128)(2,1)}, bf16[512,768]{1,0:T(8,128)(2,1)}, f32[512,768]{1,0:T(8,128)}) custom-call(s32[6]{0:T(128)} %stack.42.scalars.refs_0_, bf16[512,768]{1,0:T(8,128)(2,1)} %get-tuple-element.238.refs_5_.refs_4_.q_ref, bf16[512,768]{1,0:T(8,128)(2,1)} %get-tuple-element.258.k_ref, ...), custom_call_target="tpu_custom_call" | custom-call | flops 1048576 | bytes 65536 | tf_op jit(solution)/shard_map/attend_backward/pallas_call | solution.py:266
  230.3 5.5 %collective-permute-start.33 = (bf16[512,768]{1,0:T(8,128)(2,1)S(1)}, bf16[512,768]{1,0:T(8,128)(2,1)S(1)}, u32[]{:S(2)}, u32[]{:S(2)}) collective-permute-start(bf16[512,768]{1,0:T(8,128)(2,1)S(1)} %select_convert_fusion), channel_id=1, source_target_pairs={{0,1},{1,2},{2,3},{4,5},{5,6},{6,7},{8,9},{9,10},{10,11},{12,13},{... | collective-permute-start | bytes 2359304 | tf_op jit(solution)/shard_map/ppermute | solution.py:1100
  237.3 3.5 %collective-permute-done.32.refs_5_ = bf16[5,2,96,768]{3,2,1,0:T(8,128)(2,1)S(1)} collective-permute-done((bf16[5,2,96,768]{3,2,1,0:T(8,128)(2,1)}, bf16[5,2,96,768]{3,2,1,0:T(8,128)(2,1)S(1)}, u32[]{:S(2)}, u32[]{:S(2)}) %collective-permute-start.32) | collective-permute-done | bytes 1474592 | tf_op jit(solution)/shard_map/ppermute | solution.py:319
  241.9 19.7 %attend_backward.7 = (bf16[512,768]{1,0:T(8,128)(2,1)}, bf16[512,768]{1,0:T(8,128)(2,1)}, bf16[512,768]{1,0:T(8,128)(2,1)}, f32[512,768]{1,0:T(8,128)}, bf16[4,1...) custom-call(s32[6]{0:T(128)} %stack.42.scalars.refs_0_, ...), custom_call_target="tpu_custom_call" | custom-call | flops 1048576 | bytes 65536 | tf_op jit(solution)/shard_map/attend_backward/pallas_call | solution.py:266
  264.0 13.1 %qkv_grads.1 = (bf16[3,4,96,384]{3,2,1,0:T(8,128)(2,1)}, bf16[3,4,96,384]{3,2,1,0:T(8,128)(2,1)}, bf16[3,4,96,384]{3,2,1,0:T(8,128)(2,1)}, bf16[3,4,96,384]{3,2,1,0:T(8,128)(2,1)}, f32[16,768]{1,0:T(8,128)}) custom-call(bf16[512,768]{1,0:T(8,128)(2,1)} %copy-done.1, bf16[512,768]{1,0:T(8,128)(2,1)} %broadcast_select_fusion.refs_0_.refs_1_, ...), custom_call_target="tpu_custom_call" | custom-call | flops 1048576 | bytes 65536 | tf_op jit(solution)/shard_map/qkv_grads/pallas_call | solution.py:839
  283.9 4.0 %fold.2 = (bf16[3,2,96,384]{3,2,1,0:T(8,128)(2,1)}, bf16[3,2,96,384]{3,2,1,0:T(8,128)(2,1)}, bf16[3,2,96,384]{3,2,1,0:T(8,128)(2,1)}, bf16[3,2,96,384]{3,2,1,0:T(8,128)(2,1)}) custom-call(bf16[3,4,96,384]{3,2,1,0:T(8,128)(2,1)} %get-tuple-element.326.refs_0_, bf16[3,4,96,384]{3,2,1,0:T(8,128)(2,1)} %collective-permute-done.35.refs_1_, ...), custom_call_target="tpu_custom_call" | custom-call | bytes 16777216 | tf_op jit(solution)/shard_map/fold/pallas_call | solution.py:767
  290.2 5.2 %last_norm.1 = (f32[512,768]{1,0:T(8,128)}, f32[24,768]{1,0:T(8,128)}) custom-call(bf16[512,768]{1,0:T(8,128)(2,1)} %token_ref, f32[512,768]{1,0:T(8,128)} %get-tuple-element.344.first_ref, bf16[512,768]{1,0:T(8,128)(2,1)} %copy-done.20, bf16[512,768]{1,0:T(8,128)(2,1)} %copy-done.21, f32[512,768]{1,0:T(8,128)} %get-tuple-element.345.middle_ref, ...), custom_call_target="tpu_custom_call" | custom-call | flops 1048576 | bytes 65536 | tf_op jit(solution)/shard_map/last_norm/pallas_call | solution.py:899
  295.3 3.9 %collective-permute-done.39 = bf16[2,216,768]{2,1,0:T(8,128)(2,1)} collective-permute-done((bf16[2,216,768]{2,1,0:T(8,128)(2,1)S(1)}, bf16[2,216,768]{2,1,0:T(8,128)(2,1)}, u32[]{:S(2)}, u32[]{:S(2)}) %collective-permute-start.39) | collective-permute-done | bytes 663584 | tf_op jit(solution)/shard_map/ppermute | solution.py:319
  305.2 3.2 fold.3
  311.7 5.6 %collective-permute-done.45 = bf16[216,768]{1,0:T(8,128)(2,1)S(1)} collective-permute-done((bf16[216,768]{1,0:T(8,128)(2,1)S(1)}, bf16[216,768]{1,0:T(8,128)(2,1)S(1)}, u32[]{:S(2)}, u32[]{:S(2)}) %collective-permute-start.45) | collective-permute-done | bytes 331808 | tf_op jit(solution)/shard_map/ppermute | solution.py:319
  324.8 3.4 collective-permute-start.50
  329.6 3.8 %collective-permute-start.53 = (bf16[3,96,192]{2,1,0:T(8,128)(2,1)S(1)}, bf16[3,96,192]{2,1,0:T(8,128)(2,1)S(1)}, u32[]{:S(2)}, u32[]{:S(2)}) collective-permute-start(bf16[3,96,192]{2,1,0:T(8,128)(2,1)S(1)} %get-tuple-element.368), channel_id=1, source_target_pairs={{0,2},{1,3},{2,0},{3,1},{4,6},{5,7},{6,4},{7,5},{8,10},{9,11},{10,... | collective-permute-start | bytes 331784 | tf_op jit(solution)/shard_map/ppermute | solution.py:319
  339.5 4.8 %collective-permute-done.53 = bf16[3,96,192]{2,1,0:T(8,128)(2,1)S(1)} collective-permute-done((bf16[3,96,192]{2,1,0:T(8,128)(2,1)S(1)}, bf16[3,96,192]{2,1,0:T(8,128)(2,1)S(1)}, u32[]{:S(2)}, u32[]{:S(2)}) %collective-permute-start.53) | collective-permute-done | bytes 110624 | tf_op jit(solution)/shard_map/ppermute | solution.py:319
  (257 shorter events, 112.9 us)
Async XLA Ops:
  6.7 16.4 %collective-permute-start.1 = (bf16[192,768]{1,0:T(8,128)(2,1)S(1)}, bf16[192,768]{1,0:T(8,128)(2,1)S(1)}, u32[]{:S(2)}, u32[]{:S(2)}) collective-permute-start(bf16[192,768]{1,0:T(8,128)(2,1)S(1)} %pad_maximum_fusion.9), channel_id=1, source_target_pairs={{0,1},{1,0},{2,3},{3,2},{4,5},{5,4},{6,7},{7,6},{8,9},{9,8},{10,11... | collective-permute-start | bytes 884744 | tf_op jit(solution)/shard_map/ppermute | solution.py:319
  30.7 17.8 %collective-permute-start.3 = (bf16[512,768]{1,0:T(8,128)(2,1)S(1)}, bf16[512,768]{1,0:T(8,128)(2,1)S(1)}, u32[]{:S(2)}, u32[]{:S(2)}) collective-permute-start(bf16[512,768]{1,0:T(8,128)(2,1)S(1)} %add_convert_fusion.2.refs_0_), channel_id=1, source_target_pairs={{0,1},{1,2},{2,3},{4,5},{5,6},{6,7},{8,9},{9,10},{10,11},{12,13},{... | collective-permute-start | bytes 2359304 | tf_op jit(solution)/shard_map/ppermute | solution.py:1100
  34.0 22.4 %collective-permute-start.4 = (bf16[512,768]{1,0:T(8,128)(2,1)S(1)}, bf16[512,768]{1,0:T(8,128)(2,1)S(1)}, u32[]{:S(2)}, u32[]{:S(2)}) collective-permute-start(bf16[512,768]{1,0:T(8,128)(2,1)S(1)} %add_convert_fusion.2.refs_0_), channel_id=1, source_target_pairs={{1,0},{2,1},{3,2},{5,4},{6,5},{7,6},{9,8},{10,9},{11,10},{13,12},{... | collective-permute-start | bytes 2359304 | tf_op jit(solution)/shard_map/ppermute | solution.py:1100
  37.3 28.5 %collective-permute-start.12 = (bf16[384,768]{1,0:T(8,128)(2,1)}, bf16[384,768]{1,0:T(8,128)(2,1)}, u32[]{:S(2)}, u32[]{:S(2)}) collective-permute-start(bf16[384,768]{1,0:T(8,128)(2,1)} %collective-permute-done.7), channel_id=1, source_target_pairs={{1,0},{2,3},{5,4},{6,7},{9,8},{10,11},{13,12},{14,15},{17,16},{18,... | collective-permute-start | bytes 1769480 | tf_op jit(solution)/shard_map/ppermute | solution.py:1100
  56.4 25.4 %collective-permute-start.10 = (bf16[512,768]{1,0:T(8,128)(2,1)S(1)}, bf16[512,768]{1,0:T(8,128)(2,1)}, u32[]{:S(2)}, u32[]{:S(2)}) collective-permute-start(bf16[512,768]{1,0:T(8,128)(2,1)S(1)} %collective-permute-done.3), channel_id=1, source_target_pairs={{1,2},{2,3},{5,6},{6,7},{9,10},{10,11},{13,14},{14,15},{17,18},{18... | collective-permute-start | bytes 2359304 | tf_op jit(solution)/shard_map/ppermute | solution.py:1100
  58.7 24.4 %collective-permute-start.11 = (bf16[512,768]{1,0:T(8,128)(2,1)S(1)}, bf16[512,768]{1,0:T(8,128)(2,1)}, u32[]{:S(2)}, u32[]{:S(2)}) collective-permute-start(bf16[512,768]{1,0:T(8,128)(2,1)S(1)} %collective-permute-done.4), channel_id=1, source_target_pairs={{1,0},{2,1},{5,4},{6,5},{9,8},{10,9},{13,12},{14,13},{17,16},{18,1... | collective-permute-start | bytes 2359304 | tf_op jit(solution)/shard_map/ppermute | solution.py:1100
  67.0 17.4 %collective-permute-start.19 = (bf16[432,768]{1,0:T(8,128)(2,1)S(1)}, bf16[432,768]{1,0:T(8,128)(2,1)S(1)}, u32[]{:S(2)}, u32[]{:S(2)}) collective-permute-start(bf16[432,768]{1,0:T(8,128)(2,1)S(1)} %fusion.6), channel_id=1, source_target_pairs={{0,16},{4,20},{8,24},{12,28},{16,0},{20,4},{24,8},{28,12},{1,17},{... | collective-permute-start | bytes 1990664 | tf_op jit(solution)/shard_map/ppermute | solution.py:319
  67.6 17.1 %collective-permute-start.18 = (bf16[432,768]{1,0:T(8,128)(2,1)S(1)}, bf16[432,768]{1,0:T(8,128)(2,1)}, u32[]{:S(2)}, u32[]{:S(2)}) collective-permute-start(bf16[432,768]{1,0:T(8,128)(2,1)S(1)} %pad_maximum_fusion.4), channel_id=1, source_target_pairs={{0,8},{4,12},{8,0},{12,4},{16,24},{20,28},{24,16},{28,20},{1,9},{5... | collective-permute-start | bytes 1990664 | tf_op jit(solution)/shard_map/ppermute | solution.py:319
  86.6 38.8 %collective-permute-start.20 = (bf16[864,768]{1,0:T(8,128)(2,1)S(1)}, bf16[864,768]{1,0:T(8,128)(2,1)}, u32[]{:S(2)}, u32[]{:S(2)}) collective-permute-start(bf16[864,768]{1,0:T(8,128)(2,1)S(1)} %pad_maximum_fusion.1.refs_7_), channel_id=1, source_target_pairs={{0,16},{4,20},{8,24},{12,28},{16,0},{20,4},{24,8},{28,12},{1,17},{... | collective-permute-start | bytes 3981320 | tf_op jit(solution)/shard_map/ppermute | solution.py:319
  88.2 37.2 %collective-permute-start.21 = (bf16[864,768]{1,0:T(8,128)(2,1)S(1)}, bf16[864,768]{1,0:T(8,128)(2,1)}, u32[]{:S(2)}, u32[]{:S(2)}) collective-permute-start(bf16[864,768]{1,0:T(8,128)(2,1)S(1)} %pad_maximum_fusion.2.refs_11_), channel_id=1, source_target_pairs={{0,8},{4,12},{8,0},{12,4},{16,24},{20,28},{24,16},{28,20},{1,9},{5... | collective-permute-start | bytes 3981320 | tf_op jit(solution)/shard_map/ppermute | solution.py:319
  89.4 22.1 %collective-permute-start.17 = (bf16[512,768]{1,0:T(8,128)(2,1)S(1)}, bf16[512,768]{1,0:T(8,128)(2,1)S(1)}, u32[]{:S(2)}, u32[]{:S(2)}) collective-permute-start(bf16[512,768]{1,0:T(8,128)(2,1)S(1)} %broadcast_select_fusion.1.refs_1_.refs_2_), channel_id=1, source_target_pairs={{1,0},{2,3},{5,4},{6,7},{9,8},{10,11},{13,12},{14,15},{17,16},{18,... | collective-permute-start | bytes 2359304 | tf_op jit(solution)/shard_map/ppermute | solution.py:1100
  91.9 34.1 %collective-permute-start.22 = (bf16[864,768]{1,0:T(8,128)(2,1)S(1)}, bf16[864,768]{1,0:T(8,128)(2,1)}, u32[]{:S(2)}, u32[]{:S(2)}) collective-permute-start(bf16[864,768]{1,0:T(8,128)(2,1)S(1)} %pad_maximum_fusion.1.refs_7_), channel_id=1, source_target_pairs={{0,4},{4,0},{8,12},{12,8},{16,20},{20,16},{24,28},{28,24},{1,5},{5... | collective-permute-start | bytes 3981320 | tf_op jit(solution)/shard_map/ppermute | solution.py:319
  91.9 34.1 %collective-permute-start.24 = (bf16[864,768]{1,0:T(8,128)(2,1)S(1)}, bf16[864,768]{1,0:T(8,128)(2,1)}, u32[]{:S(2)}, u32[]{:S(2)}) collective-permute-start(bf16[864,768]{1,0:T(8,128)(2,1)S(1)} %pad_maximum_fusion.2.refs_11_), channel_id=1, source_target_pairs={{0,4},{4,0},{8,12},{12,8},{16,20},{20,16},{24,28},{28,24},{1,5},{5... | collective-permute-start | bytes 3981320 | tf_op jit(solution)/shard_map/ppermute | solution.py:319
  165.5 20.9 %collective-permute-start.27 = (bf16[5,4,96,768]{3,2,1,0:T(8,128)(2,1)}, bf16[5,4,96,768]{3,2,1,0:T(8,128)(2,1)S(1)}, u32[]{:S(2)}, u32[]{:S(2)}) collective-permute-start(bf16[5,4,96,768]{3,2,1,0:T(8,128)(2,1)} %get-tuple-element.283), channel_id=1, source_target_pairs={{0,4},{4,0},{8,12},{12,8},{16,20},{20,16},{24,28},{28,24},{1,5},{5... | collective-permute-start | bytes 8847368 | tf_op jit(solution)/shard_map/ppermute | solution.py:319
  165.7 20.6 %collective-permute-start.26 = (bf16[4,4,96,768]{3,2,1,0:T(8,128)(2,1)}, bf16[4,4,96,768]{3,2,1,0:T(8,128)(2,1)S(1)}, u32[]{:S(2)}, u32[]{:S(2)}) collective-permute-start(bf16[4,4,96,768]{3,2,1,0:T(8,128)(2,1)} %get-tuple-element.282), channel_id=1, source_target_pairs={{0,4},{4,0},{8,12},{12,8},{16,20},{20,16},{24,28},{28,24},{1,5},{5... | collective-permute-start | bytes 7077896 | tf_op jit(solution)/shard_map/ppermute | solution.py:319
  180.3 27.0 %collective-permute-start.28 = (bf16[512,768]{1,0:T(8,128)(2,1)}, bf16[512,768]{1,0:T(8,128)(2,1)S(1)}, u32[]{:S(2)}, u32[]{:S(2)}) collective-permute-start(bf16[512,768]{1,0:T(8,128)(2,1)} %get-tuple-element.288), channel_id=1, source_target_pairs={{0,1},{3,2},{4,5},{7,6},{8,9},{11,10},{12,13},{15,14},{16,17},{19,... | collective-permute-start | bytes 2359304 | tf_op jit(solution)/shard_map/ppermute | solution.py:1100
  206.5 34.3 %collective-permute-start.32 = (bf16[5,2,96,768]{3,2,1,0:T(8,128)(2,1)}, bf16[5,2,96,768]{3,2,1,0:T(8,128)(2,1)S(1)}, u32[]{:S(2)}, u32[]{:S(2)}) collective-permute-start(bf16[5,2,96,768]{3,2,1,0:T(8,128)(2,1)} %get-tuple-element.298), channel_id=1, source_target_pairs={{0,8},{4,12},{8,0},{12,4},{16,24},{20,28},{24,16},{28,20},{1,9},{5... | collective-permute-start | bytes 4423688 | tf_op jit(solution)/shard_map/ppermute | solution.py:319
  208.8 19.1 %collective-permute-start.30 = (bf16[512,768]{1,0:T(8,128)(2,1)S(1)}, bf16[512,768]{1,0:T(8,128)(2,1)S(1)}, u32[]{:S(2)}, u32[]{:S(2)}) collective-permute-start(bf16[512,768]{1,0:T(8,128)(2,1)S(1)} %add_convert_fusion.1), channel_id=1, source_target_pairs={{3,2},{2,1},{7,6},{6,5},{11,10},{10,9},{15,14},{14,13},{19,18},{18... | collective-permute-start | bytes 2359304 | tf_op jit(solution)/shard_map/ppermute | solution.py:1100
  209.6 27.7 %collective-permute-start.31 = (bf16[4,2,96,768]{3,2,1,0:T(8,128)(2,1)}, bf16[4,2,96,768]{3,2,1,0:T(8,128)(2,1)S(1)}, u32[]{:S(2)}, u32[]{:S(2)}) collective-permute-start(bf16[4,2,96,768]{3,2,1,0:T(8,128)(2,1)} %get-tuple-element.297), channel_id=1, source_target_pairs={{0,16},{4,20},{8,24},{12,28},{16,0},{20,4},{24,8},{28,12},{1,17},{... | collective-permute-start | bytes 3538952 | tf_op jit(solution)/shard_map/ppermute | solution.py:319
  211.2 18.5 %collective-permute-start.29 = (bf16[512,768]{1,0:T(8,128)(2,1)S(1)}, bf16[512,768]{1,0:T(8,128)(2,1)S(1)}, u32[]{:S(2)}, u32[]{:S(2)}) collective-permute-start(bf16[512,768]{1,0:T(8,128)(2,1)S(1)} %add_convert_fusion.1), channel_id=1, source_target_pairs={{0,1},{1,2},{4,5},{5,6},{8,9},{9,10},{12,13},{13,14},{16,17},{17,1... | collective-permute-start | bytes 2359304 | tf_op jit(solution)/shard_map/ppermute | solution.py:1100
  230.3 33.6 %collective-permute-start.33 = (bf16[512,768]{1,0:T(8,128)(2,1)S(1)}, bf16[512,768]{1,0:T(8,128)(2,1)S(1)}, u32[]{:S(2)}, u32[]{:S(2)}) collective-permute-start(bf16[512,768]{1,0:T(8,128)(2,1)S(1)} %select_convert_fusion), channel_id=1, source_target_pairs={{0,1},{1,2},{2,3},{4,5},{5,6},{6,7},{8,9},{9,10},{10,11},{12,13},{... | collective-permute-start | bytes 2359304 | tf_op jit(solution)/shard_map/ppermute | solution.py:1100
  235.8 28.2 %collective-permute-start.34 = (bf16[512,768]{1,0:T(8,128)(2,1)S(1)}, bf16[512,768]{1,0:T(8,128)(2,1)S(1)}, u32[]{:S(2)}, u32[]{:S(2)}) collective-permute-start(bf16[512,768]{1,0:T(8,128)(2,1)S(1)} %add_convert_fusion), channel_id=1, source_target_pairs={{3,2},{2,1},{1,0},{7,6},{6,5},{5,4},{11,10},{10,9},{9,8},{15,14},{... | collective-permute-start | bytes 2359304 | tf_op jit(solution)/shard_map/ppermute | solution.py:1100
  261.6 17.7 %collective-permute-start.38 = (bf16[5,1,96,768]{3,2,1,0:T(8,128)(2,1)}, bf16[5,1,96,768]{3,2,1,0:T(8,128)(2,1)}, u32[]{:S(2)}, u32[]{:S(2)}) collective-permute-start(bf16[5,1,96,768]{3,2,1,0:T(8,128)(2,1)} %get-tuple-element.316), channel_id=1, source_target_pairs={{0,16},{4,20},{8,24},{12,28},{16,0},{20,4},{24,8},{28,12},{1,17},{... | collective-permute-start | bytes 2211848 | tf_op jit(solution)/shard_map/ppermute | solution.py:319
  287.9 16.4 %collective-permute-start.41 = (bf16[3,2,96,384]{3,2,1,0:T(8,128)(2,1)}, bf16[3,2,96,384]{3,2,1,0:T(8,128)(2,1)S(1)}, u32[]{:S(2)}, u32[]{:S(2)}) collective-permute-start(bf16[3,2,96,384]{3,2,1,0:T(8,128)(2,1)} %get-tuple-element.341), channel_id=1, source_target_pairs={{0,8},{4,12},{8,0},{12,4},{16,24},{20,28},{24,16},{28,20},{1,9},{5... | collective-permute-start | bytes 1327112 | tf_op jit(solution)/shard_map/ppermute | solution.py:319
  (75 other events, 652.3 us)
